TPU v7x, 32 devices: a whole 2x2x4 slice. The times are simulated.
32 devices in a mesh: shard: 16 (over z, y, x), rep: 2 (over core).
Axes of the slice: x: 2, y: 2, z: 4, core: 2. Of those that a mesh axis runs over, the one named last changes fastest.
Arguments:
- tokens: bfloat16 [32768, 1536], P(('shard', 'rep')), may hold values from -6 to 6
- seg_ids: int32 [32, 1024], P(('shard', 'rep')), may hold values from 0 to 5, never falling along the last dimension, each value on 1 to 800 neighbouring positions
- gain_in: bfloat16 [1536], P('shard'), may hold values from 0.5 to 1.5
- w_in: bfloat16 [1536, 6448], P('shard'), may hold values from -0.15625 to 0.15625
- conv_weight: bfloat16 [4, 3328], P(None, 'shard'), may hold values from -3 to 3
- conv_bias: bfloat16 [3328], P('shard'), may hold values from -3 to 3
- dt_bias: float32 [48], replicated, may hold values from -6 to -2
- a_log: float32 [48], replicated, may hold values from 0 to 2.77
- d_skip: float32 [48], replicated, may hold values from 0.5 to 1.5
- gain_out: bfloat16 [3072], P('shard'), may hold values from 0.5 to 1.5
- w_out: bfloat16 [3072, 1536], P('shard'), may hold values from -0.109375 to 0.109375
- cotangent: bfloat16 [32768, 1536], P(('shard', 'rep')), may hold values from -6 to 6
Outputs:
- output: bfloat16 [32768, 1536], P(('shard', 'rep'))
- grad_tokens: bfloat16 [32768, 1536], P(('shard', 'rep'))
- grad_gain_in: float32 [1536], P('shard')
- grad_w_in: float32 [1536, 6448], P('shard')
- grad_conv_weight: float32 [4, 3328], P(None, 'shard')
- grad_conv_bias: float32 [3328], P('shard')
- grad_dt_bias: float32 [48], replicated
- grad_a_log: float32 [48], replicated
- grad_d_skip: float32 [48], replicated
- grad_gain_out: float32 [3072], P('shard')
- grad_w_out: float32 [3072, 1536], P('shard')
Inputs may be any that keep to these rules, and one draw needn't show every extreme that they name: `seg_ids`: within each packed sequence of 1024 tokens the document numbers never fall; each document has 1 to 800 tokens and one has exactly 800.
All inputs are finite; a program needn't handle non-finite values.
Results may differ from a plain program's by a relative error of at most 0.0068.
Values may be sent and summed in bfloat16 or wider, within the bound.
No kernel may reach another device: no remote copies, remote signals or barrier semaphores. Data moves between devices by JAX's collectives and lax.ppermute only.
A program may use at most 384 MiB of HBM per device.

v0:
```python
import jax
import jax.numpy as jnp
from jax import lax
from jax.sharding import PartitionSpec as P

H = 48
P_SIZE = 64
N = 128
SPAN = 256


EPSILON = 1e-05
HIGHEST = lax.Precision.HIGHEST


def rms_rows(values):
    return values * lax.rsqrt(jnp.mean(values * values, axis=-1, keepdims=True) + EPSILON)


def norm_input(values, gain):
    return rms_rows(values) * gain[None, :]


def conv_silu(signal, conv_kernel, conv_shift, seg_row):
    kernel_len = conv_kernel.shape[0]
    summed = conv_shift[None, :] + conv_kernel[kernel_len - 1][None, :] * signal
    for offset in range(1, kernel_len):
        shifted = jnp.concatenate(
            [jnp.zeros((offset, signal.shape[1]), jnp.float32), signal[:-offset]], axis=0
        )
        seg_moved = jnp.concatenate([jnp.full((offset,), -1, jnp.int32), seg_row[:-offset]])
        same_doc = (seg_moved == seg_row).astype(jnp.float32)
        summed = (
            summed + conv_kernel[kernel_len - 1 - offset][None, :] * shifted * same_doc[:, None]
        )
    return jax.nn.silu(summed)


def ssd_scan(values, keys_b, query_c, steps, rates, seg_row):
    length = values.shape[0]
    blocks = length // SPAN
    seg_last = seg_row[SPAN - 1 :: SPAN]
    seg_before = jnp.concatenate([seg_row[:1], seg_last[:-1]])
    position = jnp.arange(SPAN, dtype=jnp.int32)
    causal = position[:, None] >= position[None, :]

    def span_step(state, pieces):
        block_x, block_b, block_c, block_dt, block_seg, seg_prior = pieces
        cumul = jnp.cumsum(block_dt * rates[None, :], axis=0).T
        linked = causal & (block_seg[:, None] == block_seg[None, :])
        gaps = jnp.where(linked[None], cumul[:, :, None] - cumul[:, None, :], 0.0)
        decay = jnp.where(linked[None], jnp.exp(gaps), 0.0)
        scores = jnp.dot(block_c, block_b.T, precision=HIGHEST)
        mixing = decay * scores[None] * block_dt.T[:, None, :]
        inner = jnp.einsum("hij,jhp->ihp", mixing, block_x, precision=HIGHEST)
        entry = jnp.exp(cumul) * (block_seg == seg_prior).astype(jnp.float32)[None, :]
        carried = jnp.einsum("in,hpn->ihp", block_c, state, precision=HIGHEST) * entry.T[:, :, None]
        tail = (block_seg == block_seg[-1]).astype(jnp.float32)
        weights_tail = jnp.exp(cumul[:, -1:] - cumul) * block_dt.T * tail[None, :]
        retain = jnp.exp(cumul[:, -1]) * (block_seg[-1] == seg_prior).astype(jnp.float32)
        fresh = jnp.einsum("hj,jhp,jn->hpn", weights_tail, block_x, block_b, precision=HIGHEST)
        return (state * retain[:, None, None] + fresh, inner + carried)

    pieces = (
        values.reshape(blocks, SPAN, H, P_SIZE),
        keys_b.reshape(blocks, SPAN, N),
        query_c.reshape(blocks, SPAN, N),
        steps.reshape(blocks, SPAN, H),
        seg_row.reshape(blocks, SPAN),
        seg_before,
    )
    start = jnp.zeros((H, P_SIZE, N), jnp.float32)
    ending, result = lax.scan(jax.checkpoint(span_step), start, pieces)
    return result.reshape(length, H, P_SIZE)


def mixer_front(projected, conv_kernel, conv_shift, seg_row):
    inner_dim = conv_kernel.shape[1] - 2 * N
    signal = projected[:, inner_dim : inner_dim + conv_kernel.shape[1]]
    return conv_silu(signal, conv_kernel, conv_shift, seg_row)


def mixer_back(conved, projected, bias_dt, log_rate, skip_gain, norm_gain, seg_row):
    inner_dim = norm_gain.shape[0]
    length = conved.shape[0]
    gate = projected[:, :inner_dim]
    raw_step = projected[:, projected.shape[1] - H :]
    values = conved[:, :inner_dim].reshape(length, H, P_SIZE)
    keys_b = conved[:, inner_dim : inner_dim + N]
    query_c = conved[:, inner_dim + N :]
    steps = jax.nn.softplus(raw_step + bias_dt[None, :])
    rates = -jnp.exp(log_rate)
    mixed = (
        ssd_scan(values, keys_b, query_c, steps, rates, seg_row) + values * skip_gain[None, :, None]
    )
    gated = mixed.reshape(length, inner_dim) * jax.nn.silu(gate)
    return rms_rows(gated) * norm_gain[None, :]


def on_device(
    tokens,
    seg_ids,
    gain_in,
    w_in,
    conv_weight,
    conv_bias,
    dt_bias,
    a_log,
    d_skip,
    gain_out,
    w_out,
    cotangent,
):
    gathered = (
        lax.all_gather(gain_in, "shard", axis=0, tiled=True),
        lax.all_gather(w_in, "shard", axis=0, tiled=True),
        lax.all_gather(conv_weight, "shard", axis=1, tiled=True),
        lax.all_gather(conv_bias, "shard", axis=0, tiled=True),
        lax.all_gather(gain_out, "shard", axis=0, tiled=True),
        lax.all_gather(w_out, "shard", axis=0, tiled=True),
    )
    full_gain_in, full_w_in, full_conv_w, full_conv_b, full_gain_out, full_w_out = gathered
    row_count = tokens.shape[0]
    seq_count, seq_length = seg_ids.shape
    inputs = tokens.astype(jnp.float32)
    normed_full, norm_pull = jax.vjp(norm_input, inputs, full_gain_in.astype(jnp.float32))
    normed = normed_full.astype(jnp.bfloat16)
    projected = jnp.dot(normed, full_w_in, preferred_element_type=jnp.float32).reshape(
        seq_count, seq_length, -1
    )

    def front_all(proj_rows, conv_kernel, conv_shift):

        def front_per_sequence(proj_single, seg_single):
            return mixer_front(proj_single, conv_kernel, conv_shift, seg_single)

        return jax.vmap(front_per_sequence)(proj_rows, seg_ids)

    conved, front_pull = jax.vjp(
        front_all, projected, full_conv_w.astype(jnp.float32), full_conv_b.astype(jnp.float32)
    )
    rounded = lax.optimization_barrier(conved.astype(jnp.bfloat16)).astype(jnp.float32)

    def back_all(conv_rows, proj_rows, bias_dt, log_rate, skip_gain, norm_gain):

        def back_per_sequence(conv_single, proj_single, seg_single):
            return mixer_back(
                conv_single, proj_single, bias_dt, log_rate, skip_gain, norm_gain, seg_single
            )

        return jax.vmap(back_per_sequence)(conv_rows, proj_rows, seg_ids)

    ynorm_full, back_pull = jax.vjp(
        back_all, rounded, projected, dt_bias, a_log, d_skip, full_gain_out.astype(jnp.float32)
    )
    ynorm = ynorm_full.reshape(row_count, -1).astype(jnp.bfloat16)
    output = (inputs + jnp.dot(ynorm, full_w_out, preferred_element_type=jnp.float32)).astype(
        jnp.bfloat16
    )
    back_w_in, back_w_out = (
        lax.all_gather(w_in, "shard", axis=0, tiled=True),
        lax.all_gather(w_out, "shard", axis=0, tiled=True),
    )
    grad_w_out = lax.dot_general(
        ynorm, cotangent, (((0,), (0,)), ((), ())), preferred_element_type=jnp.float32
    )
    grad_ynorm = lax.dot_general(
        cotangent, back_w_out, (((1,), (1,)), ((), ())), preferred_element_type=jnp.float32
    )
    grad_rounded, grad_proj_back, grad_dt_bias, grad_a_log, grad_d_skip, grad_gain_out = back_pull(
        grad_ynorm.reshape(seq_count, seq_length, -1)
    )
    grad_proj_front, grad_conv_w, grad_conv_b = front_pull(grad_rounded)
    grad_projected = (grad_proj_front + grad_proj_back).reshape(row_count, -1).astype(jnp.bfloat16)
    grad_w_in = lax.dot_general(
        normed, grad_projected, (((0,), (0,)), ((), ())), preferred_element_type=jnp.float32
    )
    grad_normed = lax.dot_general(
        grad_projected, back_w_in, (((1,), (1,)), ((), ())), preferred_element_type=jnp.float32
    )
    grad_inputs, grad_gain_in = norm_pull(grad_normed)
    grad_tokens = (cotangent.astype(jnp.float32) + grad_inputs).astype(jnp.bfloat16)
    head_dt, head_rate, head_skip = lax.psum(
        (grad_dt_bias, grad_a_log, grad_d_skip), ("shard", "rep")
    )
    scattered = (
        lax.psum_scatter(grad_gain_in, "shard", scatter_dimension=0, tiled=True),
        lax.psum_scatter(grad_w_in, "shard", scatter_dimension=0, tiled=True),
        lax.psum_scatter(grad_conv_w, "shard", scatter_dimension=1, tiled=True),
        lax.psum_scatter(grad_conv_b, "shard", scatter_dimension=0, tiled=True),
        lax.psum_scatter(grad_gain_out, "shard", scatter_dimension=0, tiled=True),
        lax.psum_scatter(grad_w_out, "shard", scatter_dimension=0, tiled=True),
    )
    summed = lax.psum(
        (scattered[0], scattered[1], scattered[2], scattered[3], scattered[4], scattered[5]), "rep"
    )
    return (
        output,
        grad_tokens,
        summed[0],
        summed[1],
        summed[2],
        summed[3],
        head_dt,
        head_rate,
        head_skip,
        summed[4],
        summed[5],
    )


def solution(mesh):
    in_specs = (
        P(("shard", "rep"), None),
        P(("shard", "rep"), None),
        P("shard"),
        P("shard", None),
        P(None, "shard"),
        P("shard"),
        P(),
        P(),
        P(),
        P("shard"),
        P("shard", None),
        P(("shard", "rep"), None),
    )
    out_specs = (
        P(("shard", "rep"), None),
        P(("shard", "rep"), None),
        P("shard"),
        P("shard", None),
        P(None, "shard"),
        P("shard"),
        P(),
        P(),
        P(),
        P("shard"),
        P("shard", None),
    )
    return jax.shard_map(
        on_device, mesh=mesh, in_specs=in_specs, out_specs=out_specs, check_vma=False
    )
```

profile of v0, /device:TPU:0, one launch (start us, length us, event | category | flops | bytes accessed | tf_op | source)
XLA Modules:
  0.0 2698.1 jit_solution(16053708254669994004)
XLA Ops:
  20.9 80.9 %all-reduce.30 = (bf16[1536]{0:T(1024)(128)(2,1)S(1)}, bf16[3328]{0:T(1024)(128)(2,1)S(1)}, bf16[3072]{0:T(1024)(128)(2,1)S(1)}) all-reduce(bf16[1536]{0:T(1024)(128)(2,1)S(1)} %dynamic-update-slice, bf16[3328]{0:T(1024)(128)(2,1)S(1)} %dynamic-update-slice.1, ...), channel_id=1, replica_groups=mesh['shard'=16,'rep'=2] {'shard'}, use_global_device_ids=true, to_apply=%add.20 | all-reduce | flops 7936 | bytes 31744
  103.8 36.7 %all-gather = bf16[16,208,4]{1,2,0:T(4,128)(2,1)S(1)} all-gather(bf16[1,208,4]{1,2,0:T(4,128)(2,1)} %bitcast.676), channel_id=1, replica_groups=mesh['shard'=16,'rep'=2] {'shard'}, dimensions={0}, use_global_device_ids=true | all-gather | bytes 28288 | tf_op jit(solution)/shard_map/all_gather | solution.py:117
  143.1 95.5 %all-gather.4.cloned.1.call-done = bf16[1536,6448]{1,0:T(8,128)(2,1)} async-done(((bf16[96,6448]{1,0:T(8,128)(2,1)}), bf16[1536,6448]{1,0:T(8,128)(2,1)}) %all-gather.4.cloned.1.call-update) | async-done | bytes 19808272 | tf_op jit(solution)/shard_map/all_gather | solution.py:116
  238.5 28.6 %convolution_bitcast_fusion.1 = f32[1,1024,6448]{1,2,0:T(8,128)} fusion(bf16[1536,6448]{1,0:T(8,128)(2,1)} %all-gather.4.cloned.1.call-done, bf16[1024,1536]{1,0:T(8,128)(2,1)} %param.16, f32[1536]{0:T(1024)S(1)} %convert_element_type.89, f32[1024]{0:T(1024)S(1)} %fusion.144), kind=kOutput, calls=%fused_computation.178 | convolution fusion | flops 20289945600 | bytes 49375232 | tf_op jit(solution)/shard_map/dot_general | solution.py:128
  306.8 25.7 multiply_convert_fusion
  383.5 448.2 %while.42 = (s32[]{:T(128)}, f32[1,48,64,128]{3,2,1,0:T(8,128)S(1)}, f32[4,1,256,48,64]{2,0,4,3,1:T(4,128)}, f32[4,1,48,64,128]{4,3,2,1,0:T(8,128)}, f32[4,1,256...) while((s32[]{:T(128)}, ...), condition=%wide.region_4.5_spmd.clone, body=%wide.region_1.4_spmd.clone.sunk | while | flops 4954399744 | bytes 38993512 | solution.py:73
  434.8 68.2 %dynamic_update_slice.68 = f32[4,1,256,48,64]{2,0,4,3,1:T(4,128)} dynamic-update-slice(f32[4,1,256,48,64]{2,0,4,3,1:T(4,128)} %get-tuple-element.1186, f32[1,1,256,48,64]{2,0,4,3,1:T(1,128)} %copy.366, s32[]{:T(128)S(6)} %copy.401, s32[]{:T(128)} %constant.131.clone.1..sunk, s32[]{:T(128)} %constant.131.clone.1..sunk, s32[]{:T(128)} %constant.131.clone.1..sunk, s32[]{:T(128)} %constant.131.clone.1..sunk) | dynamic-update-slice | bytes 6291460 | tf_op jit(solution)/shard_map/jvp(vmap())/while/body/jit(dynamic_update_index_in_dim)/dynamic_update_slice | solution.py:73
  544.2 68.2 %dynamic_update_slice.68 = f32[4,1,256,48,64]{2,0,4,3,1:T(4,128)} dynamic-update-slice(f32[4,1,256,48,64]{2,0,4,3,1:T(4,128)} %get-tuple-element.1186, f32[1,1,256,48,64]{2,0,4,3,1:T(1,128)} %copy.366, s32[]{:T(128)S(6)} %copy.401, s32[]{:T(128)} %constant.131.clone.1..sunk, s32[]{:T(128)} %constant.131.clone.1..sunk, s32[]{:T(128)} %constant.131.clone.1..sunk, s32[]{:T(128)} %constant.131.clone.1..sunk) | dynamic-update-slice | bytes 6291460 | tf_op jit(solution)/shard_map/jvp(vmap())/while/body/jit(dynamic_update_index_in_dim)/dynamic_update_slice | solution.py:73
  653.7 68.2 %dynamic_update_slice.68 = f32[4,1,256,48,64]{2,0,4,3,1:T(4,128)} dynamic-update-slice(f32[4,1,256,48,64]{2,0,4,3,1:T(4,128)} %get-tuple-element.1186, f32[1,1,256,48,64]{2,0,4,3,1:T(1,128)} %copy.366, s32[]{:T(128)S(6)} %copy.401, s32[]{:T(128)} %constant.131.clone.1..sunk, s32[]{:T(128)} %constant.131.clone.1..sunk, s32[]{:T(128)} %constant.131.clone.1..sunk, s32[]{:T(128)} %constant.131.clone.1..sunk) | dynamic-update-slice | bytes 6291460 | tf_op jit(solution)/shard_map/jvp(vmap())/while/body/jit(dynamic_update_index_in_dim)/dynamic_update_slice | solution.py:73
  763.1 68.2 %dynamic_update_slice.68 = f32[4,1,256,48,64]{2,0,4,3,1:T(4,128)} dynamic-update-slice(f32[4,1,256,48,64]{2,0,4,3,1:T(4,128)} %get-tuple-element.1186, f32[1,1,256,48,64]{2,0,4,3,1:T(1,128)} %copy.366, s32[]{:T(128)S(6)} %copy.401, s32[]{:T(128)} %constant.131.clone.1..sunk, s32[]{:T(128)} %constant.131.clone.1..sunk, s32[]{:T(128)} %constant.131.clone.1..sunk, s32[]{:T(128)} %constant.131.clone.1..sunk) | dynamic-update-slice | bytes 6291460 | tf_op jit(solution)/shard_map/jvp(vmap())/while/body/jit(dynamic_update_index_in_dim)/dynamic_update_slice | solution.py:73
  899.4 32.9 %multiply_reduce_fusion.7 = (f32[3072]{0:T(1024)}, f32[1,1024,3072]{1,2,0:T(8,128)}, f32[1,1024,3072]{1,2,0:T(8,128)}) fusion(f32[1,1024,3328]{1,2,0:T(8,128)} %convert_element_type.94, f32[1,1024,6448]{1,2,0:T(8,128)} %convolution_bitcast_fusion.1, f32[1,1024,3072]{1,2,0:T(8,128)} %copy-done.2, f32[1024]{0:T(1024)S(1)} %multiply_multiply_fusion.2, ...), kind=kLoop, calls=%fused_computation.199 | loop fusion | flops 66057216 | bytes 88125440 | tf_op jit(solution)/shard_map/transpose(jvp(vmap()))/reduce_sum | solution.py:94
  958.2 858.4 %while.43 = (s32[]{:T(128)}, f32[48]{0:T(128)}, f32[1,48,64,128]{3,2,1,0:T(8,128)}, f32[4,1,256,48,64]{2,0,4,3,1:T(4,128)}, f32[4,1,256,128]{2,0,3,1:T(4,128)}, ...) while((s32[]{:T(128)}, f32[48]{0:T(128)}, ...), condition=%wide.region_20.21_spmd.clone, body=%wide.region_7.20_spmd.clone.sunk | while | flops 11249247232 | bytes 107387864 | solution.py:73
  1102.2 68.0 %dynamic_update_slice.71 = f32[4,1,256,48,64]{2,0,4,3,1:T(4,128)} dynamic-update-slice(f32[4,1,256,48,64]{2,0,4,3,1:T(4,128)} %get-tuple-element.1235, f32[1,1,256,48,64]{2,0,4,3,1:T(1,128)S(1)} %copy.385, s32[]{:T(128)S(6)} %sub.252, s32[]{:T(128)} %constant.131.clone.1..sunk.1, s32[]{:T(128)} %constant.131.clone.1..sunk.1, s32[]{:T(128)} %constant.131.clone.1..sunk.1, s32[]{:T(128)} %constant.131.clone.1..sunk.1) | dynamic-update-slice | bytes 6291460 | tf_op jit(solution)/shard_map/transpose(jvp(vmap()))/while/body/jit(dynamic_update_index_in_dim)/dynamic_update_slice | solution.py:73
  1315.8 67.8 %dynamic_update_slice.71 = f32[4,1,256,48,64]{2,0,4,3,1:T(4,128)} dynamic-update-slice(f32[4,1,256,48,64]{2,0,4,3,1:T(4,128)} %get-tuple-element.1235, f32[1,1,256,48,64]{2,0,4,3,1:T(1,128)S(1)} %copy.385, s32[]{:T(128)S(6)} %sub.252, s32[]{:T(128)} %constant.131.clone.1..sunk.1, s32[]{:T(128)} %constant.131.clone.1..sunk.1, s32[]{:T(128)} %constant.131.clone.1..sunk.1, s32[]{:T(128)} %constant.131.clone.1..sunk.1) | dynamic-update-slice | bytes 6291460 | tf_op jit(solution)/shard_map/transpose(jvp(vmap()))/while/body/jit(dynamic_update_index_in_dim)/dynamic_update_slice | solution.py:73
  1529.3 67.8 %dynamic_update_slice.71 = f32[4,1,256,48,64]{2,0,4,3,1:T(4,128)} dynamic-update-slice(f32[4,1,256,48,64]{2,0,4,3,1:T(4,128)} %get-tuple-element.1235, f32[1,1,256,48,64]{2,0,4,3,1:T(1,128)S(1)} %copy.385, s32[]{:T(128)S(6)} %sub.252, s32[]{:T(128)} %constant.131.clone.1..sunk.1, s32[]{:T(128)} %constant.131.clone.1..sunk.1, s32[]{:T(128)} %constant.131.clone.1..sunk.1, s32[]{:T(128)} %constant.131.clone.1..sunk.1) | dynamic-update-slice | bytes 6291460 | tf_op jit(solution)/shard_map/transpose(jvp(vmap()))/while/body/jit(dynamic_update_index_in_dim)/dynamic_update_slice | solution.py:73
  1742.5 67.8 %dynamic_update_slice.71 = f32[4,1,256,48,64]{2,0,4,3,1:T(4,128)} dynamic-update-slice(f32[4,1,256,48,64]{2,0,4,3,1:T(4,128)} %get-tuple-element.1235, f32[1,1,256,48,64]{2,0,4,3,1:T(1,128)S(1)} %copy.385, s32[]{:T(128)S(6)} %sub.252, s32[]{:T(128)} %constant.131.clone.1..sunk.1, s32[]{:T(128)} %constant.131.clone.1..sunk.1, s32[]{:T(128)} %constant.131.clone.1..sunk.1, s32[]{:T(128)} %constant.131.clone.1..sunk.1) | dynamic-update-slice | bytes 6291460 | tf_op jit(solution)/shard_map/transpose(jvp(vmap()))/while/body/jit(dynamic_update_index_in_dim)/dynamic_update_slice | solution.py:73
  1876.7 25.3 multiply_reduce_fusion.5
  1943.9 27.7 %fusion.153 = (f32[3328]{0:T(1024)S(1)}, f32[3328]{0:T(1024)S(1)}, f32[1,1024,3328]{1,2,0:T(8,128)}) fusion(f32[1,1024,3328]{1,2,0:T(8,128)} %get-tuple-element.890, f32[1,1024,6448]{1,2,0:T(8,128)} %convolution_bitcast_fusion.1, f32[3328]{0:T(1024)S(1)} %copy-done.16, f32[1,1023,3328]{1,2,0:T(8,128)} %slice_multiply_fusion, ...), kind=kLoop, calls=%fused_computation.256 | loop fusion | flops 23848448 | bytes 81748992 | tf_op jit(solution)/shard_map/transpose(jvp(vmap()))/reduce_sum | solution.py:26
  1971.6 32.5 %fusion.138 = f32[1536,6448]{1,0:T(8,128)} fusion(bf16[1024,1536]{1,0:T(8,128)(2,1)S(1)} %copy-done.3, f32[1536]{0:T(1024)S(1)} %copy-done.30, f32[1024]{0:T(1024)S(1)} %copy-done.32, f32[1,1024,3072]{1,2,0:T(8,128)} %get-tuple-element.913, f32[1,1024,48]{1,2,0:T(8,128)S(1)} %get-tuple-element.887, f32[1,1024,3328]{1,2,0:T(8,128)} %get-tuple-element.914), kind=kOutput, calls=%fused_computation.227 | convolution fusion | flops 20309753856 | bytes 69183488 | tf_op jit(solution)/shard_map/dot_general | solution.py:175
  2007.9 43.3 %fusion.129 = (f32[1536]{0:T(1024)S(1)}, f32[1024]{0:T(1024)S(1)}, f32[1024,1536]{1,0:T(8,128)}) fusion(bf16[1024,1536]{1,0:T(8,128)(2,1)S(1)} %copy-done.3, f32[1024]{0:T(1024)S(1)} %copy-done.32, f32[1536]{0:T(1024)S(1)} %copy-done.30, bf16[1536,6448]{1,0:T(8,128)(2,1)} %all-gather.4.cloned.1.call-done, f32[1,1024,3072]{1,2,0:T(8,128)} %get-tuple-element.913, ...), kind=kOutput, calls=%fused_computation.218 | convolution fusion | flops 20314468352 | bytes 55676928 | tf_op jit(solution)/shard_map/dot_general | solution.py:178
  2051.6 77.3 %all-reduce.27 = (f32[1536]{0:T(1024)S(1)}, f32[3328]{0:T(1024)S(1)}, f32[3072]{0:T(1024)S(1)}) all-reduce(f32[1536]{0:T(1024)S(1)} %get-tuple-element.799, f32[3328]{0:T(1024)S(1)} %get-tuple-element.797, f32[3072]{0:T(1024)S(1)} %copy-done.36), channel_id=2, replica_groups=mesh['shard'=16,'rep'=2] {'shard'}, use_global_device_ids=true, to_apply=%region_23.24.clone | all-reduce | flops 7936 | bytes 63488
  2129.1 40.3 %all-reduce.26 = (f32[48]{0:T(128)}, f32[48]{0:T(128)}, f32[48]{0:T(128)}) all-reduce(f32[48]{0:T(128)S(1)} %copy-done.39, f32[48]{0:T(128)S(1)} %negate_multiply_fusion, f32[48]{0:T(128)S(1)} %reduce_sum.234), channel_id=1, replica_groups=mesh['shard'=16,'rep'=2] {'shard','rep'}, use_global_device_ids=true, to_apply=%region_37.38 | all-reduce | flops 144 | bytes 1152 | tf_op jit(solution)/shard_map/psum | solution.py:183
  2169.4 411.2 %reduce-scatter.6.cloned.1.call-done = f32[96,6448]{1,0:T(8,128)} async-done(((f32[1536,6448]{1,0:T(8,128)}), f32[96,6448]{1,0:T(8,128)}) %reduce-scatter.6.cloned.1.call-update) | async-done | bytes 2476048 | tf_op jit(solution)/shard_map/reduce_scatter | solution.py:188
  2603.8 58.2 %reduce-scatter.10.cloned.1.call-done = f32[208,4]{1,0:T(8,128)} async-done(((f32[3328,4]{1,0:T(8,128)}), f32[208,4]{1,0:T(8,128)}) %reduce-scatter.10.cloned.1.call-update) | async-done | bytes 3344
  (560 shorter events, 1089.7 us)
Async XLA Ops:
  7.2 231.4 %all-gather.4.cloned.1.call-start = ((), (), s32[]{:S(2)}) async-start(), calls=%async_computation.3 | async-start | bytes 21307392 | tf_op jit(solution)/shard_map/all_gather | solution.py:116
  7.9 870.8 %all-gather.6.cloned.1.call-start = ((), (), s32[]{:S(2)}) async-start(), calls=%async_computation.4 | async-start | bytes 10027008 | tf_op jit(solution)/shard_map/all_gather | solution.py:120
  8.7 2160.7 %reduce-scatter.8.cloned.1.call-start = ((), (), s32[]{:S(2)}) async-start(), calls=%async_computation.6 | async-start | bytes 20054016 | tf_op jit(solution)/shard_map/reduce_scatter | solution.py:192
  18.3 248.8 %copy-start.31 = (f32[1024]{0:T(1024)}, f32[1024]{0:T(1024)S(1)}, u32[]{:S(2)}) copy-start(f32[1024]{0:T(1024)S(1)} %fusion.144) | copy-start | bytes 12292
  101.8 165.3 %copy-start.29 = (f32[1536]{0:T(1024)}, f32[1536]{0:T(1024)S(1)}, u32[]{:S(2)}) copy-start(f32[1536]{0:T(1024)S(1)} %convert_element_type.89) | copy-start | bytes 18436
  140.8 166.0 %copy-start.9 = (f32[3328]{0:T(1024)}, f32[3328]{0:T(1024)S(1)}, u32[]{:S(2)}) copy-start(f32[3328]{0:T(1024)S(1)} %get-tuple-element.802) | copy-start | bytes 39940
  140.8 166.0 %copy-start.11 = (f32[3328]{0:T(1024)}, f32[3328]{0:T(1024)S(1)}, u32[]{:S(2)}) copy-start(f32[3328]{0:T(1024)S(1)} %get-tuple-element.804) | copy-start | bytes 39940
  140.8 166.0 %copy-start.13 = (f32[3328]{0:T(1024)}, f32[3328]{0:T(1024)S(1)}, u32[]{:S(2)}) copy-start(f32[3328]{0:T(1024)S(1)} %get-tuple-element.803) | copy-start | bytes 39940
  140.8 165.9 %copy-start.15 = (f32[3328]{0:T(1024)}, f32[3328]{0:T(1024)S(1)}, u32[]{:S(2)}) copy-start(f32[3328]{0:T(1024)S(1)} %get-tuple-element.801) | copy-start | bytes 39940
  143.0 163.8 %copy-start.21 = (f32[1,1024]{1,0:T(1,128)}, f32[1,1024]{1,0:T(1,128)S(1)}, u32[]{:S(2)}) copy-start(f32[1,1024]{1,0:T(1,128)S(1)} %get-tuple-element.919) | copy-start | bytes 12292
  143.0 163.8 %copy-start.23 = (f32[1,1024]{1,0:T(1,128)}, f32[1,1024]{1,0:T(1,128)S(1)}, u32[]{:S(2)}) copy-start(f32[1,1024]{1,0:T(1,128)S(1)} %get-tuple-element.920) | copy-start | bytes 12292
  143.0 163.8 %copy-start.25 = (f32[1,1024]{1,0:T(1,128)}, f32[1,1024]{1,0:T(1,128)S(1)}, u32[]{:S(2)}) copy-start(f32[1,1024]{1,0:T(1,128)S(1)} %get-tuple-element.921) | copy-start | bytes 12292
  861.1 38.2 %copy-start.33 = (f32[1024]{0:T(1024)}, f32[1024]{0:T(1024)S(1)}, u32[]{:S(2)}) copy-start(f32[1024]{0:T(1024)S(1)} %fusion.145) | copy-start | bytes 12292
  899.3 1681.2 %reduce-scatter.6.cloned.1.call-start = ((), (), s32[]{:S(2)}) async-start(), calls=%async_computation.5 | async-start | bytes 42614784 | tf_op jit(solution)/shard_map/reduce_scatter | solution.py:188
  2004.0 657.9 %reduce-scatter.10.cloned.1.call-start = ((), (), s32[]{:S(2)}) async-start(), calls=%async_computation.7 | async-start | bytes 1810432
  2007.9 43.3 %copy-start.28 = (f32[1024]{0:T(1024)S(1)}, f32[1024]{0:T(1024)}, u32[]{:S(2)}) copy-start(f32[1024]{0:T(1024)} %copy-done.27) | copy-start | bytes 12292
  2007.9 43.4 %copy-start.35 = (f32[48]{0:T(128)S(1)}, f32[48]{0:T(128)}, u32[]{:S(2)}) copy-start(f32[48]{0:T(128)} %get-tuple-element.499) | copy-start | bytes 580
  2007.9 43.4 %copy-start.40 = (f32[48]{0:T(128)S(1)}, f32[48]{0:T(128)}, u32[]{:S(2)}) copy-start(f32[48]{0:T(128)} %param.23) | copy-start | bytes 580
  2007.9 43.5 %copy-start.20 = (f32[3072]{0:T(1024)S(1)}, f32[3072]{0:T(1024)}, u32[]{:S(2)}) copy-start(f32[3072]{0:T(1024)} %get-tuple-element.884) | copy-start | bytes 36868
  2007.9 43.6 %copy-start.36 = (f32[3072]{0:T(1024)S(1)}, f32[3072]{0:T(1024)}, u32[]{:S(2)}) copy-start(f32[3072]{0:T(1024)} %get-tuple-element.795) | copy-start | bytes 36868
  2007.9 121.1 %copy-start.39 = (f32[48]{0:T(128)S(1)}, f32[48]{0:T(128)}, u32[]{:S(2)}) copy-start(f32[48]{0:T(128)} %get-tuple-element.886) | copy-start | bytes 580
  2051.2 535.3 %copy-start.19 = (f32[3072]{0:T(1024)S(1)}, f32[3072]{0:T(1024)}, u32[]{:S(2)}) copy-start(f32[3072]{0:T(1024)} %convert_element_type.95) | copy-start | bytes 36868
  2051.2 535.3 %copy-start.34 = (f32[1024]{0:T(1024)S(1)}, f32[1024]{0:T(1024)}, u32[]{:S(2)}) copy-start(f32[1024]{0:T(1024)} %copy-done.33) | copy-start | bytes 12292
  2051.3 633.9 %all-reduce.33.cloned.1.call-start = ((), (), s32[]{:S(2)}) async-start(), calls=%async_computation.8 | async-start | bytes 7372800 | tf_op jit(solution)/shard_map/psum | solution.py:194
  (35 other events, 548.2 us)
Sparse Core Ops, SparseCore 0:
  10.8 227.6 all-gather.3
  241.3 120.7 all-gather.5
  899.4 283.3 reduce-scatter.7
  2004.2 576.3 reduce-scatter.5
  2583.3 78.5 reduce-scatter.9
  2664.2 20.8 all-reduce.32
where the time goes:
time: 2730 us; the launch traced here: 2700 us
  local copies, waits for them, and re-layouts  941 us (34%)
  waiting for transfers between devices  585 us (21%)
  matrix products  541 us (20%)
  other arithmetic  343 us (13%)
  blocking collectives  238 us (9%)
  loops' own time  29.1 us (1%)
    dynamic_update_slice x24, local copies, waits for them, and re-layouts, ssd_scan(): ending, result = lax.scan(jax.checkpoint(span_step), start, pieces)  596 us
    reduce_scatter x1, waiting for transfers between devices, on_device(): lax.psum_scatter(grad_w_in, 'shard', scatter_dimension=0, tiled=True)  411 us
    dot_general x12, matrix products, span_step(): inner = jnp.einsum('hij,jhp->ihp', mixing, block_x, precision=HIGHEST)  209 us
    unnamed x2, blocking collectives  158 us
    all_gather x1, waiting for transfers between devices, on_device(): lax.all_gather(w_in, 'shard', axis=0, tiled=True)  95.5 us
    dot_general x16, matrix products, span_step(): jnp.einsum('in,hpn->ihp', block_c, state, precision=HIGHEST)  80.2 us
    dot_general x12, matrix products, span_step(): jnp.einsum('hj,jhp,jn->hpn', weights_tail, block_x, block_b, precision=HI...  70.3 us
    another operation x88, local copies, waits for them, and re-layouts  63.7 us
  transfers between devices with their start and end apart: 6, of which 4 were waited for; matrix products, arithmetic and copies ran while one was open for 67% of the time, Pallas kernels for 0%

commit v1 on v0

v1 whole, which is shorter than its diff:
```python
import jax
import jax.numpy as jnp
from jax import lax
from jax.experimental import pallas as pl
from jax.experimental.pallas import tpu as pltpu
from jax.sharding import PartitionSpec as P

H = 48
P_SIZE = 64
N = 128
SPAN = 256
HALF = 128
GROUP = 8
TILE = 128
EPSILON = 1e-05
HIGHEST = lax.Precision.HIGHEST
LOG2E = 1.4426950408889634
NEG = -1e30
F32 = jnp.float32
BF16 = jnp.bfloat16


def dot_f32(a, b, contract, precision=None):
    return lax.dot_general(
        a, b, ((contract[0], contract[1]), ((), ())), preferred_element_type=F32, precision=precision
    )


def mm(a, b):
    return dot_f32(a, b, ((1,), (0,)))


def mm_nt(a, b):
    return dot_f32(a, b, ((1,), (1,)))


def lanes_of(column, rows):
    return jnp.broadcast_to(column, (rows, TILE))


def step_sizes(raw, heads):
    shifted = raw + heads[0:1]
    return jnp.maximum(shifted, 0.0) + jnp.log1p(jnp.exp(-jnp.abs(shifted)))


def conv_taps(ext, same, start, width, rows=SPAN):
    out = [ext[8 : 8 + rows, start : start + width]]
    for offset in (1, 2, 3):
        moved = ext[8 - offset : 8 - offset + rows, start : start + width]
        mask = same[offset - 1]
        if width > TILE:
            mask = jnp.concatenate([mask] * (width // TILE), axis=1)
        out.append(moved * mask)
    return out


def conv_sum(taps, weights):
    total = weights[4:5] + weights[3:4] * taps[0]
    for offset in (1, 2, 3):
        total = total + weights[3 - offset : 4 - offset] * taps[offset]
    return total


def prepare(raw_ref, heads_ref, aux_ref, pack_a, pack_b, cum_rows, same):
    aux = aux_ref[...]
    heads = heads_ref[...]
    step = step_sizes(raw_ref[...], heads)
    row = lax.broadcasted_iota(jnp.int32, (SPAN, SPAN), 0)
    col = lax.broadcasted_iota(jnp.int32, (SPAN, SPAN), 1)
    tri = (row >= col).astype(F32)
    cum = dot_f32(tri, step * heads[1:2], ((1,), (0,)), HIGHEST)
    last = cum[SPAN - 1 : SPAN]
    entry = jnp.exp2(cum) * lanes_of(aux[:, 3:4], SPAN)
    tail = jnp.exp2(last - cum) * lanes_of(aux[:, 4:5], SPAN)
    lane = lax.broadcasted_iota(jnp.int32, (SPAN, TILE), 1)
    low = lane < 64
    pack_a[...] = jnp.where(low, cum, pltpu.roll(step, 64, 1))
    pack_b[...] = jnp.where(low, entry, pltpu.roll(tail, 64, 1))
    cum_rows[...] = cum.T
    for offset in (1, 2, 3):
        same[offset - 1] = lanes_of(aux[:, offset - 1 : offset], SPAN)


def forward_kernel(
    pc_ref, halo_ref, bc_ref, bc_halo_ref, raw_ref, cw_ref, bcw_ref, aux_ref, seg_ref, heads_ref, skip_ref,
    x_out, bc_out, y_out, st_out,
    state, scores, block, same, pack_a, pack_b, cum_rows, b_t, ext, ext_bc, halo_bf,
):
    span = pl.program_id(0)
    group = pl.program_id(1)

    @pl.when((span == 0) & (group == 0))
    def _():
        state[...] = jnp.zeros_like(state)

    @pl.when(group == 0)
    def _():
        prepare(raw_ref, heads_ref, aux_ref, pack_a, pack_b, cum_rows, same)
        ext_bc[0:8] = bc_halo_ref[...]
        ext_bc[8:] = bc_ref[...]
        total = conv_sum(conv_taps(ext_bc, same, 0, 2 * N), bcw_ref[...])
        both = (total * jax.nn.sigmoid(total)).astype(BF16)
        bc_out[...] = both
        keys, query = both[:, :N], both[:, N:]
        row = lax.broadcasted_iota(jnp.int32, (SPAN, SPAN), 0)
        col = lax.broadcasted_iota(jnp.int32, (SPAN, SPAN), 1)
        linked = (row >= col) & (aux_ref[:, 5:6] == seg_ref[...])
        block[...] = jnp.where(linked, 0.0, NEG)
        scores[...] = mm_nt(query, keys)
        b_t[...] = keys.T

    ext[0:8] = halo_ref[...]
    ext[8:] = pc_ref[...]
    shift = (TILE - GROUP * group) % TILE
    cols_a = pltpu.roll(pack_a[...], shift, 1)
    cols_b = pltpu.roll(pack_b[...], shift, 1)
    retain = cols_b[SPAN - 1 : SPAN]
    lane = lax.broadcasted_iota(jnp.int32, (SPAN, TILE), 1)
    first = lane < P_SIZE
    query = bc_out[:, N:]
    for pair in range(GROUP // 2):
        at = pair * TILE
        total = conv_sum(conv_taps(ext, same, at, TILE), cw_ref[:, at : at + TILE])
        x = total * jax.nn.sigmoid(total)
        xb = x.astype(BF16)
        x_out[:, at : at + TILE] = xb
        here = group * (GROUP // 2) * TILE + at
        tile = pl.ds(pl.multiple_of(here, TILE), TILE)
        old = state[:, tile]
        old_b = old.astype(BF16)
        st_out[:, at : at + TILE] = old_b
        parts = []
        for head in (2 * pair, 2 * pair + 1):
            cum_col = lanes_of(cols_a[:, head : head + 1], SPAN)
            cum_row = cum_rows[pl.ds(group * GROUP + head, 1), :]
            step_row = None
            blocks = []
            for i, j in ((0, 0), (1, 0), (1, 1)):
                rows = slice(i * HALF, (i + 1) * HALF)
                cols = slice(j * HALF, (j + 1) * HALF)
                gap = cum_col[rows] - cum_row[:, cols] + block[rows, cols]
                blocks.append((jnp.exp2(gap) * scores[rows, cols]).astype(BF16))
            parts.append(blocks)
        step_pair = jnp.where(
            first,
            lanes_of(cols_a[:, 64 + 2 * pair : 65 + 2 * pair], SPAN),
            lanes_of(cols_a[:, 65 + 2 * pair : 66 + 2 * pair], SPAN),
        )
        xs = x * step_pair
        xs = xb.astype(F32) * step_pair
        xsb = xs.astype(BF16)
        outs = []
        for blocks in parts:
            top = mm(blocks[0], xsb[:HALF])
            bottom = mm(jnp.concatenate(blocks[1:], axis=1), xsb)
            outs.append(jnp.concatenate([top, bottom], axis=0))
        entry_pair = jnp.where(
            first,
            lanes_of(cols_b[:, 2 * pair : 2 * pair + 1], SPAN),
            lanes_of(cols_b[:, 2 * pair + 1 : 2 * pair + 2], SPAN),
        )
        tail_pair = jnp.where(
            first,
            lanes_of(cols_b[:, 64 + 2 * pair : 65 + 2 * pair], SPAN),
            lanes_of(cols_b[:, 65 + 2 * pair : 66 + 2 * pair], SPAN),
        )
        carried = mm(query, old_b)
        y_out[:, at : at + TILE] = (
            jnp.where(first, outs[0], outs[1])
            + entry_pair * carried
            + skip_ref[:, at : at + TILE] * xb.astype(F32)
        )
        retain_pair = jnp.where(
            first[:N],
            jnp.broadcast_to(retain[:, 2 * pair : 2 * pair + 1], (N, TILE)),
            jnp.broadcast_to(retain[:, 2 * pair + 1 : 2 * pair + 2], (N, TILE)),
        )
        state[:, tile] = old * retain_pair + mm(b_t[...], (xs * tail_pair).astype(BF16))


def run_forward(pc, raw, conv_all, aux, seg_row, heads, skip):
    tokens = pc.shape[0]
    spans = tokens // SPAN
    di = pc.shape[1] - 2 * N
    width = GROUP * P_SIZE
    groups = di // width
    last_block = di // (2 * N)
    grid_spec = pltpu.PrefetchScalarGridSpec(
        num_scalar_prefetch=0,
        grid=(spans, groups),
        in_specs=[
            pl.BlockSpec((SPAN, width), lambda s, g: (s, g)),
            pl.BlockSpec((8, width), lambda s, g: (jnp.maximum(s * (SPAN // 8) - 1, 0), g)),
            pl.BlockSpec((SPAN, 2 * N), lambda s, g: (s, last_block)),
            pl.BlockSpec((8, 2 * N), lambda s, g: (jnp.maximum(s * (SPAN // 8) - 1, 0), last_block)),
            pl.BlockSpec((SPAN, TILE), lambda s, g: (s, 0)),
            pl.BlockSpec((8, width), lambda s, g: (0, g)),
            pl.BlockSpec((8, 2 * N), lambda s, g: (0, last_block)),
            pl.BlockSpec((SPAN, 8), lambda s, g: (s, 0)),
            pl.BlockSpec((1, SPAN), lambda s, g: (0, s)),
            pl.BlockSpec((8, TILE), lambda s, g: (0, 0)),
            pl.BlockSpec((1, width), lambda s, g: (0, g)),
        ],
        out_specs=[
            pl.BlockSpec((SPAN, width), lambda s, g: (s, g)),
            pl.BlockSpec((SPAN, 2 * N), lambda s, g: (s, 0)),
            pl.BlockSpec((SPAN, width), lambda s, g: (s, g)),
            pl.BlockSpec((N, width), lambda s, g: (s, g)),
        ],
        scratch_shapes=[
            pltpu.VMEM((N, di), F32),
            pltpu.VMEM((SPAN, SPAN), F32),
            pltpu.VMEM((SPAN, SPAN), F32),
            pltpu.VMEM((3, SPAN, TILE), F32),
            pltpu.VMEM((SPAN, TILE), F32),
            pltpu.VMEM((SPAN, TILE), F32),
            pltpu.VMEM((TILE, SPAN), F32),
            pltpu.VMEM((N, SPAN), BF16),
            pltpu.VMEM((SPAN + 8, width), F32),
            pltpu.VMEM((SPAN + 8, 2 * N), F32),
            pltpu.VMEM((8, TILE), F32),
        ],
    )
    return pl.pallas_call(
        forward_kernel,
        grid_spec=grid_spec,
        out_shape=[
            jax.ShapeDtypeStruct((tokens, di), BF16),
            jax.ShapeDtypeStruct((tokens, 2 * N), BF16),
            jax.ShapeDtypeStruct((tokens, di), F32),
            jax.ShapeDtypeStruct((spans * N, di), BF16),
        ],
        compiler_params=pltpu.CompilerParams(dimension_semantics=("arbitrary", "arbitrary")),
        name="scan_forward",
    )(pc, pc, pc, pc, raw, conv_all, conv_all, aux, seg_row, heads, skip)


def conv_back(grad, ext, same, weights, carry, start, width):
    taps = conv_taps(ext, same, start, width)
    total = conv_sum(taps, weights)
    gate = jax.nn.sigmoid(total)
    du = grad * (gate * (1.0 + total * (1.0 - gate)))
    row_index = lax.broadcasted_iota(jnp.int32, (SPAN, width), 0)
    out = weights[3:4] * du
    sums = [jnp.sum(du.reshape(SPAN // 8, 8, width), axis=0)]
    sums.append(jnp.sum((du * taps[0]).reshape(SPAN // 8, 8, width), axis=0))
    for offset in (1, 2, 3):
        mask = same[offset - 1]
        if width > TILE:
            mask = jnp.concatenate([mask] * (width // TILE), axis=1)
        masked = du * mask
        after = carry[offset - 1]
        moved = jnp.concatenate([masked, after], axis=0)[offset : offset + SPAN]
        carry[offset - 1] = masked[0:8]
        out = out + weights[3 - offset : 4 - offset] * moved
        sums.append(jnp.sum((du * taps[offset]).reshape(SPAN // 8, 8, width), axis=0))
    return out, sums


def backward_kernel(
    dy_ref, x_ref, bcv_ref, st_ref, pc_ref, halo_ref, bc_ref, bc_halo_ref, raw_ref, cw_ref, bcw_ref,
    aux_ref, seg_ref, heads_ref, skip_ref,
    dpc_out, dbc_out, draw_out, dcw_out, dbcw_out, dskip_out, dhead_out,
    dstate, scores, block, dscores, same, pack_a, pack_b, cum_rows, c_t, ext, ext_bc,
    carry, carry_bc, d_b, d_c, per_row, dcum_rows, dlast, dcw_acc, dskip_acc,
):
    back = pl.program_id(0)
    group = pl.program_id(1)
    spans = pl.num_programs(0)
    groups = pl.num_programs(1)
    width = GROUP * P_SIZE

    @pl.when((back == 0) & (group == 0))
    def _():
        dstate[...] = jnp.zeros_like(dstate)
        carry[...] = jnp.zeros_like(carry)
        carry_bc[...] = jnp.zeros_like(carry_bc)
        dbcw_out[...] = jnp.zeros_like(dbcw_out)
        dhead_out[...] = jnp.zeros_like(dhead_out)
        dcw_acc[...] = jnp.zeros_like(dcw_acc)
        dskip_acc[...] = jnp.zeros_like(dskip_acc)

    keys = bcv_ref[:, :N]
    query = bcv_ref[:, N:]

    @pl.when(group == 0)
    def _():
        prepare(raw_ref, heads_ref, aux_ref, pack_a, pack_b, cum_rows, same)
        row = lax.broadcasted_iota(jnp.int32, (SPAN, SPAN), 0)
        col = lax.broadcasted_iota(jnp.int32, (SPAN, SPAN), 1)
        linked = (row <= col) & (aux_ref[:, 5:6] == seg_ref[...])
        block[...] = jnp.where(linked, 0.0, NEG)
        scores[...] = mm_nt(keys, query)
        c_t[...] = query.T
        dscores[...] = jnp.zeros_like(dscores)
        d_b[...] = jnp.zeros_like(d_b)
        d_c[...] = jnp.zeros_like(d_c)
        per_row[...] = jnp.zeros_like(per_row)
        dlast[...] = jnp.zeros_like(dlast)

    ext[0:8] = halo_ref[...]
    ext[8:] = pc_ref[...]
    shift = (TILE - GROUP * group) % TILE
    cols_a = pltpu.roll(pack_a[...], shift, 1)
    cols_b = pltpu.roll(pack_b[...], shift, 1)
    retain = cols_b[SPAN - 1 : SPAN]
    lane = lax.broadcasted_iota(jnp.int32, (SPAN, TILE), 1)
    first = lane < P_SIZE
    lane_row = lax.broadcasted_iota(jnp.int32, (TILE, TILE), 0)
    lane_col = lax.broadcasted_iota(jnp.int32, (TILE, TILE), 1)
    sums = jnp.zeros((SPAN, TILE), F32)
    last_sum = jnp.zeros((1, TILE), F32)
    group_at = group * width
    for pair in range(GROUP // 2):
        at = pair * TILE
        tile = pl.ds(pl.multiple_of(group_at + at, TILE), TILE)
        dy = dy_ref[:, at : at + TILE]
        dyf = dy.astype(F32)
        xf = x_ref[:, at : at + TILE].astype(F32)
        step_pair = jnp.where(
            first,
            lanes_of(cols_a[:, 64 + 2 * pair : 65 + 2 * pair], SPAN),
            lanes_of(cols_a[:, 65 + 2 * pair : 66 + 2 * pair], SPAN),
        )
        entry_pair = jnp.where(
            first,
            lanes_of(cols_b[:, 2 * pair : 2 * pair + 1], SPAN),
            lanes_of(cols_b[:, 2 * pair + 1 : 2 * pair + 2], SPAN),
        )
        tail_pair = jnp.where(
            first,
            lanes_of(cols_b[:, 64 + 2 * pair : 65 + 2 * pair], SPAN),
            lanes_of(cols_b[:, 65 + 2 * pair : 66 + 2 * pair], SPAN),
        )
        xs = xf * step_pair
        inner = []
        for which in (0, 1):
            head = 2 * pair + which
            mine = first if which == 0 else ~first
            xh = jnp.where(mine, xs, 0.0).astype(BF16)
            cum_col = lanes_of(cols_a[:, head : head + 1], SPAN)
            cum_row = cum_rows[pl.ds(group * GROUP + head, 1), :]
            g_top = mm_nt(xh[:HALF], dy)
            g_bottom = mm_nt(xh[HALF:], dy[HALF:])
            mixes = []
            across = []
            down = []
            for j, i in ((0, 0), (0, 1), (1, 1)):
                rows = slice(j * HALF, (j + 1) * HALF)
                cols = slice(i * HALF, (i + 1) * HALF)
                decay = jnp.exp2(cum_row[:, cols] - cum_col[rows] + block[rows, cols])
                mix = decay * scores[rows, cols]
                g = g_bottom if j == 1 else g_top[:, cols]
                dscores[rows, cols] += decay * g
                w = mix * g
                mixes.append(mix.astype(BF16))
                across.append(w)
                down.append(jnp.sum(w, axis=0, keepdims=True))
            row_sum = jnp.concatenate(
                [
                    jnp.sum(across[0] + across[1], axis=1, keepdims=True),
                    jnp.sum(across[2], axis=1, keepdims=True),
                ],
                axis=0,
            )
            sums = sums + jnp.where(lane == 24 + head, row_sum, 0.0)
            dcum_rows[pl.ds(group * GROUP + head, 1), :] = jnp.concatenate([down[0], down[1] + down[2]], axis=1)
            top = mm(jnp.concatenate(mixes[:2], axis=1), dy)
            bottom = mm(mixes[2], dy[HALF:])
            inner.append(jnp.concatenate([top, bottom], axis=0))
        stb = st_ref[:, at : at + TILE]
        stf = stb.astype(F32)
        ds = dstate[:, tile]
        dsb = ds.astype(BF16)
        dye = (dyf * entry_pair).astype(BF16)
        fresh = mm(keys, dsb)
        fresh = fresh * tail_pair
        total = jnp.where(first, inner[0], inner[1]) + fresh
        carried = mm(query, stb)
        d_c[...] += mm_nt(dye, stb)
        d_b[...] += mm_nt((xs * tail_pair).astype(BF16), dsb)

        def spread(kind):
            return (lane_col == kind * GROUP + 2 * pair + (lane_row >= P_SIZE).astype(jnp.int32)).astype(BF16)

        def head_sum(values, kind):
            high = values.astype(BF16)
            rest = (values - high.astype(F32)).astype(BF16)
            return mm(high, spread(kind)) + mm(rest, spread(kind))

        sums = sums + head_sum(xf * total, 0) + head_sum(xs * fresh, 1) + head_sum(dyf * entry_pair * carried, 2)
        retain_pair = jnp.where(
            first[:N],
            jnp.broadcast_to(retain[:, 2 * pair : 2 * pair + 1], (N, TILE)),
            jnp.broadcast_to(retain[:, 2 * pair + 1 : 2 * pair + 2], (N, TILE)),
        )
        kept = ds * retain_pair
        kept_sum = jnp.sum(kept * stf, axis=0, keepdims=True)
        low_sum = jnp.sum(jnp.where(first[0:1], kept_sum, 0.0), axis=1, keepdims=True)
        high_sum = jnp.sum(jnp.where(first[0:1], 0.0, kept_sum), axis=1, keepdims=True)
        last_sum = last_sum + jnp.where(lane[0:1] == 2 * pair, low_sum, 0.0)
        last_sum = last_sum + jnp.where(lane[0:1] == 2 * pair + 1, high_sum, 0.0)
        dstate[:, tile] = kept + mm(c_t[...], dye)
        dx = total * step_pair + skip_ref[:, at : at + TILE] * dyf
        dskip_acc[:, tile] += jnp.sum((dyf * xf).reshape(SPAN // 8, 8, TILE), axis=0)
        out, conv_sums = conv_back(
            dx, ext, same, cw_ref[:, at : at + TILE], carry.at[:, :, tile], at, TILE
        )
        dpc_out[:, at : at + TILE] = out.astype(BF16)
        for k, value in enumerate(conv_sums):
            dcw_acc[k, :, tile] += value

    back_shift = GROUP * group
    in_place = (lane >= back_shift) & (lane < back_shift + GROUP)
    for kind in range(4):
        moved = pltpu.roll(sums, (back_shift + TILE - GROUP * kind) % TILE, 1)
        per_row[kind] += jnp.where(in_place, moved, 0.0)
    moved = pltpu.roll(jnp.broadcast_to(last_sum, (8, TILE)), back_shift, 1)
    dlast[...] += jnp.where(in_place[0:8], moved, 0.0)

    @pl.when(group == groups - 1)
    def _():
        ds_b = dscores[...].astype(BF16)
        grad_b = d_b[...] + mm(ds_b, query)
        grad_c = d_c[...] + mm(dscores[...].T.astype(BF16), keys)
        ext_bc[0:8] = bc_halo_ref[...]
        ext_bc[8:] = bc_ref[...]
        grad = jnp.concatenate([grad_b, grad_c], axis=1)
        out, conv_sums = conv_back(grad, ext_bc, same, bcw_ref[...], carry_bc, 0, 2 * N)
        dbc_out[...] = out.astype(BF16)
        for k, value in enumerate(conv_sums):
            dbcw_out[k] += value
        heads = heads_ref[...]
        raw = raw_ref[...]
        step = step_sizes(raw, heads)
        state_part = step * 0.0 + per_row[1]
        dcum = dcum_rows[...].T - per_row[3] + per_row[2] - state_part
        dlast_all = dlast[0:1] + jnp.sum(state_part, axis=0, keepdims=True)
        row = lax.broadcasted_iota(jnp.int32, (SPAN, SPAN), 0)
        col = lax.broadcasted_iota(jnp.int32, (SPAN, SPAN), 1)
        tri = (row <= col).astype(F32)
        da = dot_f32(tri, dcum, ((1,), (0,)), HIGHEST) + dlast_all
        dstep = per_row[0] + da * heads[2:3]
        draw = dstep * jax.nn.sigmoid(raw + heads[0:1])
        live = lane < H
        draw = jnp.where(live, draw, 0.0)
        draw_out[...] = draw.astype(BF16)
        dhead_out[0] += jnp.sum(draw.reshape(SPAN // 8, 8, TILE), axis=0)
        dhead_out[1] += jnp.sum(jnp.where(live, da * step, 0.0).reshape(SPAN // 8, 8, TILE), axis=0)

    @pl.when((group == groups - 1) & (back == spans - 1))
    def _():
        dcw_out[...] = dcw_acc[...]
        dskip_out[...] = dskip_acc[...]


def run_backward(dy, x, bcv, states, pc, raw, conv_all, aux, seg_row, heads, skip):
    tokens, di = dy.shape
    spans = tokens // SPAN
    width = GROUP * P_SIZE
    groups = di // width
    last_block = di // (2 * N)
    turn = lambda s: spans - 1 - s
    halo = lambda s: jnp.maximum(turn(s) * (SPAN // 8) - 1, 0)
    grid_spec = pltpu.PrefetchScalarGridSpec(
        num_scalar_prefetch=0,
        grid=(spans, groups),
        in_specs=[
            pl.BlockSpec((SPAN, width), lambda s, g: (turn(s), g)),
            pl.BlockSpec((SPAN, width), lambda s, g: (turn(s), g)),
            pl.BlockSpec((SPAN, 2 * N), lambda s, g: (turn(s), 0)),
            pl.BlockSpec((N, width), lambda s, g: (turn(s), g)),
            pl.BlockSpec((SPAN, width), lambda s, g: (turn(s), g)),
            pl.BlockSpec((8, width), lambda s, g: (halo(s), g)),
            pl.BlockSpec((SPAN, 2 * N), lambda s, g: (turn(s), last_block)),
            pl.BlockSpec((8, 2 * N), lambda s, g: (halo(s), last_block)),
            pl.BlockSpec((SPAN, TILE), lambda s, g: (turn(s), 0)),
            pl.BlockSpec((8, width), lambda s, g: (0, g)),
            pl.BlockSpec((8, 2 * N), lambda s, g: (0, last_block)),
            pl.BlockSpec((SPAN, 8), lambda s, g: (turn(s), 0)),
            pl.BlockSpec((1, SPAN), lambda s, g: (0, turn(s))),
            pl.BlockSpec((8, TILE), lambda s, g: (0, 0)),
            pl.BlockSpec((1, width), lambda s, g: (0, g)),
        ],
        out_specs=[
            pl.BlockSpec((SPAN, width), lambda s, g: (turn(s), g)),
            pl.BlockSpec((SPAN, 2 * N), lambda s, g: (turn(s), 0)),
            pl.BlockSpec((SPAN, TILE), lambda s, g: (turn(s), 0)),
            pl.BlockSpec((5, 8, di), lambda s, g: (0, 0, 0)),
            pl.BlockSpec((5, 8, 2 * N), lambda s, g: (0, 0, 0)),
            pl.BlockSpec((8, di), lambda s, g: (0, 0)),
            pl.BlockSpec((2, 8, TILE), lambda s, g: (0, 0, 0)),
        ],
        scratch_shapes=[
            pltpu.VMEM((N, di), F32),
            pltpu.VMEM((SPAN, SPAN), F32),
            pltpu.VMEM((SPAN, SPAN), F32),
            pltpu.VMEM((SPAN, SPAN), F32),
            pltpu.VMEM((3, SPAN, TILE), F32),
            pltpu.VMEM((SPAN, TILE), F32),
            pltpu.VMEM((SPAN, TILE), F32),
            pltpu.VMEM((TILE, SPAN), F32),
            pltpu.VMEM((N, SPAN), BF16),
            pltpu.VMEM((SPAN + 8, width), F32),
            pltpu.VMEM((SPAN + 8, 2 * N), F32),
            pltpu.VMEM((3, 8, di), F32),
            pltpu.VMEM((3, 8, 2 * N), F32),
            pltpu.VMEM((SPAN, N), F32),
            pltpu.VMEM((SPAN, N), F32),
            pltpu.VMEM((4, SPAN, TILE), F32),
            pltpu.VMEM((TILE, SPAN), F32),
            pltpu.VMEM((8, TILE), F32),
            pltpu.VMEM((5, 8, di), F32),
            pltpu.VMEM((8, di), F32),
        ],
    )
    return pl.pallas_call(
        backward_kernel,
        grid_spec=grid_spec,
        out_shape=[
            jax.ShapeDtypeStruct((tokens, di), BF16),
            jax.ShapeDtypeStruct((tokens, 2 * N), BF16),
            jax.ShapeDtypeStruct((tokens, TILE), BF16),
            jax.ShapeDtypeStruct((5, 8, di), F32),
            jax.ShapeDtypeStruct((5, 8, 2 * N), F32),
            jax.ShapeDtypeStruct((8, di), F32),
            jax.ShapeDtypeStruct((2, 8, TILE), F32),
        ],
        compiler_params=pltpu.CompilerParams(dimension_semantics=("arbitrary", "arbitrary")),
        name="scan_backward",
    )(dy, x, bcv, states, pc, pc, pc, pc, raw, conv_all, conv_all, aux, seg_row, heads, skip)


def seg_facts(seg):
    length = seg.shape[0]
    cols = []
    for offset in (1, 2, 3):
        moved = jnp.concatenate([jnp.full((offset,), -1, jnp.int32), seg[:-offset]])
        cols.append((moved == seg).astype(F32))
    spans = length // SPAN
    ends = seg[SPAN - 1 :: SPAN]
    before = jnp.concatenate([seg[:1], ends[:-1]])
    cols.append((seg == jnp.repeat(before, SPAN)).astype(F32))
    cols.append((seg == jnp.repeat(ends, SPAN)).astype(F32))
    value = seg.astype(F32)
    cols.append(value)
    cols.append(value)
    cols.append(value)
    return jnp.stack(cols, axis=1), value[None, :]


def head_rows(dt_bias, a_log):
    rate = -jnp.exp(a_log)
    rows = jnp.stack([dt_bias, rate * LOG2E, rate] + [jnp.zeros_like(rate)] * 5, axis=0)
    return jnp.pad(rows, ((0, 0), (0, TILE - H)))


def pad_lanes(values, width):
    return jnp.pad(values, ((0, 0), (0, width - values.shape[1])))


def on_device(
    tokens,
    seg_ids,
    gain_in,
    w_in,
    conv_weight,
    conv_bias,
    dt_bias,
    a_log,
    d_skip,
    gain_out,
    w_out,
    cotangent,
):
    shards = lax.psum(1, "shard")
    conv_local = conv_bias.shape[0]
    small = jnp.concatenate([conv_weight.reshape(-1), conv_bias, gain_in, gain_out])
    small_all = lax.all_gather(small, "shard", axis=0, tiled=False)
    full_w_in = lax.all_gather(w_in, "shard", axis=0, tiled=True)
    full_w_out = lax.all_gather(w_out, "shard", axis=0, tiled=True)
    taps = conv_weight.shape[0]
    cut = taps * conv_local
    conv_w = small_all[:, :cut].reshape(shards, taps, conv_local).transpose(1, 0, 2).reshape(taps, -1)
    conv_b = small_all[:, cut : cut + conv_local].reshape(1, -1)
    cut += conv_local
    full_gain_in = small_all[:, cut : cut + gain_in.shape[0]].reshape(-1).astype(F32)
    full_gain_out = small_all[:, cut + gain_in.shape[0] :].reshape(-1).astype(F32)
    conv_all = jnp.concatenate(
        [conv_w.astype(F32), conv_b.astype(F32), jnp.zeros((3, conv_w.shape[1]), F32)], axis=0
    )
    di = full_gain_out.shape[0]
    conv_dim = conv_w.shape[1]
    inputs = tokens.astype(F32)
    rscale = lax.rsqrt(jnp.mean(inputs * inputs, axis=1, keepdims=True) + EPSILON)
    unit = inputs * rscale
    normed = (unit * full_gain_in[None]).astype(BF16)
    seg = seg_ids[0]
    aux, seg_row = seg_facts(seg)
    heads = head_rows(dt_bias, a_log)
    skip = jnp.repeat(d_skip, P_SIZE)[None]

    w_gate = full_w_in[:, :di]
    w_conv = full_w_in[:, di : di + conv_dim]
    w_step = pad_lanes(full_w_in[:, di + conv_dim :], TILE)
    pc = mm(normed, w_conv)
    raw = mm(normed, w_step)
    gate = mm(normed, w_gate)
    x, bcv, y, states = run_forward(pc, raw, conv_all, aux, seg_row, heads, skip)
    gated = y * (gate * jax.nn.sigmoid(gate))
    inverse = lax.rsqrt(jnp.mean(gated * gated, axis=1, keepdims=True) + EPSILON)
    ynorm = (gated * inverse * full_gain_out[None]).astype(BF16)
    projected = mm(ynorm, full_w_out)
    output = (inputs + projected).astype(BF16)
    cot = cotangent.astype(F32)
    dots = jnp.sum(cot * projected, axis=1, keepdims=True)
    grad_ynorm = mm_nt(cotangent, full_w_out)
    grad_w_out = dot_f32(ynorm, cotangent, ((0,), (0,)))
    dz = inverse * (full_gain_out[None] * grad_ynorm) - gated * (inverse * inverse * dots / di)
    sig = jax.nn.sigmoid(gate)
    dy = (dz * (gate * sig)).astype(BF16)
    dgate = (dz * y * (sig * (1.0 + gate * (1.0 - sig)))).astype(BF16)
    dpc, dbc, draw, dcw, dbcw, dskip, dhead = run_backward(
        dy, x, bcv, states, pc, raw, conv_all, aux, seg_row, heads, skip
    )
    grad_projected = jnp.concatenate([dgate, dpc, dbc, draw[:, :H]], axis=1)
    grad_w_in = dot_f32(normed, grad_projected, ((0,), (0,)))
    grad_normed = mm_nt(grad_projected, full_w_in)
    scaled = grad_normed * full_gain_in[None]
    inner = jnp.mean(unit * scaled, axis=1, keepdims=True)
    grad_tokens = (cot + rscale * (scaled - unit * inner)).astype(BF16)

    conv_sums = jnp.concatenate([dcw, dbcw], axis=2).sum(1)
    conv_sums = jnp.concatenate([conv_sums[4:5], conv_sums[3:4], conv_sums[2:3], conv_sums[1:2], conv_sums[0:1]])
    per_head = jnp.concatenate(
        [
            dhead[0].sum(0)[:H],
            dhead[1].sum(0)[:H] * -jnp.exp(a_log),
            dskip.sum(0).reshape(H, P_SIZE).sum(1),
        ]
    )
    conv_part = conv_sums.reshape(taps + 1, shards, conv_local).transpose(1, 0, 2).reshape(shards, -1)
    small_grad = jnp.concatenate([conv_part, jnp.broadcast_to(per_head[None], (shards, 3 * H))], axis=1)
    small_sum = lax.psum(lax.psum_scatter(small_grad, "shard", scatter_dimension=0, tiled=True), "rep")[0]
    sum_w_in = lax.psum_scatter(grad_w_in.astype(BF16), "shard", scatter_dimension=0, tiled=True)
    sum_w_out = lax.psum_scatter(grad_w_out.astype(BF16), "shard", scatter_dimension=0, tiled=True)
    sum_w_in, sum_w_out = lax.psum((sum_w_in.astype(F32), sum_w_out.astype(F32)), "rep")
    grad_gain_in = jnp.sum(sum_w_in * w_in.astype(F32), axis=1) / gain_in.astype(F32)
    grad_gain_out = jnp.sum(sum_w_out * w_out.astype(F32), axis=1) / gain_out.astype(F32)
    cut = taps * conv_local
    head_at = cut + conv_local
    return (
        output,
        grad_tokens,
        grad_gain_in,
        sum_w_in,
        small_sum[:cut].reshape(taps, conv_local),
        small_sum[cut:head_at],
        small_sum[head_at : head_at + H],
        small_sum[head_at + H : head_at + 2 * H],
        small_sum[head_at + 2 * H :],
        grad_gain_out,
        sum_w_out,
    )


def solution(mesh):
    rows = P(("shard", "rep"), None)
    in_specs = (
        rows, rows, P("shard"), P("shard", None), P(None, "shard"), P("shard"), P(), P(), P(), P("shard"),
        P("shard", None), rows,
    )
    out_specs = (
        rows, rows, P("shard"), P("shard", None), P(None, "shard"), P("shard"), P(), P(), P(), P("shard"),
        P("shard", None),
    )
    return jax.shard_map(
        on_device, mesh=mesh, in_specs=in_specs, out_specs=out_specs, check_vma=False
    )
```

time: 2730 us -> 1150 us (0.42); the launches traced: 2700 us -> 1150 us
  local copies, waits for them, and re-layouts: 941 us -> 16.7 us
  matrix products: 541 us -> 166 us
  other arithmetic: 343 us -> 19.4 us
  Pallas kernels: 0 us -> 173 us
  blocking collectives: 238 us -> 93.8 us
  waiting for transfers between devices: 585 us -> 661 us
  loops' own time: 29.1 us -> 0 us
    dynamic_update_slice x24 -> x0, local copies, waits for them, and re-layouts: 596 us -> none  [ssd_scan(): ending, result = lax.scan(jax.checkpoint(span_step), start, pieces)]
    dot_general x62 -> x8, matrix products: 541 us -> 166 us  [dot_f32(): lax.dot_general(a, b, ((contract[0], contract[1]), ((), ())), preferred_e...]
    pallas_call x0 -> x2, Pallas kernels: none -> 173 us  [the longest x1 122 us: run_backward(): pl.pallas_call(backward_kernel, grid_spec=grid_spec, out_shape=[jax.Shape...]
    reduce_sum x16 -> x7, other arithmetic: 137 us -> 8.77 us  [the longest x1 2.57 us: on_device(): jnp.mean(inputs * inputs, axis=1, keepdims=True) + EPSILON]
    mul x45 -> x1, other arithmetic: 77.6 us -> 0.01 us  [on_device(): dhead[1].sum(0)[:H] * -jnp.exp(a_log)]
    unnamed x2 -> x1, blocking collectives: 158 us -> 80.8 us
    reduce_scatter x2, waiting for transfers between devices: 411 us -> 482 us  [the longest x1 307 us: on_device(): lax.psum_scatter(grad_w_in.astype(BF16), 'shard', scatter_dimension=0, ti...]
    all_gather x2, waiting for transfers between devices: 95.5 us -> 159 us  [the longest x1 128 us: on_device(): full_w_in = lax.all_gather(w_in, 'shard', axis=0, tiled=True)]
  transfers between devices with their start and end apart: 6 -> 5, of which waited for: 4 -> 5; matrix products, arithmetic and copies ran while one was open for 67% -> 13% of each run, Pallas kernels for 0% -> 4%
where the time goes in v1:
time: 1150 us
  waiting for transfers between devices  661 us (57%)
  Pallas kernels  173 us (15%)
  matrix products  166 us (14%)
  blocking collectives  93.8 us (8%)
  other arithmetic  19.4 us (2%)
  local copies, waits for them, and re-layouts  16.7 us (1%)
  between operations  14.9 us (1%)
    reduce_scatter x1, waiting for transfers between devices, on_device(): lax.psum_scatter(grad_w_in.astype(BF16), 'shard', scatter_dimension=0, ti...  307 us
    reduce_scatter x1, waiting for transfers between devices, on_device(): lax.psum_scatter(grad_w_out.astype(BF16), 'shard', scatter_dimension=0, t...  175 us
    dot_general x8, matrix products, dot_f32(): lax.dot_general(a, b, ((contract[0], contract[1]), ((), ())), preferred_e...  166 us
    all_gather x1, waiting for transfers between devices, on_device(): full_w_in = lax.all_gather(w_in, 'shard', axis=0, tiled=True)  128 us
    pallas_call x1, Pallas kernels, run_backward(): pl.pallas_call(backward_kernel, grid_spec=grid_spec, out_shape=[jax.Shape...  122 us
    unnamed x1, blocking collectives  80.8 us
    pallas_call x1, Pallas kernels, run_forward(): pl.pallas_call(forward_kernel, grid_spec=grid_spec, out_shape=[jax.ShapeD...  51 us
    all_gather x1, waiting for transfers between devices, on_device(): full_w_out = lax.all_gather(w_out, 'shard', axis=0, tiled=True)  30.4 us
  transfers between devices with their start and end apart: 5, of which 5 were waited for; matrix products, arithmetic and copies ran while one was open for 13% of the time, Pallas kernels for 4%

profile of v1, /device:TPU:0, one launch (start us, length us, event | category | flops | bytes accessed | tf_op | source)
XLA Modules:
  0.0 1145.5 jit_solution(12578675813934719106)
XLA Ops:
  17.6 2.1 concatenate.42
  20.0 80.8 %all-reduce.4 = bf16[21248]{0:T(1024)(128)(2,1)S(1)} all-reduce(bf16[21248]{0:T(1024)(128)(2,1)S(1)} %dynamic-update-slice), channel_id=2, replica_groups=mesh['shard'=16,'rep'=2] {'shard'}, use_global_device_ids=true, to_apply=%add.4 | all-reduce | flops 21248 | bytes 84992
  102.4 1.4 fusion.33
  106.6 2.6 fusion.14
  109.9 128.3 %all-gather.4.cloned.1.call-done = bf16[1536,6448]{1,0:T(8,128)(2,1)} async-done(((bf16[96,6448]{1,0:T(8,128)(2,1)}), bf16[1536,6448]{1,0:T(8,128)(2,1)}) %all-gather.4.cloned.1.call-update) | async-done | bytes 19808272 | tf_op jit(solution)/shard_map/all_gather | solution.py:580
  239.2 1.8 fusion.18.raw_ref
  241.0 17.0 %fusion.1.pc_ref.halo_ref.bc_ref.bc_halo_ref = f32[1024,3328]{1,0:T(8,128)} fusion(bf16[1536,6448]{1,0:T(8,128)(2,1)} %all-gather.4.cloned.1.call-done, bf16[1024,1536]{1,0:T(8,128)(2,1)S(1)} %copy-done, f32[1536]{0:T(1024)S(1)} %reshape.215, f32[1024]{0:T(1024)S(1)} %add_rsqrt_fusion.1), kind=kOutput, calls=%fused_computation.10 | convolution fusion | flops 10475274240 | bytes 27011072 | tf_op jit(solution)/shard_map/dot_general | solution.py:24
  258.0 51.0 %scan_forward.1 = (bf16[1024,3072]{1,0:T(8,128)(2,1)}, bf16[1024,256]{1,0:T(8,128)(2,1)}, f32[1024,3072]{1,0:T(8,128)}, bf16[512,3072]{1,0:T(8,128)(2,1)}) custom-call(f32[1024,3328]{1,0:T(8,128)} %fusion.1.pc_ref.halo_ref.bc_ref.bc_halo_ref, f32[1024,3328]{1,0:T(8,128)} %fusion.1.pc_ref.halo_ref.bc_ref.bc_halo_ref, ...), custom_call_target="tpu_custom_call" | custom-call | tf_op jit(solution)/shard_map/scan_forward/pallas_call | solution.py:224
  309.1 22.2 %multiply_reduce_fusion = (f32[1024]{0:T(1024)S(1)}, f32[1024,3072]{1,0:T(8,128)}, f32[1024,3072]{1,0:T(8,128)}) fusion(f32[1024,3072]{1,0:T(8,128)} %get-tuple-element.22, bf16[1536,6448]{1,0:T(8,128)(2,1)} %all-gather.4.cloned.1.call-done, bf16[1024,1536]{1,0:T(8,128)(2,1)S(1)} %copy-done, f32[1536]{0:T(1024)S(1)} %reshape.215, f32[1024]{0:T(1024)S(1)} %add_rsqrt_fusion.1), kind=kOutput, calls=%fused_computation.6 | convolution fusion | flops 9691986944 | bytes 50345984 | tf_op jit(solution)/shard_map/dot_general | solution.py:24
  331.2 30.4 %all-gather.6.cloned.1.call-done = bf16[3072,1536]{1,0:T(8,128)(2,1)} async-done(((bf16[192,1536]{1,0:T(8,128)(2,1)}), bf16[3072,1536]{1,0:T(8,128)(2,1)}) %all-gather.6.cloned.1.call-update) | async-done | bytes 9437200 | tf_op jit(solution)/shard_map/all_gather | solution.py:581
  361.6 17.7 %fusion.8 = (f32[1024]{0:T(1024)S(1)}, bf16[1024,1536]{1,0:T(8,128)(2,1)}) fusion(bf16[1024,1536]{1,0:T(8,128)(2,1)} %param.23, bf16[1024,1536]{1,0:T(8,128)(2,1)S(1)} %copy-done, bf16[3072,1536]{1,0:T(8,128)(2,1)} %all-gather.6.cloned.1.call-done, f32[1024,3072]{1,0:T(8,128)} %get-tuple-element.39, f32[3072]{0:T(1024)S(1)} %reshape.220, ...), kind=kOutput, calls=%fused_computation.22 | convolution fusion | flops 9682549760 | bytes 31477760 | tf_op jit(solution)/shard_map/dot_general | solution.py:24
  379.4 28.8 %multiply_convert_fusion.1 = (bf16[1024,3072]{1,0:T(8,128)(2,1)}, bf16[1024,3072]{1,0:T(8,128)(2,1)}) fusion(f32[1024,3072]{1,0:T(8,128)} %get-tuple-element.63, f32[1024,3072]{1,0:T(8,128)} %get-tuple-element.22, f32[1024,3072]{1,0:T(8,128)} %get-tuple-element.39, f32[1024]{0:T(1024)S(1)} %multiply_multiply_fusion, bf16[1024,1536]{1,0:T(8,128)(2,1)} %param.23, ...), kind=kOutput, calls=%fused_computation.3 | convolution fusion | flops 9717153792 | bytes 62935040 | tf_op jit(solution)/shard_map/dot_general | solution.py:24
  408.2 121.8 %scan_backward.1 = (bf16[1024,3072]{1,0:T(8,128)(2,1)}, bf16[1024,256]{1,0:T(8,128)(2,1)}, bf16[1024,128]{1,0:T(8,128)(2,1)}, f32[5,8,3072]{2,1,0:T(8,128)}, f32...) custom-call(bf16[1024,3072]{1,0:T(8,128)(2,1)} %get-tuple-element.41.dy_ref, ...), custom_call_target="tpu_custom_call" | custom-call | tf_op jit(solution)/shard_map/scan_backward/pallas_call | solution.py:517
  534.3 16.6 %convolution_convert_fusion.1 = bf16[3072,1536]{1,0:T(8,128)(2,1)} fusion(bf16[1024,1536]{1,0:T(8,128)(2,1)} %param.23, f32[1024,3072]{1,0:T(8,128)} %get-tuple-element.39, f32[3072]{0:T(1024)S(1)} %reshape.220, f32[1024]{0:T(1024)S(1)} %add_rsqrt_fusion), kind=kOutput, calls=%fused_computation.9 | convolution fusion | flops 9677832192 | bytes 25182208 | tf_op jit(solution)/shard_map/dot_general | solution.py:24
  551.0 30.7 %convolution_convert_fusion = bf16[1536,6448]{1,0:T(8,128)(2,1)} fusion(bf16[1024,48]{1,0:T(8,128)(2,1)} %bitcast.65, bf16[1024,256]{1,0:T(8,128)(2,1)} %get-tuple-element.27, bf16[1024,3072]{1,0:T(8,128)(2,1)} %get-tuple-element.26, bf16[1024,3072]{1,0:T(8,128)(2,1)} %get-tuple-element.40, bf16[1024,1536]{1,0:T(8,128)(2,1)S(1)} %copy-done, ...), kind=kOutput, calls=%fused_computation | convolution fusion | flops 20352671744 | bytes 36169728 | tf_op jit(solution)/shard_map/dot_general | solution.py:24
  581.7 31.6 %fusion.11 = (f32[1024]{0:T(1024)S(1)}, f32[1024,1536]{1,0:T(8,128)S(1)}) fusion(bf16[1024,1536]{1,0:T(8,128)(2,1)S(1)} %copy-done, f32[1536]{0:T(1024)S(1)} %reshape.215, f32[1024]{0:T(1024)S(1)} %add_rsqrt_fusion.1, bf16[1536,6448]{1,0:T(8,128)(2,1)} %all-gather.4.cloned.1.call-done, bf16[1024,48]{1,0:T(8,128)(2,1)} %bitcast.66, ...), kind=kOutput, calls=%fused_computation.25 | convolution fusion | flops 20344340480 | bytes 42465280 | tf_op jit(solution)/shard_map/dot_general | solution.py:24
  613.4 3.4 fusion.9
  616.8 19.0 %all-reduce.10.cloned.1.call-done = f32[16,1184]{1,0:T(8,128)} async-done(((f32[16,1184]{1,0:T(8,128)}), f32[16,1184]{1,0:T(8,128)}) %all-reduce.10.cloned.1.call-update) | async-done | bytes 75792
  635.8 1.4 constant_dynamic-slice_fusion
  637.2 175.2 %reduce-scatter.5.cloned.1.call-done = bf16[192,1536]{1,0:T(8,128)(2,1)} async-done(((bf16[3072,1536]{1,0:T(8,128)(2,1)}), bf16[192,1536]{1,0:T(8,128)(2,1)}) %reduce-scatter.5.cloned.1.call-update) | async-done | bytes 589840 | tf_op jit(solution)/shard_map/reduce_scatter | solution.py:646
  812.4 306.9 %reduce-scatter.3.cloned.1.call-done = bf16[96,6448]{1,0:T(8,128)(2,1)} async-done(((bf16[1536,6448]{1,0:T(8,128)(2,1)}), bf16[96,6448]{1,0:T(8,128)(2,1)}) %reduce-scatter.3.cloned.1.call-update) | async-done | bytes 1238032 | tf_op jit(solution)/shard_map/reduce_scatter | solution.py:645
  1119.3 13.0 %all-reduce.11 = (f32[96,6448]{1,0:T(8,128)S(1)}, f32[1,1184]{1,0:T(1,128)S(1)}, f32[192,1536]{1,0:T(8,128)}) all-reduce(bf16[96,6448]{1,0:T(8,128)(2,1)} %reduce-scatter.3.cloned.1.call-done, f32[1,1184]{1,0:T(1,128)S(1)} %constant_dynamic-slice_fusion, ...), channel_id=1, replica_groups=mesh['shard'=16,'rep'=2] {'rep'}, use_global_device_ids=true, to_apply=%region_5.6 | all-reduce | flops 915104 | bytes 5492992 | tf_op jit(solution)/shard_map/psum | solution.py:647
  1133.7 1.6 multiply_reduce_fusion.1
  1135.9 1.6 multiply_reduce_fusion.2
  (83 shorter events, 23.5 us)
Async XLA Ops:
  7.2 232.0 %copy-start = (bf16[1024,1536]{1,0:T(8,128)(2,1)S(1)}, bf16[1024,1536]{1,0:T(8,128)(2,1)}, u32[]{:S(2)}) copy-start(bf16[1024,1536]{1,0:T(8,128)(2,1)} %param.12) | copy-start | bytes 9437188
  7.2 230.9 %all-gather.4.cloned.1.call-start = ((), (), s32[]{:S(2)}) async-start(), calls=%async_computation.2 | async-start | bytes 21307392 | tf_op jit(solution)/shard_map/all_gather | solution.py:580
  7.9 353.7 %all-gather.6.cloned.1.call-start = ((), (), s32[]{:S(2)}) async-start(), calls=%async_computation.3 | async-start | bytes 10027008 | tf_op jit(solution)/shard_map/all_gather | solution.py:581
  8.7 627.1 %all-reduce.10.cloned.1.call-start = ((), (), s32[]{:S(2)}) async-start(), calls=%async_computation.6 | async-start | bytes 163840
  408.2 122.5 %copy-start.5 = (f32[48]{0:T(128)S(1)}, f32[48]{0:T(128)}, u32[]{:S(2)}) copy-start(f32[48]{0:T(128)} %param.19) | copy-start | bytes 580
  534.2 278.1 %reduce-scatter.5.cloned.1.call-start = ((), (), s32[]{:S(2)}) async-start(), calls=%async_computation.5 | async-start | bytes 10027008 | tf_op jit(solution)/shard_map/reduce_scatter | solution.py:646
  550.9 568.4 %reduce-scatter.3.cloned.1.call-start = ((), (), s32[]{:S(2)}) async-start(), calls=%async_computation.4 | async-start | bytes 21307392 | tf_op jit(solution)/shard_map/reduce_scatter | solution.py:645
  581.7 31.7 %copy-start.1 = (bf16[1024,1536]{1,0:T(8,128)(2,1)S(1)}, bf16[1024,1536]{1,0:T(8,128)(2,1)}, u32[]{:S(2)}) copy-start(bf16[1024,1536]{1,0:T(8,128)(2,1)} %param.23) | copy-start | bytes 9437188
  613.3 522.0 %copy-start.4 = (bf16[96]{0:T(256)(128)(2,1)S(1)}, bf16[96]{0:T(256)(128)(2,1)}, u32[]{:S(2)}) copy-start(bf16[96]{0:T(256)(128)(2,1)} %param.14) | copy-start | bytes 580
  616.8 520.7 %copy-start.3 = (bf16[192]{0:T(256)(128)(2,1)S(1)}, bf16[192]{0:T(256)(128)(2,1)}, u32[]{:S(2)}) copy-start(bf16[192]{0:T(256)(128)(2,1)} %param.21) | copy-start | bytes 1156
  1132.3 6.4 copy-start.2
Sparse Core Ops, SparseCore 0:
  10.8 227.2 all-gather.3
  240.9 120.6 all-gather.5
  534.4 101.3 all-reduce.9
  641.3 171.0 reduce-scatter.4
  819.1 300.1 reduce-scatter.2

commit v2 on v1

--- a/solution.py
+++ b/solution.py
@@ -1,3 +1,5 @@
+import functools
+
 import jax
 import jax.numpy as jnp
 from jax import lax
@@ -133,7 +135,6 @@
         for head in (2 * pair, 2 * pair + 1):
             cum_col = lanes_of(cols_a[:, head : head + 1], SPAN)
             cum_row = cum_rows[pl.ds(group * GROUP + head, 1), :]
-            step_row = None
             blocks = []
             for i, j in ((0, 0), (1, 0), (1, 1)):
                 rows = slice(i * HALF, (i + 1) * HALF)
@@ -146,7 +147,6 @@
             lanes_of(cols_a[:, 64 + 2 * pair : 65 + 2 * pair], SPAN),
             lanes_of(cols_a[:, 65 + 2 * pair : 66 + 2 * pair], SPAN),
         )
-        xs = x * step_pair
         xs = xb.astype(F32) * step_pair
         xsb = xs.astype(BF16)
         outs = []
@@ -178,10 +178,11 @@
         state[:, tile] = old * retain_pair + mm(b_t[...], (xs * tail_pair).astype(BF16))
 
 
-def run_forward(pc, raw, conv_all, aux, seg_row, heads, skip):
+def run_forward(pc, conv_all, aux, seg_row, heads, skip):
     tokens = pc.shape[0]
     spans = tokens // SPAN
-    di = pc.shape[1] - 2 * N
+    di = skip.shape[1]
+    raw_block = (di + 2 * N) // TILE
     width = GROUP * P_SIZE
     groups = di // width
     last_block = di // (2 * N)
@@ -193,7 +194,7 @@
             pl.BlockSpec((8, width), lambda s, g: (jnp.maximum(s * (SPAN // 8) - 1, 0), g)),
             pl.BlockSpec((SPAN, 2 * N), lambda s, g: (s, last_block)),
             pl.BlockSpec((8, 2 * N), lambda s, g: (jnp.maximum(s * (SPAN // 8) - 1, 0), last_block)),
-            pl.BlockSpec((SPAN, TILE), lambda s, g: (s, 0)),
+            pl.BlockSpec((SPAN, TILE), lambda s, g: (s, raw_block)),
             pl.BlockSpec((8, width), lambda s, g: (0, g)),
             pl.BlockSpec((8, 2 * N), lambda s, g: (0, last_block)),
             pl.BlockSpec((SPAN, 8), lambda s, g: (s, 0)),
@@ -232,7 +233,7 @@
         ],
         compiler_params=pltpu.CompilerParams(dimension_semantics=("arbitrary", "arbitrary")),
         name="scan_forward",
-    )(pc, pc, pc, pc, raw, conv_all, conv_all, aux, seg_row, heads, skip)
+    )(pc, pc, pc, pc, pc, conv_all, conv_all, aux, seg_row, heads, skip)
 
 
 def conv_back(grad, ext, same, weights, carry, start, width):
@@ -260,7 +261,7 @@
 def backward_kernel(
     dy_ref, x_ref, bcv_ref, st_ref, pc_ref, halo_ref, bc_ref, bc_halo_ref, raw_ref, cw_ref, bcw_ref,
     aux_ref, seg_ref, heads_ref, skip_ref,
-    dpc_out, dbc_out, draw_out, dcw_out, dbcw_out, dskip_out, dhead_out,
+    dproj_out, dcw_out, dbcw_out, dskip_out, dhead_out,
     dstate, scores, block, dscores, same, pack_a, pack_b, cum_rows, c_t, ext, ext_bc,
     carry, carry_bc, d_b, d_c, per_row, dcum_rows, dlast, dcw_acc, dskip_acc,
 ):
@@ -406,7 +407,7 @@
         out, conv_sums = conv_back(
             dx, ext, same, cw_ref[:, at : at + TILE], carry.at[:, :, tile], at, TILE
         )
-        dpc_out[:, at : at + TILE] = out.astype(BF16)
+        dproj_out[:, tile] = out.astype(BF16)
         for k, value in enumerate(conv_sums):
             dcw_acc[k, :, tile] += value
 
@@ -427,13 +428,14 @@
         ext_bc[8:] = bc_ref[...]
         grad = jnp.concatenate([grad_b, grad_c], axis=1)
         out, conv_sums = conv_back(grad, ext_bc, same, bcw_ref[...], carry_bc, 0, 2 * N)
-        dbc_out[...] = out.astype(BF16)
+        di = dstate.shape[1]
+        dproj_out[:, di : di + 2 * N] = out.astype(BF16)
         for k, value in enumerate(conv_sums):
             dbcw_out[k] += value
         heads = heads_ref[...]
         raw = raw_ref[...]
         step = step_sizes(raw, heads)
-        state_part = step * 0.0 + per_row[1]
+        state_part = per_row[1]
         dcum = dcum_rows[...].T - per_row[3] + per_row[2] - state_part
         dlast_all = dlast[0:1] + jnp.sum(state_part, axis=0, keepdims=True)
         row = lax.broadcasted_iota(jnp.int32, (SPAN, SPAN), 0)
@@ -444,7 +446,8 @@
         draw = dstep * jax.nn.sigmoid(raw + heads[0:1])
         live = lane < H
         draw = jnp.where(live, draw, 0.0)
-        draw_out[...] = draw.astype(BF16)
+        dproj_out[:, di + 2 * N : di + 2 * N + TILE] = draw.astype(BF16)
+        dproj_out[:, di + 2 * N + TILE :] = jnp.zeros_like(dproj_out[:, di + 2 * N + TILE :])
         dhead_out[0] += jnp.sum(draw.reshape(SPAN // 8, 8, TILE), axis=0)
         dhead_out[1] += jnp.sum(jnp.where(live, da * step, 0.0).reshape(SPAN // 8, 8, TILE), axis=0)
 
@@ -454,8 +457,10 @@
         dskip_out[...] = dskip_acc[...]
 
 
-def run_backward(dy, x, bcv, states, pc, raw, conv_all, aux, seg_row, heads, skip):
+def run_backward(dy, x, bcv, states, pc, conv_all, aux, seg_row, heads, skip):
     tokens, di = dy.shape
+    full = pc.shape[1]
+    raw_block = (di + 2 * N) // TILE
     spans = tokens // SPAN
     width = GROUP * P_SIZE
     groups = di // width
@@ -474,7 +479,7 @@
             pl.BlockSpec((8, width), lambda s, g: (halo(s), g)),
             pl.BlockSpec((SPAN, 2 * N), lambda s, g: (turn(s), last_block)),
             pl.BlockSpec((8, 2 * N), lambda s, g: (halo(s), last_block)),
-            pl.BlockSpec((SPAN, TILE), lambda s, g: (turn(s), 0)),
+            pl.BlockSpec((SPAN, TILE), lambda s, g: (turn(s), raw_block)),
             pl.BlockSpec((8, width), lambda s, g: (0, g)),
             pl.BlockSpec((8, 2 * N), lambda s, g: (0, last_block)),
             pl.BlockSpec((SPAN, 8), lambda s, g: (turn(s), 0)),
@@ -483,9 +488,7 @@
             pl.BlockSpec((1, width), lambda s, g: (0, g)),
         ],
         out_specs=[
-            pl.BlockSpec((SPAN, width), lambda s, g: (turn(s), g)),
-            pl.BlockSpec((SPAN, 2 * N), lambda s, g: (turn(s), 0)),
-            pl.BlockSpec((SPAN, TILE), lambda s, g: (turn(s), 0)),
+            pl.BlockSpec((SPAN, full), lambda s, g: (turn(s), 0)),
             pl.BlockSpec((5, 8, di), lambda s, g: (0, 0, 0)),
             pl.BlockSpec((5, 8, 2 * N), lambda s, g: (0, 0, 0)),
             pl.BlockSpec((8, di), lambda s, g: (0, 0)),
@@ -518,9 +521,7 @@
         backward_kernel,
         grid_spec=grid_spec,
         out_shape=[
-            jax.ShapeDtypeStruct((tokens, di), BF16),
-            jax.ShapeDtypeStruct((tokens, 2 * N), BF16),
-            jax.ShapeDtypeStruct((tokens, TILE), BF16),
+            jax.ShapeDtypeStruct((tokens, full), BF16),
             jax.ShapeDtypeStruct((5, 8, di), F32),
             jax.ShapeDtypeStruct((5, 8, 2 * N), F32),
             jax.ShapeDtypeStruct((8, di), F32),
@@ -528,7 +529,7 @@
         ],
         compiler_params=pltpu.CompilerParams(dimension_semantics=("arbitrary", "arbitrary")),
         name="scan_backward",
-    )(dy, x, bcv, states, pc, pc, pc, pc, raw, conv_all, conv_all, aux, seg_row, heads, skip)
+    )(dy, x, bcv, states, pc, pc, pc, pc, pc, conv_all, conv_all, aux, seg_row, heads, skip)
 
 
 def seg_facts(seg):
@@ -555,11 +556,299 @@
     return jnp.pad(rows, ((0, 0), (0, TILE - H)))
 
 
-def pad_lanes(values, width):
-    return jnp.pad(values, ((0, 0), (0, width - values.shape[1])))
+BLOCKS = 32
+ORDERS = ((8, 1, 4, 2), (8, 2, 4, 1))
+
+
+def reach(masks):
+    out = [0]
+    for mask in masks:
+        out = out + [mask ^ place for place in out]
+    return out
+
+
+def exchange(values, stage):
+    pairs = []
+    for shard in range(16):
+        for core in range(2):
+            pairs.append((shard * 2 + core, (shard ^ ORDERS[core][stage]) * 2 + core))
+    return lax.ppermute(values, ("shard", "rep"), pairs)
+
+
+def swap_cores(values):
+    return lax.ppermute(values, "rep", [(0, 1), (1, 0)])
+
+
+def gather_pieces(local):
+    held = local
+    arrived = None
+    for stage in range(4):
+        arrived = exchange(held, stage)
+        if stage < 3:
+            held = jnp.concatenate([held, arrived], axis=0)
+    return held, arrived, swap_cores(held), swap_cores(arrived)
+
+
+def gather_small(local):
+    held = local[None]
+    for stage in range(4):
+        held = jnp.concatenate([held, exchange(held, stage)], axis=0)
+    core = lax.axis_index("rep")
+    places = jnp.asarray([reach(order) for order in ORDERS], jnp.int32)[core] ^ lax.axis_index("shard")
+    hot = (places[None, :] == jnp.arange(16, dtype=jnp.int32)[:, None]).astype(local.dtype)
+    return dot_f32(hot, held, ((1,), (0,)), HIGHEST).astype(local.dtype)
+
+
+def scatter_sum(mine, other, block):
+    arrived = swap_cores(other)
+    total = mine.astype(F32) + arrived.astype(F32)
+    for stage in (3, 2, 1, 0):
+        cut = block << stage
+        total = total[:cut] + exchange(total[cut:].astype(BF16), stage).astype(F32)
+    return total
+
+
+def block_order():
+    shard = lax.axis_index("shard")
+    core = lax.axis_index("rep")
+    tables = jnp.asarray([reach(order) for order in ORDERS], jnp.int32)
+    inverse = jnp.asarray(
+        [[reach(order).index(mask) for mask in range(16)] for order in ORDERS], jnp.int32
+    )
+    own = 2 * (tables[core] ^ shard) + core
+    partner = 2 * (tables[1 - core] ^ shard) + (1 - core)
+    order = jnp.concatenate([own, partner])
+    natural = jnp.arange(BLOCKS, dtype=jnp.int32)
+    which = natural % 2
+    place = inverse[which, (natural // 2) ^ shard] + 16 * (which != core).astype(jnp.int32)
+    return order, place
+
+
+def fetch_tile(order_ref, pieces, buffer, sems, tile, slot, block, width):
+    for q in range(BLOCKS):
+        pltpu.make_async_copy(
+            pieces[q // 8].at[pl.ds((q % 8) * block, block), pl.ds(pl.multiple_of(tile * width, width), width)],
+            buffer.at[slot, pl.ds(pl.multiple_of(order_ref[q] * block, block), block), :],
+            sems.at[slot],
+        ).start()
+
+
+def next_tile(order_ref, pieces, buffer, sems, block, width):
+    tile = pl.program_id(0)
+    slot = lax.rem(tile, 2)
+
+    @pl.when(tile == 0)
+    def _():
+        fetch_tile(order_ref, pieces, buffer, sems, tile, slot, block, width)
+
+    @pl.when(tile + 1 < pl.num_programs(0))
+    def _():
+        fetch_tile(order_ref, pieces, buffer, sems, tile + 1, 1 - slot, block, width)
+
+    pltpu.make_async_copy(buffer.at[slot], buffer.at[slot], sems.at[slot]).wait()
+    return slot
+
+
+def project_kernel(block, width, order_ref, x_ref, p0, p1, p2, p3, *rest):
+    out_ref, w_ref, buffer, sems = rest[-4:]
+    slot = next_tile(order_ref, (p0, p1, p2, p3), buffer, sems, block, width)
+    w = buffer[slot]
+    w_ref[...] = w
+    for i in range(x_ref.shape[0] // SPAN):
+        rows = slice(i * SPAN, (i + 1) * SPAN)
+        out_ref[rows] = mm(x_ref[rows], w)
+
+
+def project(x, pieces, order, so_far, start, full, width=512):
+    tokens, depth = x.shape
+    columns = pieces[0].shape[1]
+    block = depth // BLOCKS
+    at = start // width
+    any_spec = pl.BlockSpec(memory_space=pl.ANY)
+    extra = [] if so_far is None else list(so_far)
+    return pl.pallas_call(
+        functools.partial(project_kernel, block, width),
+        grid_spec=pltpu.PrefetchScalarGridSpec(
+            num_scalar_prefetch=1,
+            grid=(columns // width,),
+            in_specs=[pl.BlockSpec((tokens, depth), lambda j, o: (0, 0))] + [any_spec] * (4 + len(extra)),
+            out_specs=[
+                pl.BlockSpec((tokens, width), lambda j, o: (0, at + j)),
+                pl.BlockSpec((depth, width), lambda j, o: (0, at + j)),
+            ],
+            scratch_shapes=[pltpu.VMEM((2, depth, width), BF16), pltpu.SemaphoreType.DMA((2,))],
+        ),
+        out_shape=[jax.ShapeDtypeStruct((tokens, full), F32), jax.ShapeDtypeStruct((depth, full), BF16)],
+        input_output_aliases={} if so_far is None else {6: 0, 7: 1},
+        cost_estimate=pl.CostEstimate(
+            flops=2 * tokens * depth * columns,
+            bytes_accessed=4 * depth * columns + 4 * tokens * columns + 2 * tokens * depth,
+            transcendentals=0,
+        ),
+        name="project",
+    )(order, x, *pieces, *extra)
+
+
+def gate_kernel(block, width, order_ref, x_ref, p0, p1, p2, p3, y_ref, gain_ref, *rest):
+    gate_ref, w_ref, zg_ref, square_ref, buffer, sems = rest[-6:]
+    slot = next_tile(order_ref, (p0, p1, p2, p3), buffer, sems, block, width)
+    w = buffer[slot]
+    w_ref[...] = w
+
+    @pl.when(pl.program_id(0) == 0)
+    def _():
+        square_ref[...] = jnp.zeros_like(square_ref)
+
+    for i in range(x_ref.shape[0] // SPAN):
+        rows = slice(i * SPAN, (i + 1) * SPAN)
+        gate = mm(x_ref[rows], w)
+        gate_ref[rows] = gate
+        gated = y_ref[rows] * (gate * jax.nn.sigmoid(gate))
+        zg_ref[rows] = (gated * gain_ref[...]).astype(BF16)
+        square = gated * gated
+        total = square[:, :TILE]
+        for k in range(1, width // TILE):
+            total = total + square[:, k * TILE : (k + 1) * TILE]
+        square_ref[rows] += total
+
+
+def gate_project(x, pieces, order, y, gain, so_far, start, full, width=512):
+    tokens, depth = x.shape
+    columns = pieces[0].shape[1]
+    block = depth // BLOCKS
+    at = start // width
+    any_spec = pl.BlockSpec(memory_space=pl.ANY)
+    extra = [] if so_far is None else list(so_far)
+    wide = pl.BlockSpec((tokens, width), lambda j, o: (0, at + j))
+    return pl.pallas_call(
+        functools.partial(gate_kernel, block, width),
+        grid_spec=pltpu.PrefetchScalarGridSpec(
+            num_scalar_prefetch=1,
+            grid=(columns // width,),
+            in_specs=[pl.BlockSpec((tokens, depth), lambda j, o: (0, 0))]
+            + [any_spec] * 4
+            + [wide, pl.BlockSpec((1, width), lambda j, o: (0, at + j))]
+            + [any_spec] * len(extra),
+            out_specs=[
+                wide,
+                pl.BlockSpec((depth, width), lambda j, o: (0, at + j)),
+                wide,
+                pl.BlockSpec((tokens, TILE), lambda j, o: (0, 0)),
+            ],
+            scratch_shapes=[pltpu.VMEM((2, depth, width), BF16), pltpu.SemaphoreType.DMA((2,))],
+        ),
+        out_shape=[
+            jax.ShapeDtypeStruct((tokens, full), F32),
+            jax.ShapeDtypeStruct((depth, full), BF16),
+            jax.ShapeDtypeStruct((tokens, full), BF16),
+            jax.ShapeDtypeStruct((tokens, TILE), F32),
+        ],
+        input_output_aliases={} if so_far is None else {8: 0, 9: 1, 10: 2},
+        cost_estimate=pl.CostEstimate(
+            flops=2 * tokens * depth * columns,
+            bytes_accessed=4 * depth * columns + 10 * tokens * columns + 2 * tokens * depth,
+            transcendentals=tokens * columns,
+        ),
+        name="project_gate",
+    )(order, x, *pieces, y, gain, *extra)
+
+
+def restore_kernel(block, width, order_ref, p0, p1, p2, p3, *rest):
+    w_ref, buffer, sems = rest[-3:]
+    slot = next_tile(order_ref, (p0, p1, p2, p3), buffer, sems, block, width)
+    w_ref[...] = buffer[slot]
+
+
+def restore(pieces, order, so_far, start, full, width=256):
+    columns = pieces[0].shape[1]
+    block = pieces[0].shape[0] // 8
+    depth = block * BLOCKS
+    at = start // width
+    any_spec = pl.BlockSpec(memory_space=pl.ANY)
+    extra = [] if so_far is None else [so_far]
+    return pl.pallas_call(
+        functools.partial(restore_kernel, block, width),
+        grid_spec=pltpu.PrefetchScalarGridSpec(
+            num_scalar_prefetch=1,
+            grid=(columns // width,),
+            in_specs=[any_spec] * (4 + len(extra)),
+            out_specs=pl.BlockSpec((depth, width), lambda j, o: (0, at + j)),
+            scratch_shapes=[pltpu.VMEM((2, depth, width), BF16), pltpu.SemaphoreType.DMA((2,))],
+        ),
+        out_shape=jax.ShapeDtypeStruct((depth, full), BF16),
+        input_output_aliases={} if so_far is None else {5: 0},
+        cost_estimate=pl.CostEstimate(flops=0, bytes_accessed=4 * depth * columns, transcendentals=0),
+        name="restore",
+    )(order, *pieces, *extra)
+
+
+def weight_grad_kernel(block, place_ref, lhs_ref, rhs_ref, mine, other, buffer, sems):
+    step = pl.program_id(0)
+    slot = lax.rem(step, 2)
+
+    def settle(which):
+        pltpu.make_async_copy(buffer.at[which], buffer.at[which], sems.at[which]).wait()
+
+    @pl.when(step >= 2)
+    def _():
+        settle(slot)
+
+    buffer[slot] = dot_f32(lhs_ref[...], rhs_ref[...], ((0,), (0,))).astype(BF16)
+    for t in range(8):
+        q = place_ref[step * 8 + t]
+        source = buffer.at[slot, pl.ds(t * block, block), :]
+
+        @pl.when(q < 16)
+        def _():
+            pltpu.make_async_copy(
+                source, mine.at[pl.ds(pl.multiple_of(q * block, block), block), :], sems.at[slot]
+            ).start()
+
+        @pl.when(q >= 16)
+        def _():
+            pltpu.make_async_copy(
+                source, other.at[pl.ds(pl.multiple_of((q - 16) * block, block), block), :], sems.at[slot]
+            ).start()
+
+    @pl.when(step == pl.num_programs(0) - 1)
+    def _():
+        settle(1 - slot)
+        settle(slot)
+
+
+def weight_grad(lhs, rhs, place, column, columns):
+    tokens, rows = lhs.shape
+    block = rows // BLOCKS
+    any_spec = pl.BlockSpec(memory_space=pl.ANY)
+    out = jax.ShapeDtypeStruct((16 * block, columns), BF16)
+    return pl.pallas_call(
+        functools.partial(weight_grad_kernel, block),
+        grid_spec=pltpu.PrefetchScalarGridSpec(
+            num_scalar_prefetch=1,
+            grid=(4,),
+            in_specs=[
+                pl.BlockSpec((tokens, 8 * block), lambda i, o: (0, i)),
+                pl.BlockSpec((tokens, columns), lambda i, o: (0, column)),
+            ],
+            out_specs=[any_spec, any_spec],
+            scratch_shapes=[pltpu.VMEM((2, 8 * block, columns), BF16), pltpu.SemaphoreType.DMA((2,))],
+        ),
+        out_shape=[out, out],
+        cost_estimate=pl.CostEstimate(
+            flops=2 * tokens * rows * columns,
+            bytes_accessed=2 * (tokens * rows + tokens * columns + rows * columns),
+            transcendentals=0,
+        ),
+        name="weight_grad",
+    )(place, lhs, rhs)
+
+
+def rows_of(packed, start, count):
+    return packed[:, start : start + count]
 
 
 def on_device(
+    hypercube,
     tokens,
     seg_ids,
     gain_in,
@@ -574,59 +863,94 @@
     cotangent,
 ):
     shards = lax.psum(1, "shard")
-    conv_local = conv_bias.shape[0]
+    taps, conv_local = conv_weight.shape
+    model = tokens.shape[1]
+    di = gain_out.shape[0] * shards
+    conv_dim = conv_local * shards
+    wide = -(-(conv_dim + TILE) // 512) * 512
+    cuts = ((0, 1024), (1024, 1024), (2048, wide - 2048))
+    halves = ((0, di // 2), (di // 2, di // 2))
+    thirds = ((0, model // 2), (model // 2, model // 2))
+
     small = jnp.concatenate([conv_weight.reshape(-1), conv_bias, gain_in, gain_out])
-    small_all = lax.all_gather(small, "shard", axis=0, tiled=False)
-    full_w_in = lax.all_gather(w_in, "shard", axis=0, tiled=True)
-    full_w_out = lax.all_gather(w_out, "shard", axis=0, tiled=True)
-    taps = conv_weight.shape[0]
+    if hypercube:
+        core = lax.axis_index("rep")
+        order, place = block_order()
+        small_all = gather_small(small)
+        w_half = lax.dynamic_slice_in_dim(w_in, core * (w_in.shape[0] // 2), w_in.shape[0] // 2, 0)
+        o_half = lax.dynamic_slice_in_dim(w_out, core * (w_out.shape[0] // 2), w_out.shape[0] // 2, 0)
+        rest = jnp.pad(w_half[:, di:], ((0, 0), (0, wide - (w_in.shape[1] - di))))
+        conv_pieces = [gather_pieces(rest[:, a : a + n]) for a, n in cuts]
+        gate_pieces = [gather_pieces(w_half[:, a : a + n]) for a, n in halves]
+        out_pieces = [gather_pieces(o_half[:, a : a + n]) for a, n in thirds]
+    else:
+        small_all = lax.all_gather(small, "shard", axis=0, tiled=False)
+        full_w_in = lax.all_gather(w_in, "shard", axis=0, tiled=True)
+        full_w_out = lax.all_gather(w_out, "shard", axis=0, tiled=True)
     cut = taps * conv_local
     conv_w = small_all[:, :cut].reshape(shards, taps, conv_local).transpose(1, 0, 2).reshape(taps, -1)
-    conv_b = small_all[:, cut : cut + conv_local].reshape(1, -1)
+    conv_b = rows_of(small_all, cut, conv_local).reshape(1, -1)
     cut += conv_local
-    full_gain_in = small_all[:, cut : cut + gain_in.shape[0]].reshape(-1).astype(F32)
-    full_gain_out = small_all[:, cut + gain_in.shape[0] :].reshape(-1).astype(F32)
+    full_gain_in = rows_of(small_all, cut, gain_in.shape[0]).reshape(1, -1).astype(F32)
+    full_gain_out = rows_of(small_all, cut + gain_in.shape[0], gain_out.shape[0]).reshape(1, -1).astype(F32)
     conv_all = jnp.concatenate(
-        [conv_w.astype(F32), conv_b.astype(F32), jnp.zeros((3, conv_w.shape[1]), F32)], axis=0
+        [conv_w.astype(F32), conv_b.astype(F32), jnp.zeros((3, conv_dim), F32)], axis=0
     )
-    di = full_gain_out.shape[0]
-    conv_dim = conv_w.shape[1]
     inputs = tokens.astype(F32)
     rscale = lax.rsqrt(jnp.mean(inputs * inputs, axis=1, keepdims=True) + EPSILON)
     unit = inputs * rscale
-    normed = (unit * full_gain_in[None]).astype(BF16)
-    seg = seg_ids[0]
-    aux, seg_row = seg_facts(seg)
+    normed = (unit * full_gain_in).astype(BF16)
+    aux, seg_row = seg_facts(seg_ids[0])
     heads = head_rows(dt_bias, a_log)
     skip = jnp.repeat(d_skip, P_SIZE)[None]
 
-    w_gate = full_w_in[:, :di]
-    w_conv = full_w_in[:, di : di + conv_dim]
-    w_step = pad_lanes(full_w_in[:, di + conv_dim :], TILE)
-    pc = mm(normed, w_conv)
-    raw = mm(normed, w_step)
-    gate = mm(normed, w_gate)
-    x, bcv, y, states = run_forward(pc, raw, conv_all, aux, seg_row, heads, skip)
-    gated = y * (gate * jax.nn.sigmoid(gate))
-    inverse = lax.rsqrt(jnp.mean(gated * gated, axis=1, keepdims=True) + EPSILON)
-    ynorm = (gated * inverse * full_gain_out[None]).astype(BF16)
-    projected = mm(ynorm, full_w_out)
+    if hypercube:
+        front = None
+        for (a, n), pieces in zip(cuts, conv_pieces):
+            front = project(normed, pieces, order, front, a, wide)
+        pc, w_rest = front
+    else:
+        w_gate = full_w_in[:, :di]
+        w_rest = jnp.pad(full_w_in[:, di:], ((0, 0), (0, wide - (w_in.shape[1] - di))))
+        pc = mm(normed, w_rest)
+    x, bcv, y, states = run_forward(pc, conv_all, aux, seg_row, heads, skip)
+    if hypercube:
+        part = None
+        squares = 0.0
+        for (a, n), pieces in zip(halves, gate_pieces):
+            *part, square = gate_project(normed, pieces, order, y, full_gain_out, part, a, di)
+            squares = squares + square
+        gate, w_gate, zg = part
+        full_w_out = None
+        for (a, n), pieces in zip(thirds, out_pieces):
+            full_w_out = restore(pieces, order, full_w_out, a, model)
+        gated = y * (gate * jax.nn.sigmoid(gate))
+    else:
+        gate = mm(normed, w_gate)
+        gated = y * (gate * jax.nn.sigmoid(gate))
+        squares = gated * gated
+        zg = (gated * full_gain_out).astype(BF16)
+    inverse = lax.rsqrt(jnp.sum(squares, axis=1, keepdims=True) / di + EPSILON)
+    projected = inverse * mm(zg, full_w_out)
     output = (inputs + projected).astype(BF16)
     cot = cotangent.astype(F32)
     dots = jnp.sum(cot * projected, axis=1, keepdims=True)
+    cot_scaled = (inverse * cot).astype(BF16)
     grad_ynorm = mm_nt(cotangent, full_w_out)
-    grad_w_out = dot_f32(ynorm, cotangent, ((0,), (0,)))
-    dz = inverse * (full_gain_out[None] * grad_ynorm) - gated * (inverse * inverse * dots / di)
+    dz = inverse * (full_gain_out * grad_ynorm) - gated * (inverse * inverse * dots / di)
     sig = jax.nn.sigmoid(gate)
     dy = (dz * (gate * sig)).astype(BF16)
     dgate = (dz * y * (sig * (1.0 + gate * (1.0 - sig)))).astype(BF16)
-    dpc, dbc, draw, dcw, dbcw, dskip, dhead = run_backward(
-        dy, x, bcv, states, pc, raw, conv_all, aux, seg_row, heads, skip
+    if hypercube:
+        out_sum = scatter_sum(*weight_grad(zg, cot_scaled, place, 0, model), w_out.shape[0] // 2)
+        gate_sums = [
+            scatter_sum(*weight_grad(normed, dgate, place, k, n), w_in.shape[0] // 2)
+            for k, (a, n) in enumerate(halves)
+        ]
+    dproj, dcw, dbcw, dskip, dhead = run_backward(
+        dy, x, bcv, states, pc, conv_all, aux, seg_row, heads, skip
     )
-    grad_projected = jnp.concatenate([dgate, dpc, dbc, draw[:, :H]], axis=1)
-    grad_w_in = dot_f32(normed, grad_projected, ((0,), (0,)))
-    grad_normed = mm_nt(grad_projected, full_w_in)
-    scaled = grad_normed * full_gain_in[None]
+    scaled = (mm_nt(dgate, w_gate) + mm_nt(dproj, w_rest)) * full_gain_in
     inner = jnp.mean(unit * scaled, axis=1, keepdims=True)
     grad_tokens = (cot + rscale * (scaled - unit * inner)).astype(BF16)
 
@@ -641,10 +965,27 @@
     )
     conv_part = conv_sums.reshape(taps + 1, shards, conv_local).transpose(1, 0, 2).reshape(shards, -1)
     small_grad = jnp.concatenate([conv_part, jnp.broadcast_to(per_head[None], (shards, 3 * H))], axis=1)
-    small_sum = lax.psum(lax.psum_scatter(small_grad, "shard", scatter_dimension=0, tiled=True), "rep")[0]
-    sum_w_in = lax.psum_scatter(grad_w_in.astype(BF16), "shard", scatter_dimension=0, tiled=True)
-    sum_w_out = lax.psum_scatter(grad_w_out.astype(BF16), "shard", scatter_dimension=0, tiled=True)
-    sum_w_in, sum_w_out = lax.psum((sum_w_in.astype(F32), sum_w_out.astype(F32)), "rep")
+    real = w_in.shape[1] - di
+    if hypercube:
+        small_sum = reduce_small(small_grad)[0]
+        rest_sums = []
+        for k, (a, n) in enumerate(cuts):
+            part = (dproj, k) if a == k * n else (dproj[:, a : a + n], 0)
+            rest_sums.append(scatter_sum(*weight_grad(normed, part[0], place, part[1], n), w_in.shape[0] // 2))
+        rest_sums[-1] = rest_sums[-1][:, : real - cuts[-1][0]]
+        own = jnp.concatenate(gate_sums + rest_sums, axis=1)
+        sum_w_in = both_cores(own)
+        sum_w_out = both_cores(out_sum)
+    else:
+        grad_w_out = dot_f32(zg, cot_scaled, ((0,), (0,)))
+        grads = jnp.concatenate([dgate, dproj[:, :real]], axis=1)
+        grad_w_in = dot_f32(normed, grads, ((0,), (0,)))
+        small_sum = lax.psum(
+            lax.psum_scatter(small_grad, "shard", scatter_dimension=0, tiled=True), "rep"
+        )[0]
+        sum_w_in = lax.psum_scatter(grad_w_in, "shard", scatter_dimension=0, tiled=True)
+        sum_w_out = lax.psum_scatter(grad_w_out, "shard", scatter_dimension=0, tiled=True)
+        sum_w_in, sum_w_out = lax.psum((sum_w_in, sum_w_out), "rep")
     grad_gain_in = jnp.sum(sum_w_in * w_in.astype(F32), axis=1) / gain_in.astype(F32)
     grad_gain_out = jnp.sum(sum_w_out * w_out.astype(F32), axis=1) / gain_out.astype(F32)
     cut = taps * conv_local
@@ -664,6 +1005,23 @@
     )
 
 
+def both_cores(own):
+    partner = swap_cores(own)
+    first = lax.axis_index("rep") == 0
+    return jnp.concatenate([jnp.where(first, own, partner), jnp.where(first, partner, own)], axis=0)
+
+
+def reduce_small(rows):
+    core = lax.axis_index("rep")
+    places = jnp.asarray([reach(order) for order in ORDERS], jnp.int32)[core] ^ lax.axis_index("shard")
+    hot = (places[:, None] == jnp.arange(16, dtype=jnp.int32)[None, :]).astype(F32)
+    total = dot_f32(hot, rows, ((1,), (0,)), HIGHEST)
+    for stage in (3, 2, 1, 0):
+        cut = 1 << stage
+        total = total[:cut] + exchange(total[cut:], stage)
+    return total + swap_cores(total)
+
+
 def solution(mesh):
     rows = P(("shard", "rep"), None)
     in_specs = (
@@ -674,6 +1032,11 @@
         rows, rows, P("shard"), P("shard", None), P(None, "shard"), P("shard"), P(), P(), P(), P("shard"),
         P("shard", None),
     )
+    hypercube = mesh.shape["shard"] == 16 and mesh.shape["rep"] == 2
     return jax.shard_map(
-        on_device, mesh=mesh, in_specs=in_specs, out_specs=out_specs, check_vma=False
+        functools.partial(on_device, hypercube),
+        mesh=mesh,
+        in_specs=in_specs,
+        out_specs=out_specs,
+        check_vma=False,
     )

time: 1150 us -> 830 us (0.72)
  waiting for transfers between devices: 661 us -> 280 us
  Pallas kernels: 173 us -> 307 us
  matrix products: 166 us -> 66.8 us
  blocking collectives: 93.8 us -> 0 us
  starting transfers between devices: 0.2 us -> 64.3 us
  other arithmetic: 19.4 us -> 70 us
  local copies, waits for them, and re-layouts: 16.7 us -> 30.9 us
  between operations: 14.9 us -> 2.65 us
    reduce_scatter x2 -> x0, waiting for transfers between devices: 482 us -> none  [the longest x1 307 us: on_device(): lax.psum_scatter(grad_w_in.astype(BF16), 'shard', scatter_dimension=0, ti...]
    ppermute x0 -> x83, waiting for transfers between devices: none -> 280 us  [the longest x60 280 us: exchange(): return lax.ppermute(values, ('shard', 'rep'), pairs)]
    all_gather x2 -> x0, waiting for transfers between devices: 159 us -> none  [the longest x1 128 us: on_device(): full_w_in = lax.all_gather(w_in, 'shard', axis=0, tiled=True)]
    pallas_call x0 -> x13, Pallas kernels: none -> 135 us  [the longest x6 60.9 us: weight_grad(): pl.pallas_call(functools.partial(weight_grad_kernel, block), grid_spec=pl...]
    dot_general x8 -> x6, matrix products: 166 us -> 66.8 us  [dot_f32(): lax.dot_general(a, b, ((contract[0], contract[1]), ((), ())), preferred_e...]
    unnamed x1 -> x0, blocking collectives: 80.8 us -> none
    ppermute x0 -> x83, starting transfers between devices: none -> 64.3 us  [the longest x60 60.5 us: exchange(): return lax.ppermute(values, ('shard', 'rep'), pairs)]
    add x0 -> x31, other arithmetic: none -> 25 us  [the longest x6 15.3 us: scatter_sum(): total = mine.astype(F32) + arrived.astype(F32)]
  transfers between devices with their start and end apart: 5 -> 83, of which waited for: 5 -> 31; matrix products, arithmetic and copies ran while one was open for 13% -> 11% of each run, Pallas kernels for 4% -> 19%
where the time goes in v2:
time: 830 us; the launch traced here: 822 us
  Pallas kernels  307 us (37%)
  waiting for transfers between devices  280 us (34%)
  other arithmetic  70 us (8%)
  matrix products  66.8 us (8%)
  starting transfers between devices  64.3 us (8%)
  local copies, waits for them, and re-layouts  30.9 us (4%)
    ppermute x60, waiting for transfers between devices, exchange(): return lax.ppermute(values, ('shard', 'rep'), pairs)  280 us
    pallas_call x1, Pallas kernels, run_backward(): pl.pallas_call(backward_kernel, grid_spec=grid_spec, out_shape=[jax.Shape...  122 us
    dot_general x6, matrix products, dot_f32(): lax.dot_general(a, b, ((contract[0], contract[1]), ((), ())), preferred_e...  66.8 us
    pallas_call x6, Pallas kernels, weight_grad(): pl.pallas_call(functools.partial(weight_grad_kernel, block), grid_spec=pl...  60.9 us
    ppermute x60, starting transfers between devices, exchange(): return lax.ppermute(values, ('shard', 'rep'), pairs)  60.5 us
    pallas_call x1, Pallas kernels, run_forward(): pl.pallas_call(forward_kernel, grid_spec=grid_spec, out_shape=[jax.ShapeD...  50.7 us
    pallas_call x2, Pallas kernels, gate_project(): pl.pallas_call(functools.partial(gate_kernel, block, width), grid_spec=pl...  31.7 us
    pallas_call x3, Pallas kernels, project(): pl.pallas_call(functools.partial(project_kernel, block, width), grid_spec...  30 us
  transfers between devices with their start and end apart: 83, of which 31 were waited for; matrix products, arithmetic and copies ran while one was open for 11% of the time, Pallas kernels for 19%

profile of v2, /device:TPU:0, one launch (start us, length us, event | category | flops | bytes accessed | tf_op | source)
XLA Modules:
  0.0 822.0 jit_solution(1008949544098201787)
XLA Ops:
  43.3 10.0 %collective-permute-done.28 = bf16[48,1536]{1,0:T(8,128)(2,1)S(1)} collective-permute-done((bf16[48,1536]{1,0:T(8,128)(2,1)S(1)}, bf16[48,1536]{1,0:T(8,128)(2,1)S(1)}, u32[]{:S(2)}, u32[]{:S(2)}) %collective-permute-start.28) | collective-permute-done | bytes 147488 | tf_op jit(solution)/shard_map/ppermute | solution.py:575
  75.3 12.6 %collective-permute-done.6 = bf16[192,1536]{1,0:T(8,128)(2,1)S(1)} collective-permute-done((bf16[192,1536]{1,0:T(8,128)(2,1)S(1)}, bf16[192,1536]{1,0:T(8,128)(2,1)S(1)}, u32[]{:S(2)}, u32[]{:S(2)}) %collective-permute-start.6) | collective-permute-done | bytes 589856 | tf_op jit(solution)/shard_map/ppermute | solution.py:575
  89.1 55.1 %collective-permute-done.24 = bf16[192,1024]{1,0:T(8,128)(2,1)S(1)} collective-permute-done((bf16[192,1024]{1,0:T(8,128)(2,1)S(1)}, bf16[192,1024]{1,0:T(8,128)(2,1)S(1)}, u32[]{:S(2)}, u32[]{:S(2)}) %collective-permute-start.24) | collective-permute-done | bytes 393248 | tf_op jit(solution)/shard_map/ppermute | solution.py:575
  151.1 18.1 %collective-permute-done.19.p1 = bf16[384,1024]{1,0:T(8,128)(2,1)S(1)} collective-permute-done((bf16[384,1024]{1,0:T(8,128)(2,1)S(1)}, bf16[384,1024]{1,0:T(8,128)(2,1)S(1)}, u32[]{:S(2)}, u32[]{:S(2)}) %collective-permute-start.19) | collective-permute-done | bytes 786464 | tf_op jit(solution)/shard_map/ppermute | solution.py:575
  190.8 12.1 %collective-permute-done.31.p1 = bf16[384,1536]{1,0:T(8,128)(2,1)} collective-permute-done((bf16[384,1536]{1,0:T(8,128)(2,1)}, bf16[384,1536]{1,0:T(8,128)(2,1)}, u32[]{:S(2)}, u32[]{:S(2)}) %collective-permute-start.31) | collective-permute-done | bytes 1179680 | tf_op jit(solution)/shard_map/ppermute | solution.py:575
  202.9 12.6 %collective-permute-done.43.p1 = bf16[768,768]{1,0:T(8,128)(2,1)} collective-permute-done((bf16[768,768]{1,0:T(8,128)(2,1)}, bf16[768,768]{1,0:T(8,128)(2,1)}, u32[]{:S(2)}, u32[]{:S(2)}) %collective-permute-start.43) | collective-permute-done | bytes 1179680 | tf_op jit(solution)/shard_map/ppermute | solution.py:575
  241.5 11.8 %project.5 = (f32[1024,3584]{1,0:T(8,128)}, bf16[1536,3584]{1,0:T(8,128)(2,1)}) custom-call(s32[32]{0:T(128)} %pad_add_fusion.order_ref, bf16[1024,1536]{1,0:T(8,128)(2,1)} %fusion.4.x_ref.lhs_ref, bf16[384,1536]{1,0:T(8,128)(2,1)} %pad_maximum_fusion.2.p0, ...), custom_call_target="tpu_custom_call", output_to_operand_aliasing={{0}: (6, {}), {1}: (7, {})} | custom-call | flops 4831838208 | bytes 18874368 | tf_op jit(solution)/shard_map/project/pallas_call | solution.py:669
  253.2 50.7 %scan_forward.1 = (bf16[1024,3072]{1,0:T(8,128)(2,1)}, bf16[1024,256]{1,0:T(8,128)(2,1)}, f32[1024,3072]{1,0:T(8,128)}, bf16[512,3072]{1,0:T(8,128)(2,1)}) custom-call(f32[1024,3584]{1,0:T(8,128)} %get-tuple-element.50.pc_ref.halo_ref.bc_ref.bc_halo_ref.raw_ref, f32[1024,3584]{1,0:T(8,128)} %get-tuple-element.50.pc_ref.halo_ref.bc_ref.bc_halo_ref.raw_ref, ...), custom_call_target="tpu_custom_call" | custom-call | tf_op jit(solution)/shard_map/scan_forward/pallas_call | solution.py:225
  310.6 15.7 %project_gate.2 = (f32[1024,3072]{1,0:T(8,128)}, bf16[1536,3072]{1,0:T(8,128)(2,1)}, bf16[1024,3072]{1,0:T(8,128)(2,1)}, f32[1024,128]{1,0:T(8,128)}) custom-call(s32[32]{0:T(128)} %pad_add_fusion.order_ref, bf16[1024,1536]{1,0:T(8,128)(2,1)} %fusion.4.x_ref.lhs_ref, bf16[384,1536]{1,0:T(8,128)(2,1)} %pad_maximum_fusion.1.p0, ...), custom_call_target="tpu_custom_call" | custom-call | flops 4831838208 | bytes 28311552 | tf_op jit(solution)/shard_map/project_gate/pallas_call | solution.py:723
  326.3 16.0 %project_gate.3 = (f32[1024,3072]{1,0:T(8,128)}, bf16[1536,3072]{1,0:T(8,128)(2,1)}, bf16[1024,3072]{1,0:T(8,128)(2,1)}, f32[1024,128]{1,0:T(8,128)}) custom-call(s32[32]{0:T(128)} %pad_add_fusion.order_ref, bf16[1024,1536]{1,0:T(8,128)(2,1)} %fusion.4.x_ref.lhs_ref, ...), custom_call_target="tpu_custom_call", output_to_operand_aliasing={{0}: (8, {}), {1}: (9, {}), {2}: (10, {})} | custom-call | flops 4831838208 | bytes 28311552 | tf_op jit(solution)/shard_map/project_gate/pallas_call | solution.py:723
  349.8 16.3 %fusion.45 = f32[3072,1024]{0,1:T(8,128)} fusion(bf16[3072,1536]{1,0:T(8,128)(2,1)} %restore.3, bf16[1024,1536]{1,0:T(8,128)(2,1)} %param.27), kind=kOutput, calls=%fused_computation.200 | convolution fusion | flops 9663676416 | bytes 25165824 | tf_op jit(solution)/shard_map/dot_general | solution.py:26
  366.1 17.0 %fusion.10 = (f32[1024]{0:T(1024)S(1)}, bf16[1024,1536]{1,0:T(8,128)(2,1)}, bf16[1024,1536]{1,0:T(8,128)(2,1)}) fusion(bf16[1024,1536]{1,0:T(8,128)(2,1)S(1)} %copy-done.8, f32[1024]{0:T(1024)S(1)} %add_rsqrt_fusion, bf16[1024,1536]{1,0:T(8,128)(2,1)S(1)} %copy-done.1, bf16[1024,3072]{1,0:T(8,128)(2,1)} %get-tuple-element.57.lhs_ref, ...), kind=kOutput, calls=%fused_computation.22 | convolution fusion | flops 9677831168 | bytes 28319744 | tf_op jit(solution)/shard_map/dot_general | solution.py:26
  383.2 16.6 %multiply_convert_fusion.1 = (bf16[1024,3072]{1,0:T(8,128)(2,1)}, bf16[1024,3072]{1,0:T(8,128)(2,1)}) fusion(f32[1024,3072]{1,0:T(8,128)} %get-tuple-element.58, f32[1024,3072]{1,0:T(8,128)S(1)} %bitcast.67, f32[3072,1024]{0,1:T(8,128)} %fusion.45, f32[1024]{0:T(1024)S(1)} %multiply_multiply_fusion, f32[3072]{0:T(1024)S(1)} %reshape.323, ...), kind=kLoop, calls=%fused_computation.3 | loop fusion | flops 56623104 | bytes 50352128 | tf_op jit(solution)/shard_map/convert_element_type | solution.py:943
  399.7 121.5 %scan_backward.1 = (bf16[1024,3584]{1,0:T(8,128)(2,1)}, f32[5,8,3072]{2,1,0:T(8,128)}, f32[5,8,256]{2,1,0:T(8,128)}, f32[8,3072]{1,0:T(8,128)}, f32[2,8,128]{2,1,0:T(8,128)}) custom-call(bf16[1024,3072]{1,0:T(8,128)(2,1)} %get-tuple-element.88.dy_ref, bf16[1024,3072]{1,0:T(8,128)(2,1)} %get-tuple-element.60.x_ref, ...), custom_call_target="tpu_custom_call" | custom-call | tf_op jit(solution)/shard_map/scan_backward/pallas_call | solution.py:520
  537.3 17.6 %fusion.46 = f32[1024,1536]{1,0:T(8,128)} fusion(bf16[1024,3584]{1,0:T(8,128)(2,1)} %get-tuple-element.63.rhs_ref, bf16[1536,3584]{1,0:T(8,128)(2,1)} %get-tuple-element.64), kind=kOutput, calls=%fused_computation.201 | convolution fusion | flops 11274289152 | bytes 24641536 | tf_op jit(solution)/shard_map/dot_general | solution.py:26
  555.0 10.1 %weight_grad.7 = (bf16[768,1536]{1,0:T(8,128)(2,1)}, bf16[768,1536]{1,0:T(8,128)(2,1)}) custom-call(s32[32]{0:T(128)} %fusion.32.place_ref, bf16[1024,1536]{1,0:T(8,128)(2,1)} %fusion.4.x_ref.lhs_ref, bf16[1024,3072]{1,0:T(8,128)(2,1)} %get-tuple-element.87.rhs_ref), custom_call_target="tpu_custom_call" | custom-call | flops 4831838208 | bytes 11010048 | tf_op jit(solution)/shard_map/weight_grad/pallas_call | solution.py:824
  568.1 15.5 %fusion.5 = (f32[1024]{0:T(1024)S(1)}, f32[1024,1536]{1,0:T(8,128)S(1)}) fusion(bf16[1024,1536]{1,0:T(8,128)(2,1)S(1)} %copy-done.1, f32[1024]{0:T(1024)S(1)} %copy-done.39, f32[1536]{0:T(1024)S(1)} %copy-done.41, f32[1024,1536]{1,0:T(8,128)} %fusion.46, bf16[1024,3072]{1,0:T(8,128)(2,1)} %get-tuple-element.87.rhs_ref, bf16[1536,3072]{1,0:T(8,128)(2,1)} %get-tuple-element.59), kind=kOutput, calls=%fused_computation.17 | convolution fusion | flops 9673112576 | bytes 31471616 | tf_op jit(solution)/shard_map/dot_general | solution.py:26
  605.5 9.8 %weight_grad.10 = (bf16[768,1536]{1,0:T(8,128)(2,1)}, bf16[768,1536]{1,0:T(8,128)(2,1)}) custom-call(s32[32]{0:T(128)} %fusion.32.place_ref, bf16[1024,1536]{1,0:T(8,128)(2,1)} %fusion.4.x_ref.lhs_ref, bf16[1024,1536]{1,0:T(8,128)(2,1)} %slice.374.rhs_ref), custom_call_target="tpu_custom_call" | custom-call | flops 4831838208 | bytes 11010048 | tf_op jit(solution)/shard_map/weight_grad/pallas_call | solution.py:824
  626.2 15.3 %weight_grad.11 = (bf16[1536,1536]{1,0:T(8,128)(2,1)}, bf16[1536,1536]{1,0:T(8,128)(2,1)}) custom-call(s32[32]{0:T(128)} %fusion.32.place_ref, bf16[1024,3072]{1,0:T(8,128)(2,1)} %get-tuple-element.57.lhs_ref, bf16[1024,1536]{1,0:T(8,128)(2,1)} %get-tuple-element.91.rhs_ref), custom_call_target="tpu_custom_call" | custom-call | flops 9663676416 | bytes 18874368 | tf_op jit(solution)/shard_map/weight_grad/pallas_call | solution.py:824
  685.1 10.6 %collective-permute-done.67 = bf16[384,1536]{1,0:T(8,128)(2,1)S(1)} collective-permute-done((bf16[384,1536]{1,0:T(8,128)(2,1)S(1)}, bf16[384,1536]{1,0:T(8,128)(2,1)S(1)}, u32[]{:S(2)}, u32[]{:S(2)}) %collective-permute-start.67) | collective-permute-done | bytes 1179680 | tf_op jit(solution)/shard_map/ppermute | solution.py:575
  708.6 17.0 %collective-permute-done.68 = bf16[192,1536]{1,0:T(8,128)(2,1)} collective-permute-done((bf16[192,1536]{1,0:T(8,128)(2,1)}, bf16[192,1536]{1,0:T(8,128)(2,1)}, u32[]{:S(2)}, u32[]{:S(2)}) %collective-permute-start.68) | collective-permute-done | bytes 589856 | tf_op jit(solution)/shard_map/ppermute | solution.py:575
  747.8 12.9 %collective-permute-done.78 = bf16[768,1536]{1,0:T(8,128)(2,1)S(1)} collective-permute-done((bf16[768,1536]{1,0:T(8,128)(2,1)S(1)}, bf16[768,1536]{1,0:T(8,128)(2,1)S(1)}, u32[]{:S(2)}, u32[]{:S(2)}) %collective-permute-start.78) | collective-permute-done | bytes 2359328 | tf_op jit(solution)/shard_map/ppermute | solution.py:575
  764.3 26.5 %collective-permute-done.79 = bf16[384,1536]{1,0:T(8,128)(2,1)S(1)} collective-permute-done((bf16[384,1536]{1,0:T(8,128)(2,1)S(1)}, bf16[384,1536]{1,0:T(8,128)(2,1)S(1)}, u32[]{:S(2)}, u32[]{:S(2)}) %collective-permute-start.79) | collective-permute-done | bytes 1179680 | tf_op jit(solution)/shard_map/ppermute | solution.py:575
  803.5 11.6 %collective-permute-done.81 = bf16[96,1536]{1,0:T(8,128)(2,1)S(1)} collective-permute-done((bf16[96,1536]{1,0:T(8,128)(2,1)S(1)}, bf16[96,1536]{1,0:T(8,128)(2,1)S(1)}, u32[]{:S(2)}, u32[]{:S(2)}) %collective-permute-start.81) | collective-permute-done | bytes 294944 | tf_op jit(solution)/shard_map/ppermute | solution.py:575
  (454 shorter events, 286.4 us)
Async XLA Ops:
  69.5 76.0 %collective-permute-start.12 = (bf16[192,1536]{1,0:T(8,128)(2,1)S(1)}, bf16[192,1536]{1,0:T(8,128)(2,1)S(1)}, u32[]{:S(2)}, u32[]{:S(2)}) collective-permute-start(bf16[192,1536]{1,0:T(8,128)(2,1)S(1)} %pad_maximum_fusion.10), channel_id=1, source_target_pairs={{0,8},{1,9},{2,10},{3,11},{4,12},{5,13},{6,14},{7,15},{8,0},{9,1},... | collective-permute-start | bytes 1769480 | tf_op jit(solution)/shard_map/ppermute | solution.py:575
  72.7 73.8 %collective-permute-start.30 = (bf16[192,1536]{1,0:T(8,128)(2,1)S(1)}, bf16[192,1536]{1,0:T(8,128)(2,1)S(1)}, u32[]{:S(2)}, u32[]{:S(2)}) collective-permute-start(bf16[192,1536]{1,0:T(8,128)(2,1)S(1)} %pad_maximum_fusion.11), channel_id=1, source_target_pairs={{0,8},{1,9},{2,10},{3,11},{4,12},{5,13},{6,14},{7,15},{8,0},{9,1},... | collective-permute-start | bytes 1769480 | tf_op jit(solution)/shard_map/ppermute | solution.py:575
  72.7 73.7 %collective-permute-start.36 = (bf16[384,768]{1,0:T(8,128)(2,1)S(1)}, bf16[384,768]{1,0:T(8,128)(2,1)S(1)}, u32[]{:S(2)}, u32[]{:S(2)}) collective-permute-start(bf16[384,768]{1,0:T(8,128)(2,1)S(1)} %pad_maximum_fusion.12), channel_id=1, source_target_pairs={{0,8},{1,9},{2,10},{3,11},{4,12},{5,13},{6,14},{7,15},{8,0},{9,1},... | collective-permute-start | bytes 1769480 | tf_op jit(solution)/shard_map/ppermute | solution.py:575
  75.3 72.5 %collective-permute-start.42 = (bf16[384,768]{1,0:T(8,128)(2,1)S(1)}, bf16[384,768]{1,0:T(8,128)(2,1)S(1)}, u32[]{:S(2)}, u32[]{:S(2)}) collective-permute-start(bf16[384,768]{1,0:T(8,128)(2,1)S(1)} %pad_maximum_fusion.13), channel_id=1, source_target_pairs={{0,8},{1,9},{2,10},{3,11},{4,12},{5,13},{6,14},{7,15},{8,0},{9,1},... | collective-permute-start | bytes 1769480 | tf_op jit(solution)/shard_map/ppermute | solution.py:575
  87.9 56.4 %collective-permute-start.24 = (bf16[192,1024]{1,0:T(8,128)(2,1)S(1)}, bf16[192,1024]{1,0:T(8,128)(2,1)S(1)}, u32[]{:S(2)}, u32[]{:S(2)}) collective-permute-start(bf16[192,1024]{1,0:T(8,128)(2,1)S(1)} %pad_maximum_fusion.15), channel_id=1, source_target_pairs={{0,8},{1,9},{2,10},{3,11},{4,12},{5,13},{6,14},{7,15},{8,0},{9,1},... | collective-permute-start | bytes 1179656 | tf_op jit(solution)/shard_map/ppermute | solution.py:575
  144.3 35.8 %collective-permute-start.7 = (bf16[384,1536]{1,0:T(8,128)(2,1)}, bf16[384,1536]{1,0:T(8,128)(2,1)}, u32[]{:S(2)}, u32[]{:S(2)}) collective-permute-start(bf16[384,1536]{1,0:T(8,128)(2,1)} %pad_maximum_fusion.1.p0), channel_id=1, source_target_pairs={{0,4},{1,3},{2,6},{3,1},{4,0},{5,7},{6,2},{7,5},{8,12},{9,11},{10,... | collective-permute-start | bytes 3538952 | tf_op jit(solution)/shard_map/ppermute | solution.py:575
  178.8 36.8 %collective-permute-start.43 = (bf16[768,768]{1,0:T(8,128)(2,1)}, bf16[768,768]{1,0:T(8,128)(2,1)}, u32[]{:S(2)}, u32[]{:S(2)}) collective-permute-start(bf16[768,768]{1,0:T(8,128)(2,1)} %pad_maximum_fusion.5.p0), channel_id=1, source_target_pairs={{0,4},{1,3},{2,6},{3,1},{4,0},{5,7},{6,2},{7,5},{8,12},{9,11},{10,... | collective-permute-start | bytes 3538952 | tf_op jit(solution)/shard_map/ppermute | solution.py:575
  180.1 39.0 %collective-permute-start.44 = (bf16[768,768]{1,0:T(8,128)(2,1)}, bf16[768,768]{1,0:T(8,128)(2,1)}, u32[]{:S(2)}, u32[]{:S(2)}) collective-permute-start(bf16[768,768]{1,0:T(8,128)(2,1)} %pad_maximum_fusion.5.p0), channel_id=1, source_target_pairs={{0,1},{1,0},{2,3},{3,2},{4,5},{5,4},{6,7},{7,6},{8,9},{9,8},{10,11... | collective-permute-start | bytes 3538952 | tf_op jit(solution)/shard_map/ppermute | solution.py:579
  219.1 90.9 %collective-permute-start.8 = (bf16[384,1536]{1,0:T(8,128)(2,1)}, bf16[384,1536]{1,0:T(8,128)(2,1)}, u32[]{:S(2)}, u32[]{:S(2)}) collective-permute-start(bf16[384,1536]{1,0:T(8,128)(2,1)} %pad_maximum_fusion.1.p0), channel_id=1, source_target_pairs={{0,1},{1,0},{2,3},{3,2},{4,5},{5,4},{6,7},{7,6},{8,9},{9,8},{10,11... | collective-permute-start | bytes 3538952 | tf_op jit(solution)/shard_map/ppermute | solution.py:579
  219.6 90.9 %collective-permute-start.37 = (bf16[768,768]{1,0:T(8,128)(2,1)}, bf16[768,768]{1,0:T(8,128)(2,1)}, u32[]{:S(2)}, u32[]{:S(2)}) collective-permute-start(bf16[768,768]{1,0:T(8,128)(2,1)} %pad_maximum_fusion.4.p0), channel_id=1, source_target_pairs={{0,4},{1,3},{2,6},{3,1},{4,0},{5,7},{6,2},{7,5},{8,12},{9,11},{10,... | collective-permute-start | bytes 3538952 | tf_op jit(solution)/shard_map/ppermute | solution.py:575
  221.7 88.9 %collective-permute-start.9 = (bf16[384,1536]{1,0:T(8,128)(2,1)}, bf16[384,1536]{1,0:T(8,128)(2,1)}, u32[]{:S(2)}, u32[]{:S(2)}) collective-permute-start(bf16[384,1536]{1,0:T(8,128)(2,1)} %collective-permute-done.7.p1), channel_id=1, source_target_pairs={{0,1},{1,0},{2,3},{3,2},{4,5},{5,4},{6,7},{7,6},{8,9},{9,8},{10,11... | collective-permute-start | bytes 3538952 | tf_op jit(solution)/shard_map/ppermute | solution.py:579
  231.7 94.6 %collective-permute-start.32 = (bf16[384,1536]{1,0:T(8,128)(2,1)}, bf16[384,1536]{1,0:T(8,128)(2,1)}, u32[]{:S(2)}, u32[]{:S(2)}) collective-permute-start(bf16[384,1536]{1,0:T(8,128)(2,1)} %pad_maximum_fusion.3.p0), channel_id=1, source_target_pairs={{0,1},{1,0},{2,3},{3,2},{4,5},{5,4},{6,7},{7,6},{8,9},{9,8},{10,11... | collective-permute-start | bytes 3538952 | tf_op jit(solution)/shard_map/ppermute | solution.py:579
  232.3 94.0 %collective-permute-start.33 = (bf16[384,1536]{1,0:T(8,128)(2,1)}, bf16[384,1536]{1,0:T(8,128)(2,1)}, u32[]{:S(2)}, u32[]{:S(2)}) collective-permute-start(bf16[384,1536]{1,0:T(8,128)(2,1)} %collective-permute-done.31.p1), channel_id=1, source_target_pairs={{0,1},{1,0},{2,3},{3,2},{4,5},{5,4},{6,7},{7,6},{8,9},{9,8},{10,11... | collective-permute-start | bytes 3538952 | tf_op jit(solution)/shard_map/ppermute | solution.py:579
  310.0 33.8 %collective-permute-start.38 = (bf16[768,768]{1,0:T(8,128)(2,1)}, bf16[768,768]{1,0:T(8,128)(2,1)}, u32[]{:S(2)}, u32[]{:S(2)}) collective-permute-start(bf16[768,768]{1,0:T(8,128)(2,1)} %pad_maximum_fusion.4.p0), channel_id=1, source_target_pairs={{0,1},{1,0},{2,3},{3,2},{4,5},{5,4},{6,7},{7,6},{8,9},{9,8},{10,11... | collective-permute-start | bytes 3538952 | tf_op jit(solution)/shard_map/ppermute | solution.py:579
  583.7 66.2 %collective-permute-start.51 = (bf16[768,1536]{1,0:T(8,128)(2,1)}, bf16[768,1536]{1,0:T(8,128)(2,1)}, u32[]{:S(2)}, u32[]{:S(2)}) collective-permute-start(bf16[768,1536]{1,0:T(8,128)(2,1)} %get-tuple-element.68), channel_id=1, source_target_pairs={{0,1},{1,0},{2,3},{3,2},{4,5},{5,4},{6,7},{7,6},{8,9},{9,8},{10,11... | collective-permute-start | bytes 7077896 | tf_op jit(solution)/shard_map/ppermute | solution.py:579
  584.3 35.2 %collective-permute-start.61 = (bf16[768,1024]{1,0:T(8,128)(2,1)}, bf16[768,1024]{1,0:T(8,128)(2,1)}, u32[]{:S(2)}, u32[]{:S(2)}) collective-permute-start(bf16[768,1024]{1,0:T(8,128)(2,1)} %get-tuple-element.72), channel_id=1, source_target_pairs={{0,1},{1,0},{2,3},{3,2},{4,5},{5,4},{6,7},{7,6},{8,9},{9,8},{10,11... | collective-permute-start | bytes 4718600 | tf_op jit(solution)/shard_map/ppermute | solution.py:579
  603.0 43.1 %collective-permute-start.46 = (bf16[768,1536]{1,0:T(8,128)(2,1)}, bf16[768,1536]{1,0:T(8,128)(2,1)}, u32[]{:S(2)}, u32[]{:S(2)}) collective-permute-start(bf16[768,1536]{1,0:T(8,128)(2,1)} %get-tuple-element.66), channel_id=1, source_target_pairs={{0,1},{1,0},{2,3},{3,2},{4,5},{5,4},{6,7},{7,6},{8,9},{9,8},{10,11... | collective-permute-start | bytes 7077896 | tf_op jit(solution)/shard_map/ppermute | solution.py:579
  615.3 38.7 %collective-permute-start.66 = (bf16[768,1536]{1,0:T(8,128)(2,1)}, bf16[768,1536]{1,0:T(8,128)(2,1)}, u32[]{:S(2)}, u32[]{:S(2)}) collective-permute-start(bf16[768,1536]{1,0:T(8,128)(2,1)} %get-tuple-element.74), channel_id=1, source_target_pairs={{0,1},{1,0},{2,3},{3,2},{4,5},{5,4},{6,7},{7,6},{8,9},{9,8},{10,11... | collective-permute-start | bytes 7077896 | tf_op jit(solution)/shard_map/ppermute | solution.py:579
  642.2 60.2 %collective-permute-start.77 = (bf16[1536,1536]{1,0:T(8,128)(2,1)}, bf16[1536,1536]{1,0:T(8,128)(2,1)S(1)}, u32[]{:S(2)}, u32[]{:S(2)}) collective-permute-start(bf16[1536,1536]{1,0:T(8,128)(2,1)} %get-tuple-element.80), channel_id=1, source_target_pairs={{0,1},{1,0},{2,3},{3,2},{4,5},{5,4},{6,7},{7,6},{8,9},{9,8},{10,11... | collective-permute-start | bytes 14155784 | tf_op jit(solution)/shard_map/ppermute | solution.py:579
  657.9 37.7 %collective-permute-start.67 = (bf16[384,1536]{1,0:T(8,128)(2,1)S(1)}, bf16[384,1536]{1,0:T(8,128)(2,1)S(1)}, u32[]{:S(2)}, u32[]{:S(2)}) collective-permute-start(bf16[384,1536]{1,0:T(8,128)(2,1)S(1)} %slice.570), channel_id=1, source_target_pairs={{0,4},{1,3},{2,6},{3,1},{4,0},{5,7},{6,2},{7,5},{8,12},{9,11},{10,... | collective-permute-start | bytes 3538952 | tf_op jit(solution)/shard_map/ppermute | solution.py:575
  679.4 83.9 %collective-permute-start.60 = (bf16[48,1024]{1,0:T(8,128)(2,1)}, bf16[48,1024]{1,0:T(8,128)(2,1)}, u32[]{:S(2)}, u32[]{:S(2)}) collective-permute-start(bf16[48,1024]{1,0:T(8,128)(2,1)} %slice.591), channel_id=1, source_target_pairs={{0,16},{1,17},{2,18},{3,19},{4,20},{5,21},{6,22},{7,23},{8,24},{9,... | collective-permute-start | bytes 294920 | tf_op jit(solution)/shard_map/ppermute | solution.py:575
  680.2 112.1 %collective-permute-start.65 = (bf16[48,1024]{1,0:T(8,128)(2,1)S(1)}, bf16[48,1024]{1,0:T(8,128)(2,1)}, u32[]{:S(2)}, u32[]{:S(2)}) collective-permute-start(bf16[48,1024]{1,0:T(8,128)(2,1)S(1)} %slice.590), channel_id=1, source_target_pairs={{0,16},{1,17},{2,18},{3,19},{4,20},{5,21},{6,22},{7,23},{8,24},{9,... | collective-permute-start | bytes 294920 | tf_op jit(solution)/shard_map/ppermute | solution.py:575
  702.3 36.5 %collective-permute-start.49 = (bf16[96,1536]{1,0:T(8,128)(2,1)}, bf16[96,1536]{1,0:T(8,128)(2,1)}, u32[]{:S(2)}, u32[]{:S(2)}) collective-permute-start(bf16[96,1536]{1,0:T(8,128)(2,1)} %slice.584), channel_id=1, source_target_pairs={{0,2},{1,5},{2,0},{3,7},{4,6},{5,1},{6,4},{7,3},{8,10},{9,13},{10,... | collective-permute-start | bytes 884744 | tf_op jit(solution)/shard_map/ppermute | solution.py:575
  725.6 35.2 %collective-permute-start.78 = (bf16[768,1536]{1,0:T(8,128)(2,1)S(1)}, bf16[768,1536]{1,0:T(8,128)(2,1)S(1)}, u32[]{:S(2)}, u32[]{:S(2)}) collective-permute-start(bf16[768,1536]{1,0:T(8,128)(2,1)S(1)} %slice.568), channel_id=1, source_target_pairs={{0,4},{1,3},{2,6},{3,1},{4,0},{5,7},{6,2},{7,5},{8,12},{9,11},{10,... | collective-permute-start | bytes 7077896 | tf_op jit(solution)/shard_map/ppermute | solution.py:575
  (120 other events, 2252.7 us)

commit v3 on v2

--- a/solution.py
+++ b/solution.py
@@ -232,6 +232,7 @@
             jax.ShapeDtypeStruct((spans * N, di), BF16),
         ],
         compiler_params=pltpu.CompilerParams(dimension_semantics=("arbitrary", "arbitrary")),
+        cost_estimate=pl.CostEstimate(flops=int(3.5e10), bytes_accessed=40 * tokens * di, transcendentals=0),
         name="scan_forward",
     )(pc, pc, pc, pc, pc, conv_all, conv_all, aux, seg_row, heads, skip)
 
@@ -259,27 +260,40 @@
 
 
 def backward_kernel(
+    first_call, last_call,
     dy_ref, x_ref, bcv_ref, st_ref, pc_ref, halo_ref, bc_ref, bc_halo_ref, raw_ref, cw_ref, bcw_ref,
-    aux_ref, seg_ref, heads_ref, skip_ref,
-    dproj_out, dcw_out, dbcw_out, dskip_out, dhead_out,
-    dstate, scores, block, dscores, same, pack_a, pack_b, cum_rows, c_t, ext, ext_bc,
-    carry, carry_bc, d_b, d_c, per_row, dcum_rows, dlast, dcw_acc, dskip_acc,
+    aux_ref, seg_ref, heads_ref, skip_ref, *rest,
 ):
+    rest = list(rest)
+    before = None if first_call else [rest.pop(0) for _ in range(4)]
+    dproj_out, dcw_out, dskip_out = [rest.pop(0) for _ in range(3)]
+    if last_call:
+        dbcw_out, dhead_out = [rest.pop(0) for _ in range(2)]
+        after = None
+    else:
+        after = [rest.pop(0) for _ in range(4)]
+    (
+        dstate, scores, block, dscores, same, pack_a, pack_b, cum_rows, c_t, ext, ext_bc,
+        carry, carry_bc, d_bc, per_row, dcum_rows, dlast, base,
+    ) = rest
     back = pl.program_id(0)
     group = pl.program_id(1)
     spans = pl.num_programs(0)
     groups = pl.num_programs(1)
     width = GROUP * P_SIZE
+    group_head = base[0] + GROUP * group
 
     @pl.when((back == 0) & (group == 0))
     def _():
         dstate[...] = jnp.zeros_like(dstate)
         carry[...] = jnp.zeros_like(carry)
-        carry_bc[...] = jnp.zeros_like(carry_bc)
-        dbcw_out[...] = jnp.zeros_like(dbcw_out)
-        dhead_out[...] = jnp.zeros_like(dhead_out)
-        dcw_acc[...] = jnp.zeros_like(dcw_acc)
-        dskip_acc[...] = jnp.zeros_like(dskip_acc)
+        dcw_out[...] = jnp.zeros_like(dcw_out)
+        dskip_out[...] = jnp.zeros_like(dskip_out)
+        dcum_rows[...] = jnp.zeros_like(dcum_rows)
+        if last_call:
+            carry_bc[...] = jnp.zeros_like(carry_bc)
+            dbcw_out[...] = jnp.zeros_like(dbcw_out)
+            dhead_out[...] = jnp.zeros_like(dhead_out)
 
     keys = bcv_ref[:, :N]
     query = bcv_ref[:, N:]
@@ -293,15 +307,21 @@
         block[...] = jnp.where(linked, 0.0, NEG)
         scores[...] = mm_nt(keys, query)
         c_t[...] = query.T
-        dscores[...] = jnp.zeros_like(dscores)
-        d_b[...] = jnp.zeros_like(d_b)
-        d_c[...] = jnp.zeros_like(d_c)
         per_row[...] = jnp.zeros_like(per_row)
-        dlast[...] = jnp.zeros_like(dlast)
+        if first_call:
+            dscores[...] = jnp.zeros_like(dscores)
+            d_bc[...] = jnp.zeros_like(d_bc)
+            dlast[...] = jnp.zeros_like(dlast)
+        else:
+            dscores[...] = before[0][...]
+            d_bc[...] = before[1][...]
+            per_row[0] = before[2][:, :TILE]
+            per_row[2] = before[2][:, TILE:]
+            dlast[...] = before[3][...]
 
     ext[0:8] = halo_ref[...]
     ext[8:] = pc_ref[...]
-    shift = (TILE - GROUP * group) % TILE
+    shift = lax.rem(TILE - group_head, TILE)
     cols_a = pltpu.roll(pack_a[...], shift, 1)
     cols_b = pltpu.roll(pack_b[...], shift, 1)
     retain = cols_b[SPAN - 1 : SPAN]
@@ -340,7 +360,7 @@
             mine = first if which == 0 else ~first
             xh = jnp.where(mine, xs, 0.0).astype(BF16)
             cum_col = lanes_of(cols_a[:, head : head + 1], SPAN)
-            cum_row = cum_rows[pl.ds(group * GROUP + head, 1), :]
+            cum_row = cum_rows[pl.ds(group_head + head, 1), :]
             g_top = mm_nt(xh[:HALF], dy)
             g_bottom = mm_nt(xh[HALF:], dy[HALF:])
             mixes = []
@@ -364,8 +384,8 @@
                 ],
                 axis=0,
             )
-            sums = sums + jnp.where(lane == 24 + head, row_sum, 0.0)
-            dcum_rows[pl.ds(group * GROUP + head, 1), :] = jnp.concatenate([down[0], down[1] + down[2]], axis=1)
+            sums = sums - jnp.where(lane == 2 * GROUP + head, row_sum, 0.0)
+            dcum_rows[pl.ds(group_head + head, 1), :] = jnp.concatenate([down[0], down[1] + down[2]], axis=1)
             top = mm(jnp.concatenate(mixes[:2], axis=1), dy)
             bottom = mm(mixes[2], dy[HALF:])
             inner.append(jnp.concatenate([top, bottom], axis=0))
@@ -373,23 +393,21 @@
         stf = stb.astype(F32)
         ds = dstate[:, tile]
         dsb = ds.astype(BF16)
-        dye = (dyf * entry_pair).astype(BF16)
-        fresh = mm(keys, dsb)
-        fresh = fresh * tail_pair
+        dye_f = dyf * entry_pair
+        dye = dye_f.astype(BF16)
+        fresh = mm(keys, dsb) * tail_pair
         total = jnp.where(first, inner[0], inner[1]) + fresh
         carried = mm(query, stb)
-        d_c[...] += mm_nt(dye, stb)
-        d_b[...] += mm_nt((xs * tail_pair).astype(BF16), dsb)
-
-        def spread(kind):
-            return (lane_col == kind * GROUP + 2 * pair + (lane_row >= P_SIZE).astype(jnp.int32)).astype(BF16)
+        d_bc[:, N:] += mm_nt(dye, stb)
+        d_bc[:, :N] += mm_nt((xs * tail_pair).astype(BF16), dsb)
 
         def head_sum(values, kind):
+            spread = (lane_col == kind * GROUP + 2 * pair + (lane_row >= P_SIZE).astype(jnp.int32)).astype(BF16)
             high = values.astype(BF16)
             rest = (values - high.astype(F32)).astype(BF16)
-            return mm(high, spread(kind)) + mm(rest, spread(kind))
-
-        sums = sums + head_sum(xf * total, 0) + head_sum(xs * fresh, 1) + head_sum(dyf * entry_pair * carried, 2)
+            return mm(high, spread) + mm(rest, spread)
+
+        sums = sums + head_sum(xf * total, 0) + head_sum(xs * fresh, 1) + head_sum(dye_f * carried, 2)
         retain_pair = jnp.where(
             first[:N],
             jnp.broadcast_to(retain[:, 2 * pair : 2 * pair + 1], (N, TILE)),
@@ -403,41 +421,47 @@
         last_sum = last_sum + jnp.where(lane[0:1] == 2 * pair + 1, high_sum, 0.0)
         dstate[:, tile] = kept + mm(c_t[...], dye)
         dx = total * step_pair + skip_ref[:, at : at + TILE] * dyf
-        dskip_acc[:, tile] += jnp.sum((dyf * xf).reshape(SPAN // 8, 8, TILE), axis=0)
+        dskip_out[:, tile] += jnp.sum((dyf * xf).reshape(SPAN // 8, 8, TILE), axis=0)
         out, conv_sums = conv_back(
             dx, ext, same, cw_ref[:, at : at + TILE], carry.at[:, :, tile], at, TILE
         )
         dproj_out[:, tile] = out.astype(BF16)
         for k, value in enumerate(conv_sums):
-            dcw_acc[k, :, tile] += value
-
-    back_shift = GROUP * group
-    in_place = (lane >= back_shift) & (lane < back_shift + GROUP)
-    for kind in range(4):
-        moved = pltpu.roll(sums, (back_shift + TILE - GROUP * kind) % TILE, 1)
+            dcw_out[k, :, tile] += value
+
+    in_place = (lane >= group_head) & (lane < group_head + GROUP)
+    for kind in range(3):
+        moved = pltpu.roll(sums, lax.rem(group_head + TILE - GROUP * kind, TILE), 1)
         per_row[kind] += jnp.where(in_place, moved, 0.0)
-    moved = pltpu.roll(jnp.broadcast_to(last_sum, (8, TILE)), back_shift, 1)
+    moved = pltpu.roll(jnp.broadcast_to(last_sum, (8, TILE)), group_head, 1)
     dlast[...] += jnp.where(in_place[0:8], moved, 0.0)
 
     @pl.when(group == groups - 1)
     def _():
+        state_part = per_row[1]
+        dcum = dcum_rows[...].T + per_row[2] - state_part
+        dlast_all = dlast[0:1] + jnp.sum(state_part, axis=0, keepdims=True)
+        if not last_call:
+            after[0][...] = dscores[...]
+            after[1][...] = d_bc[...]
+            after[2][:, :TILE] = per_row[0]
+            after[2][:, TILE:] = dcum
+            after[3][...] = jnp.broadcast_to(dlast_all, (8, TILE))
+            return
+        start = groups * width
         ds_b = dscores[...].astype(BF16)
-        grad_b = d_b[...] + mm(ds_b, query)
-        grad_c = d_c[...] + mm(dscores[...].T.astype(BF16), keys)
+        grad_b = d_bc[:, :N] + mm(ds_b, query)
+        grad_c = d_bc[:, N:] + mm(dscores[...].T.astype(BF16), keys)
         ext_bc[0:8] = bc_halo_ref[...]
         ext_bc[8:] = bc_ref[...]
         grad = jnp.concatenate([grad_b, grad_c], axis=1)
         out, conv_sums = conv_back(grad, ext_bc, same, bcw_ref[...], carry_bc, 0, 2 * N)
-        di = dstate.shape[1]
-        dproj_out[:, di : di + 2 * N] = out.astype(BF16)
+        dproj_out[:, start : start + 2 * N] = out.astype(BF16)
         for k, value in enumerate(conv_sums):
             dbcw_out[k] += value
         heads = heads_ref[...]
         raw = raw_ref[...]
         step = step_sizes(raw, heads)
-        state_part = per_row[1]
-        dcum = dcum_rows[...].T - per_row[3] + per_row[2] - state_part
-        dlast_all = dlast[0:1] + jnp.sum(state_part, axis=0, keepdims=True)
         row = lax.broadcasted_iota(jnp.int32, (SPAN, SPAN), 0)
         col = lax.broadcasted_iota(jnp.int32, (SPAN, SPAN), 1)
         tri = (row <= col).astype(F32)
@@ -446,56 +470,82 @@
         draw = dstep * jax.nn.sigmoid(raw + heads[0:1])
         live = lane < H
         draw = jnp.where(live, draw, 0.0)
-        dproj_out[:, di + 2 * N : di + 2 * N + TILE] = draw.astype(BF16)
-        dproj_out[:, di + 2 * N + TILE :] = jnp.zeros_like(dproj_out[:, di + 2 * N + TILE :])
+        dproj_out[:, start + 2 * N : start + 2 * N + TILE] = draw.astype(BF16)
+        dproj_out[:, start + 2 * N + TILE :] = jnp.zeros_like(dproj_out[:, start + 2 * N + TILE :])
         dhead_out[0] += jnp.sum(draw.reshape(SPAN // 8, 8, TILE), axis=0)
         dhead_out[1] += jnp.sum(jnp.where(live, da * step, 0.0).reshape(SPAN // 8, 8, TILE), axis=0)
 
-    @pl.when((group == groups - 1) & (back == spans - 1))
-    def _():
-        dcw_out[...] = dcw_acc[...]
-        dskip_out[...] = dskip_acc[...]
-
-
-def run_backward(dy, x, bcv, states, pc, conv_all, aux, seg_row, heads, skip):
+
+def run_backward(dy, x, bcv, states, pc, conv_all, aux, seg_row, heads, skip, start, count, last, before):
     tokens, di = dy.shape
     full = pc.shape[1]
     raw_block = (di + 2 * N) // TILE
     spans = tokens // SPAN
     width = GROUP * P_SIZE
-    groups = di // width
     last_block = di // (2 * N)
     turn = lambda s: spans - 1 - s
     halo = lambda s: jnp.maximum(turn(s) * (SPAN // 8) - 1, 0)
+    own = count * width
+    out_width = own + (full - di if last else 0)
+    sums_specs = [
+        pl.BlockSpec((SPAN, SPAN), lambda s, g: (turn(s), 0)),
+        pl.BlockSpec((SPAN, 2 * N), lambda s, g: (turn(s), 0)),
+        pl.BlockSpec((SPAN, 2 * TILE), lambda s, g: (turn(s), 0)),
+        pl.BlockSpec((8, TILE), lambda s, g: (turn(s), 0)),
+    ]
+    sums_shapes = [
+        jax.ShapeDtypeStruct((tokens, SPAN), F32),
+        jax.ShapeDtypeStruct((tokens, 2 * N), F32),
+        jax.ShapeDtypeStruct((tokens, 2 * TILE), F32),
+        jax.ShapeDtypeStruct((spans * 8, TILE), F32),
+    ]
+    out_specs = [
+        pl.BlockSpec((SPAN, out_width), lambda s, g: (turn(s), 0)),
+        pl.BlockSpec((5, 8, own), lambda s, g: (0, 0, 0)),
+        pl.BlockSpec((8, own), lambda s, g: (0, 0)),
+    ]
+    out_shape = [
+        jax.ShapeDtypeStruct((tokens, out_width), BF16),
+        jax.ShapeDtypeStruct((5, 8, own), F32),
+        jax.ShapeDtypeStruct((8, own), F32),
+    ]
+    if last:
+        out_specs += [
+            pl.BlockSpec((5, 8, 2 * N), lambda s, g: (0, 0, 0)),
+            pl.BlockSpec((2, 8, TILE), lambda s, g: (0, 0, 0)),
+        ]
+        out_shape += [
+            jax.ShapeDtypeStruct((5, 8, 2 * N), F32),
+            jax.ShapeDtypeStruct((2, 8, TILE), F32),
+        ]
+    else:
+        out_specs += sums_specs
+        out_shape += sums_shapes
+    wide = pl.BlockSpec((SPAN, width), lambda s, g: (turn(s), start + g))
     grid_spec = pltpu.PrefetchScalarGridSpec(
         num_scalar_prefetch=0,
-        grid=(spans, groups),
+        grid=(spans, count),
         in_specs=[
-            pl.BlockSpec((SPAN, width), lambda s, g: (turn(s), g)),
-            pl.BlockSpec((SPAN, width), lambda s, g: (turn(s), g)),
+            wide,
+            wide,
             pl.BlockSpec((SPAN, 2 * N), lambda s, g: (turn(s), 0)),
-            pl.BlockSpec((N, width), lambda s, g: (turn(s), g)),
-            pl.BlockSpec((SPAN, width), lambda s, g: (turn(s), g)),
-            pl.BlockSpec((8, width), lambda s, g: (halo(s), g)),
+            pl.BlockSpec((N, width), lambda s, g: (turn(s), start + g)),
+            wide,
+            pl.BlockSpec((8, width), lambda s, g: (halo(s), start + g)),
             pl.BlockSpec((SPAN, 2 * N), lambda s, g: (turn(s), last_block)),
             pl.BlockSpec((8, 2 * N), lambda s, g: (halo(s), last_block)),
             pl.BlockSpec((SPAN, TILE), lambda s, g: (turn(s), raw_block)),
-            pl.BlockSpec((8, width), lambda s, g: (0, g)),
+            pl.BlockSpec((8, width), lambda s, g: (0, start + g)),
             pl.BlockSpec((8, 2 * N), lambda s, g: (0, last_block)),
             pl.BlockSpec((SPAN, 8), lambda s, g: (turn(s), 0)),
             pl.BlockSpec((1, SPAN), lambda s, g: (0, turn(s))),
             pl.BlockSpec((8, TILE), lambda s, g: (0, 0)),
-            pl.BlockSpec((1, width), lambda s, g: (0, g)),
-        ],
-        out_specs=[
-            pl.BlockSpec((SPAN, full), lambda s, g: (turn(s), 0)),
-            pl.BlockSpec((5, 8, di), lambda s, g: (0, 0, 0)),
-            pl.BlockSpec((5, 8, 2 * N), lambda s, g: (0, 0, 0)),
-            pl.BlockSpec((8, di), lambda s, g: (0, 0)),
-            pl.BlockSpec((2, 8, TILE), lambda s, g: (0, 0, 0)),
-        ],
+            pl.BlockSpec((1, width), lambda s, g: (0, start + g)),
+        ]
+        + ([] if before is None else sums_specs),
+        out_specs=out_specs,
         scratch_shapes=[
-            pltpu.VMEM((N, di), F32),
+            pltpu.VMEM((N, own), F32),
             pltpu.VMEM((SPAN, SPAN), F32),
             pltpu.VMEM((SPAN, SPAN), F32),
             pltpu.VMEM((SPAN, SPAN), F32),
@@ -506,30 +556,32 @@
             pltpu.VMEM((N, SPAN), BF16),
             pltpu.VMEM((SPAN + 8, width), F32),
             pltpu.VMEM((SPAN + 8, 2 * N), F32),
-            pltpu.VMEM((3, 8, di), F32),
+            pltpu.VMEM((3, 8, own), F32),
             pltpu.VMEM((3, 8, 2 * N), F32),
-            pltpu.VMEM((SPAN, N), F32),
-            pltpu.VMEM((SPAN, N), F32),
-            pltpu.VMEM((4, SPAN, TILE), F32),
+            pltpu.VMEM((SPAN, 2 * N), F32),
+            pltpu.VMEM((3, SPAN, TILE), F32),
             pltpu.VMEM((TILE, SPAN), F32),
             pltpu.VMEM((8, TILE), F32),
-            pltpu.VMEM((5, 8, di), F32),
-            pltpu.VMEM((8, di), F32),
         ],
     )
+    call = functools.partial(with_base, functools.partial(backward_kernel, before is None, last), start * GROUP)
     return pl.pallas_call(
-        backward_kernel,
+        call,
         grid_spec=grid_spec,
-        out_shape=[
-            jax.ShapeDtypeStruct((tokens, full), BF16),
-            jax.ShapeDtypeStruct((5, 8, di), F32),
-            jax.ShapeDtypeStruct((5, 8, 2 * N), F32),
-            jax.ShapeDtypeStruct((8, di), F32),
-            jax.ShapeDtypeStruct((2, 8, TILE), F32),
-        ],
+        out_shape=out_shape,
         compiler_params=pltpu.CompilerParams(dimension_semantics=("arbitrary", "arbitrary")),
+        cost_estimate=pl.CostEstimate(
+            flops=int(1.5e10 * count), bytes_accessed=12 * tokens * own, transcendentals=0
+        ),
         name="scan_backward",
-    )(dy, x, bcv, states, pc, pc, pc, pc, pc, conv_all, conv_all, aux, seg_row, heads, skip)
+    )(
+        dy, x, bcv, states, pc, pc, pc, pc, pc, conv_all, conv_all, aux, seg_row, heads, skip,
+        *([] if before is None else before),
+    )
+
+
+def with_base(kernel, base, *refs):
+    kernel(*refs, (base,))
 
 
 def seg_facts(seg):
@@ -579,14 +631,19 @@
     return lax.ppermute(values, "rep", [(0, 1), (1, 0)])
 
 
-def gather_pieces(local):
+def after(values, *others):
+    return lax.optimization_barrier((values, *others))[0]
+
+
+def gather_pieces(local, ahead=None):
     held = local
-    arrived = None
+    seen = []
     for stage in range(4):
-        arrived = exchange(held, stage)
+        send = held if ahead is None else after(held, ahead[stage])
+        seen.append(exchange(send, stage))
         if stage < 3:
-            held = jnp.concatenate([held, arrived], axis=0)
-    return held, arrived, swap_cores(held), swap_cores(arrived)
+            held = jnp.concatenate([held, seen[-1]], axis=0)
+    return (held, seen[3], swap_cores(held), swap_cores(seen[3])), seen
 
 
 def gather_small(local):
@@ -599,13 +656,26 @@
     return dot_f32(hot, held, ((1,), (0,)), HIGHEST).astype(local.dtype)
 
 
-def scatter_sum(mine, other, block):
-    arrived = swap_cores(other)
-    total = mine.astype(F32) + arrived.astype(F32)
-    for stage in (3, 2, 1, 0):
-        cut = block << stage
-        total = total[:cut] + exchange(total[cut:].astype(BF16), stage).astype(F32)
-    return total
+class Scatter:
+    def __init__(self, partial, block):
+        self.mine, self.other = partial
+        self.block = block
+        self.left = [3, 2, 1, 0]
+        self.total = None
+
+    def step(self):
+        if self.total is None:
+            self.total = self.mine.astype(F32) + swap_cores(self.other).astype(F32)
+        elif self.left:
+            stage = self.left.pop(0)
+            cut = self.block << stage
+            self.total = self.total[:cut] + exchange(self.total[cut:].astype(BF16), stage).astype(F32)
+        return self.total
+
+    def finish(self):
+        while self.left:
+            self.step()
+        return self.total
 
 
 def block_order():
@@ -869,8 +939,9 @@
     conv_dim = conv_local * shards
     wide = -(-(conv_dim + TILE) // 512) * 512
     cuts = ((0, 1024), (1024, 1024), (2048, wide - 2048))
-    halves = ((0, di // 2), (di // 2, di // 2))
-    thirds = ((0, model // 2), (model // 2, model // 2))
+    halves = ((0, di),)
+    thirds = ((0, model),)
+    per_call = (0, 2), (2, 2), (4, 2)
 
     small = jnp.concatenate([conv_weight.reshape(-1), conv_bias, gain_in, gain_out])
     if hypercube:
@@ -880,9 +951,16 @@
         w_half = lax.dynamic_slice_in_dim(w_in, core * (w_in.shape[0] // 2), w_in.shape[0] // 2, 0)
         o_half = lax.dynamic_slice_in_dim(w_out, core * (w_out.shape[0] // 2), w_out.shape[0] // 2, 0)
         rest = jnp.pad(w_half[:, di:], ((0, 0), (0, wide - (w_in.shape[1] - di))))
-        conv_pieces = [gather_pieces(rest[:, a : a + n]) for a, n in cuts]
-        gate_pieces = [gather_pieces(w_half[:, a : a + n]) for a, n in halves]
-        out_pieces = [gather_pieces(o_half[:, a : a + n]) for a, n in thirds]
+        seen = None
+        conv_pieces, gate_pieces, out_pieces = [], [], []
+        for source, parts, into in (
+            (rest, cuts, conv_pieces),
+            (w_half, halves, gate_pieces),
+            (o_half, thirds, out_pieces),
+        ):
+            for a, n in parts:
+                pieces, seen = gather_pieces(source[:, a : a + n], seen)
+                into.append(pieces)
     else:
         small_all = lax.all_gather(small, "shard", axis=0, tiled=False)
         full_w_in = lax.all_gather(w_in, "shard", axis=0, tiled=True)
@@ -941,16 +1019,42 @@
     sig = jax.nn.sigmoid(gate)
     dy = (dz * (gate * sig)).astype(BF16)
     dgate = (dz * y * (sig * (1.0 + gate * (1.0 - sig)))).astype(BF16)
+    backward_args = (x, bcv, states, pc, conv_all, aux, seg_row, heads, skip)
     if hypercube:
-        out_sum = scatter_sum(*weight_grad(zg, cot_scaled, place, 0, model), w_out.shape[0] // 2)
-        gate_sums = [
-            scatter_sum(*weight_grad(normed, dgate, place, k, n), w_in.shape[0] // 2)
-            for k, (a, n) in enumerate(halves)
-        ]
-    dproj, dcw, dbcw, dskip, dhead = run_backward(
-        dy, x, bcv, states, pc, conv_all, aux, seg_row, heads, skip
-    )
-    scaled = (mm_nt(dgate, w_gate) + mm_nt(dproj, w_rest)) * full_gain_in
+        in_block = w_in.shape[0] // 2
+        out_sum = Scatter(weight_grad(zg, cot_scaled, place, 0, model), w_out.shape[0] // 2)
+        out_sum.step()
+        gate_grad = weight_grad(normed, dgate, place, 0, di)
+        gate_sum = Scatter(gate_grad, in_block)
+        gate_sum.step()
+        flow = [out_sum, gate_sum]
+        dy = after(dy, *gate_grad, out_sum.total)
+    else:
+        flow = []
+    sums = None
+    dprojs, dcws, dskips = [], [], []
+    for index, (start, count) in enumerate(per_call):
+        last = index == len(per_call) - 1
+        dpart, dcw, dskip, *sums = run_backward(dy, *backward_args, start, count, last, sums)
+        dprojs.append(dpart)
+        dcws.append(dcw)
+        dskips.append(dskip)
+        if hypercube:
+            steps = [each.step() for each in flow]
+            grad = weight_grad(normed, dpart, place, 0, dpart.shape[1])
+            flow.append(Scatter(grad, in_block))
+            flow[-1].step()
+            if not last:
+                dy = after(dy, dpart, *grad, *steps)
+    dbcw, dhead = sums
+    dcw = jnp.concatenate(dcws, axis=2)
+    dskip = jnp.concatenate(dskips, axis=1)
+    scaled = mm_nt(dgate, w_gate)
+    column = 0
+    for dpart in dprojs:
+        scaled = scaled + mm_nt(dpart, w_rest[:, column : column + dpart.shape[1]])
+        column += dpart.shape[1]
+    scaled = scaled * full_gain_in
     inner = jnp.mean(unit * scaled, axis=1, keepdims=True)
     grad_tokens = (cot + rscale * (scaled - unit * inner)).astype(BF16)
 
@@ -968,17 +1072,17 @@
     real = w_in.shape[1] - di
     if hypercube:
         small_sum = reduce_small(small_grad)[0]
-        rest_sums = []
-        for k, (a, n) in enumerate(cuts):
-            part = (dproj, k) if a == k * n else (dproj[:, a : a + n], 0)
-            rest_sums.append(scatter_sum(*weight_grad(normed, part[0], place, part[1], n), w_in.shape[0] // 2))
-        rest_sums[-1] = rest_sums[-1][:, : real - cuts[-1][0]]
-        own = jnp.concatenate(gate_sums + rest_sums, axis=1)
+        while any(each.left for each in flow):
+            for each in flow:
+                each.step()
+        own = [each.total for each in flow[1:]]
+        own[-1] = own[-1][:, : real - cuts[-1][0]]
+        own = jnp.concatenate(own, axis=1)
         sum_w_in = both_cores(own)
-        sum_w_out = both_cores(out_sum)
+        sum_w_out = both_cores(out_sum.total)
     else:
         grad_w_out = dot_f32(zg, cot_scaled, ((0,), (0,)))
-        grads = jnp.concatenate([dgate, dproj[:, :real]], axis=1)
+        grads = jnp.concatenate([dgate, *dprojs], axis=1)[:, : w_in.shape[1]]
         grad_w_in = dot_f32(normed, grads, ((0,), (0,)))
         small_sum = lax.psum(
             lax.psum_scatter(small_grad, "shard", scatter_dimension=0, tiled=True), "rep"

time: 830 us -> 704 us (0.85)
  waiting for transfers between devices: 280 us -> 134 us
  other arithmetic: 70 us -> 80.5 us
  matrix products: 66.8 us -> 75.4 us
    ppermute x60 -> x48, waiting for transfers between devices: 280 us -> 134 us  [exchange(): return lax.ppermute(values, ('shard', 'rep'), pairs)]
    add x25, other arithmetic: 24.5 us -> 34.6 us  [the longest x20 17.9 us: step(): self.total[:cut]]
    dot_general x6 -> x8, matrix products: 66.8 us -> 75.4 us  [dot_f32(): lax.dot_general(a, b, ((contract[0], contract[1]), ((), ())), preferred_e...]
    pallas_call x1 -> x3, Pallas kernels: 122 us -> 129 us  [run_backward(): pl.pallas_call(call, grid_spec=grid_spec, out_shape=out_shape, compiler_p...]
    pallas_call x2 -> x1, Pallas kernels: 31.7 us -> 24.6 us  [gate_project(): pl.pallas_call(functools.partial(gate_kernel, block, width), grid_spec=pl...]
    pallas_call x6 -> x5, Pallas kernels: 60.9 us -> 57.4 us  [weight_grad(): pl.pallas_call(functools.partial(weight_grad_kernel, block), grid_spec=pl...]
    ppermute x60 -> x48, starting transfers between devices: 60.5 us -> 62.5 us  [exchange(): return lax.ppermute(values, ('shard', 'rep'), pairs)]
  transfers between devices with their start and end apart: 83 -> 66, of which waited for: 31 -> 28; matrix products, arithmetic and copies ran while one was open for 11% -> 23% of each run, Pallas kernels for 19% -> 40%
where the time goes in v3:
time: 704 us; the launch traced here: 696 us
  Pallas kernels  301 us (43%)
  waiting for transfers between devices  134 us (19%)
  other arithmetic  80.5 us (11%)
  matrix products  75.4 us (11%)
  starting transfers between devices  67.1 us (10%)
  local copies, waits for them, and re-layouts  35.4 us (5%)
    ppermute x48, waiting for transfers between devices, exchange(): return lax.ppermute(values, ('shard', 'rep'), pairs)  134 us
    pallas_call x3, Pallas kernels, run_backward(): pl.pallas_call(call, grid_spec=grid_spec, out_shape=out_shape, compiler_p...  129 us
    dot_general x8, matrix products, dot_f32(): lax.dot_general(a, b, ((contract[0], contract[1]), ((), ())), preferred_e...  75.4 us
    ppermute x48, starting transfers between devices, exchange(): return lax.ppermute(values, ('shard', 'rep'), pairs)  62.5 us
    pallas_call x5, Pallas kernels, weight_grad(): pl.pallas_call(functools.partial(weight_grad_kernel, block), grid_spec=pl...  57.4 us
    pallas_call x1, Pallas kernels, run_forward(): pl.pallas_call(forward_kernel, grid_spec=grid_spec, out_shape=[jax.ShapeD...  50.7 us
    pallas_call x3, Pallas kernels, project(): pl.pallas_call(functools.partial(project_kernel, block, width), grid_spec...  29.9 us
    pallas_call x1, Pallas kernels, gate_project(): pl.pallas_call(functools.partial(gate_kernel, block, width), grid_spec=pl...  24.6 us
  transfers between devices with their start and end apart: 66, of which 28 were waited for; matrix products, arithmetic and copies ran while one was open for 23% of the time, Pallas kernels for 40%

profile of v3, /device:TPU:0, one launch (start us, length us, event | category | flops | bytes accessed | tf_op | source)
XLA Modules:
  0.0 696.4 jit_solution(1689058236173921776)
XLA Ops:
  35.5 7.8 %collective-permute-done.12 = bf16[192,1024]{1,0:T(8,128)(2,1)S(1)} collective-permute-done((bf16[192,1024]{1,0:T(8,128)(2,1)S(1)}, bf16[192,1024]{1,0:T(8,128)(2,1)S(1)}, u32[]{:S(2)}, u32[]{:S(2)}) %collective-permute-start.12) | collective-permute-done | bytes 393248 | tf_op jit(solution)/shard_map/ppermute | solution.py:627
  80.1 18.9 %collective-permute-done.28 = bf16[96,1536]{1,0:T(8,128)(2,1)S(1)} collective-permute-done((bf16[96,1536]{1,0:T(8,128)(2,1)S(1)}, bf16[96,1536]{1,0:T(8,128)(2,1)S(1)}, u32[]{:S(2)}, u32[]{:S(2)}) %collective-permute-start.28) | collective-permute-done | bytes 294944 | tf_op jit(solution)/shard_map/ppermute | solution.py:627
  122.3 11.0 %collective-permute-done.3 = bf16[8,1328]{1,0:T(8,128)(2,1)S(1)} collective-permute-done((bf16[8,1328]{1,0:T(8,128)(2,1)S(1)}, bf16[8,1328]{1,0:T(8,128)(2,1)S(1)}, u32[]{:S(2)}, u32[]{:S(2)}) %collective-permute-start.3) | collective-permute-done | bytes 21280 | tf_op jit(solution)/shard_map/ppermute | solution.py:627
  145.7 9.2 %project.3 = (f32[1024,3584]{1,0:T(8,128)}, bf16[1536,3584]{1,0:T(8,128)(2,1)}) custom-call(s32[32]{0:T(128)} %pad_add_fusion.order_ref, bf16[1024,1536]{1,0:T(8,128)(2,1)} %fusion.4.x_ref.lhs_ref, bf16[384,1024]{1,0:T(8,128)(2,1)} %copy-done.16, bf16[384,1024]{1,0:T(8,128)(2,1)} %copy-done.36, bf16[384,1024]{1,0:T(8,128)(2,1)} %collective-permute-done.26.p2, ...), custom_call_target="tpu_custom_call" | custom-call | flops 3221225472 | bytes 13631488 | tf_op jit(solution)/shard_map/project/pallas_call | solution.py:739
  155.3 9.0 %project.4 = (f32[1024,3584]{1,0:T(8,128)}, bf16[1536,3584]{1,0:T(8,128)(2,1)}) custom-call(s32[32]{0:T(128)} %pad_add_fusion.order_ref, bf16[1024,1536]{1,0:T(8,128)(2,1)} %fusion.4.x_ref.lhs_ref, bf16[384,1024]{1,0:T(8,128)(2,1)} %pad_maximum_fusion.8.p0, ...), custom_call_target="tpu_custom_call", output_to_operand_aliasing={{0}: (6, {}), {1}: (7, {})} | custom-call | flops 3221225472 | bytes 13631488 | tf_op jit(solution)/shard_map/project/pallas_call | solution.py:739
  164.6 11.7 %project.5 = (f32[1024,3584]{1,0:T(8,128)}, bf16[1536,3584]{1,0:T(8,128)(2,1)}) custom-call(s32[32]{0:T(128)} %pad_add_fusion.order_ref, bf16[1024,1536]{1,0:T(8,128)(2,1)} %fusion.4.x_ref.lhs_ref, bf16[384,1536]{1,0:T(8,128)(2,1)} %pad_maximum_fusion.5.p0, ...), custom_call_target="tpu_custom_call", output_to_operand_aliasing={{0}: (6, {}), {1}: (7, {})} | custom-call | flops 4831838208 | bytes 18874368 | tf_op jit(solution)/shard_map/project/pallas_call | solution.py:739
  176.9 50.7 %scan_forward.1 = (bf16[1024,3072]{1,0:T(8,128)(2,1)}, bf16[1024,256]{1,0:T(8,128)(2,1)}, f32[1024,3072]{1,0:T(8,128)}, bf16[512,3072]{1,0:T(8,128)(2,1)}) custom-call(f32[1024,3584]{1,0:T(8,128)} %get-tuple-element.89.pc_ref.halo_ref.bc_ref.bc_halo_ref.raw_ref.refs_4_.refs_5_.refs_6_.refs_7_.refs_8_, ...), custom_call_target="tpu_custom_call" | custom-call | flops 35000000512 | bytes 125829120 | tf_op jit(solution)/shard_map/scan_forward/pallas_call | solution.py:225
  227.7 24.6 %project_gate.1 = (f32[1024,3072]{1,0:T(8,128)}, bf16[1536,3072]{1,0:T(8,128)(2,1)}, bf16[1024,3072]{1,0:T(8,128)(2,1)}, f32[1024,128]{1,0:T(8,128)}) custom-call(s32[32]{0:T(128)} %pad_add_fusion.order_ref, bf16[1024,1536]{1,0:T(8,128)(2,1)} %fusion.4.x_ref.lhs_ref, bf16[384,3072]{1,0:T(8,128)(2,1)} %pad_maximum_fusion.1.p0, ...), custom_call_target="tpu_custom_call" | custom-call | flops 9663676416 | bytes 53477376 | tf_op jit(solution)/shard_map/project_gate/pallas_call | solution.py:793
  253.6 9.2 %restore.1 = bf16[3072,1536]{1,0:T(8,128)(2,1)} custom-call(s32[32]{0:T(128)} %pad_add_fusion.order_ref, bf16[768,1536]{1,0:T(8,128)(2,1)} %pad_maximum_fusion.2.p0, bf16[768,1536]{1,0:T(8,128)(2,1)} %collective-permute-done.31.p1, bf16[768,1536]{1,0:T(8,128)(2,1)} %collective-permute-done.32.p2, bf16[768,1536]{1,0:T(8,128)(2,1)} %collective-permute-done.33.p3), custom_call_target="tpu_custom_call" | custom-call | bytes 18874368 | tf_op jit(solution)/shard_map/restore/pallas_call | solution.py:839
  262.8 17.5 %fusion.10 = (f32[1024]{0:T(1024)S(1)}, bf16[1024,1536]{1,0:T(8,128)(2,1)}, bf16[1024,1536]{1,0:T(8,128)(2,1)}) fusion(bf16[1024,1536]{1,0:T(8,128)(2,1)} %param.27, f32[1024]{0:T(1024)S(1)} %add_rsqrt_fusion, bf16[1024,1536]{1,0:T(8,128)(2,1)S(1)} %copy-done.2, bf16[1024,3072]{1,0:T(8,128)(2,1)} %get-tuple-element.92.lhs_ref, bf16[3072,1536]{1,0:T(8,128)(2,1)} %restore.1), kind=kOutput, calls=%fused_computation.23 | convolution fusion | flops 9677831168 | bytes 28319744 | tf_op jit(solution)/shard_map/dot_general | solution.py:26
  280.3 15.1 %weight_grad.6 = (bf16[1536,1536]{1,0:T(8,128)(2,1)}, bf16[1536,1536]{1,0:T(8,128)(2,1)}) custom-call(s32[32]{0:T(128)} %fusion.35.place_ref, bf16[1024,3072]{1,0:T(8,128)(2,1)} %get-tuple-element.92.lhs_ref, bf16[1024,1536]{1,0:T(8,128)(2,1)} %get-tuple-element.145.rhs_ref), custom_call_target="tpu_custom_call" | custom-call | flops 9663676416 | bytes 18874368 | tf_op jit(solution)/shard_map/weight_grad/pallas_call | solution.py:894
  295.8 16.3 %fusion.48 = f32[3072,1024]{0,1:T(8,128)} fusion(bf16[3072,1536]{1,0:T(8,128)(2,1)} %restore.1, bf16[1024,1536]{1,0:T(8,128)(2,1)} %param.27), kind=kOutput, calls=%fused_computation.187 | convolution fusion | flops 9663676416 | bytes 25165824 | tf_op jit(solution)/shard_map/dot_general | solution.py:26
  312.2 13.9 %multiply_convert_fusion.1 = (bf16[1024,3072]{1,0:T(8,128)(2,1)}, bf16[1024,3072]{1,0:T(8,128)(2,1)}) fusion(f32[1024,3072]{1,0:T(8,128)S(1)} %bitcast.72, f32[1024,3072]{1,0:T(8,128)S(1)} %bitcast.70, f32[3072,1024]{0,1:T(8,128)} %fusion.48, f32[1024]{0:T(1024)S(1)} %multiply_multiply_fusion, f32[3072]{0:T(1024)S(1)} %reshape.323, f32[1024]{0:T(1024)S(1)} %add_rsqrt_fusion), kind=kLoop, calls=%fused_computation.3 | loop fusion | flops 56623104 | bytes 50352128 | tf_op jit(solution)/shard_map/convert_element_type | solution.py:1021
  326.1 16.2 %weight_grad.5 = (bf16[768,3072]{1,0:T(8,128)(2,1)}, bf16[768,3072]{1,0:T(8,128)(2,1)}) custom-call(s32[32]{0:T(128)} %fusion.35.place_ref, bf16[1024,1536]{1,0:T(8,128)(2,1)} %fusion.4.x_ref.lhs_ref, bf16[1024,3072]{1,0:T(8,128)(2,1)} %get-tuple-element.141.rhs_ref), custom_call_target="tpu_custom_call" | custom-call | flops 9663676416 | bytes 18874368 | tf_op jit(solution)/shard_map/weight_grad/pallas_call | solution.py:894
  354.4 41.8 %scan_backward.3 = (bf16[1024,1024]{1,0:T(8,128)(2,1)}, f32[5,8,1024]{2,1,0:T(8,128)}, f32[8,1024]{1,0:T(8,128)}, f32[1024,256]{1,0:T(8,128)}, f32[1024,256]{1,0...) custom-call(bf16[1024,3072]{1,0:T(8,128)(2,1)} %get-tuple-element.119.refs_0_, ...), custom_call_target="tpu_custom_call" | custom-call | flops 30000001024 | bytes 12582912 | tf_op jit(solution)/shard_map/scan_backward/pallas_call | solution.py:568
  396.2 8.1 %weight_grad.7 = (bf16[768,1024]{1,0:T(8,128)(2,1)}, bf16[768,1024]{1,0:T(8,128)(2,1)}) custom-call(s32[32]{0:T(128)} %fusion.35.place_ref, bf16[1024,1536]{1,0:T(8,128)(2,1)} %fusion.4.x_ref.lhs_ref, bf16[1024,1024]{1,0:T(8,128)(2,1)} %get-tuple-element.107.rhs_ref), custom_call_target="tpu_custom_call" | custom-call | flops 3221225472 | bytes 8388608 | tf_op jit(solution)/shard_map/weight_grad/pallas_call | solution.py:894
  412.7 14.0 %fusion.49 = f32[1024,1536]{1,0:T(8,128)} fusion(bf16[1024,3072]{1,0:T(8,128)(2,1)S(1)} %bitcast.74, bf16[1536,3072]{1,0:T(8,128)(2,1)} %get-tuple-element.98), kind=kOutput, calls=%fused_computation.188 | convolution fusion | flops 9663676416 | bytes 22020096 | tf_op jit(solution)/shard_map/dot_general | solution.py:26
  449.5 42.2 %scan_backward.4 = (bf16[1024,1024]{1,0:T(8,128)(2,1)}, f32[5,8,1024]{2,1,0:T(8,128)}, f32[8,1024]{1,0:T(8,128)}, f32[1024,256]{1,0:T(8,128)}, f32[1024,256]{1,0...) custom-call(bf16[1024,3072]{1,0:T(8,128)(2,1)} %get-tuple-element.119.refs_0_, ...), custom_call_target="tpu_custom_call" | custom-call | flops 30000001024 | bytes 12582912 | tf_op jit(solution)/shard_map/scan_backward/pallas_call | solution.py:568
  510.8 8.0 %weight_grad.8 = (bf16[768,1024]{1,0:T(8,128)(2,1)}, bf16[768,1024]{1,0:T(8,128)(2,1)}) custom-call(s32[32]{0:T(128)} %fusion.35.place_ref, bf16[1024,1536]{1,0:T(8,128)(2,1)} %fusion.4.x_ref.lhs_ref, bf16[1024,1024]{1,0:T(8,128)(2,1)} %get-tuple-element.116.rhs_ref), custom_call_target="tpu_custom_call" | custom-call | flops 3221225472 | bytes 8388608 | tf_op jit(solution)/shard_map/weight_grad/pallas_call | solution.py:894
  528.4 45.4 %scan_backward.5 = (bf16[1024,1536]{1,0:T(8,128)(2,1)}, f32[5,8,1024]{2,1,0:T(8,128)}, f32[8,1024]{1,0:T(8,128)}, f32[5,8,256]{2,1,0:T(8,128)}, f32[2,8,128]{2,1,0:T(8,128)}) custom-call(bf16[1024,3072]{1,0:T(8,128)(2,1)} %get-tuple-element.119.refs_0_, bf16[1024,3072]{1,0:T(8,128)(2,1)} %get-tuple-element.104.refs_1_, ...), custom_call_target="tpu_custom_call" | custom-call | flops 30000001024 | bytes 12582912 | tf_op jit(solution)/shard_map/scan_backward/pallas_call | solution.py:568
  582.1 10.0 %weight_grad.9 = (bf16[768,1536]{1,0:T(8,128)(2,1)}, bf16[768,1536]{1,0:T(8,128)(2,1)}) custom-call(s32[32]{0:T(128)} %fusion.35.place_ref, bf16[1024,1536]{1,0:T(8,128)(2,1)} %fusion.4.x_ref.lhs_ref, bf16[1024,1536]{1,0:T(8,128)(2,1)} %get-tuple-element.124.rhs_ref), custom_call_target="tpu_custom_call" | custom-call | flops 4831838208 | bytes 11010048 | tf_op jit(solution)/shard_map/weight_grad/pallas_call | solution.py:894
  593.8 12.6 %fusion.5 = (f32[1024]{0:T(1024)S(1)}, f32[1024,1536]{1,0:T(8,128)S(1)}) fusion(bf16[1024,1536]{1,0:T(8,128)(2,1)S(1)} %copy-done.3, f32[1024]{0:T(1024)S(1)} %copy-done.23, f32[1536]{0:T(1024)S(1)} %copy-done.25, bf16[1024,1536]{1,0:T(8,128)(2,1)} %get-tuple-element.124.rhs_ref, bf16[1536,3584]{1,0:T(8,128)(2,1)} %get-tuple-element.108, ...), kind=kOutput, calls=%fused_computation.18 | convolution fusion | flops 4844420096 | bytes 36190208 | tf_op jit(solution)/shard_map/dot_general | solution.py:26
  637.2 12.0 %collective-permute-done.53 = bf16[384,1536]{1,0:T(8,128)(2,1)S(1)} collective-permute-done((bf16[384,1536]{1,0:T(8,128)(2,1)S(1)}, bf16[384,1536]{1,0:T(8,128)(2,1)S(1)}, u32[]{:S(2)}, u32[]{:S(2)}) %collective-permute-start.53) | collective-permute-done | bytes 1179680 | tf_op jit(solution)/shard_map/ppermute | solution.py:627
  662.8 11.0 %collective-permute-done.54 = bf16[192,1536]{1,0:T(8,128)(2,1)S(1)} collective-permute-done((bf16[192,1536]{1,0:T(8,128)(2,1)S(1)}, bf16[192,1536]{1,0:T(8,128)(2,1)S(1)}, u32[]{:S(2)}, u32[]{:S(2)}) %collective-permute-start.54) | collective-permute-done | bytes 589856 | tf_op jit(solution)/shard_map/ppermute | solution.py:627
  (391 shorter events, 257.6 us)
Async XLA Ops:
  3.5 75.0 %collective-permute-start = (bf16[1,1328]{1,0:T(2,128)(2,1)S(1)}, bf16[1,1328]{1,0:T(2,128)(2,1)S(1)}, u32[]{:S(2)}, u32[]{:S(2)}) collective-permute-start(bf16[1,1328]{1,0:T(2,128)(2,1)S(1)} %broadcast_in_dim.12), channel_id=1, source_target_pairs={{0,16},{1,17},{2,18},{3,19},{4,20},{5,21},{6,22},{7,23},{8,24},{9,... | collective-permute-start | bytes 7976 | tf_op jit(solution)/shard_map/ppermute | solution.py:627
  68.7 32.4 %collective-permute-start.15 = (bf16[192,3072]{1,0:T(8,128)(2,1)}, bf16[192,3072]{1,0:T(8,128)(2,1)}, u32[]{:S(2)}, u32[]{:S(2)}) collective-permute-start(bf16[192,3072]{1,0:T(8,128)(2,1)} %pad_maximum_fusion.4), channel_id=1, source_target_pairs={{0,8},{1,9},{2,10},{3,11},{4,12},{5,13},{6,14},{7,15},{8,0},{9,1},... | collective-permute-start | bytes 3538952 | tf_op jit(solution)/shard_map/ppermute | solution.py:627
  73.9 30.0 %collective-permute-start.18 = (bf16[384,1536]{1,0:T(8,128)(2,1)}, bf16[384,1536]{1,0:T(8,128)(2,1)}, u32[]{:S(2)}, u32[]{:S(2)}) collective-permute-start(bf16[384,1536]{1,0:T(8,128)(2,1)} %pad_maximum_fusion.5.p0), channel_id=1, source_target_pairs={{0,4},{1,3},{2,6},{3,1},{4,0},{5,7},{6,2},{7,5},{8,12},{9,11},{10,... | collective-permute-start | bytes 3538952 | tf_op jit(solution)/shard_map/ppermute | solution.py:627
  78.5 27.0 %collective-permute-start.1 = (bf16[2,1328]{1,0:T(2,128)(2,1)S(1)}, bf16[2,1328]{1,0:T(2,128)(2,1)S(1)}, u32[]{:S(2)}, u32[]{:S(2)}) collective-permute-start(bf16[2,1328]{1,0:T(2,128)(2,1)S(1)} %pad_maximum_fusion.22), channel_id=1, source_target_pairs={{0,2},{1,5},{2,0},{3,7},{4,6},{5,1},{6,4},{7,3},{8,10},{9,13},{10,... | collective-permute-start | bytes 15944 | tf_op jit(solution)/shard_map/ppermute | solution.py:627
  103.9 36.1 %collective-permute-start.19 = (bf16[384,3072]{1,0:T(8,128)(2,1)}, bf16[384,3072]{1,0:T(8,128)(2,1)}, u32[]{:S(2)}, u32[]{:S(2)}) collective-permute-start(bf16[384,3072]{1,0:T(8,128)(2,1)} %pad_maximum_fusion.1.p0), channel_id=1, source_target_pairs={{0,4},{1,3},{2,6},{3,1},{4,0},{5,7},{6,2},{7,5},{8,12},{9,11},{10,... | collective-permute-start | bytes 7077896 | tf_op jit(solution)/shard_map/ppermute | solution.py:627
  140.0 36.6 %collective-permute-start.31 = (bf16[768,1536]{1,0:T(8,128)(2,1)}, bf16[768,1536]{1,0:T(8,128)(2,1)}, u32[]{:S(2)}, u32[]{:S(2)}) collective-permute-start(bf16[768,1536]{1,0:T(8,128)(2,1)} %pad_maximum_fusion.2.p0), channel_id=1, source_target_pairs={{0,4},{1,3},{2,6},{3,1},{4,0},{5,7},{6,2},{7,5},{8,12},{9,11},{10,... | collective-permute-start | bytes 7077896 | tf_op jit(solution)/shard_map/ppermute | solution.py:627
  155.0 72.7 %collective-permute-start.20 = (bf16[384,3072]{1,0:T(8,128)(2,1)}, bf16[384,3072]{1,0:T(8,128)(2,1)}, u32[]{:S(2)}, u32[]{:S(2)}) collective-permute-start(bf16[384,3072]{1,0:T(8,128)(2,1)} %pad_maximum_fusion.1.p0), channel_id=1, source_target_pairs={{0,1},{1,0},{2,3},{3,2},{4,5},{5,4},{6,7},{7,6},{8,9},{9,8},{10,11... | collective-permute-start | bytes 7077896 | tf_op jit(solution)/shard_map/ppermute | solution.py:631
  164.3 89.3 %collective-permute-start.32 = (bf16[768,1536]{1,0:T(8,128)(2,1)}, bf16[768,1536]{1,0:T(8,128)(2,1)}, u32[]{:S(2)}, u32[]{:S(2)}) collective-permute-start(bf16[768,1536]{1,0:T(8,128)(2,1)} %pad_maximum_fusion.2.p0), channel_id=1, source_target_pairs={{0,1},{1,0},{2,3},{3,2},{4,5},{5,4},{6,7},{7,6},{8,9},{9,8},{10,11... | collective-permute-start | bytes 7077896 | tf_op jit(solution)/shard_map/ppermute | solution.py:631
  176.3 51.3 %collective-permute-start.21 = (bf16[384,3072]{1,0:T(8,128)(2,1)}, bf16[384,3072]{1,0:T(8,128)(2,1)}, u32[]{:S(2)}, u32[]{:S(2)}) collective-permute-start(bf16[384,3072]{1,0:T(8,128)(2,1)} %collective-permute-done.19.p1), channel_id=1, source_target_pairs={{0,1},{1,0},{2,3},{3,2},{4,5},{5,4},{6,7},{7,6},{8,9},{9,8},{10,11... | collective-permute-start | bytes 7077896 | tf_op jit(solution)/shard_map/ppermute | solution.py:631
  176.6 76.9 %collective-permute-start.33 = (bf16[768,1536]{1,0:T(8,128)(2,1)}, bf16[768,1536]{1,0:T(8,128)(2,1)}, u32[]{:S(2)}, u32[]{:S(2)}) collective-permute-start(bf16[768,1536]{1,0:T(8,128)(2,1)} %collective-permute-done.31.p1), channel_id=1, source_target_pairs={{0,1},{1,0},{2,3},{3,2},{4,5},{5,4},{6,7},{7,6},{8,9},{9,8},{10,11... | collective-permute-start | bytes 7077896 | tf_op jit(solution)/shard_map/ppermute | solution.py:631
  295.5 47.1 %collective-permute-start.34 = (bf16[1536,1536]{1,0:T(8,128)(2,1)}, bf16[1536,1536]{1,0:T(8,128)(2,1)}, u32[]{:S(2)}, u32[]{:S(2)}) collective-permute-start(bf16[1536,1536]{1,0:T(8,128)(2,1)} %get-tuple-element.102), channel_id=1, source_target_pairs={{0,1},{1,0},{2,3},{3,2},{4,5},{5,4},{6,7},{7,6},{8,9},{9,8},{10,11... | collective-permute-start | bytes 14155784 | tf_op jit(solution)/shard_map/ppermute | solution.py:631
  342.3 62.1 %collective-permute-start.36 = (bf16[768,3072]{1,0:T(8,128)(2,1)}, bf16[768,3072]{1,0:T(8,128)(2,1)}, u32[]{:S(2)}, u32[]{:S(2)}) collective-permute-start(bf16[768,3072]{1,0:T(8,128)(2,1)} %get-tuple-element.100), channel_id=1, source_target_pairs={{0,1},{1,0},{2,3},{3,2},{4,5},{5,4},{6,7},{7,6},{8,9},{9,8},{10,11... | collective-permute-start | bytes 14155784 | tf_op jit(solution)/shard_map/ppermute | solution.py:631
  353.1 84.0 %collective-permute-start.35 = (bf16[768,1536]{1,0:T(8,128)(2,1)}, bf16[768,1536]{1,0:T(8,128)(2,1)}, u32[]{:S(2)}, u32[]{:S(2)}) collective-permute-start(bf16[768,1536]{1,0:T(8,128)(2,1)} %slice.511), channel_id=1, source_target_pairs={{0,4},{1,3},{2,6},{3,1},{4,0},{5,7},{6,2},{7,5},{8,12},{9,11},{10,... | collective-permute-start | bytes 7077896 | tf_op jit(solution)/shard_map/ppermute | solution.py:627
  411.9 29.2 %collective-permute-start.37 = (bf16[384,3072]{1,0:T(8,128)(2,1)}, bf16[384,3072]{1,0:T(8,128)(2,1)}, u32[]{:S(2)}, u32[]{:S(2)}) collective-permute-start(bf16[384,3072]{1,0:T(8,128)(2,1)} %slice.510), channel_id=1, source_target_pairs={{0,4},{1,3},{2,6},{3,1},{4,0},{5,7},{6,2},{7,5},{8,12},{9,11},{10,... | collective-permute-start | bytes 7077896 | tf_op jit(solution)/shard_map/ppermute | solution.py:627
  435.8 56.0 %collective-permute-start.41 = (bf16[384,1024]{1,0:T(8,128)(2,1)}, bf16[384,1024]{1,0:T(8,128)(2,1)}, u32[]{:S(2)}, u32[]{:S(2)}) collective-permute-start(bf16[384,1024]{1,0:T(8,128)(2,1)} %slice.516), channel_id=1, source_target_pairs={{0,4},{1,3},{2,6},{3,1},{4,0},{5,7},{6,2},{7,5},{8,12},{9,11},{10,... | collective-permute-start | bytes 2359304 | tf_op jit(solution)/shard_map/ppermute | solution.py:627
  446.6 74.3 %collective-permute-start.38 = (bf16[384,1536]{1,0:T(8,128)(2,1)}, bf16[384,1536]{1,0:T(8,128)(2,1)}, u32[]{:S(2)}, u32[]{:S(2)}) collective-permute-start(bf16[384,1536]{1,0:T(8,128)(2,1)} %slice.514), channel_id=1, source_target_pairs={{0,8},{1,9},{2,10},{3,11},{4,12},{5,13},{6,14},{7,15},{8,0},{9,1},... | collective-permute-start | bytes 3538952 | tf_op jit(solution)/shard_map/ppermute | solution.py:627
  449.5 75.1 %collective-permute-start.39 = (bf16[192,3072]{1,0:T(8,128)(2,1)}, bf16[192,3072]{1,0:T(8,128)(2,1)}, u32[]{:S(2)}, u32[]{:S(2)}) collective-permute-start(bf16[192,3072]{1,0:T(8,128)(2,1)} %slice.513), channel_id=1, source_target_pairs={{0,8},{1,9},{2,10},{3,11},{4,12},{5,13},{6,14},{7,15},{8,0},{9,1},... | collective-permute-start | bytes 3538952 | tf_op jit(solution)/shard_map/ppermute | solution.py:627
  518.8 100.8 %collective-permute-start.47 = (bf16[768,1024]{1,0:T(8,128)(2,1)}, bf16[768,1024]{1,0:T(8,128)(2,1)}, u32[]{:S(2)}, u32[]{:S(2)}) collective-permute-start(bf16[768,1024]{1,0:T(8,128)(2,1)} %get-tuple-element.118), channel_id=1, source_target_pairs={{0,1},{1,0},{2,3},{3,2},{4,5},{5,4},{6,7},{7,6},{8,9},{9,8},{10,11... | collective-permute-start | bytes 4718600 | tf_op jit(solution)/shard_map/ppermute | solution.py:631
  519.0 59.5 %collective-permute-start.46 = (bf16[48,1024]{1,0:T(8,128)(2,1)S(1)}, bf16[48,1024]{1,0:T(8,128)(2,1)S(1)}, u32[]{:S(2)}, u32[]{:S(2)}) collective-permute-start(bf16[48,1024]{1,0:T(8,128)(2,1)S(1)} %slice.529), channel_id=1, source_target_pairs={{0,16},{1,17},{2,18},{3,19},{4,20},{5,21},{6,22},{7,23},{8,24},{9,... | collective-permute-start | bytes 294920 | tf_op jit(solution)/shard_map/ppermute | solution.py:627
  592.1 31.5 %collective-permute-start.52 = (bf16[768,1536]{1,0:T(8,128)(2,1)}, bf16[768,1536]{1,0:T(8,128)(2,1)}, u32[]{:S(2)}, u32[]{:S(2)}) collective-permute-start(bf16[768,1536]{1,0:T(8,128)(2,1)} %get-tuple-element.126), channel_id=1, source_target_pairs={{0,1},{1,0},{2,3},{3,2},{4,5},{5,4},{6,7},{7,6},{8,9},{9,8},{10,11... | collective-permute-start | bytes 7077896 | tf_op jit(solution)/shard_map/ppermute | solution.py:631
  628.5 46.9 %collective-permute-start.43 = (bf16[48,3072]{1,0:T(8,128)(2,1)S(1)}, bf16[48,3072]{1,0:T(8,128)(2,1)S(1)}, u32[]{:S(2)}, u32[]{:S(2)}) collective-permute-start(bf16[48,3072]{1,0:T(8,128)(2,1)S(1)} %slice.524), channel_id=1, source_target_pairs={{0,16},{1,17},{2,18},{3,19},{4,20},{5,21},{6,22},{7,23},{8,24},{9,... | collective-permute-start | bytes 884744 | tf_op jit(solution)/shard_map/ppermute | solution.py:627
  636.9 24.3 %collective-permute-start.49 = (bf16[192,1024]{1,0:T(8,128)(2,1)S(1)}, bf16[192,1024]{1,0:T(8,128)(2,1)S(1)}, u32[]{:S(2)}, u32[]{:S(2)}) collective-permute-start(bf16[192,1024]{1,0:T(8,128)(2,1)S(1)} %slice.520), channel_id=1, source_target_pairs={{0,8},{1,9},{2,10},{3,11},{4,12},{5,13},{6,14},{7,15},{8,0},{9,1},... | collective-permute-start | bytes 1179656 | tf_op jit(solution)/shard_map/ppermute | solution.py:627
  649.6 24.2 %collective-permute-start.54 = (bf16[192,1536]{1,0:T(8,128)(2,1)S(1)}, bf16[192,1536]{1,0:T(8,128)(2,1)S(1)}, u32[]{:S(2)}, u32[]{:S(2)}) collective-permute-start(bf16[192,1536]{1,0:T(8,128)(2,1)S(1)} %slice.518), channel_id=1, source_target_pairs={{0,8},{1,9},{2,10},{3,11},{4,12},{5,13},{6,14},{7,15},{8,0},{9,1},... | collective-permute-start | bytes 1769480 | tf_op jit(solution)/shard_map/ppermute | solution.py:627
  657.1 33.0 %collective-permute-start.65 = (f32[96,1536]{1,0:T(8,128)S(1)}, f32[96,1536]{1,0:T(8,128)S(1)}, u32[]{:S(2)}, u32[]{:S(2)}) collective-permute-start(f32[96,1536]{1,0:T(8,128)S(1)} %slice_add_fusion.12), channel_id=1, source_target_pairs={{0,1},{1,0},{2,3},{3,2},{4,5},{5,4},{6,7},{7,6},{8,9},{9,8},{10,11... | collective-permute-start | bytes 1769480 | tf_op jit(solution)/shard_map/ppermute | solution.py:631
  (94 other events, 1391.1 us)

commit v4 on v3

v4 whole, which is shorter than its diff:
```python
import functools

import jax
import jax.numpy as jnp
from jax import lax
from jax.experimental import pallas as pl
from jax.experimental.pallas import tpu as pltpu
from jax.sharding import PartitionSpec as P
from jax.sharding import PartitionSpec as P

H = 48
P_SIZE = 64
N = 128
SPAN = 256
HALF = 128
GROUP = 8
TILE = 128
EPSILON = 1e-05
HIGHEST = lax.Precision.HIGHEST
LOG2E = 1.4426950408889634
NEG = -1e30
F32 = jnp.float32
BF16 = jnp.bfloat16


def dot_f32(a, b, contract, precision=None):
    return lax.dot_general(
        a, b, ((contract[0], contract[1]), ((), ())), preferred_element_type=F32, precision=precision
    )


def mm(a, b):
    return dot_f32(a, b, ((1,), (0,)))


def mm_nt(a, b):
    return dot_f32(a, b, ((1,), (1,)))


def lanes_of(column, rows):
    return jnp.broadcast_to(column, (rows, TILE))


def step_sizes(raw, heads):
    shifted = raw + heads[0:1]
    return jnp.maximum(shifted, 0.0) + jnp.log1p(jnp.exp(-jnp.abs(shifted)))


def conv_taps(ext, same, start, width, rows=SPAN):
    out = [ext[8 : 8 + rows, start : start + width]]
    for offset in (1, 2, 3):
        moved = ext[8 - offset : 8 - offset + rows, start : start + width]
        mask = same[offset - 1]
        if width > TILE:
            mask = jnp.concatenate([mask] * (width // TILE), axis=1)
        out.append(moved * mask)
    return out


def conv_sum(taps, weights):
    total = weights[4:5] + weights[3:4] * taps[0]
    for offset in (1, 2, 3):
        total = total + weights[3 - offset : 4 - offset] * taps[offset]
    return total


def prepare(raw_ref, heads_ref, aux_ref, same):
    aux = aux_ref[...]
    heads = heads_ref[...]
    step = step_sizes(raw_ref[...], heads)
    row = lax.broadcasted_iota(jnp.int32, (SPAN, SPAN), 0)
    col = lax.broadcasted_iota(jnp.int32, (SPAN, SPAN), 1)
    tri = (row >= col).astype(F32)
    cum = dot_f32(tri, step * heads[1:2], ((1,), (0,)), HIGHEST)
    for place in range(5):
        same[place] = lanes_of(aux[:, place : place + 1], SPAN)
    return step, cum, cum - jnp.log2(step)


def pick(first, columns, at):
    return jnp.where(first, lanes_of(columns[:, at : at + 1], first.shape[0]), lanes_of(columns[:, at + 1 : at + 2], first.shape[0]))


def forward_kernel(first_call, base, pc_ref, halo_ref, raw_ref, cw_ref, aux_ref, seg_ref, heads_ref, skip_ref, *rest):
    rest = list(rest)
    if first_call:
        bc_ref, bc_halo_ref, bcw_ref = [rest.pop(0) for _ in range(3)]
        x_out, y_out, st_out, slope_out, mark, bc_out, bc_slope_out = [rest.pop(0) for _ in range(7)]
    else:
        bc_out = rest.pop(0)
        mark_ref = rest[4]
        rest = rest[5:]
        x_out, y_out, st_out, slope_out, mark = [rest.pop(0) for _ in range(5)]
    state, scores, block, same, pack, cum_rows, w_rows, keep_row, b_t, ext, ext_bc = rest
    span = pl.program_id(0)
    group = pl.program_id(1)
    group_head = base + GROUP * group

    @pl.when((span == 0) & (group == 0))
    def _():
        state[...] = jnp.zeros_like(state)
        mark[...] = jnp.zeros_like(mark) if first_call else mark_ref[...]

    @pl.when(group == 0)
    def _():
        step, cum, shifted = prepare(raw_ref, heads_ref, aux_ref, same)
        last = cum[SPAN - 1 : SPAN]
        pack[...] = cum
        cum_rows[...] = shifted.T
        w_rows[...] = (jnp.exp2(last - shifted) * same[4]).T
        keep_row[...] = jnp.broadcast_to(jnp.exp2(last) * same[3, SPAN - 1 : SPAN], (8, TILE))
        if first_call:
            ext_bc[0:8] = bc_halo_ref[...]
            ext_bc[8:] = bc_ref[...]
            total = conv_sum(conv_taps(ext_bc, same, 0, 2 * N), bcw_ref[...])
            gate = jax.nn.sigmoid(total)
            both = total * gate
            bc_out[...] = both.astype(BF16)
            bc_slope_out[...] = (gate + both * (1.0 - gate)).astype(BF16)
        row = lax.broadcasted_iota(jnp.int32, (SPAN, SPAN), 0)
        col = lax.broadcasted_iota(jnp.int32, (SPAN, SPAN), 1)
        linked = (row >= col) & (aux_ref[:, 5:6] == seg_ref[...])
        block[...] = jnp.where(linked, 0.0, NEG)
        scores[...] = mm_nt(bc_out[:, N:], bc_out[:, :N])
        b_t[...] = bc_out[:, :N].astype(F32).T

    ext[0:8] = halo_ref[...]
    ext[8:] = pc_ref[...]
    shift = lax.rem(TILE - group_head, TILE)
    cums = pltpu.roll(pack[...], shift, 1)
    keep = jnp.broadcast_to(pltpu.roll(keep_row[...], shift, 1)[0:1], (N, TILE))
    first = lax.broadcasted_iota(jnp.int32, (SPAN, TILE), 1) < P_SIZE
    query = bc_out[:, N:]
    empty = jnp.zeros((HALF, HALF), BF16)
    wide = lambda parts: jnp.concatenate(parts, axis=1)
    for quad in range(GROUP // 4):
        xbs, outs, entries, keeps, fresh = [], [], [], [], []
        for pair in (2 * quad, 2 * quad + 1):
            at = pair * TILE
            total = conv_sum(conv_taps(ext, same, at, TILE), cw_ref[:, at : at + TILE])
            gate = jax.nn.sigmoid(total)
            x = total * gate
            xb = x.astype(BF16)
            x_out[:, at : at + TILE] = xb
            slope_out[:, at : at + TILE] = (gate + x * (1.0 - gate)).astype(BF16)
            mixes, weighted, cum_cols = [], [], []
            for head in (2 * pair, 2 * pair + 1):
                cum_col = lanes_of(cums[:, head : head + 1], SPAN)
                cum_cols.append(cum_col)
                cum_row = cum_rows[pl.ds(group_head + head, 1), :]
                blocks = []
                for i, j in ((0, 0), (1, 0), (1, 1)):
                    rows = slice(i * HALF, (i + 1) * HALF)
                    cols = slice(j * HALF, (j + 1) * HALF)
                    gap = cum_col[rows] - cum_row[:, cols] + block[rows, cols]
                    blocks.append((jnp.exp2(gap) * scores[rows, cols]).astype(BF16))
                mixes.append(wide([blocks[0], empty]))
                mixes.append(wide(blocks[1:]))
                weighted.append((b_t[...] * w_rows[pl.ds(group_head + head, 1), :]).astype(BF16))
            inner = mm(jnp.concatenate(mixes + weighted, axis=0), xb)
            outs.append(jnp.where(first, inner[:SPAN], inner[SPAN : 2 * SPAN]))
            fresh.append(jnp.where(first[:N], inner[2 * SPAN : 2 * SPAN + N], inner[2 * SPAN + N :]))
            xbs.append(xb)
            entries.append(jnp.exp2(jnp.where(first, cum_cols[0], cum_cols[1])) * same[3])
            keeps.append(pick(first[:N], keep, 2 * pair))
        both = slice(quad * 2 * TILE, (quad + 1) * 2 * TILE)
        tile = pl.ds(pl.multiple_of(group * GROUP * P_SIZE + quad * 2 * TILE, 2 * TILE), 2 * TILE)
        old = state[:, tile]
        old_b = old.astype(BF16)
        st_out[:, both] = old_b
        carried = mm(query, old_b)
        y_out[:, both] = wide(outs) + wide(entries) * carried + skip_ref[:, both] * wide(xbs).astype(F32)
        state[:, tile] = old * wide(keeps) + wide(fresh)


def run_forward(pc, first_x, pc_bc, conv_x, conv_bc, aux, seg_row, heads, skip, start, count, bcv, before):
    tokens = pc.shape[0]
    spans = tokens // SPAN
    di = skip.shape[1]
    width = GROUP * P_SIZE
    own = count * width
    first_call = before is None
    any_spec = pl.BlockSpec(memory_space=pl.ANY)
    halo = lambda s: jnp.maximum(s * (SPAN // 8) - 1, 0)
    wide = pl.BlockSpec((SPAN, width), lambda s, g: (s, start + g))
    bcv_spec = pl.BlockSpec((SPAN, 2 * N), lambda s, g: (s, 0))
    in_specs = [
        pl.BlockSpec((SPAN, width), lambda s, g: (s, first_x + g)),
        pl.BlockSpec((8, width), lambda s, g: (halo(s), first_x + g)),
        pl.BlockSpec((SPAN, TILE), lambda s, g: (s, 2)),
        pl.BlockSpec((8, width), lambda s, g: (0, start + g)),
        pl.BlockSpec((SPAN, 8), lambda s, g: (s, 0)),
        pl.BlockSpec((1, SPAN), lambda s, g: (0, s)),
        pl.BlockSpec((8, TILE), lambda s, g: (0, 0)),
        pl.BlockSpec((1, width), lambda s, g: (0, start + g)),
    ]
    args = [pc, pc, pc_bc, conv_x, aux, seg_row, heads, skip]
    mark_spec = pl.BlockSpec((8, TILE), lambda s, g: (0, 0))
    out_specs = [wide, wide, pl.BlockSpec((N, width), lambda s, g: (s, start + g)), wide, mark_spec]
    out_shape = [
        jax.ShapeDtypeStruct((tokens, di), BF16),
        jax.ShapeDtypeStruct((tokens, di), F32),
        jax.ShapeDtypeStruct((spans * N, di), BF16),
        jax.ShapeDtypeStruct((tokens, di), BF16),
        jax.ShapeDtypeStruct((8, TILE), F32),
    ]
    if first_call:
        in_specs += [
            pl.BlockSpec((SPAN, 2 * N), lambda s, g: (s, 0)),
            pl.BlockSpec((8, 2 * N), lambda s, g: (halo(s), 0)),
            pl.BlockSpec((8, 2 * N), lambda s, g: (0, 0)),
        ]
        args += [pc_bc, pc_bc, conv_bc]
        out_specs += [bcv_spec, bcv_spec]
        out_shape += [jax.ShapeDtypeStruct((tokens, 2 * N), BF16)] * 2
        aliases = {}
    else:
        in_specs += [bcv_spec, any_spec, any_spec, any_spec, any_spec, mark_spec]
        args += [bcv, *before]
        aliases = {9: 0, 10: 1, 11: 2, 12: 3}
    return pl.pallas_call(
        functools.partial(forward_kernel, first_call, start * GROUP),
        grid_spec=pltpu.PrefetchScalarGridSpec(
            num_scalar_prefetch=0,
            grid=(spans, count),
            in_specs=in_specs,
            out_specs=out_specs,
            scratch_shapes=[
                pltpu.VMEM((N, own), F32),
                pltpu.VMEM((SPAN, SPAN), F32),
                pltpu.VMEM((SPAN, SPAN), F32),
                pltpu.VMEM((5, SPAN, TILE), F32),
                pltpu.VMEM((SPAN, TILE), F32),
                pltpu.VMEM((TILE, SPAN), F32),
                pltpu.VMEM((TILE, SPAN), F32),
                pltpu.VMEM((8, TILE), F32),
                pltpu.VMEM((N, SPAN), F32),
                pltpu.VMEM((SPAN + 8, width), F32),
                pltpu.VMEM((SPAN + 8, 2 * N), F32),
            ],
        ),
        out_shape=out_shape,
        input_output_aliases=aliases,
        compiler_params=pltpu.CompilerParams(dimension_semantics=("arbitrary", "arbitrary")),
        cost_estimate=pl.CostEstimate(flops=int(5e9 * count), bytes_accessed=14 * tokens * own, transcendentals=0),
        name="scan_forward",
    )(*args)


def conv_back(grad, slope, signal, same, weights, carry):
    width = grad.shape[1]
    du = grad * slope.astype(F32)

    def add_rows(values):
        return jnp.sum(values.reshape(SPAN // 8, 8, width), axis=0)

    out = weights[3:4] * du
    sums = [add_rows(du), add_rows(du * signal)]
    for offset in (1, 2, 3):
        mask = same[offset - 1]
        if width > TILE:
            mask = jnp.concatenate([mask] * (width // TILE), axis=1)
        masked = du * mask
        moved = jnp.concatenate([masked, carry[offset - 1]], axis=0)[offset : offset + SPAN]
        carry[offset - 1] = masked[0:8]
        out = out + weights[3 - offset : 4 - offset] * moved
        sums.append(add_rows(moved * signal))
    return out, sums


def backward_kernel(
    first_call, last_call, base,
    dy_ref, x_ref, bcv_ref, st_ref, slope_ref, pc_ref, raw_ref, cw_ref, aux_ref, seg_ref, heads_ref, skip_ref, *rest,
):
    rest = list(rest)
    before = None if first_call else [rest.pop(0) for _ in range(4)]
    if last_call:
        bc_ref, bc_slope_ref, bcw_ref = [rest.pop(0) for _ in range(3)]
    dproj_out, dcw_out, dskip_out = [rest.pop(0) for _ in range(3)]
    if last_call:
        dbcw_out, dhead_out = [rest.pop(0) for _ in range(2)]
    else:
        after_out = [rest.pop(0) for _ in range(4)]
    (
        dstate, scores, block, dscores, same, pack, last_row, cum_rows, c_t,
        carry, carry_bc, d_bc, per_row, dcum_rows, dlast,
    ) = rest
    back = pl.program_id(0)
    group = pl.program_id(1)
    groups = pl.num_programs(1)
    width = GROUP * P_SIZE
    group_head = base + GROUP * group
    first_x = 4 * N if last_call else 0

    @pl.when((back == 0) & (group == 0))
    def _():
        dstate[...] = jnp.zeros_like(dstate)
        carry[...] = jnp.zeros_like(carry)
        dcw_out[...] = jnp.zeros_like(dcw_out)
        dskip_out[...] = jnp.zeros_like(dskip_out)
        dcum_rows[...] = jnp.zeros_like(dcum_rows)
        if last_call:
            carry_bc[...] = jnp.zeros_like(carry_bc)
            dbcw_out[...] = jnp.zeros_like(dbcw_out)
            dhead_out[...] = jnp.zeros_like(dhead_out)

    keys = bcv_ref[:, :N]
    query = bcv_ref[:, N:]
    lane = lax.broadcasted_iota(jnp.int32, (SPAN, TILE), 1)

    @pl.when(group == 0)
    def _():
        step, cum, shifted = prepare(raw_ref, heads_ref, aux_ref, same)
        entry = jnp.exp2(cum) * same[3]
        pack[...] = jnp.where(lane < 64, shifted, pltpu.roll(entry, 64, 1))
        last_row[...] = jnp.broadcast_to(cum[SPAN - 1 : SPAN], (8, TILE))
        cum_rows[...] = cum.T
        row = lax.broadcasted_iota(jnp.int32, (SPAN, SPAN), 0)
        col = lax.broadcasted_iota(jnp.int32, (SPAN, SPAN), 1)
        linked = (row <= col) & (aux_ref[:, 5:6] == seg_ref[...])
        block[...] = jnp.where(linked, 0.0, NEG)
        scores[...] = mm_nt(keys, query)
        c_t[...] = query.T
        per_row[...] = jnp.zeros_like(per_row)
        if first_call:
            dscores[...] = jnp.zeros_like(dscores)
            d_bc[...] = jnp.zeros_like(d_bc)
            dlast[...] = jnp.zeros_like(dlast)
        else:
            dscores[...] = before[0][...]
            d_bc[...] = before[1][...]
            per_row[0] = before[2][:, :TILE]
            per_row[2] = before[2][:, TILE:]
            dlast[...] = before[3][...]

    shift = lax.rem(TILE - group_head, TILE)
    cols = pltpu.roll(pack[...], shift, 1)
    last_cum = pltpu.roll(last_row[...], shift, 1)[0:1]
    keep_mask = same[3, SPAN - 1 : SPAN]
    first = lane < P_SIZE
    lane_row = lax.broadcasted_iota(jnp.int32, (2 * TILE, TILE), 0) // P_SIZE
    lane_col = lax.broadcasted_iota(jnp.int32, (2 * TILE, TILE), 1)
    sums = jnp.zeros((SPAN, TILE), F32)
    last_sum = jnp.zeros((1, TILE), F32)
    group_at = group * width
    empty = jnp.zeros((HALF, HALF), BF16)
    wide = lambda parts: jnp.concatenate(parts, axis=1)
    for quad in range(GROUP // 4):
        both = slice(quad * 2 * TILE, (quad + 1) * 2 * TILE)
        tile = pl.ds(pl.multiple_of(group_at + quad * 2 * TILE, 2 * TILE), 2 * TILE)
        entries, tails, keeps, inners = [], [], [], []
        for pair in (2 * quad, 2 * quad + 1):
            at = pair * TILE
            heads = (2 * pair, 2 * pair + 1)
            dy_pair = dy_ref[:, at : at + TILE]
            xb = x_ref[:, at : at + TILE]
            nothing = jnp.zeros_like(xb)
            split = jnp.concatenate([jnp.where(first, xb, nothing), jnp.where(first, nothing, xb)], axis=0)
            g_both = mm_nt(split, dy_pair)
            cum_cols = [lanes_of(cols[:, head : head + 1], SPAN) for head in heads]
            cum_lines = [cum_rows[pl.ds(group_head + head, 1), :] for head in heads]
            mixes = [[], []]
            across = [[], []]
            down = [[], []]
            for j, i in ((0, 0), (0, 1), (1, 1)):
                rows = slice(j * HALF, (j + 1) * HALF)
                cells = slice(i * HALF, (i + 1) * HALF)
                spread = jnp.zeros((HALF, HALF), F32)
                for which in (0, 1):
                    decay = jnp.exp2(cum_lines[which][:, cells] - cum_cols[which][rows] + block[rows, cells])
                    mix = decay * scores[rows, cells]
                    g = g_both[which * SPAN + j * HALF : which * SPAN + (j + 1) * HALF, cells]
                    spread = spread + decay * g
                    w = mix * g
                    mixes[which].append(mix.astype(BF16))
                    across[which].append(w)
                    down[which].append(jnp.sum(w, axis=0, keepdims=True))
                dscores[rows, cells] += spread
            lefts = []
            for which in (0, 1):
                row_sum = jnp.concatenate(
                    [
                        jnp.sum(across[which][0] + across[which][1], axis=1, keepdims=True),
                        jnp.sum(across[which][2], axis=1, keepdims=True),
                    ],
                    axis=0,
                )
                sums = sums - jnp.where(lane == 2 * GROUP + heads[which], row_sum, 0.0)
                dcum_rows[pl.ds(group_head + heads[which], 1), :] = wide(
                    [down[which][0], down[which][1] + down[which][2]]
                )
                lefts += [wide(mixes[which][:2]), wide([empty, mixes[which][2]])]
            inner = mm(jnp.concatenate(lefts, axis=0), dy_pair)
            inners.append(jnp.where(first, inner[:SPAN], inner[SPAN:]))
            last_pair = jnp.where(
                first[0:1],
                jnp.broadcast_to(last_cum[:, heads[0] : heads[0] + 1], (1, TILE)),
                jnp.broadcast_to(last_cum[:, heads[1] : heads[1] + 1], (1, TILE)),
            )
            tails.append(jnp.exp2(last_pair - jnp.where(first, cum_cols[0], cum_cols[1])) * same[4])
            keeps.append(jnp.exp2(last_pair) * keep_mask)
            entries.append(pick(first, cols, 64 + 2 * pair))
        dyf = dy_ref[:, both].astype(F32)
        xf = x_ref[:, both].astype(F32)
        tail = wide(tails)
        stb = st_ref[:, both]
        ds = dstate[:, tile]
        dsb = ds.astype(BF16)
        dye_f = dyf * wide(entries)
        dye = dye_f.astype(BF16)
        fresh = mm(keys, dsb) * tail
        total = wide(inners) + fresh
        d_bc[:, N:] += mm_nt(dye, stb)
        d_bc[:, :N] += mm_nt((xf * tail).astype(BF16), dsb)

        def head_sum(values, kind):
            spread = (lane_col == kind * GROUP + 4 * quad + lane_row).astype(BF16)
            return mm(values.astype(BF16), spread)

        sums = sums + head_sum(xf * total, 0) + head_sum(xf * fresh, 1) + head_sum(dye_f * mm(query, stb), 2)
        kept = ds * wide(keeps)
        kept_sum = jnp.sum(kept * stb.astype(F32), axis=0, keepdims=True)
        lane_pair = lax.broadcasted_iota(jnp.int32, (1, 2 * TILE), 1) // P_SIZE
        for head in range(4):
            one = jnp.sum(jnp.where(lane_pair == head, kept_sum, 0.0), axis=1, keepdims=True)
            last_sum = last_sum + jnp.where(lane[0:1] == 4 * quad + head, one, 0.0)
        dstate[:, tile] = kept + mm(c_t[...], dye)
        dskip_out[:, tile] += jnp.sum((dyf * xf).reshape(SPAN // 8, 8, 2 * TILE), axis=0)
        dx = total + skip_ref[:, both] * dyf
        for part in (0, 1):
            at = (2 * quad + part) * TILE
            one = pl.ds(pl.multiple_of(group_at + at, TILE), TILE)
            out, conv_sums = conv_back(
                dx[:, part * TILE : (part + 1) * TILE], slope_ref[:, at : at + TILE], pc_ref[:, at : at + TILE],
                same, cw_ref[:, at : at + TILE], carry.at[:, :, one],
            )
            dproj_out[:, pl.ds(pl.multiple_of(first_x + group_at + at, TILE), TILE)] = out.astype(BF16)
            for k, value in enumerate(conv_sums):
                dcw_out[k, :, one] += value

    in_place = (lane >= group_head) & (lane < group_head + GROUP)
    for kind in range(3):
        moved = pltpu.roll(sums, lax.rem(group_head + TILE - GROUP * kind, TILE), 1)
        per_row[kind] += jnp.where(in_place, moved, 0.0)
    moved = pltpu.roll(jnp.broadcast_to(last_sum, (8, TILE)), group_head, 1)
    dlast[...] += jnp.where(in_place[0:8], moved, 0.0)

    @pl.when(group == groups - 1)
    def _():
        state_part = per_row[1]
        dcum = dcum_rows[...].T + per_row[2] - state_part
        dlast_all = dlast[0:1] + jnp.sum(state_part, axis=0, keepdims=True)
        if not last_call:
            after_out[0][...] = dscores[...]
            after_out[1][...] = d_bc[...]
            after_out[2][:, :TILE] = per_row[0]
            after_out[2][:, TILE:] = dcum
            after_out[3][...] = jnp.broadcast_to(dlast_all, (8, TILE))
            return
        ds_b = dscores[...].astype(BF16)
        grad_b = d_bc[:, :N] + mm(ds_b, query)
        grad_c = d_bc[:, N:] + mm(dscores[...].T.astype(BF16), keys)
        out, conv_sums = conv_back(
            wide([grad_b, grad_c]), bc_slope_ref[...], bc_ref[...], same, bcw_ref[...], carry_bc
        )
        dproj_out[:, : 2 * N] = out.astype(BF16)
        for k, value in enumerate(conv_sums):
            dbcw_out[k] += value
        heads = heads_ref[...]
        shifted = raw_ref[...] + heads[0:1]
        step = step_sizes(raw_ref[...], heads)
        slope = jax.nn.sigmoid(shifted)
        row = lax.broadcasted_iota(jnp.int32, (SPAN, SPAN), 0)
        col = lax.broadcasted_iota(jnp.int32, (SPAN, SPAN), 1)
        tri = (row <= col).astype(F32)
        da = dot_f32(tri, dcum, ((1,), (0,)), HIGHEST) + dlast_all
        small = shifted < -16.0
        ratio = jnp.where(small, 1.0, slope / jnp.where(small, 1.0, step))
        live = lane < H
        draw = jnp.where(live, per_row[0] * ratio + da * heads[2:3] * slope, 0.0)
        dproj_out[:, 2 * N : 3 * N] = draw.astype(BF16)
        dproj_out[:, 3 * N : 4 * N] = jnp.zeros((SPAN, N), BF16)
        dhead_out[0] += jnp.sum(draw.reshape(SPAN // 8, 8, TILE), axis=0)
        dhead_out[1] += jnp.sum(jnp.where(live, da * step, 0.0).reshape(SPAN // 8, 8, TILE), axis=0)


def run_backward(
    dy, x, bcv, states, slope, bc_slope, pc, first_x, pc_bc, conv_x, conv_bc, aux, seg_row, heads, skip, start, count, last, before
):
    tokens, di = dy.shape
    spans = tokens // SPAN
    width = GROUP * P_SIZE
    turn = lambda s: spans - 1 - s
    own = count * width
    out_width = own + (4 * N if last else 0)
    sums_specs = [
        pl.BlockSpec((SPAN, SPAN), lambda s, g: (turn(s), 0)),
        pl.BlockSpec((SPAN, 2 * N), lambda s, g: (turn(s), 0)),
        pl.BlockSpec((SPAN, 2 * TILE), lambda s, g: (turn(s), 0)),
        pl.BlockSpec((8, TILE), lambda s, g: (turn(s), 0)),
    ]
    sums_shapes = [
        jax.ShapeDtypeStruct((tokens, SPAN), F32),
        jax.ShapeDtypeStruct((tokens, 2 * N), F32),
        jax.ShapeDtypeStruct((tokens, 2 * TILE), F32),
        jax.ShapeDtypeStruct((spans * 8, TILE), F32),
    ]
    out_specs = [
        pl.BlockSpec((SPAN, out_width), lambda s, g: (turn(s), 0)),
        pl.BlockSpec((5, 8, own), lambda s, g: (0, 0, 0)),
        pl.BlockSpec((8, own), lambda s, g: (0, 0)),
    ]
    out_shape = [
        jax.ShapeDtypeStruct((tokens, out_width), BF16),
        jax.ShapeDtypeStruct((5, 8, own), F32),
        jax.ShapeDtypeStruct((8, own), F32),
    ]
    wide = pl.BlockSpec((SPAN, width), lambda s, g: (turn(s), start + g))
    in_specs = [
        wide,
        wide,
        pl.BlockSpec((SPAN, 2 * N), lambda s, g: (turn(s), 0)),
        pl.BlockSpec((N, width), lambda s, g: (turn(s), start + g)),
        wide,
        pl.BlockSpec((SPAN, width), lambda s, g: (turn(s), first_x + g)),
        pl.BlockSpec((SPAN, TILE), lambda s, g: (turn(s), 2)),
        pl.BlockSpec((8, width), lambda s, g: (0, start + g)),
        pl.BlockSpec((SPAN, 8), lambda s, g: (turn(s), 0)),
        pl.BlockSpec((1, SPAN), lambda s, g: (0, turn(s))),
        pl.BlockSpec((8, TILE), lambda s, g: (0, 0)),
        pl.BlockSpec((1, width), lambda s, g: (0, start + g)),
    ]
    args = [dy, x, bcv, states, slope, pc, pc_bc, conv_x, aux, seg_row, heads, skip]
    if before is not None:
        in_specs += sums_specs
        args += before
    if last:
        in_specs += [
            pl.BlockSpec((SPAN, 2 * N), lambda s, g: (turn(s), 0)),
            pl.BlockSpec((SPAN, 2 * N), lambda s, g: (turn(s), 0)),
            pl.BlockSpec((8, 2 * N), lambda s, g: (0, 0)),
        ]
        args += [pc_bc, bc_slope, conv_bc]
        out_specs += [
            pl.BlockSpec((5, 8, 2 * N), lambda s, g: (0, 0, 0)),
            pl.BlockSpec((2, 8, TILE), lambda s, g: (0, 0, 0)),
        ]
        out_shape += [
            jax.ShapeDtypeStruct((5, 8, 2 * N), F32),
            jax.ShapeDtypeStruct((2, 8, TILE), F32),
        ]
    else:
        out_specs += sums_specs
        out_shape += sums_shapes
    return pl.pallas_call(
        functools.partial(backward_kernel, before is None, last, start * GROUP),
        grid_spec=pltpu.PrefetchScalarGridSpec(
            num_scalar_prefetch=0,
            grid=(spans, count),
            in_specs=in_specs,
            out_specs=out_specs,
            scratch_shapes=[
                pltpu.VMEM((N, own), F32),
                pltpu.VMEM((SPAN, SPAN), F32),
                pltpu.VMEM((SPAN, SPAN), F32),
                pltpu.VMEM((SPAN, SPAN), F32),
                pltpu.VMEM((5, SPAN, TILE), F32),
                pltpu.VMEM((SPAN, TILE), F32),
                pltpu.VMEM((8, TILE), F32),
                pltpu.VMEM((TILE, SPAN), F32),
                pltpu.VMEM((N, SPAN), BF16),
                pltpu.VMEM((3, 8, own), F32),
                pltpu.VMEM((3, 8, 2 * N), F32),
                pltpu.VMEM((SPAN, 2 * N), F32),
                pltpu.VMEM((3, SPAN, TILE), F32),
                pltpu.VMEM((TILE, SPAN), F32),
                pltpu.VMEM((8, TILE), F32),
            ],
        ),
        out_shape=out_shape,
        compiler_params=pltpu.CompilerParams(dimension_semantics=("arbitrary", "arbitrary")),
        cost_estimate=pl.CostEstimate(
            flops=int(1.2e10 * count), bytes_accessed=12 * tokens * own, transcendentals=0
        ),
        name="scan_backward",
    )(*args)


def seg_facts(seg):
    length = seg.shape[0]
    cols = []
    for offset in (1, 2, 3):
        moved = jnp.concatenate([jnp.full((offset,), -1, jnp.int32), seg[:-offset]])
        cols.append((moved == seg).astype(F32))
    spans = length // SPAN
    ends = seg[SPAN - 1 :: SPAN]
    before = jnp.concatenate([seg[:1], ends[:-1]])
    cols.append((seg == jnp.repeat(before, SPAN)).astype(F32))
    cols.append((seg == jnp.repeat(ends, SPAN)).astype(F32))
    value = seg.astype(F32)
    cols.append(value)
    cols.append(value)
    cols.append(value)
    return jnp.stack(cols, axis=1), value[None, :]


def head_rows(dt_bias, a_log):
    rate = -jnp.exp(a_log)
    rows = jnp.stack([dt_bias, rate * LOG2E, rate] + [jnp.zeros_like(rate)] * 5, axis=0)
    return jnp.pad(rows, ((0, 0), (0, TILE - H)))


BLOCKS = 32
ORDERS = ((8, 1, 4, 2), (8, 2, 4, 1))


def reach(masks):
    out = [0]
    for mask in masks:
        out = out + [mask ^ place for place in out]
    return out


def exchange(values, stage):
    pairs = []
    for shard in range(16):
        for core in range(2):
            pairs.append((shard * 2 + core, (shard ^ ORDERS[core][stage]) * 2 + core))
    return lax.ppermute(values, ("shard", "rep"), pairs)


def swap_cores(values):
    return lax.ppermute(values, "rep", [(0, 1), (1, 0)])


def after(values, *others):
    return lax.optimization_barrier((values, *others))[0]


class Gather:
    def __init__(self, local):
        self.held = local
        self.seen = []
        self.swapped = []

    def step(self, *ahead):
        stage = len(self.seen)
        send = after(self.held, *ahead)
        got = exchange(send, stage)
        self.seen.append(got)
        if stage < 3:
            self.held = jnp.concatenate([send, got], axis=0)
        return send, got

    def swap(self, *ahead):
        send = after(self.held if not self.swapped else self.seen[3], *ahead)
        self.swapped.append(swap_cores(send))
        return send, self.swapped[-1]

    def pieces(self):
        return self.held, self.seen[3], *self.swapped


def gather_small(local):
    held = local[None]
    ahead = yield None
    for stage in range(4):
        send = after(held, *ahead)
        got = exchange(send, stage)
        ahead = yield send, got
        held = jnp.concatenate([send, got], axis=0)
    core = lax.axis_index("rep")
    places = jnp.asarray([reach(order) for order in ORDERS], jnp.int32)[core] ^ lax.axis_index("shard")
    hot = (places[None, :] == jnp.arange(16, dtype=jnp.int32)[:, None]).astype(local.dtype)
    yield dot_f32(hot, held, ((1,), (0,)), HIGHEST).astype(local.dtype)


class Scatter:
    def __init__(self, partial, block):
        mine, self.other = partial
        self.terms = [mine]
        self.block = block
        self.left = [3, 2, 1, 0]

    def rows(self, start, stop):
        total = self.terms[0][start:stop].astype(F32)
        for term in self.terms[1:]:
            total = total + term[start:stop].astype(F32)
        return total

    def step(self, *ahead):
        if len(self.terms) == 1:
            send = after(self.other, *ahead)
            self.terms.append(swap_cores(send))
            return send, self.terms[-1]
        if self.left:
            stage = self.left.pop(0)
            cut = self.block << stage
            send = after(self.rows(cut, 2 * cut).astype(BF16), *ahead)
            self.terms.append(exchange(send, stage))
            return send, self.terms[-1]
        return self.terms[-1], self.terms[-1]

    def finish(self):
        while self.left:
            self.step()
        return self.rows(0, self.block)


def block_order(core):
    shard = lax.axis_index("shard")
    tables = jnp.asarray([reach(order) for order in ORDERS], jnp.int32)
    inverse = jnp.asarray(
        [[reach(order).index(mask) for mask in range(16)] for order in ORDERS], jnp.int32
    )
    own = 2 * (tables[core] ^ shard) + core
    partner = 2 * (tables[1 - core] ^ shard) + (1 - core)
    order = jnp.concatenate([own, partner])
    natural = jnp.arange(BLOCKS, dtype=jnp.int32)
    which = natural % 2
    place = inverse[which, (natural // 2) ^ shard] + 16 * (which != core).astype(jnp.int32)
    return order, place


def fetch_tile(order_ref, pieces, buffer, sems, tile, slot, block, width):
    for q in range(BLOCKS):
        pltpu.make_async_copy(
            pieces[q // 8].at[pl.ds((q % 8) * block, block), pl.ds(pl.multiple_of(tile * width, width), width)],
            buffer.at[slot, pl.ds(pl.multiple_of(order_ref[q] * block, block), block), :],
            sems.at[slot],
        ).start()


def next_tile(order_ref, pieces, buffer, sems, block, width):
    tile = pl.program_id(0)
    slot = lax.rem(tile, 2)

    @pl.when(tile == 0)
    def _():
        fetch_tile(order_ref, pieces, buffer, sems, tile, slot, block, width)

    @pl.when(tile + 1 < pl.num_programs(0))
    def _():
        fetch_tile(order_ref, pieces, buffer, sems, tile + 1, 1 - slot, block, width)

    pltpu.make_async_copy(buffer.at[slot], buffer.at[slot], sems.at[slot]).wait()
    return slot


def project_kernel(block, width, order_ref, x_ref, p0, p1, p2, p3, *rest):
    out_ref, w_ref, buffer, sems = rest[-4:]
    slot = next_tile(order_ref, (p0, p1, p2, p3), buffer, sems, block, width)
    w = buffer[slot]
    w_ref[...] = w
    for i in range(x_ref.shape[0] // SPAN):
        rows = slice(i * SPAN, (i + 1) * SPAN)
        out_ref[rows] = mm(x_ref[rows], w)


def project(x, pieces, order, so_far, start, full, width=512):
    tokens, depth = x.shape
    columns = pieces[0].shape[1]
    block = depth // BLOCKS
    at = start // width
    any_spec = pl.BlockSpec(memory_space=pl.ANY)
    extra = [] if so_far is None else list(so_far)
    return pl.pallas_call(
        functools.partial(project_kernel, block, width),
        grid_spec=pltpu.PrefetchScalarGridSpec(
            num_scalar_prefetch=1,
            grid=(columns // width,),
            in_specs=[pl.BlockSpec((tokens, depth), lambda j, o: (0, 0))] + [any_spec] * (4 + len(extra)),
            out_specs=[
                pl.BlockSpec((tokens, width), lambda j, o: (0, at + j)),
                pl.BlockSpec((depth, width), lambda j, o: (0, at + j)),
            ],
            scratch_shapes=[pltpu.VMEM((2, depth, width), BF16), pltpu.SemaphoreType.DMA((2,))],
        ),
        out_shape=[jax.ShapeDtypeStruct((tokens, full), F32), jax.ShapeDtypeStruct((depth, full), BF16)],
        input_output_aliases={} if so_far is None else {6: 0, 7: 1},
        cost_estimate=pl.CostEstimate(
            flops=2 * tokens * depth * columns,
            bytes_accessed=4 * depth * columns + 4 * tokens * columns + 2 * tokens * depth,
            transcendentals=0,
        ),
        name="project",
    )(order, x, *pieces, *extra)


def gate_kernel(block, width, order_ref, x_ref, p0, p1, p2, p3, y_ref, gain_ref, *rest):
    gate_ref, w_ref, zg_ref, square_ref, buffer, sems = rest[-6:]
    slot = next_tile(order_ref, (p0, p1, p2, p3), buffer, sems, block, width)
    w = buffer[slot]
    w_ref[...] = w

    @pl.when(pl.program_id(0) == 0)
    def _():
        square_ref[...] = jnp.zeros_like(square_ref)

    for i in range(x_ref.shape[0] // SPAN):
        rows = slice(i * SPAN, (i + 1) * SPAN)
        gate = mm(x_ref[rows], w)
        gate_ref[rows] = gate
        gated = y_ref[rows] * (gate * jax.nn.sigmoid(gate))
        zg_ref[rows] = (gated * gain_ref[...]).astype(BF16)
        square = gated * gated
        total = square[:, :TILE]
        for k in range(1, width // TILE):
            total = total + square[:, k * TILE : (k + 1) * TILE]
        square_ref[rows] += total


def gate_project(x, pieces, order, y, gain, so_far, start, full, width=512):
    tokens, depth = x.shape
    columns = pieces[0].shape[1]
    block = depth // BLOCKS
    at = start // width
    any_spec = pl.BlockSpec(memory_space=pl.ANY)
    extra = [] if so_far is None else list(so_far)
    wide = pl.BlockSpec((tokens, width), lambda j, o: (0, at + j))
    return pl.pallas_call(
        functools.partial(gate_kernel, block, width),
        grid_spec=pltpu.PrefetchScalarGridSpec(
            num_scalar_prefetch=1,
            grid=(columns // width,),
            in_specs=[pl.BlockSpec((tokens, depth), lambda j, o: (0, 0))]
            + [any_spec] * 4
            + [wide, pl.BlockSpec((1, width), lambda j, o: (0, at + j))]
            + [any_spec] * len(extra),
            out_specs=[
                wide,
                pl.BlockSpec((depth, width), lambda j, o: (0, at + j)),
                wide,
                pl.BlockSpec((tokens, TILE), lambda j, o: (0, 0)),
            ],
            scratch_shapes=[pltpu.VMEM((2, depth, width), BF16), pltpu.SemaphoreType.DMA((2,))],
        ),
        out_shape=[
            jax.ShapeDtypeStruct((tokens, full), F32),
            jax.ShapeDtypeStruct((depth, full), BF16),
            jax.ShapeDtypeStruct((tokens, full), BF16),
            jax.ShapeDtypeStruct((tokens, TILE), F32),
        ],
        input_output_aliases={} if so_far is None else {8: 0, 9: 1, 10: 2},
        cost_estimate=pl.CostEstimate(
            flops=2 * tokens * depth * columns,
            bytes_accessed=4 * depth * columns + 10 * tokens * columns + 2 * tokens * depth,
            transcendentals=tokens * columns,
        ),
        name="project_gate",
    )(order, x, *pieces, y, gain, *extra)


def restore_kernel(block, width, order_ref, p0, p1, p2, p3, *rest):
    w_ref, buffer, sems = rest[-3:]
    slot = next_tile(order_ref, (p0, p1, p2, p3), buffer, sems, block, width)
    w_ref[...] = buffer[slot]


def restore(pieces, order, so_far, start, full, width=256):
    columns = pieces[0].shape[1]
    block = pieces[0].shape[0] // 8
    depth = block * BLOCKS
    at = start // width
    any_spec = pl.BlockSpec(memory_space=pl.ANY)
    extra = [] if so_far is None else [so_far]
    return pl.pallas_call(
        functools.partial(restore_kernel, block, width),
        grid_spec=pltpu.PrefetchScalarGridSpec(
            num_scalar_prefetch=1,
            grid=(columns // width,),
            in_specs=[any_spec] * (4 + len(extra)),
            out_specs=pl.BlockSpec((depth, width), lambda j, o: (0, at + j)),
            scratch_shapes=[pltpu.VMEM((2, depth, width), BF16), pltpu.SemaphoreType.DMA((2,))],
        ),
        out_shape=jax.ShapeDtypeStruct((depth, full), BF16),
        input_output_aliases={} if so_far is None else {5: 0},
        cost_estimate=pl.CostEstimate(flops=0, bytes_accessed=4 * depth * columns, transcendentals=0),
        name="restore",
    )(order, *pieces, *extra)


def weight_grad_kernel(block, place_ref, lhs_ref, rhs_ref, mine, other, buffer, sems):
    step = pl.program_id(0)
    slot = lax.rem(step, 2)

    def settle(which):
        pltpu.make_async_copy(buffer.at[which], buffer.at[which], sems.at[which]).wait()

    @pl.when(step >= 2)
    def _():
        settle(slot)

    buffer[slot] = dot_f32(lhs_ref[...], rhs_ref[...], ((0,), (0,))).astype(BF16)
    for t in range(8):
        q = place_ref[step * 8 + t]
        source = buffer.at[slot, pl.ds(t * block, block), :]

        @pl.when(q < 16)
        def _():
            pltpu.make_async_copy(
                source, mine.at[pl.ds(pl.multiple_of(q * block, block), block), :], sems.at[slot]
            ).start()

        @pl.when(q >= 16)
        def _():
            pltpu.make_async_copy(
                source, other.at[pl.ds(pl.multiple_of((q - 16) * block, block), block), :], sems.at[slot]
            ).start()

    @pl.when(step == pl.num_programs(0) - 1)
    def _():
        settle(1 - slot)
        settle(slot)


def weight_grad(lhs, rhs, place, column, columns):
    tokens, rows = lhs.shape
    block = rows // BLOCKS
    any_spec = pl.BlockSpec(memory_space=pl.ANY)
    out = jax.ShapeDtypeStruct((16 * block, columns), BF16)
    return pl.pallas_call(
        functools.partial(weight_grad_kernel, block),
        grid_spec=pltpu.PrefetchScalarGridSpec(
            num_scalar_prefetch=1,
            grid=(4,),
            in_specs=[
                pl.BlockSpec((tokens, 8 * block), lambda i, o: (0, i)),
                pl.BlockSpec((tokens, columns), lambda i, o: (0, column)),
            ],
            out_specs=[any_spec, any_spec],
            scratch_shapes=[pltpu.VMEM((2, 8 * block, columns), BF16), pltpu.SemaphoreType.DMA((2,))],
        ),
        out_shape=[out, out],
        cost_estimate=pl.CostEstimate(
            flops=2 * tokens * rows * columns,
            bytes_accessed=2 * (tokens * rows + tokens * columns + rows * columns),
            transcendentals=0,
        ),
        name="weight_grad",
    )(place, lhs, rhs)


def rows_of(packed, start, count):
    return packed[:, start : start + count]


def on_device(
    hypercube,
    tokens,
    seg_ids,
    gain_in,
    w_in,
    conv_weight,
    conv_bias,
    dt_bias,
    a_log,
    d_skip,
    gain_out,
    w_out,
    cotangent,
):
    shards = lax.psum(1, "shard")
    taps, conv_local = conv_weight.shape
    model = tokens.shape[1]
    di = gain_out.shape[0] * shards
    conv_dim = conv_local * shards
    calls = ((0, 1), (1, 2), (3, 3))
    width = GROUP * P_SIZE

    def columns(w, call):
        start, count = call
        own = w[:, di + start * width : di + (start + count) * width]
        if start > 0:
            return own
        head = w[:, 2 * di :]
        return jnp.concatenate([jnp.pad(head, ((0, 0), (0, 4 * N - head.shape[1]))), own], axis=1)

    small = jnp.concatenate([conv_weight.reshape(-1), conv_bias, gain_in, gain_out])
    if hypercube:
        core = lax.axis_index("rep")
        w_half = lax.dynamic_slice_in_dim(w_in, core * (w_in.shape[0] // 2), w_in.shape[0] // 2, 0)
        o_half = lax.dynamic_slice_in_dim(w_out, core * (w_out.shape[0] // 2), w_out.shape[0] // 2, 0)
        near, middle, far = [Gather(columns(w_half, call)) for call in calls]
        gate_gather, out_gather = Gather(w_half[:, :di]), Gather(o_half)
        small_flow = gather_small(small)
        next(small_flow)
        got = []
        for starts in ((near,), (near, middle), (near, middle, far), (near, middle, far)):
            pairs = [each.step(*got) for each in starts] + [small_flow.send(got)]
            got = [pair[1] for pair in pairs]
            if len(starts) == 1:
                later = (far.held, gate_gather.held, out_gather.held), (tokens, seg_ids, dt_bias, a_log, d_skip, core)
                helds, (tokens, seg_ids, dt_bias, a_log, d_skip, core) = after(later, *got)
                far.held, gate_gather.held, out_gather.held = helds
        small_all = small_flow.send(got)
        order, place = block_order(core)
        sent, got = zip(middle.step(*got), far.step(*got), near.swap(*got), near.swap(*got))
        normed_tie = sent + got[2:]
        last_pair = got[:2]
    else:
        small_all = lax.all_gather(small, "shard", axis=0, tiled=False)
        full_w_in = lax.all_gather(w_in, "shard", axis=0, tiled=True)
        full_w_out = lax.all_gather(w_out, "shard", axis=0, tiled=True)
    cut = taps * conv_local
    conv_w = small_all[:, :cut].reshape(shards, taps, conv_local).transpose(1, 0, 2).reshape(taps, -1)
    conv_b = rows_of(small_all, cut, conv_local).reshape(1, -1)
    cut += conv_local
    full_gain_in = rows_of(small_all, cut, gain_in.shape[0]).reshape(1, -1).astype(F32)
    full_gain_out = rows_of(small_all, cut + gain_in.shape[0], gain_out.shape[0]).reshape(1, -1).astype(F32)
    conv_all = jnp.concatenate(
        [conv_w.astype(F32), conv_b.astype(F32), jnp.zeros((3, conv_dim), F32)], axis=0
    )
    conv_x, conv_bc = conv_all[:, :di], conv_all[:, di:]
    inputs = tokens.astype(F32)
    rscale = lax.rsqrt(jnp.mean(inputs * inputs, axis=1, keepdims=True) + EPSILON)
    unit = inputs * rscale
    normed = (unit * full_gain_in).astype(BF16)
    if hypercube:
        normed = after(normed, *normed_tie)
    aux, seg_row = seg_facts(seg_ids[0])
    heads = head_rows(dt_bias, a_log)
    skip = jnp.repeat(d_skip, P_SIZE)[None]

    pcs, w_parts = [], []
    bcv = written = mark = None
    if hypercube:
        sent, got = zip(
            far.step(*last_pair), middle.swap(*last_pair), middle.swap(*last_pair), gate_gather.step(*last_pair)
        )
        pending = {"project": sent, "scan": got[1:3]}
    for index, call in enumerate(calls):
        if hypercube:
            flow = (near, middle, far)[index]
            pieces = flow.pieces()
            pc, w_part = project(
                after(normed, *pending["project"]), pieces, order, None, 0, pieces[0].shape[1]
            )
        else:
            w_part = columns(full_w_in, call)
            pc = mm(normed, w_part)
        if hypercube and index == 0:
            done = far.seen[3], gate_gather.seen[0], pc
            sent, got = zip(far.swap(*done), far.swap(*done), gate_gather.step(*done))
            pc = after(pc, *sent, *done)
        if hypercube and index == 2:
            done = out_gather.seen[1], pc
            sent, got = out_gather.step(*done)
            pc = after(pc, sent, out_gather.seen[1])
        pcs.append((pc, 1 if index == 0 else 0))
        w_parts.append(w_part)
        written = run_forward(
            pc, pcs[-1][1], pcs[0][0], conv_x, conv_bc, aux, seg_row, heads, skip, *call, bcv, written
        )
        mark = written[4]
        if index == 0:
            bcv, bc_slope = written[5:]
        written = written[:5]
        if hypercube and index == 0:
            done = gate_gather.seen[1], mark
            sent, got = zip(gate_gather.step(*done), out_gather.step(*done))
            pending["project"] = (*sent, *far.swapped, done[0])
        if hypercube and index == 1:
            done = gate_gather.seen[2], out_gather.seen[0], mark
            sent, got = zip(gate_gather.step(*done), gate_gather.swap(*done), out_gather.step(*done))
            pending["project"] = sent + done[:2]
    if hypercube:
        done = gate_gather.seen[3], gate_gather.swapped[0], out_gather.seen[2], mark
        sent, got = zip(gate_gather.swap(*done), out_gather.step(*done), out_gather.swap(*done))
        gate_tie = sent + done
    x, y, states, slope, mark = written
    if hypercube:
        gate, w_gate, zg, squares = gate_project(
            after(normed, *gate_tie), gate_gather.pieces(), order, y, full_gain_out + mark[0, 0], None, 0, di
        )
        out_gather.swap(out_gather.seen[3], squares)
        full_w_out = restore(out_gather.pieces(), order, None, 0, model)
    else:
        w_gate = full_w_in[:, :di]
        gate = mm(normed, w_gate)
        gated = y * (gate * jax.nn.sigmoid(gate))
        squares = gated * gated
        zg = (gated * full_gain_out).astype(BF16)
    inverse = lax.rsqrt(jnp.sum(squares, axis=1, keepdims=True) / di + EPSILON)
    projected = inverse * mm(zg, full_w_out)
    output = (inputs + projected).astype(BF16)
    cot = cotangent.astype(F32)
    dots = jnp.sum(cot * projected, axis=1, keepdims=True)
    cot_scaled = (inverse * cot).astype(BF16)
    sig = jax.nn.sigmoid(gate)
    sums = None
    parts = {}
    if hypercube:
        in_block = w_in.shape[0] // 2
        out_sum = Scatter(weight_grad(zg, cot_scaled, place, 0, model), w_out.shape[0] // 2)
        sent, got_out = out_sum.step()
        grad_ynorm = mm_nt(after(cotangent, sent), full_w_out)
    else:
        grad_ynorm = mm_nt(cotangent, full_w_out)
    dz = inverse * (full_gain_out * grad_ynorm) - (y * (gate * sig)) * (inverse * inverse * dots / di)
    dy = (dz * (gate * sig)).astype(BF16)
    dgate = (dz * y * (sig * (1.0 + gate * (1.0 - sig)))).astype(BF16)
    if hypercube:
        sent, got_out = out_sum.step(dgate)
        gate_grad = weight_grad(normed, after(dgate, sent), place, 0, di)
        gate_sum = Scatter(gate_grad, in_block)
        sent, got_gate = gate_sum.step()
        scaled = mm_nt(after(dgate, sent), w_gate)
        done = got_out, got_gate, scaled
        sent, got = zip(out_sum.step(*done), gate_sum.step(*done))
        dy = after(dy, *sent, *done)
    else:
        scaled = mm_nt(dgate, w_gate)
    grad_sums = {}
    for index, call in reversed(list(enumerate(calls))):
        pc, first_x = pcs[index]
        dpart, dcw, dskip, *sums = run_backward(
            dy, x, bcv, states, slope, bc_slope, pc, first_x, pcs[0][0], conv_x, conv_bc, aux, seg_row, heads, skip, *call,
            index == 0, sums,
        )
        parts[index] = (dpart, dcw, dskip)
        if not hypercube:
            scaled = scaled + mm_nt(dpart, w_parts[index])
            continue
        done = *got, dpart
        if index == 2:
            moves = [out_sum, gate_sum]
        elif index == 1:
            moves = [gate_sum, grad_sums[2]]
        else:
            moves = [grad_sums[2], grad_sums[1]]
        sent, got = zip(*[each.step(*done) for each in moves])
        grad = weight_grad(normed, after(dpart, *sent, *done), place, 0, dpart.shape[1])
        grad_sums[index] = Scatter(grad, in_block)
        swap_sent, swap_got = grad_sums[index].step()
        scaled = scaled + mm_nt(after(dpart, swap_sent), w_parts[index])
        if index == 2:
            done = got[0], swap_got, scaled
            sent, late = zip(out_sum.step(*done), grad_sums[2].step(*done))
            got = late + got[1:]
            dy = after(dy, *sent, *done)
        elif index == 1:
            done = *got, swap_got, scaled
            sent, got = zip(gate_sum.step(*done), grad_sums[2].step(*done), grad_sums[1].step(*done))
            dy = after(dy, *sent, *done)
        else:
            last_got = got
    dbcw, dhead = sums
    dcw = jnp.concatenate([parts[index][1] for index in range(len(calls))] + [dbcw], axis=2)
    dskip = jnp.concatenate([parts[index][2] for index in range(len(calls))], axis=1)
    scaled = scaled * full_gain_in
    inner = jnp.mean(unit * scaled, axis=1, keepdims=True)
    grad_tokens = (cot + rscale * (scaled - unit * inner)).astype(BF16)

    conv_sums = dcw.sum(1)
    conv_sums = jnp.concatenate([conv_sums[4:5], conv_sums[3:4], conv_sums[2:3], conv_sums[1:2], conv_sums[0:1]])
    per_head = jnp.concatenate(
        [
            dhead[0].sum(0)[:H],
            dhead[1].sum(0)[:H] * -jnp.exp(a_log),
            dskip.sum(0).reshape(H, P_SIZE).sum(1),
        ]
    )
    conv_part = conv_sums.reshape(taps + 1, shards, conv_local).transpose(1, 0, 2).reshape(shards, -1)
    small_grad = jnp.concatenate([conv_part, jnp.broadcast_to(per_head[None], (shards, 3 * H))], axis=1)
    real = w_in.shape[1] - 2 * di
    if hypercube:
        small_sum = reduce_small(small_grad)[0]
        _, got = grad_sums[0].step(swap_got, *last_got)
        _, late = grad_sums[1].step(swap_got, *last_got)
        _, got = grad_sums[0].step(got, late, grad_tokens)
        grad_sums[1].step(late)
        gate_part, *rest = [each.finish() for each in (gate_sum, grad_sums[2], grad_sums[1], grad_sums[0])]
        rest = rest[::-1]
        own = jnp.concatenate([gate_part, rest[0][:, 4 * N :], *rest[1:], rest[0][:, :real]], axis=1)
        sum_w_in = both_cores(own)
        sum_w_out = both_cores(out_sum.finish())
    else:
        grad_w_out = dot_f32(zg, cot_scaled, ((0,), (0,)))
        rest = [parts[index][0] for index in range(len(calls))]
        grads = jnp.concatenate([dgate, rest[0][:, 4 * N :], *rest[1:], rest[0][:, :real]], axis=1)
        grad_w_in = dot_f32(normed, grads, ((0,), (0,)))
        small_sum = lax.psum(
            lax.psum_scatter(small_grad, "shard", scatter_dimension=0, tiled=True), "rep"
        )[0]
        sum_w_in = lax.psum_scatter(grad_w_in, "shard", scatter_dimension=0, tiled=True)
        sum_w_out = lax.psum_scatter(grad_w_out, "shard", scatter_dimension=0, tiled=True)
        sum_w_in, sum_w_out = lax.psum((sum_w_in, sum_w_out), "rep")
    grad_gain_in = jnp.sum(sum_w_in * w_in.astype(F32), axis=1) / gain_in.astype(F32)
    grad_gain_out = jnp.sum(sum_w_out * w_out.astype(F32), axis=1) / gain_out.astype(F32)
    cut = taps * conv_local
    head_at = cut + conv_local
    return (
        output,
        grad_tokens,
        grad_gain_in,
        sum_w_in,
        small_sum[:cut].reshape(taps, conv_local),
        small_sum[cut:head_at],
        small_sum[head_at : head_at + H],
        small_sum[head_at + H : head_at + 2 * H],
        small_sum[head_at + 2 * H :],
        grad_gain_out,
        sum_w_out,
    )


def both_cores(own):
    partner = swap_cores(own)
    first = lax.axis_index("rep") == 0
    return jnp.concatenate([jnp.where(first, own, partner), jnp.where(first, partner, own)], axis=0)


def reduce_small(rows):
    core = lax.axis_index("rep")
    places = jnp.asarray([reach(order) for order in ORDERS], jnp.int32)[core] ^ lax.axis_index("shard")
    hot = (places[:, None] == jnp.arange(16, dtype=jnp.int32)[None, :]).astype(F32)
    total = dot_f32(hot, rows, ((1,), (0,)), HIGHEST)
    for stage in (3, 2, 1, 0):
        cut = 1 << stage
        total = total[:cut] + exchange(total[cut:], stage)
    return total + swap_cores(total)


def solution(mesh):
    rows = P(("shard", "rep"), None)
    in_specs = (
        rows, rows, P("shard"), P("shard", None), P(None, "shard"), P("shard"), P(), P(), P(), P("shard"),
        P("shard", None), rows,
    )
    out_specs = (
        rows, rows, P("shard"), P("shard", None), P(None, "shard"), P("shard"), P(), P(), P(), P("shard"),
        P("shard", None),
    )
    hypercube = mesh.shape["shard"] == 16 and mesh.shape["rep"] == 2
    return jax.shard_map(
        functools.partial(on_device, hypercube),
        mesh=mesh,
        in_specs=in_specs,
        out_specs=out_specs,
        check_vma=False,
    )
```

time: 704 us -> 652 us (0.926)
  waiting for transfers between devices: 134 us -> 103 us
  Pallas kernels: 301 us -> 281 us
  starting transfers between devices: 67.1 us -> 55.3 us
  matrix products: 75.4 us -> 85.2 us
  local copies, waits for them, and re-layouts: 35.4 us -> 42.6 us
    ppermute x48, waiting for transfers between devices: 134 us -> 100 us  [exchange(): return lax.ppermute(values, ('shard', 'rep'), pairs)]
    add x25 -> x3, other arithmetic: 34.6 us -> 2.42 us  [the longest x2 1.7 us: rows(): total = total + term[start:stop].astype(F32)]
    convert_element_type x1 -> x20, other arithmetic: 13.9 us -> 36.4 us  [step(): send = after(self.rows(cut, 2 * cut).astype(BF16), *ahead)]
    pallas_call x4 -> x6, Pallas kernels: 180 us -> 160 us  [the longest x3 112 us: run_backward(): pl.pallas_call(functools.partial(backward_kernel, before is None, last, s...]
    ppermute x48, starting transfers between devices: 62.5 us -> 50.6 us  [exchange(): return lax.ppermute(values, ('shard', 'rep'), pairs)]
    dot_general x8, matrix products: 75.4 us -> 85.2 us  [dot_f32(): lax.dot_general(a, b, ((contract[0], contract[1]), ((), ())), preferred_e...]
    slice x25 -> x8, local copies, waits for them, and re-layouts: 15.1 us -> 7.55 us  [the longest x3 2.63 us: columns(): own = w[:, di + start * width:di + (start + count) * width]]
    concatenate x1 -> x6, local copies, waits for them, and re-layouts: 0.06 us -> 7.44 us  [the longest x5 7.43 us: step(): self.held = jnp.concatenate([send, got], axis=0)]
  transfers between devices with their start and end apart: 66 -> 66, of which waited for: 28 -> 23; matrix products, arithmetic and copies ran while one was open for 23% -> 27% of each run, Pallas kernels for 40% -> 37%
where the time goes in v4:
time: 652 us; the launch traced here: 645 us
  Pallas kernels  281 us (43%)
  waiting for transfers between devices  103 us (16%)
  matrix products  85.2 us (13%)
  other arithmetic  76.3 us (12%)
  starting transfers between devices  55.3 us (8%)
  local copies, waits for them, and re-layouts  42.6 us (7%)
    pallas_call x3, Pallas kernels, run_backward(): pl.pallas_call(functools.partial(backward_kernel, before is None, last, s...  112 us
    ppermute x48, waiting for transfers between devices, exchange(): return lax.ppermute(values, ('shard', 'rep'), pairs)  100 us
    dot_general x8, matrix products, dot_f32(): lax.dot_general(a, b, ((contract[0], contract[1]), ((), ())), preferred_e...  85.2 us
    pallas_call x5, Pallas kernels, weight_grad(): pl.pallas_call(functools.partial(weight_grad_kernel, block), grid_spec=pl...  57.1 us
    ppermute x48, starting transfers between devices, exchange(): return lax.ppermute(values, ('shard', 'rep'), pairs)  50.6 us
    pallas_call x3, Pallas kernels, run_forward(): pl.pallas_call(functools.partial(forward_kernel, first_call, start * GROU...  47.4 us
    convert_element_type x20, other arithmetic, step(): send = after(self.rows(cut, 2 * cut).astype(BF16), *ahead)  36.4 us
    pallas_call x3, Pallas kernels, project(): pl.pallas_call(functools.partial(project_kernel, block, width), grid_spec...  29.8 us
  transfers between devices with their start and end apart: 66, of which 23 were waited for; matrix products, arithmetic and copies ran while one was open for 27% of the time, Pallas kernels for 37%

profile of v4, /device:TPU:0, one launch (start us, length us, event | category | flops | bytes accessed | tf_op | source)
XLA Modules:
  0.0 644.9 jit_solution(11507136204673665362)
XLA Ops:
  80.5 9.2 %project.3 = (f32[1024,1024]{1,0:T(8,128)}, bf16[1536,1024]{1,0:T(8,128)(2,1)}) custom-call(s32[32]{0:T(128)} %pad_add_fusion.order_ref, bf16[1024,1536]{1,0:T(8,128)(2,1)} %fusion.4.x_ref.lhs_ref, bf16[384,1024]{1,0:T(8,128)(2,1)} %copy-done.29, bf16[384,1024]{1,0:T(8,128)(2,1)} %copy-done.44, bf16[384,1024]{1,0:T(8,128)(2,1)} %collective-permute-done.13.p2, ...), custom_call_target="tpu_custom_call" | custom-call | flops 3221225472 | bytes 13631488 | tf_op jit(solution)/shard_map/project/pallas_call | solution.py:767
  102.3 10.1 %scan_forward.3 = (bf16[1024,3072]{1,0:T(8,128)(2,1)}, f32[1024,3072]{1,0:T(8,128)}, bf16[512,3072]{1,0:T(8,128)(2,1)}, bf16[1024,3072]{1,0:T(8,128)(2,1)}, f32[...) custom-call(f32[1024,1024]{1,0:T(8,128)} %get-tuple-element.172.pc_ref.halo_ref.raw_ref.rest_0_.rest_1_.rest_4_, ...), custom_call_target="tpu_custom_call" | custom-call | flops 5000000000 | bytes 7340032 | tf_op jit(solution)/shard_map/scan_forward/pallas_call | solution.py:221
  118.9 9.0 %project.4 = (f32[1024,1024]{1,0:T(8,128)}, bf16[1536,1024]{1,0:T(8,128)(2,1)}) custom-call(s32[32]{0:T(128)} %pad_add_fusion.order_ref, bf16[1024,1536]{1,0:T(8,128)(2,1)} %fusion.4.x_ref.lhs_ref, bf16[384,1024]{1,0:T(8,128)(2,1)} %constant_dynamic-update-slice_fusion.p0, bf16[384,1024]{1,0:T(8,128)(2,1)} %collective-permute-done.15.p1, ...), custom_call_target="tpu_custom_call" | custom-call | flops 3221225472 | bytes 13631488 | tf_op jit(solution)/shard_map/project/pallas_call | solution.py:767
  127.9 15.8 %scan_forward.4 = (bf16[1024,3072]{1,0:T(8,128)(2,1)}, f32[1024,3072]{1,0:T(8,128)}, bf16[512,3072]{1,0:T(8,128)(2,1)}, bf16[1024,3072]{1,0:T(8,128)(2,1)}, f32[8,128]{1,0:T(8,128)}) custom-call(f32[1024,1024]{1,0:T(8,128)} %get-tuple-element.182.pc_ref.halo_ref, ...), custom_call_target="tpu_custom_call", output_to_operand_aliasing={{0}: (9, {}), {1}: (10, {}), {2}: (11, {}), {3}: (12, {})} | custom-call | flops 10000000000 | bytes 14680064 | tf_op jit(solution)/shard_map/scan_forward/pallas_call | solution.py:221
  154.3 11.7 %project.5 = (f32[1024,1536]{1,0:T(8,128)}, bf16[1536,1536]{1,0:T(8,128)(2,1)}) custom-call(s32[32]{0:T(128)} %pad_add_fusion.order_ref, bf16[1024,1536]{1,0:T(8,128)(2,1)} %fusion.4.x_ref.lhs_ref, bf16[384,1536]{1,0:T(8,128)(2,1)} %constant_dynamic-update-slice_fusion.4.p0, bf16[384,1536]{1,0:T(8,128)(2,1)} %collective-permute-done.18.p1, ...), custom_call_target="tpu_custom_call" | custom-call | flops 4831838208 | bytes 18874368 | tf_op jit(solution)/shard_map/project/pallas_call | solution.py:767
  172.4 21.6 %scan_forward.5 = (bf16[1024,3072]{1,0:T(8,128)(2,1)}, f32[1024,3072]{1,0:T(8,128)}, bf16[512,3072]{1,0:T(8,128)(2,1)}, bf16[1024,3072]{1,0:T(8,128)(2,1)}, f32[8,128]{1,0:T(8,128)}) custom-call(f32[1024,1536]{1,0:T(8,128)} %get-tuple-element.194.pc_ref.halo_ref, ...), custom_call_target="tpu_custom_call", output_to_operand_aliasing={{0}: (9, {}), {1}: (10, {}), {2}: (11, {}), {3}: (12, {})} | custom-call | flops 15000000512 | bytes 22020096 | tf_op jit(solution)/shard_map/scan_forward/pallas_call | solution.py:221
  209.5 24.9 %project_gate.1 = (f32[1024,3072]{1,0:T(8,128)}, bf16[1536,3072]{1,0:T(8,128)(2,1)}, bf16[1024,3072]{1,0:T(8,128)(2,1)}, f32[1024,128]{1,0:T(8,128)}) custom-call(s32[32]{0:T(128)} %pad_add_fusion.order_ref, bf16[1024,1536]{1,0:T(8,128)(2,1)} %fusion.4.x_ref.lhs_ref, bf16[384,3072]{1,0:T(8,128)(2,1)} %constant_dynamic-update-slice_fusion.6.p0, ...), custom_call_target="tpu_custom_call" | custom-call | flops 9663676416 | bytes 53477376 | tf_op jit(solution)/shard_map/project_gate/pallas_call | solution.py:821
  239.4 9.2 %restore.1 = bf16[3072,1536]{1,0:T(8,128)(2,1)} custom-call(s32[32]{0:T(128)} %pad_add_fusion.order_ref, bf16[768,1536]{1,0:T(8,128)(2,1)} %constant_dynamic-update-slice_fusion.8.p0, bf16[768,1536]{1,0:T(8,128)(2,1)} %collective-permute-done.31.p1, bf16[768,1536]{1,0:T(8,128)(2,1)} %collective-permute-done.32.p2, bf16[768,1536]{1,0:T(8,128)(2,1)} %collective-permute-done.33.p3), custom_call_target="tpu_custom_call" | custom-call | bytes 18874368 | tf_op jit(solution)/shard_map/restore/pallas_call | solution.py:867
  248.5 17.3 %fusion.11 = (f32[1024]{0:T(1024)S(1)}, bf16[1024,1536]{1,0:T(8,128)(2,1)}, bf16[1024,1536]{1,0:T(8,128)(2,1)}) fusion(bf16[1024,1536]{1,0:T(8,128)(2,1)} %param.27, f32[1024]{0:T(1024)S(1)} %add_rsqrt_fusion, bf16[1024,1536]{1,0:T(8,128)(2,1)S(1)} %copy-done.1, bf16[1024,3072]{1,0:T(8,128)(2,1)} %get-tuple-element.205.lhs_ref, bf16[3072,1536]{1,0:T(8,128)(2,1)} %restore.1), kind=kOutput, calls=%fused_computation.22 | convolution fusion | flops 9677831168 | bytes 28319744 | tf_op jit(solution)/shard_map/dot_general | solution.py:27
  265.8 15.3 %weight_grad.5 = (bf16[1536,1536]{1,0:T(8,128)(2,1)}, bf16[1536,1536]{1,0:T(8,128)(2,1)}) custom-call(s32[32]{0:T(128)} %fusion.37.place_ref, bf16[1024,3072]{1,0:T(8,128)(2,1)} %get-tuple-element.205.lhs_ref, bf16[1024,1536]{1,0:T(8,128)(2,1)} %get-tuple-element.285.rhs_ref), custom_call_target="tpu_custom_call" | custom-call | flops 9663676416 | bytes 18874368 | tf_op jit(solution)/shard_map/weight_grad/pallas_call | solution.py:922
  281.5 22.6 %multiply_convert_fusion = (bf16[1024,3072]{1,0:T(8,128)(2,1)}, bf16[1024,3072]{1,0:T(8,128)(2,1)}) fusion(f32[1024,3072]{1,0:T(8,128)} %get-tuple-element.203.y_ref, f32[1024]{0:T(1024)S(1)} %multiply_multiply_fusion, f32[1024,3072]{1,0:T(8,128)} %get-tuple-element.209, f32[3072]{0:T(1024)S(1)} %reshape.329, f32[1024]{0:T(1024)S(1)} %add_rsqrt_fusion, ...), kind=kOutput, calls=%fused_computation.1 | convolution fusion | flops 9720299520 | bytes 50352128 | tf_op jit(solution)/shard_map/dot_general | solution.py:27
  307.1 15.8 %weight_grad.6 = (bf16[768,3072]{1,0:T(8,128)(2,1)}, bf16[768,3072]{1,0:T(8,128)(2,1)}) custom-call(s32[32]{0:T(128)} %fusion.37.place_ref, bf16[1024,1536]{1,0:T(8,128)(2,1)} %fusion.4.x_ref.lhs_ref, bf16[1024,3072]{1,0:T(8,128)(2,1)} %get-tuple-element.214.rhs_ref), custom_call_target="tpu_custom_call" | custom-call | flops 9663676416 | bytes 18874368 | tf_op jit(solution)/shard_map/weight_grad/pallas_call | solution.py:922
  323.8 15.5 %fusion.49 = f32[1024,1536]{1,0:T(8,128)} fusion(bf16[1024,3072]{1,0:T(8,128)(2,1)} %get-tuple-element.214.rhs_ref, bf16[1536,3072]{1,0:T(8,128)(2,1)} %get-tuple-element.215), kind=kOutput, calls=%fused_computation.179 | convolution fusion | flops 9663676416 | bytes 22020096 | tf_op jit(solution)/shard_map/dot_general | solution.py:27
  339.3 13.0 %collective-permute-done.35 = bf16[768,1536]{1,0:T(8,128)(2,1)} collective-permute-done((bf16[768,1536]{1,0:T(8,128)(2,1)S(1)}, bf16[768,1536]{1,0:T(8,128)(2,1)}, u32[]{:S(2)}, u32[]{:S(2)}) %collective-permute-start.35) | collective-permute-done | bytes 2359328 | tf_op jit(solution)/shard_map/ppermute | solution.py:629
  359.2 51.2 %scan_backward.3 = (bf16[1024,1536]{1,0:T(8,128)(2,1)}, f32[5,8,1536]{2,1,0:T(8,128)}, f32[8,1536]{1,0:T(8,128)}, f32[1024,256]{1,0:T(8,128)}, f32[1024,256]{1,0...) custom-call(bf16[1024,3072]{1,0:T(8,128)(2,1)} %get-tuple-element.249.dy_ref, ...), custom_call_target="tpu_custom_call" | custom-call | flops 35999997952 | bytes 18874368 | tf_op jit(solution)/shard_map/scan_backward/pallas_call | solution.py:555
  420.1 9.7 %weight_grad.7 = (bf16[768,1536]{1,0:T(8,128)(2,1)}, bf16[768,1536]{1,0:T(8,128)(2,1)}) custom-call(s32[32]{0:T(128)} %fusion.37.place_ref, bf16[1024,1536]{1,0:T(8,128)(2,1)} %fusion.4.x_ref.lhs_ref, bf16[1024,1536]{1,0:T(8,128)(2,1)} %get-tuple-element.228.rhs_ref), custom_call_target="tpu_custom_call" | custom-call | flops 4831838208 | bytes 11010048 | tf_op jit(solution)/shard_map/weight_grad/pallas_call | solution.py:922
  429.9 10.8 %convolution_add_fusion = f32[1024,1536]{1,0:T(8,128)} fusion(f32[1024,1536]{1,0:T(8,128)} %fusion.49, bf16[1024,1536]{1,0:T(8,128)(2,1)} %get-tuple-element.228.rhs_ref, bf16[1536,1536]{1,0:T(8,128)(2,1)} %get-tuple-element.229), kind=kOutput, calls=%fused_computation.27 | convolution fusion | flops 4833411072 | bytes 20447232 | tf_op jit(solution)/shard_map/dot_general | solution.py:27
  452.2 36.2 %scan_backward.4 = (bf16[1024,1024]{1,0:T(8,128)(2,1)}, f32[5,8,1024]{2,1,0:T(8,128)}, f32[8,1024]{1,0:T(8,128)}, f32[1024,256]{1,0:T(8,128)}, f32[1024,256]{1,0...) custom-call(bf16[1024,3072]{1,0:T(8,128)(2,1)} %get-tuple-element.249.dy_ref, ...), custom_call_target="tpu_custom_call" | custom-call | flops 24000000000 | bytes 12582912 | tf_op jit(solution)/shard_map/scan_backward/pallas_call | solution.py:555
  494.7 8.0 %weight_grad.8 = (bf16[768,1024]{1,0:T(8,128)(2,1)}, bf16[768,1024]{1,0:T(8,128)(2,1)}) custom-call(s32[32]{0:T(128)} %fusion.37.place_ref, bf16[1024,1536]{1,0:T(8,128)(2,1)} %fusion.4.x_ref.lhs_ref, bf16[1024,1024]{1,0:T(8,128)(2,1)} %get-tuple-element.243.rhs_ref), custom_call_target="tpu_custom_call" | custom-call | flops 3221225472 | bytes 8388608 | tf_op jit(solution)/shard_map/weight_grad/pallas_call | solution.py:922
  502.9 10.4 %convolution_add_fusion.1 = f32[1024,1536]{1,0:T(8,128)} fusion(f32[1024,1536]{1,0:T(8,128)} %convolution_add_fusion, bf16[1024,1024]{1,0:T(8,128)(2,1)} %get-tuple-element.243.rhs_ref, bf16[1536,1024]{1,0:T(8,128)(2,1)} %get-tuple-element.244), kind=kOutput, calls=%fused_computation.28 | convolution fusion | flops 3222798336 | bytes 17825792 | tf_op jit(solution)/shard_map/dot_general | solution.py:27
  519.2 24.7 %scan_backward.5 = (bf16[1024,1024]{1,0:T(8,128)(2,1)}, f32[5,8,512]{2,1,0:T(8,128)}, f32[8,512]{1,0:T(8,128)}, f32[5,8,256]{2,1,0:T(8,128)}, f32[2,8,128]{2,1,0:T(8,128)}) custom-call(bf16[1024,3072]{1,0:T(8,128)(2,1)} %get-tuple-element.249.dy_ref, bf16[1024,3072]{1,0:T(8,128)(2,1)} %get-tuple-element.220.x_ref, ...), custom_call_target="tpu_custom_call" | custom-call | flops 12000000000 | bytes 6291456 | tf_op jit(solution)/shard_map/scan_backward/pallas_call | solution.py:555
  570.4 8.2 %weight_grad.9 = (bf16[768,1024]{1,0:T(8,128)(2,1)}, bf16[768,1024]{1,0:T(8,128)(2,1)}) custom-call(s32[32]{0:T(128)} %fusion.37.place_ref, bf16[1024,1536]{1,0:T(8,128)(2,1)} %fusion.4.x_ref.lhs_ref, bf16[1024,1024]{1,0:T(8,128)(2,1)} %get-tuple-element.260.rhs_ref), custom_call_target="tpu_custom_call" | custom-call | flops 3221225472 | bytes 8388608 | tf_op jit(solution)/shard_map/weight_grad/pallas_call | solution.py:922
  582.4 8.3 %fusion.5 = (f32[1024]{0:T(1024)S(1)}, f32[1024,1536]{1,0:T(8,128)S(1)}) fusion(bf16[1024,1536]{1,0:T(8,128)(2,1)S(1)} %copy-done.2, f32[1024]{0:T(1024)S(1)} %copy-done.33, f32[1536]{0:T(1024)S(1)} %copy-done.35, f32[1024,1536]{1,0:T(8,128)} %convolution_add_fusion.1, bf16[1024,1024]{1,0:T(8,128)(2,1)} %get-tuple-element.260.rhs_ref, ...), kind=kOutput, calls=%fused_computation.16 | convolution fusion | flops 3230661632 | bytes 20985856 | tf_op jit(solution)/shard_map/dot_general | solution.py:27
  601.3 7.7 %collective-permute-done.53 = bf16[384,1024]{1,0:T(8,128)(2,1)S(1)} collective-permute-done((bf16[384,1024]{1,0:T(8,128)(2,1)S(1)}, bf16[384,1024]{1,0:T(8,128)(2,1)S(1)}, u32[]{:S(2)}, u32[]{:S(2)}) %collective-permute-start.53) | collective-permute-done | bytes 786464 | tf_op jit(solution)/shard_map/ppermute | solution.py:629
  (368 shorter events, 256.7 us)
Async XLA Ops:
  77.6 20.1 %collective-permute-start.18 = (bf16[384,1536]{1,0:T(8,128)(2,1)}, bf16[384,1536]{1,0:T(8,128)(2,1)}, u32[]{:S(2)}, u32[]{:S(2)}) collective-permute-start(bf16[384,1536]{1,0:T(8,128)(2,1)} %constant_dynamic-update-slice_fusion.4.p0), channel_id=1, source_target_pairs={{0,4},{1,3},{2,6},{3,1},{4,0},{5,7},{6,2},{7,5},{8,12},{9,11},{10,... | collective-permute-start | bytes 3538952 | tf_op jit(solution)/shard_map/ppermute | solution.py:629
  114.7 34.5 %collective-permute-start.20 = (bf16[192,3072]{1,0:T(8,128)(2,1)}, bf16[192,3072]{1,0:T(8,128)(2,1)}, u32[]{:S(2)}, u32[]{:S(2)}) collective-permute-start(bf16[192,3072]{1,0:T(8,128)(2,1)} %pad_maximum_fusion.1), channel_id=1, source_target_pairs={{0,8},{1,9},{2,10},{3,11},{4,12},{5,13},{6,14},{7,15},{8,0},{9,1},... | collective-permute-start | bytes 3538952 | tf_op jit(solution)/shard_map/ppermute | solution.py:629
  117.1 34.5 %collective-permute-start.21 = (bf16[96,1536]{1,0:T(8,128)(2,1)S(1)}, bf16[96,1536]{1,0:T(8,128)(2,1)}, u32[]{:S(2)}, u32[]{:S(2)}) collective-permute-start(bf16[96,1536]{1,0:T(8,128)(2,1)S(1)} %constant_dynamic-slice_fusion.4), channel_id=1, source_target_pairs={{0,16},{1,17},{2,18},{3,19},{4,20},{5,21},{6,22},{7,23},{8,24},{9,... | collective-permute-start | bytes 884744 | tf_op jit(solution)/shard_map/ppermute | solution.py:629
  151.6 48.9 %collective-permute-start.27 = (bf16[384,3072]{1,0:T(8,128)(2,1)}, bf16[384,3072]{1,0:T(8,128)(2,1)}, u32[]{:S(2)}, u32[]{:S(2)}) collective-permute-start(bf16[384,3072]{1,0:T(8,128)(2,1)} %constant_dynamic-update-slice_fusion.6.p0), channel_id=1, source_target_pairs={{0,1},{1,0},{2,3},{3,2},{4,5},{5,4},{6,7},{7,6},{8,9},{9,8},{10,11... | collective-permute-start | bytes 7077896 | tf_op jit(solution)/shard_map/ppermute | solution.py:633
  151.6 48.9 %collective-permute-start.26 = (bf16[384,3072]{1,0:T(8,128)(2,1)}, bf16[384,3072]{1,0:T(8,128)(2,1)}, u32[]{:S(2)}, u32[]{:S(2)}) collective-permute-start(bf16[384,3072]{1,0:T(8,128)(2,1)} %constant_dynamic-update-slice_fusion.6.p0), channel_id=1, source_target_pairs={{0,4},{1,3},{2,6},{3,1},{4,0},{5,7},{6,2},{7,5},{8,12},{9,11},{10,... | collective-permute-start | bytes 7077896 | tf_op jit(solution)/shard_map/ppermute | solution.py:629
  172.4 28.1 %collective-permute-start.29 = (bf16[384,1536]{1,0:T(8,128)(2,1)}, bf16[384,1536]{1,0:T(8,128)(2,1)}, u32[]{:S(2)}, u32[]{:S(2)}) collective-permute-start(bf16[384,1536]{1,0:T(8,128)(2,1)} %pad_maximum_fusion.2), channel_id=1, source_target_pairs={{0,8},{1,9},{2,10},{3,11},{4,12},{5,13},{6,14},{7,15},{8,0},{9,1},... | collective-permute-start | bytes 3538952 | tf_op jit(solution)/shard_map/ppermute | solution.py:629
  205.2 29.2 %collective-permute-start.31 = (bf16[768,1536]{1,0:T(8,128)(2,1)}, bf16[768,1536]{1,0:T(8,128)(2,1)}, u32[]{:S(2)}, u32[]{:S(2)}) collective-permute-start(bf16[768,1536]{1,0:T(8,128)(2,1)} %constant_dynamic-update-slice_fusion.8.p0), channel_id=1, source_target_pairs={{0,4},{1,3},{2,6},{3,1},{4,0},{5,7},{6,2},{7,5},{8,12},{9,11},{10,... | collective-permute-start | bytes 7077896 | tf_op jit(solution)/shard_map/ppermute | solution.py:629
  208.1 28.9 %collective-permute-start.32 = (bf16[768,1536]{1,0:T(8,128)(2,1)}, bf16[768,1536]{1,0:T(8,128)(2,1)}, u32[]{:S(2)}, u32[]{:S(2)}) collective-permute-start(bf16[768,1536]{1,0:T(8,128)(2,1)} %constant_dynamic-update-slice_fusion.8.p0), channel_id=1, source_target_pairs={{0,1},{1,0},{2,3},{3,2},{4,5},{5,4},{6,7},{7,6},{8,9},{9,8},{10,11... | collective-permute-start | bytes 7077896 | tf_op jit(solution)/shard_map/ppermute | solution.py:633
  281.1 23.0 %collective-permute-start.34 = (bf16[1536,1536]{1,0:T(8,128)(2,1)}, bf16[1536,1536]{1,0:T(8,128)(2,1)}, u32[]{:S(2)}, u32[]{:S(2)}) collective-permute-start(bf16[1536,1536]{1,0:T(8,128)(2,1)} %get-tuple-element.207), channel_id=1, source_target_pairs={{0,1},{1,0},{2,3},{3,2},{4,5},{5,4},{6,7},{7,6},{8,9},{9,8},{10,11... | collective-permute-start | bytes 14155784 | tf_op jit(solution)/shard_map/ppermute | solution.py:633
  322.9 32.8 %collective-permute-start.36 = (bf16[768,3072]{1,0:T(8,128)(2,1)}, bf16[768,3072]{1,0:T(8,128)(2,1)}, u32[]{:S(2)}, u32[]{:S(2)}) collective-permute-start(bf16[768,3072]{1,0:T(8,128)(2,1)} %get-tuple-element.213), channel_id=1, source_target_pairs={{0,1},{1,0},{2,3},{3,2},{4,5},{5,4},{6,7},{7,6},{8,9},{9,8},{10,11... | collective-permute-start | bytes 14155784 | tf_op jit(solution)/shard_map/ppermute | solution.py:633
  323.4 28.9 %collective-permute-start.35 = (bf16[768,1536]{1,0:T(8,128)(2,1)S(1)}, bf16[768,1536]{1,0:T(8,128)(2,1)}, u32[]{:S(2)}, u32[]{:S(2)}) collective-permute-start(bf16[768,1536]{1,0:T(8,128)(2,1)S(1)} %add_convert_fusion.1), channel_id=1, source_target_pairs={{0,4},{1,3},{2,6},{3,1},{4,0},{5,7},{6,2},{7,5},{8,12},{9,11},{10,... | collective-permute-start | bytes 7077896 | tf_op jit(solution)/shard_map/ppermute | solution.py:629
  355.7 54.7 %collective-permute-start.37 = (bf16[384,1536]{1,0:T(8,128)(2,1)}, bf16[384,1536]{1,0:T(8,128)(2,1)S(1)}, u32[]{:S(2)}, u32[]{:S(2)}) collective-permute-start(bf16[384,1536]{1,0:T(8,128)(2,1)} %add_convert_fusion.4), channel_id=1, source_target_pairs={{0,8},{1,9},{2,10},{3,11},{4,12},{5,13},{6,14},{7,15},{8,0},{9,1},... | collective-permute-start | bytes 3538952 | tf_op jit(solution)/shard_map/ppermute | solution.py:629
  358.7 54.7 %collective-permute-start.38 = (bf16[384,3072]{1,0:T(8,128)(2,1)S(1)}, bf16[384,3072]{1,0:T(8,128)(2,1)}, u32[]{:S(2)}, u32[]{:S(2)}) collective-permute-start(bf16[384,3072]{1,0:T(8,128)(2,1)S(1)} %add_convert_fusion), channel_id=1, source_target_pairs={{0,4},{1,3},{2,6},{3,1},{4,0},{5,7},{6,2},{7,5},{8,12},{9,11},{10,... | collective-permute-start | bytes 7077896 | tf_op jit(solution)/shard_map/ppermute | solution.py:629
  413.4 27.3 %collective-permute-start.39 = (bf16[192,1536]{1,0:T(8,128)(2,1)}, bf16[192,1536]{1,0:T(8,128)(2,1)}, u32[]{:S(2)}, u32[]{:S(2)}) collective-permute-start(bf16[192,1536]{1,0:T(8,128)(2,1)} %add_convert_fusion.9), channel_id=1, source_target_pairs={{0,2},{1,5},{2,0},{3,7},{4,6},{5,1},{6,4},{7,3},{8,10},{9,13},{10,... | collective-permute-start | bytes 1769480 | tf_op jit(solution)/shard_map/ppermute | solution.py:629
  418.4 26.8 %collective-permute-start.41 = (bf16[192,3072]{1,0:T(8,128)(2,1)}, bf16[192,3072]{1,0:T(8,128)(2,1)S(1)}, u32[]{:S(2)}, u32[]{:S(2)}) collective-permute-start(bf16[192,3072]{1,0:T(8,128)(2,1)} %add_convert_fusion.3), channel_id=1, source_target_pairs={{0,8},{1,9},{2,10},{3,11},{4,12},{5,13},{6,14},{7,15},{8,0},{9,1},... | collective-permute-start | bytes 3538952 | tf_op jit(solution)/shard_map/ppermute | solution.py:629
  429.8 18.4 %collective-permute-start.40 = (bf16[768,1536]{1,0:T(8,128)(2,1)}, bf16[768,1536]{1,0:T(8,128)(2,1)S(1)}, u32[]{:S(2)}, u32[]{:S(2)}) collective-permute-start(bf16[768,1536]{1,0:T(8,128)(2,1)} %get-tuple-element.227), channel_id=1, source_target_pairs={{0,1},{1,0},{2,3},{3,2},{4,5},{5,4},{6,7},{7,6},{8,9},{9,8},{10,11... | collective-permute-start | bytes 7077896 | tf_op jit(solution)/shard_map/ppermute | solution.py:633
  448.3 40.2 %collective-permute-start.42 = (bf16[96,1536]{1,0:T(8,128)(2,1)}, bf16[96,1536]{1,0:T(8,128)(2,1)}, u32[]{:S(2)}, u32[]{:S(2)}) collective-permute-start(bf16[96,1536]{1,0:T(8,128)(2,1)} %add_convert_fusion.14), channel_id=1, source_target_pairs={{0,16},{1,17},{2,18},{3,19},{4,20},{5,21},{6,22},{7,23},{8,24},{9,... | collective-permute-start | bytes 884744 | tf_op jit(solution)/shard_map/ppermute | solution.py:629
  451.0 39.2 %collective-permute-start.43 = (bf16[384,1536]{1,0:T(8,128)(2,1)}, bf16[384,1536]{1,0:T(8,128)(2,1)}, u32[]{:S(2)}, u32[]{:S(2)}) collective-permute-start(bf16[384,1536]{1,0:T(8,128)(2,1)} %add_convert_fusion.2), channel_id=1, source_target_pairs={{0,4},{1,3},{2,6},{3,1},{4,0},{5,7},{6,2},{7,5},{8,12},{9,11},{10,... | collective-permute-start | bytes 3538952 | tf_op jit(solution)/shard_map/ppermute | solution.py:629
  490.1 58.9 %collective-permute-start.65 = (f32[96,1536]{1,0:T(8,128)S(1)}, f32[96,1536]{1,0:T(8,128)}, u32[]{:S(2)}, u32[]{:S(2)}) collective-permute-start(f32[96,1536]{1,0:T(8,128)S(1)} %convert_add_fusion.2), channel_id=1, source_target_pairs={{0,1},{1,0},{2,3},{3,2},{4,5},{5,4},{6,7},{7,6},{8,9},{9,8},{10,11... | collective-permute-start | bytes 1769480 | tf_op jit(solution)/shard_map/ppermute | solution.py:633
  492.5 20.9 %collective-permute-start.45 = (bf16[192,1536]{1,0:T(8,128)(2,1)}, bf16[192,1536]{1,0:T(8,128)(2,1)}, u32[]{:S(2)}, u32[]{:S(2)}) collective-permute-start(bf16[192,1536]{1,0:T(8,128)(2,1)} %add_convert_fusion.7), channel_id=1, source_target_pairs={{0,8},{1,9},{2,10},{3,11},{4,12},{5,13},{6,14},{7,15},{8,0},{9,1},... | collective-permute-start | bytes 1769480 | tf_op jit(solution)/shard_map/ppermute | solution.py:629
  494.1 21.4 %collective-permute-start.44 = (bf16[96,3072]{1,0:T(8,128)(2,1)}, bf16[96,3072]{1,0:T(8,128)(2,1)S(1)}, u32[]{:S(2)}, u32[]{:S(2)}) collective-permute-start(bf16[96,3072]{1,0:T(8,128)(2,1)} %add_convert_fusion.8), channel_id=1, source_target_pairs={{0,2},{1,5},{2,0},{3,7},{4,6},{5,1},{6,4},{7,3},{8,10},{9,13},{10,... | collective-permute-start | bytes 1769480 | tf_op jit(solution)/shard_map/ppermute | solution.py:629
  555.4 23.3 %collective-permute-start.61 = (f32[4,1184]{1,0:T(4,128)}, f32[4,1184]{1,0:T(4,128)}, u32[]{:S(2)}, u32[]{:S(2)}) collective-permute-start(f32[4,1184]{1,0:T(4,128)} %slice.662), channel_id=1, source_target_pairs={{0,8},{1,9},{2,10},{3,11},{4,12},{5,13},{6,14},{7,15},{8,0},{9,1},... | collective-permute-start | bytes 56840 | tf_op jit(solution)/shard_map/ppermute | solution.py:629
  579.5 30.3 %collective-permute-start.62 = (f32[2,1184]{1,0:T(2,128)S(1)}, f32[2,1184]{1,0:T(2,128)S(1)}, u32[]{:S(2)}, u32[]{:S(2)}) collective-permute-start(f32[2,1184]{1,0:T(2,128)S(1)} %slice.664), channel_id=1, source_target_pairs={{0,2},{1,5},{2,0},{3,7},{4,6},{5,1},{6,4},{7,3},{8,10},{9,13},{10,... | collective-permute-start | bytes 28424 | tf_op jit(solution)/shard_map/ppermute | solution.py:629
  609.9 27.0 %collective-permute-start.63 = (f32[1,1184]{1,0:T(1,128)S(1)}, f32[1,1184]{1,0:T(1,128)S(1)}, u32[]{:S(2)}, u32[]{:S(2)}) collective-permute-start(f32[1,1184]{1,0:T(1,128)S(1)} %slice.666), channel_id=1, source_target_pairs={{0,16},{1,17},{2,18},{3,19},{4,20},{5,21},{6,22},{7,23},{8,24},{9,... | collective-permute-start | bytes 14216 | tf_op jit(solution)/shard_map/ppermute | solution.py:629
  (89 other events, 1103.2 us)

commit v5 on v4

--- a/solution.py
+++ b/solution.py
@@ -169,7 +169,8 @@
         old_b = old.astype(BF16)
         st_out[:, both] = old_b
         carried = mm(query, old_b)
-        y_out[:, both] = wide(outs) + wide(entries) * carried + skip_ref[:, both] * wide(xbs).astype(F32)
+        y = wide(outs) + wide(entries) * carried + skip_ref[:, both] * wide(xbs).astype(F32)
+        y_out[:, both] = y.astype(BF16)
         state[:, tile] = old * wide(keeps) + wide(fresh)
 
 
@@ -199,7 +200,7 @@
     out_specs = [wide, wide, pl.BlockSpec((N, width), lambda s, g: (s, start + g)), wide, mark_spec]
     out_shape = [
         jax.ShapeDtypeStruct((tokens, di), BF16),
-        jax.ShapeDtypeStruct((tokens, di), F32),
+        jax.ShapeDtypeStruct((tokens, di), BF16),
         jax.ShapeDtypeStruct((spans * N, di), BF16),
         jax.ShapeDtypeStruct((tokens, di), BF16),
         jax.ShapeDtypeStruct((8, TILE), F32),
@@ -645,12 +646,13 @@
 
     def step(self, *ahead):
         stage = len(self.seen)
-        send = after(self.held, *ahead)
-        got = exchange(send, stage)
+        if stage > 0:
+            self.held = jnp.concatenate([self.held, after(self.seen[-1], *ahead)], axis=0)
+        elif ahead:
+            self.held = after(self.held, *ahead)
+        got = exchange(self.held, stage)
         self.seen.append(got)
-        if stage < 3:
-            self.held = jnp.concatenate([send, got], axis=0)
-        return send, got
+        return self.held, got
 
     def swap(self, *ahead):
         send = after(self.held if not self.swapped else self.seen[3], *ahead)
@@ -690,13 +692,14 @@
 
     def step(self, *ahead):
         if len(self.terms) == 1:
-            send = after(self.other, *ahead)
-            self.terms.append(swap_cores(send))
-            return send, self.terms[-1]
+            self.other = after(self.other, *ahead)
+            self.terms.append(swap_cores(self.other))
+            return self.other, self.terms[-1]
         if self.left:
             stage = self.left.pop(0)
             cut = self.block << stage
-            send = after(self.rows(cut, 2 * cut).astype(BF16), *ahead)
+            self.terms[-1] = after(self.terms[-1], *ahead)
+            send = self.rows(cut, 2 * cut).astype(BF16)
             self.terms.append(exchange(send, stage))
             return send, self.terms[-1]
         return self.terms[-1], self.terms[-1]
@@ -800,8 +803,8 @@
     for i in range(x_ref.shape[0] // SPAN):
         rows = slice(i * SPAN, (i + 1) * SPAN)
         gate = mm(x_ref[rows], w)
-        gate_ref[rows] = gate
-        gated = y_ref[rows] * (gate * jax.nn.sigmoid(gate))
+        gate_ref[rows] = gate.astype(BF16)
+        gated = y_ref[rows].astype(F32) * (gate * jax.nn.sigmoid(gate))
         zg_ref[rows] = (gated * gain_ref[...]).astype(BF16)
         square = gated * gated
         total = square[:, :TILE]
@@ -836,7 +839,7 @@
             scratch_shapes=[pltpu.VMEM((2, depth, width), BF16), pltpu.SemaphoreType.DMA((2,))],
         ),
         out_shape=[
-            jax.ShapeDtypeStruct((tokens, full), F32),
+            jax.ShapeDtypeStruct((tokens, full), BF16),
             jax.ShapeDtypeStruct((depth, full), BF16),
             jax.ShapeDtypeStruct((tokens, full), BF16),
             jax.ShapeDtypeStruct((tokens, TILE), F32),
@@ -878,6 +881,57 @@
         cost_estimate=pl.CostEstimate(flops=0, bytes_accessed=4 * depth * columns, transcendentals=0),
         name="restore",
     )(order, *pieces, *extra)
+
+
+def output_kernel(block, width, order_ref, zg_ref, inverse_ref, tokens_ref, cot_ref, p0, p1, p2, p3, w_ref, out_ref, dots_ref, buffer, sems):
+    slot = next_tile(order_ref, (p0, p1, p2, p3), buffer, sems, block, width)
+    w = buffer[slot]
+    w_ref[...] = w
+
+    @pl.when(pl.program_id(0) == 0)
+    def _():
+        dots_ref[...] = jnp.zeros_like(dots_ref)
+
+    for i in range(zg_ref.shape[0] // SPAN):
+        rows = slice(i * SPAN, (i + 1) * SPAN)
+        projected = inverse_ref[rows] * mm(zg_ref[rows], w)
+        out_ref[rows] = (tokens_ref[rows].astype(F32) + projected).astype(BF16)
+        dots_ref[rows] += jnp.sum(cot_ref[rows].astype(F32) * projected, axis=1, keepdims=True)
+
+
+def output_project(zg, inverse, tokens, cot, pieces, order, width=512):
+    count, depth = zg.shape
+    model = tokens.shape[1]
+    block = depth // BLOCKS
+    any_spec = pl.BlockSpec(memory_space=pl.ANY)
+    whole = lambda i, o: (0, 0)
+    part = pl.BlockSpec((count, width), lambda i, o: (0, i))
+    return pl.pallas_call(
+        functools.partial(output_kernel, block, width),
+        grid_spec=pltpu.PrefetchScalarGridSpec(
+            num_scalar_prefetch=1,
+            grid=(model // width,),
+            in_specs=[pl.BlockSpec((count, depth), whole), pl.BlockSpec((count, 1), whole), part, part]
+            + [any_spec] * 4,
+            out_specs=[
+                pl.BlockSpec((depth, width), lambda i, o: (0, i)),
+                part,
+                pl.BlockSpec((count, 1), whole),
+            ],
+            scratch_shapes=[pltpu.VMEM((2, depth, width), BF16), pltpu.SemaphoreType.DMA((2,))],
+        ),
+        out_shape=[
+            jax.ShapeDtypeStruct((depth, model), BF16),
+            jax.ShapeDtypeStruct((count, model), BF16),
+            jax.ShapeDtypeStruct((count, 1), F32),
+        ],
+        cost_estimate=pl.CostEstimate(
+            flops=2 * count * depth * model,
+            bytes_accessed=4 * depth * model + 2 * count * (depth + 3 * model),
+            transcendentals=0,
+        ),
+        name="project_out",
+    )(order, zg, inverse, tokens, cot, *pieces)
 
 
 def weight_grad_kernel(block, place_ref, lhs_ref, rhs_ref, mine, other, buffer, sems):
@@ -995,19 +1049,23 @@
                 far.held, gate_gather.held, out_gather.held = helds
         small_all = small_flow.send(got)
         order, place = block_order(core)
-        sent, got = zip(middle.step(*got), far.step(*got), near.swap(*got), near.swap(*got))
-        normed_tie = sent + got[2:]
-        last_pair = got[:2]
+        sent, got = zip(
+            middle.step(*got), far.step(*got), near.swap(*got), near.swap(*got), gate_gather.step(*got)
+        )
+        normed_tie = sent
+        conv_tie = sent
+        last_pair = got[0], got[1], got[4]
     else:
         small_all = lax.all_gather(small, "shard", axis=0, tiled=False)
         full_w_in = lax.all_gather(w_in, "shard", axis=0, tiled=True)
         full_w_out = lax.all_gather(w_out, "shard", axis=0, tiled=True)
     cut = taps * conv_local
-    conv_w = small_all[:, :cut].reshape(shards, taps, conv_local).transpose(1, 0, 2).reshape(taps, -1)
-    conv_b = rows_of(small_all, cut, conv_local).reshape(1, -1)
+    small_conv = after(small_all, *conv_tie) if hypercube else small_all
+    conv_w = small_conv[:, :cut].reshape(shards, taps, conv_local).transpose(1, 0, 2).reshape(taps, -1)
+    conv_b = rows_of(small_conv, cut, conv_local).reshape(1, -1)
     cut += conv_local
     full_gain_in = rows_of(small_all, cut, gain_in.shape[0]).reshape(1, -1).astype(F32)
-    full_gain_out = rows_of(small_all, cut + gain_in.shape[0], gain_out.shape[0]).reshape(1, -1).astype(F32)
+    full_gain_out = rows_of(small_conv, cut + gain_in.shape[0], gain_out.shape[0]).reshape(1, -1).astype(F32)
     conv_all = jnp.concatenate(
         [conv_w.astype(F32), conv_b.astype(F32), jnp.zeros((3, conv_dim), F32)], axis=0
     )
@@ -1024,29 +1082,24 @@
 
     pcs, w_parts = [], []
     bcv = written = mark = None
-    if hypercube:
-        sent, got = zip(
-            far.step(*last_pair), middle.swap(*last_pair), middle.swap(*last_pair), gate_gather.step(*last_pair)
-        )
-        pending = {"project": sent, "scan": got[1:3]}
+    project_tie = ()
     for index, call in enumerate(calls):
         if hypercube:
-            flow = (near, middle, far)[index]
-            pieces = flow.pieces()
-            pc, w_part = project(
-                after(normed, *pending["project"]), pieces, order, None, 0, pieces[0].shape[1]
-            )
+            pieces = (near, middle, far)[index].pieces()
+            pc, w_part = project(after(normed, *project_tie), pieces, order, None, 0, pieces[0].shape[1])
+            if index == 0:
+                done = last_pair[0], last_pair[2], pc
+                sent, got = zip(
+                    middle.swap(*done), middle.swap(*done), gate_gather.step(*done), out_gather.step(*done)
+                )
+                pc = after(pc, *sent)
+            if index == 1:
+                done = got[0], pc
+                sent, _ = zip(far.swap(*done), far.swap(*done))
+                pc = after(pc, *sent)
         else:
             w_part = columns(full_w_in, call)
             pc = mm(normed, w_part)
-        if hypercube and index == 0:
-            done = far.seen[3], gate_gather.seen[0], pc
-            sent, got = zip(far.swap(*done), far.swap(*done), gate_gather.step(*done))
-            pc = after(pc, *sent, *done)
-        if hypercube and index == 2:
-            done = out_gather.seen[1], pc
-            sent, got = out_gather.step(*done)
-            pc = after(pc, sent, out_gather.seen[1])
         pcs.append((pc, 1 if index == 0 else 0))
         w_parts.append(w_part)
         written = run_forward(
@@ -1057,58 +1110,61 @@
             bcv, bc_slope = written[5:]
         written = written[:5]
         if hypercube and index == 0:
-            done = gate_gather.seen[1], mark
-            sent, got = zip(gate_gather.step(*done), out_gather.step(*done))
-            pending["project"] = (*sent, *far.swapped, done[0])
+            done = last_pair[1], got[2], got[3], mark
+            sent, got = zip(far.step(*done), gate_gather.step(*done), out_gather.step(*done))
+            project_tie = sent
         if hypercube and index == 1:
-            done = gate_gather.seen[2], out_gather.seen[0], mark
+            done = got[1], got[2], mark
             sent, got = zip(gate_gather.step(*done), gate_gather.swap(*done), out_gather.step(*done))
-            pending["project"] = sent + done[:2]
+            project_tie = sent
     if hypercube:
-        done = gate_gather.seen[3], gate_gather.swapped[0], out_gather.seen[2], mark
+        done = got[0], got[1], got[2], mark
         sent, got = zip(gate_gather.swap(*done), out_gather.step(*done), out_gather.swap(*done))
-        gate_tie = sent + done
+        gate_tie = sent
     x, y, states, slope, mark = written
     if hypercube:
         gate, w_gate, zg, squares = gate_project(
             after(normed, *gate_tie), gate_gather.pieces(), order, y, full_gain_out + mark[0, 0], None, 0, di
         )
-        out_gather.swap(out_gather.seen[3], squares)
-        full_w_out = restore(out_gather.pieces(), order, None, 0, model)
     else:
         w_gate = full_w_in[:, :di]
         gate = mm(normed, w_gate)
-        gated = y * (gate * jax.nn.sigmoid(gate))
+        gated = y.astype(F32) * (gate * jax.nn.sigmoid(gate))
         squares = gated * gated
         zg = (gated * full_gain_out).astype(BF16)
     inverse = lax.rsqrt(jnp.sum(squares, axis=1, keepdims=True) / di + EPSILON)
-    projected = inverse * mm(zg, full_w_out)
-    output = (inputs + projected).astype(BF16)
     cot = cotangent.astype(F32)
-    dots = jnp.sum(cot * projected, axis=1, keepdims=True)
     cot_scaled = (inverse * cot).astype(BF16)
+    y, gate = y.astype(F32), gate.astype(F32)
     sig = jax.nn.sigmoid(gate)
     sums = None
     parts = {}
     if hypercube:
         in_block = w_in.shape[0] // 2
-        out_sum = Scatter(weight_grad(zg, cot_scaled, place, 0, model), w_out.shape[0] // 2)
-        sent, got_out = out_sum.step()
+        out_tie, out_got = out_gather.swap(out_gather.seen[3], zg)
+        out_grad = weight_grad(zg, after(cot_scaled, out_tie), place, 0, model)
+        out_sum = Scatter(out_grad, w_out.shape[0] // 2)
+        sent, got = out_sum.step(*out_gather.swapped)
+        full_w_out, output, dots = output_project(
+            after(zg, sent), inverse, tokens, cotangent, out_gather.pieces(), order
+        )
+        sent, got = out_sum.step(got, dots)
         grad_ynorm = mm_nt(after(cotangent, sent), full_w_out)
     else:
+        projected = inverse * mm(zg, full_w_out)
+        output = (inputs + projected).astype(BF16)
+        dots = jnp.sum(cot * projected, axis=1, keepdims=True)
         grad_ynorm = mm_nt(cotangent, full_w_out)
     dz = inverse * (full_gain_out * grad_ynorm) - (y * (gate * sig)) * (inverse * inverse * dots / di)
     dy = (dz * (gate * sig)).astype(BF16)
     dgate = (dz * y * (sig * (1.0 + gate * (1.0 - sig)))).astype(BF16)
     if hypercube:
-        sent, got_out = out_sum.step(dgate)
-        gate_grad = weight_grad(normed, after(dgate, sent), place, 0, di)
+        gate_grad = weight_grad(normed, after(dgate, got), place, 0, di)
         gate_sum = Scatter(gate_grad, in_block)
-        sent, got_gate = gate_sum.step()
+        sent, gate_got = gate_sum.step()
         scaled = mm_nt(after(dgate, sent), w_gate)
-        done = got_out, got_gate, scaled
-        sent, got = zip(out_sum.step(*done), gate_sum.step(*done))
-        dy = after(dy, *sent, *done)
+        sent, got = zip(out_sum.step(got, scaled), gate_sum.step(gate_got, scaled))
+        dy = after(dy, *sent, gate_got, scaled)
     else:
         scaled = mm_nt(dgate, w_gate)
     grad_sums = {}
@@ -1124,27 +1180,32 @@
             continue
         done = *got, dpart
         if index == 2:
-            moves = [out_sum, gate_sum]
+            sent, out_got = out_sum.step(*done)
+            early = (sent,)
         elif index == 1:
-            moves = [gate_sum, grad_sums[2]]
+            sent, gate_got = gate_sum.step(*done)
+            early = (sent,)
         else:
-            moves = [grad_sums[2], grad_sums[1]]
-        sent, got = zip(*[each.step(*done) for each in moves])
-        grad = weight_grad(normed, after(dpart, *sent, *done), place, 0, dpart.shape[1])
+            early, late = zip(grad_sums[2].step(*done), grad_sums[1].step(*done))
+        grad = weight_grad(normed, after(dpart, *early, *done), place, 0, dpart.shape[1])
         grad_sums[index] = Scatter(grad, in_block)
         swap_sent, swap_got = grad_sums[index].step()
-        scaled = scaled + mm_nt(after(dpart, swap_sent), w_parts[index])
         if index == 2:
-            done = got[0], swap_got, scaled
-            sent, late = zip(out_sum.step(*done), grad_sums[2].step(*done))
-            got = late + got[1:]
+            scaled = scaled + mm_nt(after(dpart, swap_sent), w_parts[index])
+            done = swap_got, scaled
+            sent, got = zip(out_sum.step(out_got, *done), gate_sum.step(got[1], *done), grad_sums[2].step(*done))
             dy = after(dy, *sent, *done)
         elif index == 1:
-            done = *got, swap_got, scaled
-            sent, got = zip(gate_sum.step(*done), grad_sums[2].step(*done), grad_sums[1].step(*done))
+            scaled = scaled + mm_nt(after(dpart, swap_sent), w_parts[index])
+            done = swap_got, scaled
+            sent, got = zip(gate_sum.step(gate_got, *done), grad_sums[2].step(got[2], *done), grad_sums[1].step(*done))
             dy = after(dy, *sent, *done)
         else:
-            last_got = got
+            sent, late = zip(grad_sums[2].step(*late, grad[0]), grad_sums[1].step(*late, grad[0]))
+            scaled = scaled + mm_nt(after(dpart, swap_sent, *sent), w_parts[index])
+            sent, got = grad_sums[0].step(swap_got, *late, scaled)
+            grad_sums[1].step(*late, scaled)
+            scaled = after(scaled, sent)
     dbcw, dhead = sums
     dcw = jnp.concatenate([parts[index][1] for index in range(len(calls))] + [dbcw], axis=2)
     dskip = jnp.concatenate([parts[index][2] for index in range(len(calls))], axis=1)
@@ -1165,11 +1226,11 @@
     small_grad = jnp.concatenate([conv_part, jnp.broadcast_to(per_head[None], (shards, 3 * H))], axis=1)
     real = w_in.shape[1] - 2 * di
     if hypercube:
-        small_sum = reduce_small(small_grad)[0]
-        _, got = grad_sums[0].step(swap_got, *last_got)
-        _, late = grad_sums[1].step(swap_got, *last_got)
-        _, got = grad_sums[0].step(got, late, grad_tokens)
-        grad_sums[1].step(late)
+        small_sum = reduce_small(small_grad, (grad[0], swap_got, got, grad_tokens))[0]
+        sent, got = grad_sums[0].step(got, grad_tokens)
+        grad_sums[1].step(sent)
+        _, got = grad_sums[0].step(got)
+        grad_sums[0].step(got)
         gate_part, *rest = [each.finish() for each in (gate_sum, grad_sums[2], grad_sums[1], grad_sums[0])]
         rest = rest[::-1]
         own = jnp.concatenate([gate_part, rest[0][:, 4 * N :], *rest[1:], rest[0][:, :real]], axis=1)
@@ -1211,13 +1272,14 @@
     return jnp.concatenate([jnp.where(first, own, partner), jnp.where(first, partner, own)], axis=0)
 
 
-def reduce_small(rows):
+def reduce_small(rows, ties):
     core = lax.axis_index("rep")
     places = jnp.asarray([reach(order) for order in ORDERS], jnp.int32)[core] ^ lax.axis_index("shard")
     hot = (places[:, None] == jnp.arange(16, dtype=jnp.int32)[None, :]).astype(F32)
     total = dot_f32(hot, rows, ((1,), (0,)), HIGHEST)
-    for stage in (3, 2, 1, 0):
+    for stage, tie in zip((3, 2, 1, 0), ties):
         cut = 1 << stage
+        total = after(total, tie)
         total = total[:cut] + exchange(total[cut:], stage)
     return total + swap_cores(total)
 

time: 652 us -> 600 us (0.920)
  waiting for transfers between devices: 103 us -> 63.7 us
  matrix products: 85.2 us -> 65.9 us
  Pallas kernels: 281 us -> 288 us
    ppermute x48, waiting for transfers between devices: 100 us -> 63.1 us  [exchange(): return lax.ppermute(values, ('shard', 'rep'), pairs)]
    dot_general x8 -> x7, matrix products: 85.2 us -> 65.9 us  [dot_f32(): lax.dot_general(a, b, ((contract[0], contract[1]), ((), ())), preferred_e...]
    pallas_call x1, Pallas kernels: 9.16 us -> 20.2 us  [output_project(): pl.pallas_call(functools.partial(output_kernel, block, width), grid_spec=...]
    convert_element_type x21 -> x22, other arithmetic: 36.5 us -> 39.7 us  [the longest x20 37.4 us: step(): send = self.rows(cut, 2 * cut).astype(BF16)]
  transfers between devices with their start and end apart: 66 -> 66, of which waited for: 23 -> 15; matrix products, arithmetic and copies ran while one was open for 27% -> 26% of each run, Pallas kernels for 37% -> 44%
where the time goes in v5:
time: 600 us; the launch traced here: 594 us
  Pallas kernels  288 us (48%)
  other arithmetic  77.1 us (13%)
  matrix products  65.9 us (11%)
  waiting for transfers between devices  63.7 us (11%)
  starting transfers between devices  56.6 us (9%)
  local copies, waits for them, and re-layouts  40.7 us (7%)
    pallas_call x3, Pallas kernels, run_backward(): pl.pallas_call(functools.partial(backward_kernel, before is None, last, s...  112 us
    dot_general x7, matrix products, dot_f32(): lax.dot_general(a, b, ((contract[0], contract[1]), ((), ())), preferred_e...  65.9 us
    ppermute x48, waiting for transfers between devices, exchange(): return lax.ppermute(values, ('shard', 'rep'), pairs)  63.1 us
    pallas_call x5, Pallas kernels, weight_grad(): pl.pallas_call(functools.partial(weight_grad_kernel, block), grid_spec=pl...  56.7 us
    ppermute x48, starting transfers between devices, exchange(): return lax.ppermute(values, ('shard', 'rep'), pairs)  52.8 us
    pallas_call x3, Pallas kernels, run_forward(): pl.pallas_call(functools.partial(forward_kernel, first_call, start * GROU...  47.8 us
    convert_element_type x20, other arithmetic, step(): send = self.rows(cut, 2 * cut).astype(BF16)  37.4 us
    pallas_call x3, Pallas kernels, project(): pl.pallas_call(functools.partial(project_kernel, block, width), grid_spec...  30.1 us
  transfers between devices with their start and end apart: 66, of which 15 were waited for; matrix products, arithmetic and copies ran while one was open for 26% of the time, Pallas kernels for 44%

profile of v5, /device:TPU:0, one launch (start us, length us, event | category | flops | bytes accessed | tf_op | source)
XLA Modules:
  0.0 594.1 jit_solution(8197619310388834092)
XLA Ops:
  75.7 9.4 %project.3 = (f32[1024,1024]{1,0:T(8,128)}, bf16[1536,1024]{1,0:T(8,128)(2,1)}) custom-call(s32[32]{0:T(128)} %pad_add_fusion.order_ref, bf16[1024,1536]{1,0:T(8,128)(2,1)} %fusion.12.x_ref.lhs_ref, bf16[384,1024]{1,0:T(8,128)(2,1)} %pad_maximum_fusion.2.p0, bf16[384,1024]{1,0:T(8,128)(2,1)} %collective-permute-done.11.p1, ...), custom_call_target="tpu_custom_call" | custom-call | flops 3221225472 | bytes 13631488 | tf_op jit(solution)/shard_map/project/pallas_call | solution.py:770
  88.8 10.0 %scan_forward.3 = (bf16[1024,3072]{1,0:T(8,128)(2,1)}, bf16[1024,3072]{1,0:T(8,128)(2,1)}, bf16[512,3072]{1,0:T(8,128)(2,1)}, bf16[1024,3072]{1,0:T(8,128)(2,1)}...) custom-call(f32[1024,1024]{1,0:T(8,128)} %get-tuple-element.183.pc_ref.halo_ref.raw_ref.rest_0_.rest_1_.rest, ...), custom_call_target="tpu_custom_call" | custom-call | flops 5000000000 | bytes 7340032 | tf_op jit(solution)/shard_map/scan_forward/pallas_call | solution.py:222
  109.9 9.0 %project.4 = (f32[1024,1024]{1,0:T(8,128)}, bf16[1536,1024]{1,0:T(8,128)(2,1)}) custom-call(s32[32]{0:T(128)} %pad_add_fusion.order_ref, bf16[1024,1536]{1,0:T(8,128)(2,1)} %fusion.12.x_ref.lhs_ref, bf16[384,1024]{1,0:T(8,128)(2,1)} %constant_dynamic-update-slice_fusion.p0, bf16[384,1024]{1,0:T(8,128)(2,1)} %copy-done.42, ...), custom_call_target="tpu_custom_call" | custom-call | flops 3221225472 | bytes 13631488 | tf_op jit(solution)/shard_map/project/pallas_call | solution.py:770
  118.9 9.3 %collective-permute-done.24.p1 = bf16[384,1536]{1,0:T(8,128)(2,1)} collective-permute-done((bf16[384,1536]{1,0:T(8,128)(2,1)}, bf16[384,1536]{1,0:T(8,128)(2,1)}, u32[]{:S(2)}, u32[]{:S(2)}) %collective-permute-start.24) | collective-permute-done | bytes 1179680 | tf_op jit(solution)/shard_map/ppermute | solution.py:630
  128.8 15.8 %scan_forward.4 = (bf16[1024,3072]{1,0:T(8,128)(2,1)}, bf16[1024,3072]{1,0:T(8,128)(2,1)}, bf16[512,3072]{1,0:T(8,128)(2,1)}, bf16[1024,3072]{1,0:T(8,128)(2,1)}, f32[8,128]{1,0:T(8,128)}) custom-call(f32[1024,1024]{1,0:T(8,128)} %get-tuple-element.197.pc_ref.halo_ref, ...), custom_call_target="tpu_custom_call", output_to_operand_aliasing={{0}: (9, {}), {1}: (10, {}), {2}: (11, {}), {3}: (12, {})} | custom-call | flops 10000000000 | bytes 14680064 | tf_op jit(solution)/shard_map/scan_forward/pallas_call | solution.py:222
  147.3 11.7 %project.5 = (f32[1024,1536]{1,0:T(8,128)}, bf16[1536,1536]{1,0:T(8,128)(2,1)}) custom-call(s32[32]{0:T(128)} %pad_add_fusion.order_ref, bf16[1024,1536]{1,0:T(8,128)(2,1)} %fusion.12.x_ref.lhs_ref, bf16[384,1536]{1,0:T(8,128)(2,1)} %constant_dynamic-update-slice_fusion.14.p0, bf16[384,1536]{1,0:T(8,128)(2,1)} %collective-permute-done.24.p1, ...), custom_call_target="tpu_custom_call" | custom-call | flops 4831838208 | bytes 18874368 | tf_op jit(solution)/shard_map/project/pallas_call | solution.py:770
  159.0 22.0 %scan_forward.5 = (bf16[1024,3072]{1,0:T(8,128)(2,1)}, bf16[1024,3072]{1,0:T(8,128)(2,1)}, bf16[512,3072]{1,0:T(8,128)(2,1)}, bf16[1024,3072]{1,0:T(8,128)(2,1)}, f32[8,128]{1,0:T(8,128)}) custom-call(f32[1024,1536]{1,0:T(8,128)} %get-tuple-element.208.pc_ref.halo_ref, ...), custom_call_target="tpu_custom_call", output_to_operand_aliasing={{0}: (9, {}), {1}: (10, {}), {2}: (11, {}), {3}: (12, {})} | custom-call | flops 15000000512 | bytes 22020096 | tf_op jit(solution)/shard_map/scan_forward/pallas_call | solution.py:222
  186.4 20.9 %project_gate.1 = (bf16[1024,3072]{1,0:T(8,128)(2,1)}, bf16[1536,3072]{1,0:T(8,128)(2,1)}, bf16[1024,3072]{1,0:T(8,128)(2,1)}, f32[1024,128]{1,0:T(8,128)}) custom-call(s32[32]{0:T(128)} %pad_add_fusion.order_ref, bf16[1024,1536]{1,0:T(8,128)(2,1)} %fusion.12.x_ref.lhs_ref, bf16[384,3072]{1,0:T(8,128)(2,1)} %constant_dynamic-update-slice_fusion.18.p0, ...), custom_call_target="tpu_custom_call" | custom-call | flops 9663676416 | bytes 53477376 | tf_op jit(solution)/shard_map/project_gate/pallas_call | solution.py:824
  216.5 15.1 %weight_grad.5 = (bf16[1536,1536]{1,0:T(8,128)(2,1)}, bf16[1536,1536]{1,0:T(8,128)(2,1)}) custom-call(s32[32]{0:T(128)} %fusion.41.place_ref, bf16[1024,3072]{1,0:T(8,128)(2,1)} %get-tuple-element.225.lhs_ref.zg_ref, bf16[1024,1536]{1,0:T(8,128)(2,1)} %fusion.17.rhs_ref), custom_call_target="tpu_custom_call" | custom-call | flops 9663676416 | bytes 18874368 | tf_op jit(solution)/shard_map/weight_grad/pallas_call | solution.py:976
  233.4 20.2 %project_out.1 = (bf16[3072,1536]{1,0:T(8,128)(2,1)}, bf16[1024,1536]{1,0:T(8,128)(2,1)}, f32[1024,1]{1,0:T(8,128)}) custom-call(s32[32]{0:T(128)} %pad_add_fusion.order_ref, bf16[1024,3072]{1,0:T(8,128)(2,1)} %get-tuple-element.225.lhs_ref.zg_ref, f32[1024,1]{1,0:T(8,128)} %copy.78.inverse_ref, bf16[1024,1536]{1,0:T(8,128)(2,1)} %tokens_ref, ...), custom_call_target="tpu_custom_call" | custom-call | flops 9663676416 | bytes 34603008 | tf_op jit(solution)/shard_map/project_out/pallas_call | solution.py:909
  260.7 23.2 %multiply_convert_fusion = (bf16[1024,3072]{1,0:T(8,128)(2,1)}, bf16[1024,3072]{1,0:T(8,128)(2,1)}) fusion(bf16[1024,3072]{1,0:T(8,128)(2,1)} %get-tuple-element.218.y_ref, f32[1024]{0:T(1024)S(1)} %multiply_reduce_fusion.2, bf16[1024,3072]{1,0:T(8,128)(2,1)} %get-tuple-element.232, f32[3072]{0:T(1024)S(1)} %reshape.340, f32[1024]{0:T(1024)S(1)} %add_rsqrt_fusion, ...), kind=kOutput, calls=%fused_computation.15 | convolution fusion | flops 9726590976 | bytes 37769216 | tf_op jit(solution)/shard_map/dot_general | solution.py:27
  288.6 15.8 %weight_grad.6 = (bf16[768,3072]{1,0:T(8,128)(2,1)}, bf16[768,3072]{1,0:T(8,128)(2,1)}) custom-call(s32[32]{0:T(128)} %fusion.41.place_ref, bf16[1024,1536]{1,0:T(8,128)(2,1)} %fusion.12.x_ref.lhs_ref, bf16[1024,3072]{1,0:T(8,128)(2,1)} %get-tuple-element.235.rhs_ref), custom_call_target="tpu_custom_call" | custom-call | flops 9663676416 | bytes 18874368 | tf_op jit(solution)/shard_map/weight_grad/pallas_call | solution.py:976
  304.4 15.5 %fusion.53 = f32[1024,1536]{1,0:T(8,128)} fusion(bf16[1024,3072]{1,0:T(8,128)(2,1)} %get-tuple-element.235.rhs_ref, bf16[1536,3072]{1,0:T(8,128)(2,1)} %get-tuple-element.236), kind=kOutput, calls=%fused_computation.198 | convolution fusion | flops 9663676416 | bytes 22020096 | tf_op jit(solution)/shard_map/dot_general | solution.py:27
  329.0 51.3 %scan_backward.3 = (bf16[1024,1536]{1,0:T(8,128)(2,1)}, f32[5,8,1536]{2,1,0:T(8,128)}, f32[8,1536]{1,0:T(8,128)}, f32[1024,256]{1,0:T(8,128)}, f32[1024,256]{1,0...) custom-call(bf16[1024,3072]{1,0:T(8,128)(2,1)} %get-tuple-element.269.dy_ref, ...), custom_call_target="tpu_custom_call" | custom-call | flops 35999997952 | bytes 18874368 | tf_op jit(solution)/shard_map/scan_backward/pallas_call | solution.py:556
  382.5 9.7 %weight_grad.7 = (bf16[768,1536]{1,0:T(8,128)(2,1)}, bf16[768,1536]{1,0:T(8,128)(2,1)}) custom-call(s32[32]{0:T(128)} %fusion.41.place_ref, bf16[1024,1536]{1,0:T(8,128)(2,1)} %fusion.12.x_ref.lhs_ref, bf16[1024,1536]{1,0:T(8,128)(2,1)} %get-tuple-element.248.rhs_ref), custom_call_target="tpu_custom_call" | custom-call | flops 4831838208 | bytes 11010048 | tf_op jit(solution)/shard_map/weight_grad/pallas_call | solution.py:976
  392.9 10.7 %convolution_add_fusion = f32[1024,1536]{1,0:T(8,128)} fusion(f32[1024,1536]{1,0:T(8,128)} %fusion.53, bf16[1024,1536]{1,0:T(8,128)(2,1)} %get-tuple-element.248.rhs_ref, bf16[1536,1536]{1,0:T(8,128)(2,1)} %get-tuple-element.249), kind=kOutput, calls=%fused_computation.32 | convolution fusion | flops 4833411072 | bytes 20447232 | tf_op jit(solution)/shard_map/dot_general | solution.py:27
  414.1 36.3 %scan_backward.4 = (bf16[1024,1024]{1,0:T(8,128)(2,1)}, f32[5,8,1024]{2,1,0:T(8,128)}, f32[8,1024]{1,0:T(8,128)}, f32[1024,256]{1,0:T(8,128)}, f32[1024,256]{1,0...) custom-call(bf16[1024,3072]{1,0:T(8,128)(2,1)} %get-tuple-element.269.dy_ref, ...), custom_call_target="tpu_custom_call" | custom-call | flops 24000000000 | bytes 12582912 | tf_op jit(solution)/shard_map/scan_backward/pallas_call | solution.py:556
  454.9 8.0 %weight_grad.8 = (bf16[768,1024]{1,0:T(8,128)(2,1)}, bf16[768,1024]{1,0:T(8,128)(2,1)}) custom-call(s32[32]{0:T(128)} %fusion.41.place_ref, bf16[1024,1536]{1,0:T(8,128)(2,1)} %fusion.12.x_ref.lhs_ref, bf16[1024,1024]{1,0:T(8,128)(2,1)} %get-tuple-element.263.rhs_ref), custom_call_target="tpu_custom_call" | custom-call | flops 3221225472 | bytes 8388608 | tf_op jit(solution)/shard_map/weight_grad/pallas_call | solution.py:976
  465.5 8.2 %convolution_add_fusion.2 = f32[1024,1536]{1,0:T(8,128)} fusion(f32[1024,1536]{1,0:T(8,128)} %convolution_add_fusion, bf16[1024,1024]{1,0:T(8,128)(2,1)S(1)} %copy-done.45, bf16[1536,1024]{1,0:T(8,128)(2,1)} %get-tuple-element.264), kind=kOutput, calls=%fused_computation.34 | convolution fusion | flops 3222798336 | bytes 17825792 | tf_op jit(solution)/shard_map/dot_general | solution.py:27
  486.1 24.9 %scan_backward.5 = (bf16[1024,1024]{1,0:T(8,128)(2,1)}, f32[5,8,512]{2,1,0:T(8,128)}, f32[8,512]{1,0:T(8,128)}, f32[5,8,256]{2,1,0:T(8,128)}, f32[2,8,128]{2,1,0:T(8,128)}) custom-call(bf16[1024,3072]{1,0:T(8,128)(2,1)} %get-tuple-element.269.dy_ref, bf16[1024,3072]{1,0:T(8,128)(2,1)} %get-tuple-element.241.x_ref, ...), custom_call_target="tpu_custom_call" | custom-call | flops 12000000000 | bytes 6291456 | tf_op jit(solution)/shard_map/scan_backward/pallas_call | solution.py:556
  522.2 8.1 %weight_grad.9 = (bf16[768,1024]{1,0:T(8,128)(2,1)}, bf16[768,1024]{1,0:T(8,128)(2,1)}) custom-call(s32[32]{0:T(128)} %fusion.41.place_ref, bf16[1024,1536]{1,0:T(8,128)(2,1)} %fusion.12.x_ref.lhs_ref, bf16[1024,1024]{1,0:T(8,128)(2,1)} %get-tuple-element.283.rhs_ref), custom_call_target="tpu_custom_call" | custom-call | flops 3221225472 | bytes 8388608 | tf_op jit(solution)/shard_map/weight_grad/pallas_call | solution.py:976
  536.5 8.0 %convolution_add_fusion.1 = f32[1024,1536]{1,0:T(8,128)S(1)} fusion(f32[1024,1536]{1,0:T(8,128)} %convolution_add_fusion.2, bf16[1024,1024]{1,0:T(8,128)(2,1)} %get-tuple-element.283.rhs_ref, bf16[1536,1024]{1,0:T(8,128)(2,1)} %get-tuple-element.284), kind=kOutput, calls=%fused_computation.33 | convolution fusion | flops 3222798336 | bytes 17825792 | tf_op jit(solution)/shard_map/dot_general | solution.py:27
  549.9 7.0 %collective-permute-done.54 = bf16[384,1024]{1,0:T(8,128)(2,1)S(1)} collective-permute-done((bf16[384,1024]{1,0:T(8,128)(2,1)S(1)}, bf16[384,1024]{1,0:T(8,128)(2,1)S(1)}, u32[]{:S(2)}, u32[]{:S(2)}) %collective-permute-start.54) | collective-permute-done | bytes 786464 | tf_op jit(solution)/shard_map/ppermute | solution.py:630
  562.1 7.5 %collective-permute-done.55 = bf16[192,1024]{1,0:T(8,128)(2,1)S(1)} collective-permute-done((bf16[192,1024]{1,0:T(8,128)(2,1)S(1)}, bf16[192,1024]{1,0:T(8,128)(2,1)S(1)}, u32[]{:S(2)}, u32[]{:S(2)}) %collective-permute-start.55) | collective-permute-done | bytes 393248 | tf_op jit(solution)/shard_map/ppermute | solution.py:630
  (371 shorter events, 214.7 us)
Async XLA Ops:
  65.6 19.5 %collective-permute-start.13 = (bf16[48,3072]{1,0:T(8,128)(2,1)S(1)}, bf16[48,3072]{1,0:T(8,128)(2,1)S(1)}, u32[]{:S(2)}, u32[]{:S(2)}) collective-permute-start(bf16[48,3072]{1,0:T(8,128)(2,1)S(1)} %copy-done.18), channel_id=1, source_target_pairs={{0,16},{1,17},{2,18},{3,19},{4,20},{5,21},{6,22},{7,23},{8,24},{9,... | collective-permute-start | bytes 884744 | tf_op jit(solution)/shard_map/ppermute | solution.py:630
  73.5 25.3 %collective-permute-start.18 = (bf16[192,1536]{1,0:T(8,128)(2,1)}, bf16[192,1536]{1,0:T(8,128)(2,1)S(1)}, u32[]{:S(2)}, u32[]{:S(2)}) collective-permute-start(bf16[192,1536]{1,0:T(8,128)(2,1)} %get-tuple-element.324), channel_id=1, source_target_pairs={{0,8},{1,9},{2,10},{3,11},{4,12},{5,13},{6,14},{7,15},{8,0},{9,1},... | collective-permute-start | bytes 1769480 | tf_op jit(solution)/shard_map/ppermute | solution.py:630
  105.4 22.8 %collective-permute-start.24 = (bf16[384,1536]{1,0:T(8,128)(2,1)}, bf16[384,1536]{1,0:T(8,128)(2,1)}, u32[]{:S(2)}, u32[]{:S(2)}) collective-permute-start(bf16[384,1536]{1,0:T(8,128)(2,1)} %constant_dynamic-update-slice_fusion.14.p0), channel_id=1, source_target_pairs={{0,4},{1,3},{2,6},{3,1},{4,0},{5,7},{6,2},{7,5},{8,12},{9,11},{10,... | collective-permute-start | bytes 3538952 | tf_op jit(solution)/shard_map/ppermute | solution.py:630
  108.2 36.4 %collective-permute-start.21 = (bf16[192,1536]{1,0:T(8,128)(2,1)S(1)}, bf16[192,1536]{1,0:T(8,128)(2,1)S(1)}, u32[]{:S(2)}, u32[]{:S(2)}) collective-permute-start(bf16[192,1536]{1,0:T(8,128)(2,1)S(1)} %get-tuple-element.319), channel_id=1, source_target_pairs={{0,2},{1,5},{2,0},{3,7},{4,6},{5,1},{6,4},{7,3},{8,10},{9,13},{10,... | collective-permute-start | bytes 1769480 | tf_op jit(solution)/shard_map/ppermute | solution.py:630
  109.9 34.7 %collective-permute-start.20 = (bf16[192,3072]{1,0:T(8,128)(2,1)}, bf16[192,3072]{1,0:T(8,128)(2,1)S(1)}, u32[]{:S(2)}, u32[]{:S(2)}) collective-permute-start(bf16[192,3072]{1,0:T(8,128)(2,1)} %get-tuple-element.315), channel_id=1, source_target_pairs={{0,8},{1,9},{2,10},{3,11},{4,12},{5,13},{6,14},{7,15},{8,0},{9,1},... | collective-permute-start | bytes 3538952 | tf_op jit(solution)/shard_map/ppermute | solution.py:630
  145.7 35.3 %collective-permute-start.26 = (bf16[384,3072]{1,0:T(8,128)(2,1)}, bf16[384,3072]{1,0:T(8,128)(2,1)}, u32[]{:S(2)}, u32[]{:S(2)}) collective-permute-start(bf16[384,3072]{1,0:T(8,128)(2,1)} %constant_dynamic-update-slice_fusion.18.p0), channel_id=1, source_target_pairs={{0,1},{1,0},{2,3},{3,2},{4,5},{5,4},{6,7},{7,6},{8,9},{9,8},{10,11... | collective-permute-start | bytes 7077896 | tf_op jit(solution)/shard_map/ppermute | solution.py:634
  145.7 35.3 %collective-permute-start.25 = (bf16[384,3072]{1,0:T(8,128)(2,1)}, bf16[384,3072]{1,0:T(8,128)(2,1)}, u32[]{:S(2)}, u32[]{:S(2)}) collective-permute-start(bf16[384,3072]{1,0:T(8,128)(2,1)} %constant_dynamic-update-slice_fusion.18.p0), channel_id=1, source_target_pairs={{0,4},{1,3},{2,6},{3,1},{4,0},{5,7},{6,2},{7,5},{8,12},{9,11},{10,... | collective-permute-start | bytes 7077896 | tf_op jit(solution)/shard_map/ppermute | solution.py:630
  147.3 33.7 %collective-permute-start.27 = (bf16[384,1536]{1,0:T(8,128)(2,1)}, bf16[384,1536]{1,0:T(8,128)(2,1)S(1)}, u32[]{:S(2)}, u32[]{:S(2)}) collective-permute-start(bf16[384,1536]{1,0:T(8,128)(2,1)} %get-tuple-element.314), channel_id=1, source_target_pairs={{0,8},{1,9},{2,10},{3,11},{4,12},{5,13},{6,14},{7,15},{8,0},{9,1},... | collective-permute-start | bytes 3538952 | tf_op jit(solution)/shard_map/ppermute | solution.py:630
  182.5 29.2 %collective-permute-start.31 = (bf16[768,1536]{1,0:T(8,128)(2,1)}, bf16[768,1536]{1,0:T(8,128)(2,1)}, u32[]{:S(2)}, u32[]{:S(2)}) collective-permute-start(bf16[768,1536]{1,0:T(8,128)(2,1)} %constant_dynamic-update-slice_fusion.25.p0), channel_id=1, source_target_pairs={{0,4},{1,3},{2,6},{3,1},{4,0},{5,7},{6,2},{7,5},{8,12},{9,11},{10,... | collective-permute-start | bytes 7077896 | tf_op jit(solution)/shard_map/ppermute | solution.py:630
  186.4 45.2 %collective-permute-start.32 = (bf16[768,1536]{1,0:T(8,128)(2,1)}, bf16[768,1536]{1,0:T(8,128)(2,1)}, u32[]{:S(2)}, u32[]{:S(2)}) collective-permute-start(bf16[768,1536]{1,0:T(8,128)(2,1)} %constant_dynamic-update-slice_fusion.25.p0), channel_id=1, source_target_pairs={{0,1},{1,0},{2,3},{3,2},{4,5},{5,4},{6,7},{7,6},{8,9},{9,8},{10,11... | collective-permute-start | bytes 7077896 | tf_op jit(solution)/shard_map/ppermute | solution.py:634
  211.6 19.9 %collective-permute-start.33 = (bf16[768,1536]{1,0:T(8,128)(2,1)}, bf16[768,1536]{1,0:T(8,128)(2,1)}, u32[]{:S(2)}, u32[]{:S(2)}) collective-permute-start(bf16[768,1536]{1,0:T(8,128)(2,1)} %collective-permute-done.31.p1), channel_id=1, source_target_pairs={{0,1},{1,0},{2,3},{3,2},{4,5},{5,4},{6,7},{7,6},{8,9},{9,8},{10,11... | collective-permute-start | bytes 7077896 | tf_op jit(solution)/shard_map/ppermute | solution.py:634
  231.6 23.3 %collective-permute-start.34 = (bf16[1536,1536]{1,0:T(8,128)(2,1)}, bf16[1536,1536]{1,0:T(8,128)(2,1)}, u32[]{:S(2)}, u32[]{:S(2)}) collective-permute-start(bf16[1536,1536]{1,0:T(8,128)(2,1)} %get-tuple-element.224), channel_id=1, source_target_pairs={{0,1},{1,0},{2,3},{3,2},{4,5},{5,4},{6,7},{7,6},{8,9},{9,8},{10,11... | collective-permute-start | bytes 14155784 | tf_op jit(solution)/shard_map/ppermute | solution.py:634
  259.4 29.2 %collective-permute-start.35 = (bf16[768,1536]{1,0:T(8,128)(2,1)}, bf16[768,1536]{1,0:T(8,128)(2,1)}, u32[]{:S(2)}, u32[]{:S(2)}) collective-permute-start(bf16[768,1536]{1,0:T(8,128)(2,1)} %add_convert_fusion.1), channel_id=1, source_target_pairs={{0,4},{1,3},{2,6},{3,1},{4,0},{5,7},{6,2},{7,5},{8,12},{9,11},{10,... | collective-permute-start | bytes 7077896 | tf_op jit(solution)/shard_map/ppermute | solution.py:630
  304.4 20.9 %collective-permute-start.36 = (bf16[768,3072]{1,0:T(8,128)(2,1)}, bf16[768,3072]{1,0:T(8,128)(2,1)S(1)}, u32[]{:S(2)}, u32[]{:S(2)}) collective-permute-start(bf16[768,3072]{1,0:T(8,128)(2,1)} %get-tuple-element.234), channel_id=1, source_target_pairs={{0,1},{1,0},{2,3},{3,2},{4,5},{5,4},{6,7},{7,6},{8,9},{9,8},{10,11... | collective-permute-start | bytes 14155784 | tf_op jit(solution)/shard_map/ppermute | solution.py:634
  323.5 56.8 %collective-permute-start.37 = (bf16[384,1536]{1,0:T(8,128)(2,1)}, bf16[384,1536]{1,0:T(8,128)(2,1)S(1)}, u32[]{:S(2)}, u32[]{:S(2)}) collective-permute-start(bf16[384,1536]{1,0:T(8,128)(2,1)} %add_convert_fusion.4), channel_id=1, source_target_pairs={{0,8},{1,9},{2,10},{3,11},{4,12},{5,13},{6,14},{7,15},{8,0},{9,1},... | collective-permute-start | bytes 3538952 | tf_op jit(solution)/shard_map/ppermute | solution.py:630
  327.5 52.8 %collective-permute-start.38 = (bf16[384,3072]{1,0:T(8,128)(2,1)S(1)}, bf16[384,3072]{1,0:T(8,128)(2,1)}, u32[]{:S(2)}, u32[]{:S(2)}) collective-permute-start(bf16[384,3072]{1,0:T(8,128)(2,1)S(1)} %add_convert_fusion), channel_id=1, source_target_pairs={{0,4},{1,3},{2,6},{3,1},{4,0},{5,7},{6,2},{7,5},{8,12},{9,11},{10,... | collective-permute-start | bytes 7077896 | tf_op jit(solution)/shard_map/ppermute | solution.py:630
  406.3 44.1 %collective-permute-start.42 = (bf16[96,1536]{1,0:T(8,128)(2,1)}, bf16[96,1536]{1,0:T(8,128)(2,1)}, u32[]{:S(2)}, u32[]{:S(2)}) collective-permute-start(bf16[96,1536]{1,0:T(8,128)(2,1)} %add_convert_fusion.14), channel_id=1, source_target_pairs={{0,16},{1,17},{2,18},{3,19},{4,20},{5,21},{6,22},{7,23},{8,24},{9,... | collective-permute-start | bytes 884744 | tf_op jit(solution)/shard_map/ppermute | solution.py:630
  411.3 40.7 %collective-permute-start.43 = (bf16[384,1536]{1,0:T(8,128)(2,1)}, bf16[384,1536]{1,0:T(8,128)(2,1)}, u32[]{:S(2)}, u32[]{:S(2)}) collective-permute-start(bf16[384,1536]{1,0:T(8,128)(2,1)} %add_convert_fusion.2), channel_id=1, source_target_pairs={{0,4},{1,3},{2,6},{3,1},{4,0},{5,7},{6,2},{7,5},{8,12},{9,11},{10,... | collective-permute-start | bytes 3538952 | tf_op jit(solution)/shard_map/ppermute | solution.py:630
  412.7 39.3 %collective-permute-start.41 = (bf16[192,3072]{1,0:T(8,128)(2,1)}, bf16[192,3072]{1,0:T(8,128)(2,1)}, u32[]{:S(2)}, u32[]{:S(2)}) collective-permute-start(bf16[192,3072]{1,0:T(8,128)(2,1)} %add_convert_fusion.3), channel_id=1, source_target_pairs={{0,8},{1,9},{2,10},{3,11},{4,12},{5,13},{6,14},{7,15},{8,0},{9,1},... | collective-permute-start | bytes 3538952 | tf_op jit(solution)/shard_map/ppermute | solution.py:630
  477.3 37.2 %collective-permute-start.47 = (bf16[48,3072]{1,0:T(8,128)(2,1)}, bf16[48,3072]{1,0:T(8,128)(2,1)}, u32[]{:S(2)}, u32[]{:S(2)}) collective-permute-start(bf16[48,3072]{1,0:T(8,128)(2,1)} %add_convert_fusion.13), channel_id=1, source_target_pairs={{0,16},{1,17},{2,18},{3,19},{4,20},{5,21},{6,22},{7,23},{8,24},{9,... | collective-permute-start | bytes 884744 | tf_op jit(solution)/shard_map/ppermute | solution.py:630
  481.4 34.8 %collective-permute-start.46 = (bf16[192,1536]{1,0:T(8,128)(2,1)}, bf16[192,1536]{1,0:T(8,128)(2,1)}, u32[]{:S(2)}, u32[]{:S(2)}) collective-permute-start(bf16[192,1536]{1,0:T(8,128)(2,1)} %add_convert_fusion.7), channel_id=1, source_target_pairs={{0,8},{1,9},{2,10},{3,11},{4,12},{5,13},{6,14},{7,15},{8,0},{9,1},... | collective-permute-start | bytes 1769480 | tf_op jit(solution)/shard_map/ppermute | solution.py:630
  485.4 30.8 %collective-permute-start.48 = (bf16[384,1024]{1,0:T(8,128)(2,1)}, bf16[384,1024]{1,0:T(8,128)(2,1)S(1)}, u32[]{:S(2)}, u32[]{:S(2)}) collective-permute-start(bf16[384,1024]{1,0:T(8,128)(2,1)} %add_convert_fusion.6), channel_id=1, source_target_pairs={{0,4},{1,3},{2,6},{3,1},{4,0},{5,7},{6,2},{7,5},{8,12},{9,11},{10,... | collective-permute-start | bytes 2359304 | tf_op jit(solution)/shard_map/ppermute | solution.py:630
  530.4 27.5 %collective-permute-start.60 = (f32[8,1184]{1,0:T(8,128)S(1)}, f32[8,1184]{1,0:T(8,128)S(1)}, u32[]{:S(2)}, u32[]{:S(2)}) collective-permute-start(f32[8,1184]{1,0:T(8,128)S(1)} %slice.557), channel_id=1, source_target_pairs={{0,4},{1,3},{2,6},{3,1},{4,0},{5,7},{6,2},{7,5},{8,12},{9,11},{10,... | collective-permute-start | bytes 113672 | tf_op jit(solution)/shard_map/ppermute | solution.py:630
  558.9 23.4 %collective-permute-start.58 = (bf16[48,1024]{1,0:T(8,128)(2,1)S(1)}, bf16[48,1024]{1,0:T(8,128)(2,1)S(1)}, u32[]{:S(2)}, u32[]{:S(2)}) collective-permute-start(bf16[48,1024]{1,0:T(8,128)(2,1)S(1)} %add_convert_fusion.18), channel_id=1, source_target_pairs={{0,16},{1,17},{2,18},{3,19},{4,20},{5,21},{6,22},{7,23},{8,24},{9,... | collective-permute-start | bytes 294920 | tf_op jit(solution)/shard_map/ppermute | solution.py:630
  (88 other events, 1093.2 us)

commit v6 on v5

--- a/solution.py
+++ b/solution.py
@@ -64,34 +64,32 @@
     return total
 
 
-def prepare(raw_ref, heads_ref, aux_ref, same):
-    aux = aux_ref[...]
+def prepare(raw_ref, heads_ref):
     heads = heads_ref[...]
     step = step_sizes(raw_ref[...], heads)
     row = lax.broadcasted_iota(jnp.int32, (SPAN, SPAN), 0)
     col = lax.broadcasted_iota(jnp.int32, (SPAN, SPAN), 1)
     tri = (row >= col).astype(F32)
     cum = dot_f32(tri, step * heads[1:2], ((1,), (0,)), HIGHEST)
-    for place in range(5):
-        same[place] = lanes_of(aux[:, place : place + 1], SPAN)
-    return step, cum, cum - jnp.log2(step)
+    return cum, cum - jnp.log2(step)
 
 
 def pick(first, columns, at):
     return jnp.where(first, lanes_of(columns[:, at : at + 1], first.shape[0]), lanes_of(columns[:, at + 1 : at + 2], first.shape[0]))
 
 
-def forward_kernel(first_call, base, pc_ref, halo_ref, raw_ref, cw_ref, aux_ref, seg_ref, heads_ref, skip_ref, *rest):
+def forward_kernel(first_call, base, pc_ref, halo_ref, cw_ref, same, seg_col_ref, seg_ref, skip_ref, *rest):
     rest = list(rest)
     if first_call:
-        bc_ref, bc_halo_ref, bcw_ref = [rest.pop(0) for _ in range(3)]
+        raw_ref, heads_ref, bc_ref, bc_halo_ref, bcw_ref = [rest.pop(0) for _ in range(5)]
         x_out, y_out, st_out, slope_out, mark, bc_out, bc_slope_out = [rest.pop(0) for _ in range(7)]
+        pack, shifted_out, cum_out, cum_rows, w_rows = [rest.pop(0) for _ in range(5)]
     else:
-        bc_out = rest.pop(0)
+        bc_out, pack, cum_rows, w_rows = [rest.pop(0) for _ in range(4)]
         mark_ref = rest[4]
         rest = rest[5:]
         x_out, y_out, st_out, slope_out, mark = [rest.pop(0) for _ in range(5)]
-    state, scores, block, same, pack, cum_rows, w_rows, keep_row, b_t, ext, ext_bc = rest
+    state, scores, block, keep_row, b_t, ext, ext_bc = rest
     span = pl.program_id(0)
     group = pl.program_id(1)
     group_head = base + GROUP * group
@@ -103,11 +101,14 @@
 
     @pl.when(group == 0)
     def _():
-        step, cum, shifted = prepare(raw_ref, heads_ref, aux_ref, same)
-        last = cum[SPAN - 1 : SPAN]
-        pack[...] = cum
-        cum_rows[...] = shifted.T
-        w_rows[...] = (jnp.exp2(last - shifted) * same[4]).T
+        if first_call:
+            cum, shifted = prepare(raw_ref, heads_ref)
+            pack[...] = cum
+            shifted_out[...] = shifted
+            cum_out[...] = cum.T
+            cum_rows[...] = shifted.T
+            w_rows[...] = (jnp.exp2(cum[SPAN - 1 : SPAN] - shifted) * same[4]).T
+        last = pack[SPAN - 1 : SPAN]
         keep_row[...] = jnp.broadcast_to(jnp.exp2(last) * same[3, SPAN - 1 : SPAN], (8, TILE))
         if first_call:
             ext_bc[0:8] = bc_halo_ref[...]
@@ -119,7 +120,7 @@
             bc_slope_out[...] = (gate + both * (1.0 - gate)).astype(BF16)
         row = lax.broadcasted_iota(jnp.int32, (SPAN, SPAN), 0)
         col = lax.broadcasted_iota(jnp.int32, (SPAN, SPAN), 1)
-        linked = (row >= col) & (aux_ref[:, 5:6] == seg_ref[...])
+        linked = (row >= col) & (seg_col_ref[...] == seg_ref[...])
         block[...] = jnp.where(linked, 0.0, NEG)
         scores[...] = mm_nt(bc_out[:, N:], bc_out[:, :N])
         b_t[...] = bc_out[:, :N].astype(F32).T
@@ -174,7 +175,7 @@
         state[:, tile] = old * wide(keeps) + wide(fresh)
 
 
-def run_forward(pc, first_x, pc_bc, conv_x, conv_bc, aux, seg_row, heads, skip, start, count, bcv, before):
+def run_forward(pc, first_x, pc_bc, conv_x, conv_bc, same, seg_col, seg_row, heads, skip, start, count, shared, before):
     tokens = pc.shape[0]
     spans = tokens // SPAN
     di = skip.shape[1]
@@ -188,14 +189,17 @@
     in_specs = [
         pl.BlockSpec((SPAN, width), lambda s, g: (s, first_x + g)),
         pl.BlockSpec((8, width), lambda s, g: (halo(s), first_x + g)),
-        pl.BlockSpec((SPAN, TILE), lambda s, g: (s, 2)),
         pl.BlockSpec((8, width), lambda s, g: (0, start + g)),
-        pl.BlockSpec((SPAN, 8), lambda s, g: (s, 0)),
+        pl.BlockSpec((5, SPAN, TILE), lambda s, g: (0, s, 0)),
+        pl.BlockSpec((SPAN, 1), lambda s, g: (s, 0)),
         pl.BlockSpec((1, SPAN), lambda s, g: (0, s)),
-        pl.BlockSpec((8, TILE), lambda s, g: (0, 0)),
         pl.BlockSpec((1, width), lambda s, g: (0, start + g)),
     ]
-    args = [pc, pc, pc_bc, conv_x, aux, seg_row, heads, skip]
+    args = [pc, pc, conv_x, same, seg_col, seg_row, skip]
+    column_spec = pl.BlockSpec((SPAN, TILE), lambda s, g: (s, 0))
+    row_spec = pl.BlockSpec((TILE, SPAN), lambda s, g: (s, 0))
+    columns_shape = jax.ShapeDtypeStruct((tokens, TILE), F32)
+    rows_shape = jax.ShapeDtypeStruct((spans * TILE, SPAN), F32)
     mark_spec = pl.BlockSpec((8, TILE), lambda s, g: (0, 0))
     out_specs = [wide, wide, pl.BlockSpec((N, width), lambda s, g: (s, start + g)), wide, mark_spec]
     out_shape = [
@@ -207,18 +211,21 @@
     ]
     if first_call:
         in_specs += [
+            pl.BlockSpec((SPAN, TILE), lambda s, g: (s, 2)),
+            pl.BlockSpec((8, TILE), lambda s, g: (0, 0)),
             pl.BlockSpec((SPAN, 2 * N), lambda s, g: (s, 0)),
             pl.BlockSpec((8, 2 * N), lambda s, g: (halo(s), 0)),
             pl.BlockSpec((8, 2 * N), lambda s, g: (0, 0)),
         ]
-        args += [pc_bc, pc_bc, conv_bc]
-        out_specs += [bcv_spec, bcv_spec]
+        args += [pc_bc, heads, pc_bc, pc_bc, conv_bc]
+        out_specs += [bcv_spec, bcv_spec, column_spec, column_spec, row_spec, row_spec, row_spec]
         out_shape += [jax.ShapeDtypeStruct((tokens, 2 * N), BF16)] * 2
+        out_shape += [columns_shape] * 2 + [rows_shape] * 3
         aliases = {}
     else:
-        in_specs += [bcv_spec, any_spec, any_spec, any_spec, any_spec, mark_spec]
-        args += [bcv, *before]
-        aliases = {9: 0, 10: 1, 11: 2, 12: 3}
+        in_specs += [bcv_spec, column_spec, row_spec, row_spec, any_spec, any_spec, any_spec, any_spec, mark_spec]
+        args += [*shared, *before]
+        aliases = {11: 0, 12: 1, 13: 2, 14: 3}
     return pl.pallas_call(
         functools.partial(forward_kernel, first_call, start * GROUP),
         grid_spec=pltpu.PrefetchScalarGridSpec(
@@ -230,10 +237,6 @@
                 pltpu.VMEM((N, own), F32),
                 pltpu.VMEM((SPAN, SPAN), F32),
                 pltpu.VMEM((SPAN, SPAN), F32),
-                pltpu.VMEM((5, SPAN, TILE), F32),
-                pltpu.VMEM((SPAN, TILE), F32),
-                pltpu.VMEM((TILE, SPAN), F32),
-                pltpu.VMEM((TILE, SPAN), F32),
                 pltpu.VMEM((8, TILE), F32),
                 pltpu.VMEM((N, SPAN), F32),
                 pltpu.VMEM((SPAN + 8, width), F32),
@@ -271,19 +274,20 @@
 
 def backward_kernel(
     first_call, last_call, base,
-    dy_ref, x_ref, bcv_ref, st_ref, slope_ref, pc_ref, raw_ref, cw_ref, aux_ref, seg_ref, heads_ref, skip_ref, *rest,
+    dy_ref, x_ref, bcv_ref, st_ref, slope_ref, pc_ref, cw_ref, same, seg_col_ref, seg_ref, skip_ref,
+    cum_ref, shifted_ref, cum_rows, *rest,
 ):
     rest = list(rest)
     before = None if first_call else [rest.pop(0) for _ in range(4)]
     if last_call:
-        bc_ref, bc_slope_ref, bcw_ref = [rest.pop(0) for _ in range(3)]
+        raw_ref, heads_ref, bc_ref, bc_slope_ref, bcw_ref = [rest.pop(0) for _ in range(5)]
     dproj_out, dcw_out, dskip_out = [rest.pop(0) for _ in range(3)]
     if last_call:
         dbcw_out, dhead_out = [rest.pop(0) for _ in range(2)]
     else:
         after_out = [rest.pop(0) for _ in range(4)]
     (
-        dstate, scores, block, dscores, same, pack, last_row, cum_rows, c_t,
+        dstate, scores, block, dscores, pack, c_t,
         carry, carry_bc, d_bc, per_row, dcum_rows, dlast,
     ) = rest
     back = pl.program_id(0)
@@ -311,14 +315,11 @@
 
     @pl.when(group == 0)
     def _():
-        step, cum, shifted = prepare(raw_ref, heads_ref, aux_ref, same)
-        entry = jnp.exp2(cum) * same[3]
-        pack[...] = jnp.where(lane < 64, shifted, pltpu.roll(entry, 64, 1))
-        last_row[...] = jnp.broadcast_to(cum[SPAN - 1 : SPAN], (8, TILE))
-        cum_rows[...] = cum.T
+        entry = jnp.exp2(cum_ref[...]) * same[3]
+        pack[...] = jnp.where(lane < 64, shifted_ref[...], pltpu.roll(entry, 64, 1))
         row = lax.broadcasted_iota(jnp.int32, (SPAN, SPAN), 0)
         col = lax.broadcasted_iota(jnp.int32, (SPAN, SPAN), 1)
-        linked = (row <= col) & (aux_ref[:, 5:6] == seg_ref[...])
+        linked = (row <= col) & (seg_col_ref[...] == seg_ref[...])
         block[...] = jnp.where(linked, 0.0, NEG)
         scores[...] = mm_nt(keys, query)
         c_t[...] = query.T
@@ -336,7 +337,7 @@
 
     shift = lax.rem(TILE - group_head, TILE)
     cols = pltpu.roll(pack[...], shift, 1)
-    last_cum = pltpu.roll(last_row[...], shift, 1)[0:1]
+    last_cum = pltpu.roll(jnp.broadcast_to(cum_ref[SPAN - 1 : SPAN], (8, TILE)), shift, 1)[0:1]
     keep_mask = same[3, SPAN - 1 : SPAN]
     first = lane < P_SIZE
     lane_row = lax.broadcasted_iota(jnp.int32, (2 * TILE, TILE), 0) // P_SIZE
@@ -486,7 +487,8 @@
 
 
 def run_backward(
-    dy, x, bcv, states, slope, bc_slope, pc, first_x, pc_bc, conv_x, conv_bc, aux, seg_row, heads, skip, start, count, last, before
+    dy, x, bcv, states, slope, bc_slope, pc, first_x, pc_bc, conv_x, conv_bc, same, seg_col, seg_row, heads, skip,
+    cums, start, count, last, before,
 ):
     tokens, di = dy.shape
     spans = tokens // SPAN
@@ -524,24 +526,28 @@
         pl.BlockSpec((N, width), lambda s, g: (turn(s), start + g)),
         wide,
         pl.BlockSpec((SPAN, width), lambda s, g: (turn(s), first_x + g)),
-        pl.BlockSpec((SPAN, TILE), lambda s, g: (turn(s), 2)),
         pl.BlockSpec((8, width), lambda s, g: (0, start + g)),
-        pl.BlockSpec((SPAN, 8), lambda s, g: (turn(s), 0)),
+        pl.BlockSpec((5, SPAN, TILE), lambda s, g: (0, turn(s), 0)),
+        pl.BlockSpec((SPAN, 1), lambda s, g: (turn(s), 0)),
         pl.BlockSpec((1, SPAN), lambda s, g: (0, turn(s))),
-        pl.BlockSpec((8, TILE), lambda s, g: (0, 0)),
         pl.BlockSpec((1, width), lambda s, g: (0, start + g)),
+        pl.BlockSpec((SPAN, TILE), lambda s, g: (turn(s), 0)),
+        pl.BlockSpec((SPAN, TILE), lambda s, g: (turn(s), 0)),
+        pl.BlockSpec((TILE, SPAN), lambda s, g: (turn(s), 0)),
     ]
-    args = [dy, x, bcv, states, slope, pc, pc_bc, conv_x, aux, seg_row, heads, skip]
+    args = [dy, x, bcv, states, slope, pc, conv_x, same, seg_col, seg_row, skip, *cums]
     if before is not None:
         in_specs += sums_specs
         args += before
     if last:
         in_specs += [
+            pl.BlockSpec((SPAN, TILE), lambda s, g: (turn(s), 2)),
+            pl.BlockSpec((8, TILE), lambda s, g: (0, 0)),
             pl.BlockSpec((SPAN, 2 * N), lambda s, g: (turn(s), 0)),
             pl.BlockSpec((SPAN, 2 * N), lambda s, g: (turn(s), 0)),
             pl.BlockSpec((8, 2 * N), lambda s, g: (0, 0)),
         ]
-        args += [pc_bc, bc_slope, conv_bc]
+        args += [pc_bc, heads, pc_bc, bc_slope, conv_bc]
         out_specs += [
             pl.BlockSpec((5, 8, 2 * N), lambda s, g: (0, 0, 0)),
             pl.BlockSpec((2, 8, TILE), lambda s, g: (0, 0, 0)),
@@ -565,10 +571,7 @@
                 pltpu.VMEM((SPAN, SPAN), F32),
                 pltpu.VMEM((SPAN, SPAN), F32),
                 pltpu.VMEM((SPAN, SPAN), F32),
-                pltpu.VMEM((5, SPAN, TILE), F32),
                 pltpu.VMEM((SPAN, TILE), F32),
-                pltpu.VMEM((8, TILE), F32),
-                pltpu.VMEM((TILE, SPAN), F32),
                 pltpu.VMEM((N, SPAN), BF16),
                 pltpu.VMEM((3, 8, own), F32),
                 pltpu.VMEM((3, 8, 2 * N), F32),
@@ -599,10 +602,8 @@
     cols.append((seg == jnp.repeat(before, SPAN)).astype(F32))
     cols.append((seg == jnp.repeat(ends, SPAN)).astype(F32))
     value = seg.astype(F32)
-    cols.append(value)
-    cols.append(value)
-    cols.append(value)
-    return jnp.stack(cols, axis=1), value[None, :]
+    same = jnp.broadcast_to(jnp.stack(cols, axis=0)[:, :, None], (5, length, TILE))
+    return same, value[:, None], value[None, :]
 
 
 def head_rows(dt_bias, a_log):
@@ -704,9 +705,11 @@
             return send, self.terms[-1]
         return self.terms[-1], self.terms[-1]
 
-    def finish(self):
+    def finish(self, *ahead):
         while self.left:
             self.step()
+        if ahead:
+            self.terms[-1] = after(self.terms[-1], *ahead)
         return self.rows(0, self.block)
 
 
@@ -1076,12 +1079,12 @@
     normed = (unit * full_gain_in).astype(BF16)
     if hypercube:
         normed = after(normed, *normed_tie)
-    aux, seg_row = seg_facts(seg_ids[0])
+    same, seg_col, seg_row = seg_facts(seg_ids[0])
     heads = head_rows(dt_bias, a_log)
     skip = jnp.repeat(d_skip, P_SIZE)[None]
 
     pcs, w_parts = [], []
-    bcv = written = mark = None
+    shared = written = mark = None
     project_tie = ()
     for index, call in enumerate(calls):
         if hypercube:
@@ -1103,11 +1106,12 @@
         pcs.append((pc, 1 if index == 0 else 0))
         w_parts.append(w_part)
         written = run_forward(
-            pc, pcs[-1][1], pcs[0][0], conv_x, conv_bc, aux, seg_row, heads, skip, *call, bcv, written
+            pc, pcs[-1][1], pcs[0][0], conv_x, conv_bc, same, seg_col, seg_row, heads, skip, *call, shared, written
         )
         mark = written[4]
         if index == 0:
-            bcv, bc_slope = written[5:]
+            bcv, bc_slope, cum, shifted, cum_lines, shifted_lines, weight_lines = written[5:]
+            shared = bcv, cum, shifted_lines, weight_lines
         written = written[:5]
         if hypercube and index == 0:
             done = last_pair[1], got[2], got[3], mark
@@ -1171,8 +1175,8 @@
     for index, call in reversed(list(enumerate(calls))):
         pc, first_x = pcs[index]
         dpart, dcw, dskip, *sums = run_backward(
-            dy, x, bcv, states, slope, bc_slope, pc, first_x, pcs[0][0], conv_x, conv_bc, aux, seg_row, heads, skip, *call,
-            index == 0, sums,
+            dy, x, bcv, states, slope, bc_slope, pc, first_x, pcs[0][0], conv_x, conv_bc,
+            same, seg_col, seg_row, heads, skip, (cum, shifted, cum_lines), *call, index == 0, sums,
         )
         parts[index] = (dpart, dcw, dskip)
         if not hypercube:
@@ -1181,13 +1185,14 @@
         done = *got, dpart
         if index == 2:
             sent, out_got = out_sum.step(*done)
-            early = (sent,)
+            early = (sent, *done)
         elif index == 1:
             sent, gate_got = gate_sum.step(*done)
-            early = (sent,)
+            early = (sent, *done)
         else:
-            early, late = zip(grad_sums[2].step(*done), grad_sums[1].step(*done))
-        grad = weight_grad(normed, after(dpart, *early, *done), place, 0, dpart.shape[1])
+            sent, late = grad_sums[1].step(*got)
+            early = (sent, *got)
+        grad = weight_grad(normed, after(dpart, *early), place, 0, dpart.shape[1])
         grad_sums[index] = Scatter(grad, in_block)
         swap_sent, swap_got = grad_sums[index].step()
         if index == 2:
@@ -1196,19 +1201,24 @@
             sent, got = zip(out_sum.step(out_got, *done), gate_sum.step(got[1], *done), grad_sums[2].step(*done))
             dy = after(dy, *sent, *done)
         elif index == 1:
-            scaled = scaled + mm_nt(after(dpart, swap_sent), w_parts[index])
-            done = swap_got, scaled
-            sent, got = zip(gate_sum.step(gate_got, *done), grad_sums[2].step(got[2], *done), grad_sums[1].step(*done))
-            dy = after(dy, *sent, *done)
+            sent, got = zip(gate_sum.step(gate_got, swap_sent), grad_sums[2].step(got[2], swap_sent))
+            got = got + (swap_got,)
+            dy = after(dy, *sent, swap_sent)
         else:
-            sent, late = zip(grad_sums[2].step(*late, grad[0]), grad_sums[1].step(*late, grad[0]))
-            scaled = scaled + mm_nt(after(dpart, swap_sent, *sent), w_parts[index])
-            sent, got = grad_sums[0].step(swap_got, *late, scaled)
-            grad_sums[1].step(*late, scaled)
-            scaled = after(scaled, sent)
-    dbcw, dhead = sums
+            sent, late = zip(grad_sums[1].step(late, swap_sent), grad_sums[2].step(swap_sent))
+            sent, got = grad_sums[0].step(swap_got, *sent)
+            scaled = scaled + mm_nt(after(dpart, sent), w_parts[index])
+    dbcw, dhead = after(tuple(sums), swap_sent) if hypercube else sums
+    dbcw, dhead = after(tuple(sums), swap_sent) if hypercube else sums
     dcw = jnp.concatenate([parts[index][1] for index in range(len(calls))] + [dbcw], axis=2)
     dskip = jnp.concatenate([parts[index][2] for index in range(len(calls))], axis=1)
+    if hypercube:
+        ties = [swap_sent, swap_got, got]
+        sent, got = grad_sums[0].step(got, scaled)
+        ties.append(got)
+        sent, late = zip(grad_sums[1].step(*late, sent), grad_sums[2].step(*late, sent))
+        late = late[0]
+        scaled = scaled + mm_nt(after(parts[1][0], *sent), w_parts[1])
     scaled = scaled * full_gain_in
     inner = jnp.mean(unit * scaled, axis=1, keepdims=True)
     grad_tokens = (cot + rscale * (scaled - unit * inner)).astype(BF16)
@@ -1226,15 +1236,20 @@
     small_grad = jnp.concatenate([conv_part, jnp.broadcast_to(per_head[None], (shards, 3 * H))], axis=1)
     real = w_in.shape[1] - 2 * di
     if hypercube:
-        small_sum = reduce_small(small_grad, (grad[0], swap_got, got, grad_tokens))[0]
-        sent, got = grad_sums[0].step(got, grad_tokens)
-        grad_sums[1].step(sent)
-        _, got = grad_sums[0].step(got)
+        last_sent, got = grad_sums[0].step(got, grad_tokens)
+        ties.append(got)
+        grad_sums[1].step(late, last_sent)
         grad_sums[0].step(got)
-        gate_part, *rest = [each.finish() for each in (gate_sum, grad_sums[2], grad_sums[1], grad_sums[0])]
-        rest = rest[::-1]
-        own = jnp.concatenate([gate_part, rest[0][:, 4 * N :], *rest[1:], rest[0][:, :real]], axis=1)
-        sum_w_in = both_cores(own)
+        small_sum = reduce_small(small_grad, ties)[0]
+        whole = [gate_sum.finish(last_sent), grad_sums[2].finish(last_sent)]
+        whole = [both_cores(part) for part in whole + [grad_sums[1].finish(), grad_sums[0].finish()]]
+        head = whole.pop()
+        whole = [whole[0], head[:, 4 * N :], whole[2], whole[1], head[:, :real]]
+        sum_w_in = jnp.concatenate(whole, axis=1)
+        edges = [0, di, di + width, di + 3 * width, 2 * di, w_in.shape[1]]
+        gain_sum = 0.0
+        for part, a, b in zip(whole, edges, edges[1:]):
+            gain_sum = gain_sum + jnp.sum(part * w_in[:, a:b].astype(F32), axis=1)
         sum_w_out = both_cores(out_sum.finish())
     else:
         grad_w_out = dot_f32(zg, cot_scaled, ((0,), (0,)))
@@ -1247,7 +1262,8 @@
         sum_w_in = lax.psum_scatter(grad_w_in, "shard", scatter_dimension=0, tiled=True)
         sum_w_out = lax.psum_scatter(grad_w_out, "shard", scatter_dimension=0, tiled=True)
         sum_w_in, sum_w_out = lax.psum((sum_w_in, sum_w_out), "rep")
-    grad_gain_in = jnp.sum(sum_w_in * w_in.astype(F32), axis=1) / gain_in.astype(F32)
+        gain_sum = jnp.sum(sum_w_in * w_in.astype(F32), axis=1)
+    grad_gain_in = gain_sum / gain_in.astype(F32)
     grad_gain_out = jnp.sum(sum_w_out * w_out.astype(F32), axis=1) / gain_out.astype(F32)
     cut = taps * conv_local
     head_at = cut + conv_local
@@ -1277,10 +1293,11 @@
     places = jnp.asarray([reach(order) for order in ORDERS], jnp.int32)[core] ^ lax.axis_index("shard")
     hot = (places[:, None] == jnp.arange(16, dtype=jnp.int32)[None, :]).astype(F32)
     total = dot_f32(hot, rows, ((1,), (0,)), HIGHEST)
-    for stage, tie in zip((3, 2, 1, 0), ties):
+    for stage, tie in zip((3, 2, 1, 0), ties[:4]):
         cut = 1 << stage
         total = after(total, tie)
         total = total[:cut] + exchange(total[cut:], stage)
+    total = after(total, ties[4])
     return total + swap_cores(total)
 
 

time: 600 us -> 587 us (0.978)
  Pallas kernels: 288 us -> 279 us
  waiting for transfers between devices: 63.7 us -> 55.4 us
    pallas_call x3, Pallas kernels: 112 us -> 104 us  [run_backward(): pl.pallas_call(functools.partial(backward_kernel, before is None, last, s...]
    ppermute x48, waiting for transfers between devices: 63.1 us -> 55.1 us  [exchange(): return lax.ppermute(values, ('shard', 'rep'), pairs)]
    unnamed x108 -> x113, local copies, waits for them, and re-layouts: 12.7 us -> 16.6 us
  transfers between devices with their start and end apart: 66 -> 69, of which waited for: 15 -> 15; matrix products, arithmetic and copies ran while one was open for 26% -> 27% of each run, Pallas kernels for 44% -> 44%
where the time goes in v6:
time: 587 us; the launch traced here: 580 us
  Pallas kernels  279 us (48%)
  other arithmetic  74.9 us (13%)
  matrix products  65.2 us (11%)
  starting transfers between devices  57.3 us (10%)
  waiting for transfers between devices  55.4 us (9%)
  local copies, waits for them, and re-layouts  45.9 us (8%)
    pallas_call x3, Pallas kernels, run_backward(): pl.pallas_call(functools.partial(backward_kernel, before is None, last, s...  104 us
    dot_general x7, matrix products, dot_f32(): lax.dot_general(a, b, ((contract[0], contract[1]), ((), ())), preferred_e...  65.2 us
    pallas_call x5, Pallas kernels, weight_grad(): pl.pallas_call(functools.partial(weight_grad_kernel, block), grid_spec=pl...  57 us
    ppermute x48, waiting for transfers between devices, exchange(): return lax.ppermute(values, ('shard', 'rep'), pairs)  55.1 us
    ppermute x48, starting transfers between devices, exchange(): return lax.ppermute(values, ('shard', 'rep'), pairs)  53.3 us
    pallas_call x3, Pallas kernels, run_forward(): pl.pallas_call(functools.partial(forward_kernel, first_call, start * GROU...  46.8 us
    convert_element_type x20, other arithmetic, step(): send = self.rows(cut, 2 * cut).astype(BF16)  39.4 us
    pallas_call x3, Pallas kernels, project(): pl.pallas_call(functools.partial(project_kernel, block, width), grid_spec...  30.1 us
  transfers between devices with their start and end apart: 69, of which 15 were waited for; matrix products, arithmetic and copies ran while one was open for 27% of the time, Pallas kernels for 44%

profile of v6, /device:TPU:0, one launch (start us, length us, event | category | flops | bytes accessed | tf_op | source)
XLA Modules:
  0.0 580.0 jit_solution(186655454547456656)
XLA Ops:
  74.9 9.3 %project.3 = (f32[1024,1024]{1,0:T(8,128)}, bf16[1536,1024]{1,0:T(8,128)(2,1)}) custom-call(s32[32]{0:T(128)} %pad_add_fusion.order_ref, bf16[1024,1536]{1,0:T(8,128)(2,1)} %fusion.12.x_ref.lhs_ref, bf16[384,1024]{1,0:T(8,128)(2,1)} %pad_maximum_fusion.2.p0, bf16[384,1024]{1,0:T(8,128)(2,1)} %collective-permute-done.11.p1, ...), custom_call_target="tpu_custom_call" | custom-call | flops 3221225472 | bytes 13631488 | tf_op jit(solution)/shard_map/project/pallas_call | solution.py:773
  90.0 11.4 %scan_forward.3 = (bf16[1024,3072]{1,0:T(8,128)(2,1)}, bf16[1024,3072]{1,0:T(8,128)(2,1)}, bf16[512,3072]{1,0:T(8,128)(2,1)}, bf16[1024,3072]{1,0:T(8,128)(2,1)}...) custom-call(f32[1024,1024]{1,0:T(8,128)} %get-tuple-element.194.pc_r, ...), custom_call_target="tpu_custom_call" | custom-call | flops 5000000000 | bytes 7340032 | tf_op jit(solution)/shard_map/scan_forward/pallas_call | solution.py:229
  109.1 9.0 %project.4 = (f32[1024,1024]{1,0:T(8,128)}, bf16[1536,1024]{1,0:T(8,128)(2,1)}) custom-call(s32[32]{0:T(128)} %pad_add_fusion.order_ref, bf16[1024,1536]{1,0:T(8,128)(2,1)} %fusion.12.x_ref.lhs_ref, bf16[384,1024]{1,0:T(8,128)(2,1)} %constant_dynamic-update-slice_fusion.p0, bf16[384,1024]{1,0:T(8,128)(2,1)} %copy-done.44, ...), custom_call_target="tpu_custom_call" | custom-call | flops 3221225472 | bytes 13631488 | tf_op jit(solution)/shard_map/project/pallas_call | solution.py:773
  118.1 9.3 %collective-permute-done.24.p1 = bf16[384,1536]{1,0:T(8,128)(2,1)} collective-permute-done((bf16[384,1536]{1,0:T(8,128)(2,1)}, bf16[384,1536]{1,0:T(8,128)(2,1)}, u32[]{:S(2)}, u32[]{:S(2)}) %collective-permute-start.24) | collective-permute-done | bytes 1179680 | tf_op jit(solution)/shard_map/ppermute | solution.py:631
  127.9 14.7 %scan_forward.4 = (bf16[1024,3072]{1,0:T(8,128)(2,1)}, bf16[1024,3072]{1,0:T(8,128)(2,1)}, bf16[512,3072]{1,0:T(8,128)(2,1)}, bf16[1024,3072]{1,0:T(8,128)(2,1)}, f32[8,128]{1,0:T(8,128)}) custom-call(f32[1024,1024]{1,0:T(8,128)} %get-tuple-element.208.pc_ref.halo_ref, ...), custom_call_target="tpu_custom_call", output_to_operand_aliasing={{0}: (11, {}), {1}: (12, {}), {2}: (13, {}), {3}: (14, {})} | custom-call | flops 10000000000 | bytes 14680064 | tf_op jit(solution)/shard_map/scan_forward/pallas_call | solution.py:229
  145.4 11.8 %project.5 = (f32[1024,1536]{1,0:T(8,128)}, bf16[1536,1536]{1,0:T(8,128)(2,1)}) custom-call(s32[32]{0:T(128)} %pad_add_fusion.order_ref, bf16[1024,1536]{1,0:T(8,128)(2,1)} %fusion.12.x_ref.lhs_ref, bf16[384,1536]{1,0:T(8,128)(2,1)} %constant_dynamic-update-slice_fusion.14.p0, bf16[384,1536]{1,0:T(8,128)(2,1)} %collective-permute-done.24.p1, ...), custom_call_target="tpu_custom_call" | custom-call | flops 4831838208 | bytes 18874368 | tf_op jit(solution)/shard_map/project/pallas_call | solution.py:773
  157.1 20.7 %scan_forward.5 = (bf16[1024,3072]{1,0:T(8,128)(2,1)}, bf16[1024,3072]{1,0:T(8,128)(2,1)}, bf16[512,3072]{1,0:T(8,128)(2,1)}, bf16[1024,3072]{1,0:T(8,128)(2,1)}, f32[8,128]{1,0:T(8,128)}) custom-call(f32[1024,1536]{1,0:T(8,128)} %get-tuple-element.222.pc_ref.halo_ref, ...), custom_call_target="tpu_custom_call", output_to_operand_aliasing={{0}: (11, {}), {1}: (12, {}), {2}: (13, {}), {3}: (14, {})} | custom-call | flops 15000000512 | bytes 22020096 | tf_op jit(solution)/shard_map/scan_forward/pallas_call | solution.py:229
  183.3 20.9 %project_gate.1 = (bf16[1024,3072]{1,0:T(8,128)(2,1)}, bf16[1536,3072]{1,0:T(8,128)(2,1)}, bf16[1024,3072]{1,0:T(8,128)(2,1)}, f32[1024,128]{1,0:T(8,128)}) custom-call(s32[32]{0:T(128)} %pad_add_fusion.order_ref, bf16[1024,1536]{1,0:T(8,128)(2,1)} %fusion.12.x_ref.lhs_ref, bf16[384,3072]{1,0:T(8,128)(2,1)} %constant_dynamic-update-slice_fusion.18.p0, ...), custom_call_target="tpu_custom_call" | custom-call | flops 9663676416 | bytes 53477376 | tf_op jit(solution)/shard_map/project_gate/pallas_call | solution.py:827
  213.3 15.2 %weight_grad.5 = (bf16[1536,1536]{1,0:T(8,128)(2,1)}, bf16[1536,1536]{1,0:T(8,128)(2,1)}) custom-call(s32[32]{0:T(128)} %fusion.43.place_ref, bf16[1024,3072]{1,0:T(8,128)(2,1)} %get-tuple-element.239.lhs_ref.zg_ref, bf16[1024,1536]{1,0:T(8,128)(2,1)} %fusion.17.rhs_ref), custom_call_target="tpu_custom_call" | custom-call | flops 9663676416 | bytes 18874368 | tf_op jit(solution)/shard_map/weight_grad/pallas_call | solution.py:979
  230.3 20.2 %project_out.1 = (bf16[3072,1536]{1,0:T(8,128)(2,1)}, bf16[1024,1536]{1,0:T(8,128)(2,1)}, f32[1024,1]{1,0:T(8,128)}) custom-call(s32[32]{0:T(128)} %pad_add_fusion.order_ref, bf16[1024,3072]{1,0:T(8,128)(2,1)} %get-tuple-element.239.lhs_ref.zg_ref, f32[1024,1]{1,0:T(8,128)} %copy.61.inverse_ref, bf16[1024,1536]{1,0:T(8,128)(2,1)} %tokens_ref, ...), custom_call_target="tpu_custom_call" | custom-call | flops 9663676416 | bytes 34603008 | tf_op jit(solution)/shard_map/project_out/pallas_call | solution.py:912
  257.7 23.4 %multiply_convert_fusion = (bf16[1024,3072]{1,0:T(8,128)(2,1)}, bf16[1024,3072]{1,0:T(8,128)(2,1)}) fusion(bf16[1024,3072]{1,0:T(8,128)(2,1)} %get-tuple-element.232.y_ref, f32[1024]{0:T(1024)S(1)} %multiply_reduce_fusion.3, bf16[1024,3072]{1,0:T(8,128)(2,1)} %get-tuple-element.246, f32[3072]{0:T(1024)S(1)} %reshape.268, f32[1024]{0:T(1024)S(1)} %add_rsqrt_fusion, ...), kind=kOutput, calls=%fused_computation.15 | convolution fusion | flops 9726590976 | bytes 37769216 | tf_op jit(solution)/shard_map/dot_general | solution.py:27
  285.5 15.8 %weight_grad.6 = (bf16[768,3072]{1,0:T(8,128)(2,1)}, bf16[768,3072]{1,0:T(8,128)(2,1)}) custom-call(s32[32]{0:T(128)} %fusion.43.place_ref, bf16[1024,1536]{1,0:T(8,128)(2,1)} %fusion.12.x_ref.lhs_ref, bf16[1024,3072]{1,0:T(8,128)(2,1)} %get-tuple-element.249.rhs_ref), custom_call_target="tpu_custom_call" | custom-call | flops 9663676416 | bytes 18874368 | tf_op jit(solution)/shard_map/weight_grad/pallas_call | solution.py:979
  301.4 15.6 %fusion.56 = f32[1024,1536]{1,0:T(8,128)} fusion(bf16[1024,3072]{1,0:T(8,128)(2,1)} %get-tuple-element.249.rhs_ref, bf16[1536,3072]{1,0:T(8,128)(2,1)} %get-tuple-element.250), kind=kOutput, calls=%fused_computation.213 | convolution fusion | flops 9663676416 | bytes 22020096 | tf_op jit(solution)/shard_map/dot_general | solution.py:27
  326.0 49.7 %scan_backward.3 = (bf16[1024,1536]{1,0:T(8,128)(2,1)}, f32[5,8,1536]{2,1,0:T(8,128)}, f32[8,1536]{1,0:T(8,128)}, f32[1024,256]{1,0:T(8,128)}, f32[1024,256]{1,0...) custom-call(bf16[1024,3072]{1,0:T(8,128)(2,1)} %get-tuple-element.281.dy_ref, ...), custom_call_target="tpu_custom_call" | custom-call | flops 35999997952 | bytes 18874368 | tf_op jit(solution)/shard_map/scan_backward/pallas_call | solution.py:562
  378.7 9.7 %weight_grad.7 = (bf16[768,1536]{1,0:T(8,128)(2,1)}, bf16[768,1536]{1,0:T(8,128)(2,1)}) custom-call(s32[32]{0:T(128)} %fusion.43.place_ref, bf16[1024,1536]{1,0:T(8,128)(2,1)} %fusion.12.x_ref.lhs_ref, bf16[1024,1536]{1,0:T(8,128)(2,1)} %get-tuple-element.264.rhs_ref), custom_call_target="tpu_custom_call" | custom-call | flops 4831838208 | bytes 11010048 | tf_op jit(solution)/shard_map/weight_grad/pallas_call | solution.py:979
  389.1 10.7 %convolution_add_fusion = f32[1024,1536]{1,0:T(8,128)} fusion(f32[1024,1536]{1,0:T(8,128)} %fusion.56, bf16[1024,1536]{1,0:T(8,128)(2,1)} %get-tuple-element.264.rhs_ref, bf16[1536,1536]{1,0:T(8,128)(2,1)} %get-tuple-element.265), kind=kOutput, calls=%fused_computation.33 | convolution fusion | flops 4833411072 | bytes 20447232 | tf_op jit(solution)/shard_map/dot_general | solution.py:27
  411.1 7.6 %collective-permute-done.42 = bf16[96,1536]{1,0:T(8,128)(2,1)S(1)} collective-permute-done((bf16[96,1536]{1,0:T(8,128)(2,1)S(1)}, bf16[96,1536]{1,0:T(8,128)(2,1)S(1)}, u32[]{:S(2)}, u32[]{:S(2)}) %collective-permute-start.42) | collective-permute-done | bytes 294944 | tf_op jit(solution)/shard_map/ppermute | solution.py:631
  420.3 34.8 %scan_backward.4 = (bf16[1024,1024]{1,0:T(8,128)(2,1)}, f32[5,8,1024]{2,1,0:T(8,128)}, f32[8,1024]{1,0:T(8,128)}, f32[1024,256]{1,0:T(8,128)}, f32[1024,256]{1,0...) custom-call(bf16[1024,3072]{1,0:T(8,128)(2,1)} %get-tuple-element.281.dy_ref, ...), custom_call_target="tpu_custom_call" | custom-call | flops 24000000000 | bytes 12582912 | tf_op jit(solution)/shard_map/scan_backward/pallas_call | solution.py:562
  462.2 8.0 %weight_grad.8 = (bf16[768,1024]{1,0:T(8,128)(2,1)}, bf16[768,1024]{1,0:T(8,128)(2,1)}) custom-call(s32[32]{0:T(128)} %fusion.43.place_ref, bf16[1024,1536]{1,0:T(8,128)(2,1)} %fusion.12.x_ref.lhs_ref, bf16[1024,1024]{1,0:T(8,128)(2,1)} %get-tuple-element.301.rhs_ref), custom_call_target="tpu_custom_call" | custom-call | flops 3221225472 | bytes 8388608 | tf_op jit(solution)/shard_map/weight_grad/pallas_call | solution.py:979
  477.3 19.6 %scan_backward.5 = (bf16[1024,1024]{1,0:T(8,128)(2,1)}, f32[5,8,512]{2,1,0:T(8,128)}, f32[8,512]{1,0:T(8,128)}, f32[5,8,256]{2,1,0:T(8,128)}, f32[2,8,128]{2,1,0:T(8,128)}) custom-call(bf16[1024,3072]{1,0:T(8,128)(2,1)} %get-tuple-element.281.dy_ref, bf16[1024,3072]{1,0:T(8,128)(2,1)} %get-tuple-element.255.x_ref, ...), custom_call_target="tpu_custom_call" | custom-call | flops 12000000000 | bytes 6291456 | tf_op jit(solution)/shard_map/scan_backward/pallas_call | solution.py:562
  502.0 8.4 %weight_grad.9 = (bf16[768,1024]{1,0:T(8,128)(2,1)}, bf16[768,1024]{1,0:T(8,128)(2,1)}) custom-call(s32[32]{0:T(128)} %fusion.43.place_ref, bf16[1024,1536]{1,0:T(8,128)(2,1)} %fusion.12.x_ref.lhs_ref, bf16[1024,1024]{1,0:T(8,128)(2,1)} %get-tuple-element.296.rhs_ref), custom_call_target="tpu_custom_call" | custom-call | flops 3221225472 | bytes 8388608 | tf_op jit(solution)/shard_map/weight_grad/pallas_call | solution.py:979
  522.9 8.3 %convolution_add_fusion.1 = f32[1024,1536]{1,0:T(8,128)} fusion(f32[1024,1536]{1,0:T(8,128)} %convolution_add_fusion, bf16[1024,1024]{1,0:T(8,128)(2,1)S(1)} %copy-done.47, bf16[1536,1024]{1,0:T(8,128)(2,1)} %get-tuple-element.297), kind=kOutput, calls=%fused_computation.34 | convolution fusion | flops 3222798336 | bytes 17825792 | tf_op jit(solution)/shard_map/dot_general | solution.py:27
  540.1 6.9 %fusion.13 = (f32[1024]{0:T(1024)S(1)}, f32[1024,1536]{1,0:T(8,128)S(1)}) fusion(bf16[1024,1536]{1,0:T(8,128)(2,1)S(1)} %copy-done.2, f32[1024]{0:T(1024)S(1)} %copy-done.33, f32[1536]{0:T(1024)S(1)} %copy-done.35, f32[1024,1536]{1,0:T(8,128)} %convolution_add_fusion.1, bf16[1024,1024]{1,0:T(8,128)(2,1)} %get-tuple-element.301.rhs_ref, ...), kind=kOutput, calls=%fused_computation.24 | convolution fusion | flops 3230661632 | bytes 20985856 | tf_op jit(solution)/shard_map/dot_general | solution.py:27
  569.4 5.1 collective-permute-done.56
  (389 shorter events, 211.8 us)
Async XLA Ops:
  64.8 19.4 %collective-permute-start.13 = (bf16[48,3072]{1,0:T(8,128)(2,1)S(1)}, bf16[48,3072]{1,0:T(8,128)(2,1)S(1)}, u32[]{:S(2)}, u32[]{:S(2)}) collective-permute-start(bf16[48,3072]{1,0:T(8,128)(2,1)S(1)} %copy-done.17), channel_id=1, source_target_pairs={{0,16},{1,17},{2,18},{3,19},{4,20},{5,21},{6,22},{7,23},{8,24},{9,... | collective-permute-start | bytes 884744 | tf_op jit(solution)/shard_map/ppermute | solution.py:631
  72.7 28.7 %collective-permute-start.18 = (bf16[192,1536]{1,0:T(8,128)(2,1)}, bf16[192,1536]{1,0:T(8,128)(2,1)S(1)}, u32[]{:S(2)}, u32[]{:S(2)}) collective-permute-start(bf16[192,1536]{1,0:T(8,128)(2,1)} %get-tuple-element.360), channel_id=1, source_target_pairs={{0,8},{1,9},{2,10},{3,11},{4,12},{5,13},{6,14},{7,15},{8,0},{9,1},... | collective-permute-start | bytes 1769480 | tf_op jit(solution)/shard_map/ppermute | solution.py:631
  85.3 18.4 %collective-permute-start.17 = (bf16[96,3072]{1,0:T(8,128)(2,1)S(1)}, bf16[96,3072]{1,0:T(8,128)(2,1)S(1)}, u32[]{:S(2)}, u32[]{:S(2)}) collective-permute-start(bf16[96,3072]{1,0:T(8,128)(2,1)S(1)} %get-tuple-element.363), channel_id=1, source_target_pairs={{0,2},{1,5},{2,0},{3,7},{4,6},{5,1},{6,4},{7,3},{8,10},{9,13},{10,... | collective-permute-start | bytes 1769480 | tf_op jit(solution)/shard_map/ppermute | solution.py:631
  104.6 22.8 %collective-permute-start.24 = (bf16[384,1536]{1,0:T(8,128)(2,1)}, bf16[384,1536]{1,0:T(8,128)(2,1)}, u32[]{:S(2)}, u32[]{:S(2)}) collective-permute-start(bf16[384,1536]{1,0:T(8,128)(2,1)} %constant_dynamic-update-slice_fusion.14.p0), channel_id=1, source_target_pairs={{0,4},{1,3},{2,6},{3,1},{4,0},{5,7},{6,2},{7,5},{8,12},{9,11},{10,... | collective-permute-start | bytes 3538952 | tf_op jit(solution)/shard_map/ppermute | solution.py:631
  107.4 35.3 %collective-permute-start.21 = (bf16[192,1536]{1,0:T(8,128)(2,1)S(1)}, bf16[192,1536]{1,0:T(8,128)(2,1)S(1)}, u32[]{:S(2)}, u32[]{:S(2)}) collective-permute-start(bf16[192,1536]{1,0:T(8,128)(2,1)S(1)} %get-tuple-element.355), channel_id=1, source_target_pairs={{0,2},{1,5},{2,0},{3,7},{4,6},{5,1},{6,4},{7,3},{8,10},{9,13},{10,... | collective-permute-start | bytes 1769480 | tf_op jit(solution)/shard_map/ppermute | solution.py:631
  109.0 33.6 %collective-permute-start.20 = (bf16[192,3072]{1,0:T(8,128)(2,1)}, bf16[192,3072]{1,0:T(8,128)(2,1)S(1)}, u32[]{:S(2)}, u32[]{:S(2)}) collective-permute-start(bf16[192,3072]{1,0:T(8,128)(2,1)} %get-tuple-element.341), channel_id=1, source_target_pairs={{0,8},{1,9},{2,10},{3,11},{4,12},{5,13},{6,14},{7,15},{8,0},{9,1},... | collective-permute-start | bytes 3538952 | tf_op jit(solution)/shard_map/ppermute | solution.py:631
  143.7 34.1 %collective-permute-start.26 = (bf16[384,3072]{1,0:T(8,128)(2,1)}, bf16[384,3072]{1,0:T(8,128)(2,1)}, u32[]{:S(2)}, u32[]{:S(2)}) collective-permute-start(bf16[384,3072]{1,0:T(8,128)(2,1)} %constant_dynamic-update-slice_fusion.18.p0), channel_id=1, source_target_pairs={{0,1},{1,0},{2,3},{3,2},{4,5},{5,4},{6,7},{7,6},{8,9},{9,8},{10,11... | collective-permute-start | bytes 7077896 | tf_op jit(solution)/shard_map/ppermute | solution.py:635
  143.7 34.1 %collective-permute-start.25 = (bf16[384,3072]{1,0:T(8,128)(2,1)}, bf16[384,3072]{1,0:T(8,128)(2,1)}, u32[]{:S(2)}, u32[]{:S(2)}) collective-permute-start(bf16[384,3072]{1,0:T(8,128)(2,1)} %constant_dynamic-update-slice_fusion.18.p0), channel_id=1, source_target_pairs={{0,4},{1,3},{2,6},{3,1},{4,0},{5,7},{6,2},{7,5},{8,12},{9,11},{10,... | collective-permute-start | bytes 7077896 | tf_op jit(solution)/shard_map/ppermute | solution.py:631
  145.4 32.5 %collective-permute-start.27 = (bf16[384,1536]{1,0:T(8,128)(2,1)}, bf16[384,1536]{1,0:T(8,128)(2,1)S(1)}, u32[]{:S(2)}, u32[]{:S(2)}) collective-permute-start(bf16[384,1536]{1,0:T(8,128)(2,1)} %get-tuple-element.340), channel_id=1, source_target_pairs={{0,8},{1,9},{2,10},{3,11},{4,12},{5,13},{6,14},{7,15},{8,0},{9,1},... | collective-permute-start | bytes 3538952 | tf_op jit(solution)/shard_map/ppermute | solution.py:631
  179.3 29.2 %collective-permute-start.31 = (bf16[768,1536]{1,0:T(8,128)(2,1)}, bf16[768,1536]{1,0:T(8,128)(2,1)}, u32[]{:S(2)}, u32[]{:S(2)}) collective-permute-start(bf16[768,1536]{1,0:T(8,128)(2,1)} %constant_dynamic-update-slice_fusion.25.p0), channel_id=1, source_target_pairs={{0,4},{1,3},{2,6},{3,1},{4,0},{5,7},{6,2},{7,5},{8,12},{9,11},{10,... | collective-permute-start | bytes 7077896 | tf_op jit(solution)/shard_map/ppermute | solution.py:631
  183.2 45.3 %collective-permute-start.32 = (bf16[768,1536]{1,0:T(8,128)(2,1)}, bf16[768,1536]{1,0:T(8,128)(2,1)}, u32[]{:S(2)}, u32[]{:S(2)}) collective-permute-start(bf16[768,1536]{1,0:T(8,128)(2,1)} %constant_dynamic-update-slice_fusion.25.p0), channel_id=1, source_target_pairs={{0,1},{1,0},{2,3},{3,2},{4,5},{5,4},{6,7},{7,6},{8,9},{9,8},{10,11... | collective-permute-start | bytes 7077896 | tf_op jit(solution)/shard_map/ppermute | solution.py:635
  208.5 20.0 %collective-permute-start.33 = (bf16[768,1536]{1,0:T(8,128)(2,1)}, bf16[768,1536]{1,0:T(8,128)(2,1)}, u32[]{:S(2)}, u32[]{:S(2)}) collective-permute-start(bf16[768,1536]{1,0:T(8,128)(2,1)} %collective-permute-done.31.p1), channel_id=1, source_target_pairs={{0,1},{1,0},{2,3},{3,2},{4,5},{5,4},{6,7},{7,6},{8,9},{9,8},{10,11... | collective-permute-start | bytes 7077896 | tf_op jit(solution)/shard_map/ppermute | solution.py:635
  228.5 23.3 %collective-permute-start.34 = (bf16[1536,1536]{1,0:T(8,128)(2,1)}, bf16[1536,1536]{1,0:T(8,128)(2,1)}, u32[]{:S(2)}, u32[]{:S(2)}) collective-permute-start(bf16[1536,1536]{1,0:T(8,128)(2,1)} %get-tuple-element.238), channel_id=1, source_target_pairs={{0,1},{1,0},{2,3},{3,2},{4,5},{5,4},{6,7},{7,6},{8,9},{9,8},{10,11... | collective-permute-start | bytes 14155784 | tf_op jit(solution)/shard_map/ppermute | solution.py:635
  256.4 29.2 %collective-permute-start.35 = (bf16[768,1536]{1,0:T(8,128)(2,1)}, bf16[768,1536]{1,0:T(8,128)(2,1)}, u32[]{:S(2)}, u32[]{:S(2)}) collective-permute-start(bf16[768,1536]{1,0:T(8,128)(2,1)} %add_convert_fusion.1), channel_id=1, source_target_pairs={{0,4},{1,3},{2,6},{3,1},{4,0},{5,7},{6,2},{7,5},{8,12},{9,11},{10,... | collective-permute-start | bytes 7077896 | tf_op jit(solution)/shard_map/ppermute | solution.py:631
  301.3 21.0 %collective-permute-start.36 = (bf16[768,3072]{1,0:T(8,128)(2,1)}, bf16[768,3072]{1,0:T(8,128)(2,1)S(1)}, u32[]{:S(2)}, u32[]{:S(2)}) collective-permute-start(bf16[768,3072]{1,0:T(8,128)(2,1)} %get-tuple-element.248), channel_id=1, source_target_pairs={{0,1},{1,0},{2,3},{3,2},{4,5},{5,4},{6,7},{7,6},{8,9},{9,8},{10,11... | collective-permute-start | bytes 14155784 | tf_op jit(solution)/shard_map/ppermute | solution.py:635
  320.5 55.2 %collective-permute-start.37 = (bf16[384,1536]{1,0:T(8,128)(2,1)}, bf16[384,1536]{1,0:T(8,128)(2,1)S(1)}, u32[]{:S(2)}, u32[]{:S(2)}) collective-permute-start(bf16[384,1536]{1,0:T(8,128)(2,1)} %add_convert_fusion.4), channel_id=1, source_target_pairs={{0,8},{1,9},{2,10},{3,11},{4,12},{5,13},{6,14},{7,15},{8,0},{9,1},... | collective-permute-start | bytes 3538952 | tf_op jit(solution)/shard_map/ppermute | solution.py:631
  324.5 51.2 %collective-permute-start.38 = (bf16[384,3072]{1,0:T(8,128)(2,1)S(1)}, bf16[384,3072]{1,0:T(8,128)(2,1)}, u32[]{:S(2)}, u32[]{:S(2)}) collective-permute-start(bf16[384,3072]{1,0:T(8,128)(2,1)S(1)} %add_convert_fusion), channel_id=1, source_target_pairs={{0,4},{1,3},{2,6},{3,1},{4,0},{5,7},{6,2},{7,5},{8,12},{9,11},{10,... | collective-permute-start | bytes 7077896 | tf_op jit(solution)/shard_map/ppermute | solution.py:631
  408.9 49.0 %collective-permute-start.43 = (bf16[384,1536]{1,0:T(8,128)(2,1)}, bf16[384,1536]{1,0:T(8,128)(2,1)}, u32[]{:S(2)}, u32[]{:S(2)}) collective-permute-start(bf16[384,1536]{1,0:T(8,128)(2,1)} %add_convert_fusion.2), channel_id=1, source_target_pairs={{0,4},{1,3},{2,6},{3,1},{4,0},{5,7},{6,2},{7,5},{8,12},{9,11},{10,... | collective-permute-start | bytes 3538952 | tf_op jit(solution)/shard_map/ppermute | solution.py:631
  410.3 47.6 %collective-permute-start.41 = (bf16[192,3072]{1,0:T(8,128)(2,1)}, bf16[192,3072]{1,0:T(8,128)(2,1)}, u32[]{:S(2)}, u32[]{:S(2)}) collective-permute-start(bf16[192,3072]{1,0:T(8,128)(2,1)} %add_convert_fusion.3), channel_id=1, source_target_pairs={{0,8},{1,9},{2,10},{3,11},{4,12},{5,13},{6,14},{7,15},{8,0},{9,1},... | collective-permute-start | bytes 3538952 | tf_op jit(solution)/shard_map/ppermute | solution.py:631
  420.2 34.9 %collective-permute-start.68 = (f32[96,1536]{1,0:T(8,128)S(1)}, f32[96,1536]{1,0:T(8,128)S(1)}, u32[]{:S(2)}, u32[]{:S(2)}) collective-permute-start(f32[96,1536]{1,0:T(8,128)S(1)} %convert_add_fusion.1), channel_id=1, source_target_pairs={{0,1},{1,0},{2,3},{3,2},{4,5},{5,4},{6,7},{7,6},{8,9},{9,8},{10,11... | collective-permute-start | bytes 1769480 | tf_op jit(solution)/shard_map/ppermute | solution.py:635
  470.2 27.8 %collective-permute-start.45 = (bf16[768,1024]{1,0:T(8,128)(2,1)}, bf16[768,1024]{1,0:T(8,128)(2,1)}, u32[]{:S(2)}, u32[]{:S(2)}) collective-permute-start(bf16[768,1024]{1,0:T(8,128)(2,1)} %get-tuple-element.278), channel_id=1, source_target_pairs={{0,1},{1,0},{2,3},{3,2},{4,5},{5,4},{6,7},{7,6},{8,9},{9,8},{10,11... | collective-permute-start | bytes 4718600 | tf_op jit(solution)/shard_map/ppermute | solution.py:635
  472.5 25.4 %collective-permute-start.47 = (bf16[192,1536]{1,0:T(8,128)(2,1)}, bf16[192,1536]{1,0:T(8,128)(2,1)S(1)}, u32[]{:S(2)}, u32[]{:S(2)}) collective-permute-start(bf16[192,1536]{1,0:T(8,128)(2,1)} %add_convert_fusion.7), channel_id=1, source_target_pairs={{0,8},{1,9},{2,10},{3,11},{4,12},{5,13},{6,14},{7,15},{8,0},{9,1},... | collective-permute-start | bytes 1769480 | tf_op jit(solution)/shard_map/ppermute | solution.py:631
  474.9 23.1 %collective-permute-start.46 = (bf16[48,3072]{1,0:T(8,128)(2,1)}, bf16[48,3072]{1,0:T(8,128)(2,1)}, u32[]{:S(2)}, u32[]{:S(2)}) collective-permute-start(bf16[48,3072]{1,0:T(8,128)(2,1)} %add_convert_fusion.13), channel_id=1, source_target_pairs={{0,16},{1,17},{2,18},{3,19},{4,20},{5,21},{6,22},{7,23},{8,24},{9,... | collective-permute-start | bytes 884744 | tf_op jit(solution)/shard_map/ppermute | solution.py:631
  534.2 20.8 %collective-permute-start.61 = (bf16[48,1536]{1,0:T(8,128)(2,1)S(1)}, bf16[48,1536]{1,0:T(8,128)(2,1)S(1)}, u32[]{:S(2)}, u32[]{:S(2)}) collective-permute-start(bf16[48,1536]{1,0:T(8,128)(2,1)S(1)} %add_convert_fusion.17), channel_id=1, source_target_pairs={{0,16},{1,17},{2,18},{3,19},{4,20},{5,21},{6,22},{7,23},{8,24},{9,... | collective-permute-start | bytes 442376 | tf_op jit(solution)/shard_map/ppermute | solution.py:631
  (94 other events, 1031.1 us)

commit v7 on v6

--- a/solution.py
+++ b/solution.py
@@ -793,7 +793,7 @@
     )(order, x, *pieces, *extra)
 
 
-def gate_kernel(block, width, order_ref, x_ref, p0, p1, p2, p3, y_ref, gain_ref, *rest):
+def gate_kernel(block, width, order_ref, x_ref, p0, p1, p2, p3, y_ref, gain_ref, mark_ref, *rest):
     gate_ref, w_ref, zg_ref, square_ref, buffer, sems = rest[-6:]
     slot = next_tile(order_ref, (p0, p1, p2, p3), buffer, sems, block, width)
     w = buffer[slot]
@@ -816,7 +816,7 @@
         square_ref[rows] += total
 
 
-def gate_project(x, pieces, order, y, gain, so_far, start, full, width=512):
+def gate_project(x, pieces, order, y, gain, mark, so_far, start, full, width=512):
     tokens, depth = x.shape
     columns = pieces[0].shape[1]
     block = depth // BLOCKS
@@ -831,7 +831,7 @@
             grid=(columns // width,),
             in_specs=[pl.BlockSpec((tokens, depth), lambda j, o: (0, 0))]
             + [any_spec] * 4
-            + [wide, pl.BlockSpec((1, width), lambda j, o: (0, at + j))]
+            + [wide, pl.BlockSpec((1, width), lambda j, o: (0, at + j)), pl.BlockSpec((8, TILE), lambda j, o: (0, 0))]
             + [any_spec] * len(extra),
             out_specs=[
                 wide,
@@ -847,14 +847,14 @@
             jax.ShapeDtypeStruct((tokens, full), BF16),
             jax.ShapeDtypeStruct((tokens, TILE), F32),
         ],
-        input_output_aliases={} if so_far is None else {8: 0, 9: 1, 10: 2},
+        input_output_aliases={} if so_far is None else {9: 0, 10: 1, 11: 2},
         cost_estimate=pl.CostEstimate(
             flops=2 * tokens * depth * columns,
             bytes_accessed=4 * depth * columns + 10 * tokens * columns + 2 * tokens * depth,
             transcendentals=tokens * columns,
         ),
         name="project_gate",
-    )(order, x, *pieces, y, gain, *extra)
+    )(order, x, *pieces, y, gain, mark, *extra)
 
 
 def restore_kernel(block, width, order_ref, p0, p1, p2, p3, *rest):
@@ -935,6 +935,49 @@
         ),
         name="project_out",
     )(order, zg, inverse, tokens, cot, *pieces)
+
+
+def gate_back_kernel(cot_ref, w_ref, gate_ref, y_ref, gain_ref, inverse_ref, less_ref, dy_ref, dgate_ref):
+    w = w_ref[...]
+    for i in range(cot_ref.shape[0] // SPAN):
+        rows = slice(i * SPAN, (i + 1) * SPAN)
+        gate = gate_ref[rows].astype(F32)
+        y = y_ref[rows].astype(F32)
+        part = jax.nn.sigmoid(gate)
+        opened = gate * part
+        dz = inverse_ref[rows] * (gain_ref[...] * mm_nt(cot_ref[rows], w)) - (y * opened) * less_ref[rows]
+        dy_ref[rows] = (dz * opened).astype(BF16)
+        dgate_ref[rows] = (dz * y * (part + opened * (1.0 - part))).astype(BF16)
+
+
+def gate_back(cot, w, gate, y, gain, inverse, less, width=512):
+    count, model = cot.shape
+    di = w.shape[0]
+    part = pl.BlockSpec((count, width), lambda i: (0, i))
+    column = pl.BlockSpec((count, 1), lambda i: (0, 0))
+    shape = jax.ShapeDtypeStruct((count, di), BF16)
+    return pl.pallas_call(
+        gate_back_kernel,
+        grid_spec=pltpu.PrefetchScalarGridSpec(
+            num_scalar_prefetch=0,
+            grid=(di // width,),
+            in_specs=[
+                pl.BlockSpec((count, model), lambda i: (0, 0)),
+                pl.BlockSpec((width, model), lambda i: (i, 0)),
+                part,
+                part,
+                pl.BlockSpec((1, width), lambda i: (0, i)),
+                column,
+                column,
+            ],
+            out_specs=[part, part],
+        ),
+        out_shape=[shape, shape],
+        cost_estimate=pl.CostEstimate(
+            flops=2 * count * di * model, bytes_accessed=2 * (di * model + 4 * count * di), transcendentals=count * di
+        ),
+        name="gate_back",
+    )(cot, w, gate, y, gain, inverse, less)
 
 
 def weight_grad_kernel(block, place_ref, lhs_ref, rhs_ref, mine, other, buffer, sems):
@@ -1077,9 +1120,9 @@
     rscale = lax.rsqrt(jnp.mean(inputs * inputs, axis=1, keepdims=True) + EPSILON)
     unit = inputs * rscale
     normed = (unit * full_gain_in).astype(BF16)
+    same, seg_col, seg_row = seg_facts(seg_ids[0])
     if hypercube:
-        normed = after(normed, *normed_tie)
-    same, seg_col, seg_row = seg_facts(seg_ids[0])
+        normed, same = after((normed, same), *normed_tie)
     heads = head_rows(dt_bias, a_log)
     skip = jnp.repeat(d_skip, P_SIZE)[None]
 
@@ -1097,9 +1140,8 @@
                 )
                 pc = after(pc, *sent)
             if index == 1:
-                done = got[0], pc
-                sent, _ = zip(far.swap(*done), far.swap(*done))
-                pc = after(pc, *sent)
+                sent, _ = far.swap(pc)
+                pc = after(pc, sent)
         else:
             w_part = columns(full_w_in, call)
             pc = mm(normed, w_part)
@@ -1118,6 +1160,7 @@
             sent, got = zip(far.step(*done), gate_gather.step(*done), out_gather.step(*done))
             project_tie = sent
         if hypercube and index == 1:
+            far.swap(got[0], mark)
             done = got[1], got[2], mark
             sent, got = zip(gate_gather.step(*done), gate_gather.swap(*done), out_gather.step(*done))
             project_tie = sent
@@ -1128,7 +1171,7 @@
     x, y, states, slope, mark = written
     if hypercube:
         gate, w_gate, zg, squares = gate_project(
-            after(normed, *gate_tie), gate_gather.pieces(), order, y, full_gain_out + mark[0, 0], None, 0, di
+            after(normed, *gate_tie), gate_gather.pieces(), order, y, full_gain_out, mark, None, 0, di
         )
     else:
         w_gate = full_w_in[:, :di]
@@ -1139,13 +1182,11 @@
     inverse = lax.rsqrt(jnp.sum(squares, axis=1, keepdims=True) / di + EPSILON)
     cot = cotangent.astype(F32)
     cot_scaled = (inverse * cot).astype(BF16)
-    y, gate = y.astype(F32), gate.astype(F32)
-    sig = jax.nn.sigmoid(gate)
     sums = None
     parts = {}
     if hypercube:
         in_block = w_in.shape[0] // 2
-        out_tie, out_got = out_gather.swap(out_gather.seen[3], zg)
+        out_tie, out_got = out_gather.swap(cot_scaled)
         out_grad = weight_grad(zg, after(cot_scaled, out_tie), place, 0, model)
         out_sum = Scatter(out_grad, w_out.shape[0] // 2)
         sent, got = out_sum.step(*out_gather.swapped)
@@ -1153,15 +1194,20 @@
             after(zg, sent), inverse, tokens, cotangent, out_gather.pieces(), order
         )
         sent, got = out_sum.step(got, dots)
-        grad_ynorm = mm_nt(after(cotangent, sent), full_w_out)
+        less = inverse * inverse * dots / di
+        dy, dgate = gate_back(
+            after(cotangent, sent), full_w_out, gate, y, full_gain_out, inverse, less
+        )
     else:
         projected = inverse * mm(zg, full_w_out)
         output = (inputs + projected).astype(BF16)
         dots = jnp.sum(cot * projected, axis=1, keepdims=True)
         grad_ynorm = mm_nt(cotangent, full_w_out)
-    dz = inverse * (full_gain_out * grad_ynorm) - (y * (gate * sig)) * (inverse * inverse * dots / di)
-    dy = (dz * (gate * sig)).astype(BF16)
-    dgate = (dz * y * (sig * (1.0 + gate * (1.0 - sig)))).astype(BF16)
+        y, gate = y.astype(F32), gate.astype(F32)
+        sig = jax.nn.sigmoid(gate)
+        dz = inverse * (full_gain_out * grad_ynorm) - (y * (gate * sig)) * (inverse * inverse * dots / di)
+        dy = (dz * (gate * sig)).astype(BF16)
+        dgate = (dz * y * (sig * (1.0 + gate * (1.0 - sig)))).astype(BF16)
     if hypercube:
         gate_grad = weight_grad(normed, after(dgate, got), place, 0, di)
         gate_sum = Scatter(gate_grad, in_block)
@@ -1213,9 +1259,9 @@
     dcw = jnp.concatenate([parts[index][1] for index in range(len(calls))] + [dbcw], axis=2)
     dskip = jnp.concatenate([parts[index][2] for index in range(len(calls))], axis=1)
     if hypercube:
-        ties = [swap_sent, swap_got, got]
+        ties = [swap_sent, sent]
         sent, got = grad_sums[0].step(got, scaled)
-        ties.append(got)
+        ties.append(sent)
         sent, late = zip(grad_sums[1].step(*late, sent), grad_sums[2].step(*late, sent))
         late = late[0]
         scaled = scaled + mm_nt(after(parts[1][0], *sent), w_parts[1])
@@ -1237,12 +1283,13 @@
     real = w_in.shape[1] - 2 * di
     if hypercube:
         last_sent, got = grad_sums[0].step(got, grad_tokens)
-        ties.append(got)
+        ties.append(last_sent)
         grad_sums[1].step(late, last_sent)
-        grad_sums[0].step(got)
+        end_sent, _ = grad_sums[0].step(got)
+        ties.append(end_sent)
         small_sum = reduce_small(small_grad, ties)[0]
-        whole = [gate_sum.finish(last_sent), grad_sums[2].finish(last_sent)]
-        whole = [both_cores(part) for part in whole + [grad_sums[1].finish(), grad_sums[0].finish()]]
+        whole = [each.finish(end_sent) for each in (gate_sum, grad_sums[2], grad_sums[1])]
+        whole = [both_cores(part) for part in whole + [grad_sums[0].finish()]]
         head = whole.pop()
         whole = [whole[0], head[:, 4 * N :], whole[2], whole[1], head[:, :real]]
         sum_w_in = jnp.concatenate(whole, axis=1)

time: 587 us -> 566 us (0.964)
  matrix products: 65.2 us -> 41.7 us
  Pallas kernels: 279 us -> 300 us
  waiting for transfers between devices: 55.4 us -> 37.9 us
    dot_general x7 -> x6, matrix products: 65.2 us -> 41.7 us  [dot_f32(): lax.dot_general(a, b, ((contract[0], contract[1]), ((), ())), preferred_e...]
    pallas_call x0 -> x1, Pallas kernels: none -> 21.2 us  [gate_back(): pl.pallas_call(gate_back_kernel, grid_spec=pltpu.PrefetchScalarGridSpec(n...]
    ppermute x48, waiting for transfers between devices: 55.1 us -> 36.1 us  [exchange(): return lax.ppermute(values, ('shard', 'rep'), pairs)]
    unnamed x113 -> x115, local copies, waits for them, and re-layouts: 16.6 us -> 19 us
  transfers between devices with their start and end apart: 69 -> 69, of which waited for: 15 -> 15; matrix products, arithmetic and copies ran while one was open for 27% -> 23% of each run, Pallas kernels for 44% -> 49%
where the time goes in v7:
time: 566 us; the launch traced here: 560 us
  Pallas kernels  300 us (53%)
  other arithmetic  70.3 us (12%)
  starting transfers between devices  61.2 us (11%)
  local copies, waits for them, and re-layouts  47.1 us (8%)
  matrix products  41.7 us (7%)
  waiting for transfers between devices  37.9 us (7%)
    pallas_call x3, Pallas kernels, run_backward(): pl.pallas_call(functools.partial(backward_kernel, before is None, last, s...  104 us
    pallas_call x5, Pallas kernels, weight_grad(): pl.pallas_call(functools.partial(weight_grad_kernel, block), grid_spec=pl...  57.1 us
    ppermute x48, starting transfers between devices, exchange(): return lax.ppermute(values, ('shard', 'rep'), pairs)  56.2 us
    pallas_call x3, Pallas kernels, run_forward(): pl.pallas_call(functools.partial(forward_kernel, first_call, start * GROU...  46.9 us
    dot_general x6, matrix products, dot_f32(): lax.dot_general(a, b, ((contract[0], contract[1]), ((), ())), preferred_e...  41.7 us
    convert_element_type x20, other arithmetic, step(): send = self.rows(cut, 2 * cut).astype(BF16)  37.2 us
    ppermute x48, waiting for transfers between devices, exchange(): return lax.ppermute(values, ('shard', 'rep'), pairs)  36.1 us
    pallas_call x3, Pallas kernels, project(): pl.pallas_call(functools.partial(project_kernel, block, width), grid_spec...  29.9 us
  transfers between devices with their start and end apart: 69, of which 15 were waited for; matrix products, arithmetic and copies ran while one was open for 23% of the time, Pallas kernels for 49%

profile of v7, /device:TPU:0, one launch (start us, length us, event | category | flops | bytes accessed | tf_op | source)
XLA Modules:
  0.0 560.0 jit_solution(785169377291736969)
XLA Ops:
  59.9 4.8 collective-permute-done.11.p1
  78.9 9.2 %project.3 = (f32[1024,1024]{1,0:T(8,128)}, bf16[1536,1024]{1,0:T(8,128)(2,1)}) custom-call(s32[32]{0:T(128)} %pad_add_fusion.order_ref, bf16[1024,1536]{1,0:T(8,128)(2,1)} %fusion.3.x_ref.lhs_ref, bf16[384,1024]{1,0:T(8,128)(2,1)} %pad_maximum_fusion.2.p0, bf16[384,1024]{1,0:T(8,128)(2,1)} %collective-permute-done.11.p1, ...), custom_call_target="tpu_custom_call" | custom-call | flops 3221225472 | bytes 13631488 | tf_op jit(solution)/shard_map/project/pallas_call | solution.py:773
  91.8 11.5 %scan_forward.3 = (bf16[1024,3072]{1,0:T(8,128)(2,1)}, bf16[1024,3072]{1,0:T(8,128)(2,1)}, bf16[512,3072]{1,0:T(8,128)(2,1)}, bf16[1024,3072]{1,0:T(8,128)(2,1)}...) custom-call(f32[1024,1024]{1,0:T(8,128)} %get-tuple-element.198.pc_r, ...), custom_call_target="tpu_custom_call" | custom-call | flops 5000000000 | bytes 7340032 | tf_op jit(solution)/shard_map/scan_forward/pallas_call | solution.py:229
  110.5 9.0 %project.4 = (f32[1024,1024]{1,0:T(8,128)}, bf16[1536,1024]{1,0:T(8,128)(2,1)}) custom-call(s32[32]{0:T(128)} %pad_add_fusion.order_ref, bf16[1024,1536]{1,0:T(8,128)(2,1)} %fusion.3.x_ref.lhs_ref, bf16[384,1024]{1,0:T(8,128)(2,1)} %constant_dynamic-update-slice_fusion.p0, bf16[384,1024]{1,0:T(8,128)(2,1)} %copy-done.45, ...), custom_call_target="tpu_custom_call" | custom-call | flops 3221225472 | bytes 13631488 | tf_op jit(solution)/shard_map/project/pallas_call | solution.py:773
  119.6 14.7 %scan_forward.4 = (bf16[1024,3072]{1,0:T(8,128)(2,1)}, bf16[1024,3072]{1,0:T(8,128)(2,1)}, bf16[512,3072]{1,0:T(8,128)(2,1)}, bf16[1024,3072]{1,0:T(8,128)(2,1)}, f32[8,128]{1,0:T(8,128)}) custom-call(f32[1024,1024]{1,0:T(8,128)} %get-tuple-element.211.pc_ref.halo_ref, ...), custom_call_target="tpu_custom_call", output_to_operand_aliasing={{0}: (11, {}), {1}: (12, {}), {2}: (13, {}), {3}: (14, {})} | custom-call | flops 10000000000 | bytes 14680064 | tf_op jit(solution)/shard_map/scan_forward/pallas_call | solution.py:229
  139.1 11.7 %project.5 = (f32[1024,1536]{1,0:T(8,128)}, bf16[1536,1536]{1,0:T(8,128)(2,1)}) custom-call(s32[32]{0:T(128)} %pad_add_fusion.order_ref, bf16[1024,1536]{1,0:T(8,128)(2,1)} %fusion.3.x_ref.lhs_ref, bf16[384,1536]{1,0:T(8,128)(2,1)} %constant_dynamic-update-slice_fusion.14.p0, bf16[384,1536]{1,0:T(8,128)(2,1)} %collective-permute-done.27.p1, ...), custom_call_target="tpu_custom_call" | custom-call | flops 4831838208 | bytes 18874368 | tf_op jit(solution)/shard_map/project/pallas_call | solution.py:773
  150.9 20.7 %scan_forward.5 = (bf16[1024,3072]{1,0:T(8,128)(2,1)}, bf16[1024,3072]{1,0:T(8,128)(2,1)}, bf16[512,3072]{1,0:T(8,128)(2,1)}, bf16[1024,3072]{1,0:T(8,128)(2,1)}, f32[8,128]{1,0:T(8,128)}) custom-call(f32[1024,1536]{1,0:T(8,128)} %get-tuple-element.226.pc_ref.halo_ref, ...), custom_call_target="tpu_custom_call", output_to_operand_aliasing={{0}: (11, {}), {1}: (12, {}), {2}: (13, {}), {3}: (14, {})} | custom-call | flops 15000000512 | bytes 22020096 | tf_op jit(solution)/shard_map/scan_forward/pallas_call | solution.py:229
  176.9 20.9 %project_gate.1 = (bf16[1024,3072]{1,0:T(8,128)(2,1)}, bf16[1536,3072]{1,0:T(8,128)(2,1)}, bf16[1024,3072]{1,0:T(8,128)(2,1)}, f32[1024,128]{1,0:T(8,128)}) custom-call(s32[32]{0:T(128)} %pad_add_fusion.order_ref, bf16[1024,1536]{1,0:T(8,128)(2,1)} %fusion.3.x_ref.lhs_ref, bf16[384,3072]{1,0:T(8,128)(2,1)} %constant_dynamic-update-slice_fusion.18.p0, ...), custom_call_target="tpu_custom_call" | custom-call | flops 9663676416 | bytes 53477376 | tf_op jit(solution)/shard_map/project_gate/pallas_call | solution.py:827
  204.0 15.2 %weight_grad.5 = (bf16[1536,1536]{1,0:T(8,128)(2,1)}, bf16[1536,1536]{1,0:T(8,128)(2,1)}) custom-call(s32[32]{0:T(128)} %fusion.34.place_ref, bf16[1024,3072]{1,0:T(8,128)(2,1)} %get-tuple-element.243.lhs_ref.zg_ref, bf16[1024,1536]{1,0:T(8,128)(2,1)} %fusion.8.rhs_ref), custom_call_target="tpu_custom_call" | custom-call | flops 9663676416 | bytes 18874368 | tf_op jit(solution)/shard_map/weight_grad/pallas_call | solution.py:1022
  220.8 19.6 %project_out.1 = (bf16[3072,1536]{1,0:T(8,128)(2,1)}, bf16[1024,1536]{1,0:T(8,128)(2,1)}, f32[1024,1]{1,0:T(8,128)}) custom-call(s32[32]{0:T(128)} %pad_add_fusion.order_ref, bf16[1024,3072]{1,0:T(8,128)(2,1)} %get-tuple-element.243.lhs_ref.zg_ref, f32[1024,1]{1,0:T(8,128)} %copy.63.inverse_ref, bf16[1024,1536]{1,0:T(8,128)(2,1)} %tokens_ref, ...), custom_call_target="tpu_custom_call" | custom-call | flops 9663676416 | bytes 34603008 | tf_op jit(solution)/shard_map/project_out/pallas_call | solution.py:912
  245.2 21.2 %gate_back.1 = (bf16[1024,3072]{1,0:T(8,128)(2,1)}, bf16[1024,3072]{1,0:T(8,128)(2,1)}) custom-call(bf16[1024,1536]{1,0:T(8,128)(2,1)} %cot_ref.2, bf16[3072,1536]{1,0:T(8,128)(2,1)} %get-tuple-element.249.w_ref, bf16[1024,3072]{1,0:T(8,128)(2,1)} %get-tuple-element.250.gate_ref, bf16[1024,3072]{1,0:T(8,128)(2,1)} %get-tuple-element.236.y_ref, ...), custom_call_target="tpu_custom_call" | custom-call | flops 9663676416 | bytes 34603008 | tf_op jit(solution)/shard_map/gate_back/pallas_call | solution.py:959
  266.5 6.0 %collective-permute-done.35 = bf16[768,1536]{1,0:T(8,128)(2,1)} collective-permute-done((bf16[768,1536]{1,0:T(8,128)(2,1)S(1)}, bf16[768,1536]{1,0:T(8,128)(2,1)}, u32[]{:S(2)}, u32[]{:S(2)}) %collective-permute-start.35) | collective-permute-done | bytes 2359328 | tf_op jit(solution)/shard_map/ppermute | solution.py:631
  272.5 15.8 %weight_grad.6 = (bf16[768,3072]{1,0:T(8,128)(2,1)}, bf16[768,3072]{1,0:T(8,128)(2,1)}) custom-call(s32[32]{0:T(128)} %fusion.34.place_ref, bf16[1024,1536]{1,0:T(8,128)(2,1)} %fusion.3.x_ref.lhs_ref, bf16[1024,3072]{1,0:T(8,128)(2,1)} %get-tuple-element.254.rhs_ref), custom_call_target="tpu_custom_call" | custom-call | flops 9663676416 | bytes 18874368 | tf_op jit(solution)/shard_map/weight_grad/pallas_call | solution.py:1022
  288.4 15.5 %fusion.47 = f32[1024,1536]{1,0:T(8,128)} fusion(bf16[1024,3072]{1,0:T(8,128)(2,1)} %get-tuple-element.254.rhs_ref, bf16[1536,3072]{1,0:T(8,128)(2,1)} %get-tuple-element.255), kind=kOutput, calls=%fused_computation.197 | convolution fusion | flops 9663676416 | bytes 22020096 | tf_op jit(solution)/shard_map/dot_general | solution.py:27
  311.6 49.7 %scan_backward.3 = (bf16[1024,1536]{1,0:T(8,128)(2,1)}, f32[5,8,1536]{2,1,0:T(8,128)}, f32[8,1536]{1,0:T(8,128)}, f32[1024,256]{1,0:T(8,128)}, f32[1024,256]{1,0...) custom-call(bf16[1024,3072]{1,0:T(8,128)(2,1)} %get-tuple-element.287.dy_ref, ...), custom_call_target="tpu_custom_call" | custom-call | flops 35999997952 | bytes 18874368 | tf_op jit(solution)/shard_map/scan_backward/pallas_call | solution.py:562
  364.3 9.7 %weight_grad.7 = (bf16[768,1536]{1,0:T(8,128)(2,1)}, bf16[768,1536]{1,0:T(8,128)(2,1)}) custom-call(s32[32]{0:T(128)} %fusion.34.place_ref, bf16[1024,1536]{1,0:T(8,128)(2,1)} %fusion.3.x_ref.lhs_ref, bf16[1024,1536]{1,0:T(8,128)(2,1)} %get-tuple-element.270.rhs_ref), custom_call_target="tpu_custom_call" | custom-call | flops 4831838208 | bytes 11010048 | tf_op jit(solution)/shard_map/weight_grad/pallas_call | solution.py:1022
  375.6 10.7 %convolution_add_fusion = f32[1024,1536]{1,0:T(8,128)} fusion(f32[1024,1536]{1,0:T(8,128)} %fusion.47, bf16[1024,1536]{1,0:T(8,128)(2,1)} %get-tuple-element.270.rhs_ref, bf16[1536,1536]{1,0:T(8,128)(2,1)} %get-tuple-element.271), kind=kOutput, calls=%fused_computation.18 | convolution fusion | flops 4833411072 | bytes 20447232 | tf_op jit(solution)/shard_map/dot_general | solution.py:27
  397.9 7.5 %collective-permute-done.42 = bf16[96,1536]{1,0:T(8,128)(2,1)S(1)} collective-permute-done((bf16[96,1536]{1,0:T(8,128)(2,1)S(1)}, bf16[96,1536]{1,0:T(8,128)(2,1)S(1)}, u32[]{:S(2)}, u32[]{:S(2)}) %collective-permute-start.42) | collective-permute-done | bytes 294944 | tf_op jit(solution)/shard_map/ppermute | solution.py:631
  406.9 34.8 %scan_backward.4 = (bf16[1024,1024]{1,0:T(8,128)(2,1)}, f32[5,8,1024]{2,1,0:T(8,128)}, f32[8,1024]{1,0:T(8,128)}, f32[1024,256]{1,0:T(8,128)}, f32[1024,256]{1,0...) custom-call(bf16[1024,3072]{1,0:T(8,128)(2,1)} %get-tuple-element.287.dy_ref, ...), custom_call_target="tpu_custom_call" | custom-call | flops 24000000000 | bytes 12582912 | tf_op jit(solution)/shard_map/scan_backward/pallas_call | solution.py:562
  447.9 8.0 %weight_grad.8 = (bf16[768,1024]{1,0:T(8,128)(2,1)}, bf16[768,1024]{1,0:T(8,128)(2,1)}) custom-call(s32[32]{0:T(128)} %fusion.34.place_ref, bf16[1024,1536]{1,0:T(8,128)(2,1)} %fusion.3.x_ref.lhs_ref, bf16[1024,1024]{1,0:T(8,128)(2,1)} %get-tuple-element.307.rhs_ref), custom_call_target="tpu_custom_call" | custom-call | flops 3221225472 | bytes 8388608 | tf_op jit(solution)/shard_map/weight_grad/pallas_call | solution.py:1022
  464.2 19.6 %scan_backward.5 = (bf16[1024,1024]{1,0:T(8,128)(2,1)}, f32[5,8,512]{2,1,0:T(8,128)}, f32[8,512]{1,0:T(8,128)}, f32[5,8,256]{2,1,0:T(8,128)}, f32[2,8,128]{2,1,0:T(8,128)}) custom-call(bf16[1024,3072]{1,0:T(8,128)(2,1)} %get-tuple-element.287.dy_ref, bf16[1024,3072]{1,0:T(8,128)(2,1)} %get-tuple-element.261.x_ref, ...), custom_call_target="tpu_custom_call" | custom-call | flops 12000000000 | bytes 6291456 | tf_op jit(solution)/shard_map/scan_backward/pallas_call | solution.py:562
  489.7 8.3 %weight_grad.9 = (bf16[768,1024]{1,0:T(8,128)(2,1)}, bf16[768,1024]{1,0:T(8,128)(2,1)}) custom-call(s32[32]{0:T(128)} %fusion.34.place_ref, bf16[1024,1536]{1,0:T(8,128)(2,1)} %fusion.3.x_ref.lhs_ref, bf16[1024,1024]{1,0:T(8,128)(2,1)} %get-tuple-element.302.rhs_ref), custom_call_target="tpu_custom_call" | custom-call | flops 3221225472 | bytes 8388608 | tf_op jit(solution)/shard_map/weight_grad/pallas_call | solution.py:1022
  509.7 8.3 %convolution_add_fusion.1 = f32[1024,1536]{1,0:T(8,128)} fusion(f32[1024,1536]{1,0:T(8,128)} %convolution_add_fusion, bf16[1024,1024]{1,0:T(8,128)(2,1)S(1)} %copy-done.48, bf16[1536,1024]{1,0:T(8,128)(2,1)} %get-tuple-element.303), kind=kOutput, calls=%fused_computation.19 | convolution fusion | flops 3222798336 | bytes 17825792 | tf_op jit(solution)/shard_map/dot_general | solution.py:27
  526.8 6.9 %fusion.4 = (f32[1024]{0:T(1024)S(1)}, f32[1024,1536]{1,0:T(8,128)S(1)}) fusion(bf16[1024,1536]{1,0:T(8,128)(2,1)S(1)} %copy-done.2, f32[1024]{0:T(1024)S(1)} %copy-done.33, f32[1536]{0:T(1024)S(1)} %copy-done.35, f32[1024,1536]{1,0:T(8,128)} %convolution_add_fusion.1, bf16[1024,1024]{1,0:T(8,128)(2,1)} %get-tuple-element.307.rhs_ref, ...), kind=kOutput, calls=%fused_computation.9 | convolution fusion | flops 3230661632 | bytes 20985856 | tf_op jit(solution)/shard_map/dot_general | solution.py:27
  (388 shorter events, 198.7 us)
Async XLA Ops:
  64.7 23.4 %collective-permute-start.13 = (bf16[48,3072]{1,0:T(8,128)(2,1)S(1)}, bf16[48,3072]{1,0:T(8,128)(2,1)S(1)}, u32[]{:S(2)}, u32[]{:S(2)}) collective-permute-start(bf16[48,3072]{1,0:T(8,128)(2,1)S(1)} %copy-done.16), channel_id=1, source_target_pairs={{0,16},{1,17},{2,18},{3,19},{4,20},{5,21},{6,22},{7,23},{8,24},{9,... | collective-permute-start | bytes 884744 | tf_op jit(solution)/shard_map/ppermute | solution.py:631
  75.1 29.0 %collective-permute-start.18 = (bf16[192,1536]{1,0:T(8,128)(2,1)}, bf16[192,1536]{1,0:T(8,128)(2,1)S(1)}, u32[]{:S(2)}, u32[]{:S(2)}) collective-permute-start(bf16[192,1536]{1,0:T(8,128)(2,1)} %copy-done.31), channel_id=1, source_target_pairs={{0,8},{1,9},{2,10},{3,11},{4,12},{5,13},{6,14},{7,15},{8,0},{9,1},... | collective-permute-start | bytes 1769480 | tf_op jit(solution)/shard_map/ppermute | solution.py:631
  91.3 19.2 %collective-permute-start.22 = (bf16[384,1024]{1,0:T(8,128)(2,1)}, bf16[384,1024]{1,0:T(8,128)(2,1)}, u32[]{:S(2)}, u32[]{:S(2)}) collective-permute-start(bf16[384,1024]{1,0:T(8,128)(2,1)} %constant_dynamic-update-slice_fusion.p0), channel_id=1, source_target_pairs={{0,1},{1,0},{2,3},{3,2},{4,5},{5,4},{6,7},{7,6},{8,9},{9,8},{10,11... | collective-permute-start | bytes 2359304 | tf_op jit(solution)/shard_map/ppermute | solution.py:635
  105.8 29.0 %collective-permute-start.21 = (bf16[192,1536]{1,0:T(8,128)(2,1)S(1)}, bf16[192,1536]{1,0:T(8,128)(2,1)S(1)}, u32[]{:S(2)}, u32[]{:S(2)}) collective-permute-start(bf16[192,1536]{1,0:T(8,128)(2,1)S(1)} %get-tuple-element.359), channel_id=1, source_target_pairs={{0,2},{1,5},{2,0},{3,7},{4,6},{5,1},{6,4},{7,3},{8,10},{9,13},{10,... | collective-permute-start | bytes 1769480 | tf_op jit(solution)/shard_map/ppermute | solution.py:631
  107.7 27.9 %collective-permute-start.20 = (bf16[192,3072]{1,0:T(8,128)(2,1)}, bf16[192,3072]{1,0:T(8,128)(2,1)S(1)}, u32[]{:S(2)}, u32[]{:S(2)}) collective-permute-start(bf16[192,3072]{1,0:T(8,128)(2,1)} %get-tuple-element.345), channel_id=1, source_target_pairs={{0,8},{1,9},{2,10},{3,11},{4,12},{5,13},{6,14},{7,15},{8,0},{9,1},... | collective-permute-start | bytes 3538952 | tf_op jit(solution)/shard_map/ppermute | solution.py:631
  109.0 25.3 %collective-permute-start.27 = (bf16[384,1536]{1,0:T(8,128)(2,1)}, bf16[384,1536]{1,0:T(8,128)(2,1)}, u32[]{:S(2)}, u32[]{:S(2)}) collective-permute-start(bf16[384,1536]{1,0:T(8,128)(2,1)} %constant_dynamic-update-slice_fusion.14.p0), channel_id=1, source_target_pairs={{0,4},{1,3},{2,6},{3,1},{4,0},{5,7},{6,2},{7,5},{8,12},{9,11},{10,... | collective-permute-start | bytes 3538952 | tf_op jit(solution)/shard_map/ppermute | solution.py:631
  119.5 19.7 %collective-permute-start.28 = (bf16[384,1536]{1,0:T(8,128)(2,1)}, bf16[384,1536]{1,0:T(8,128)(2,1)}, u32[]{:S(2)}, u32[]{:S(2)}) collective-permute-start(bf16[384,1536]{1,0:T(8,128)(2,1)} %constant_dynamic-update-slice_fusion.14.p0), channel_id=1, source_target_pairs={{0,1},{1,0},{2,3},{3,2},{4,5},{5,4},{6,7},{7,6},{8,9},{9,8},{10,11... | collective-permute-start | bytes 3538952 | tf_op jit(solution)/shard_map/ppermute | solution.py:635
  136.7 35.0 %collective-permute-start.25 = (bf16[384,3072]{1,0:T(8,128)(2,1)}, bf16[384,3072]{1,0:T(8,128)(2,1)}, u32[]{:S(2)}, u32[]{:S(2)}) collective-permute-start(bf16[384,3072]{1,0:T(8,128)(2,1)} %constant_dynamic-update-slice_fusion.18.p0), channel_id=1, source_target_pairs={{0,1},{1,0},{2,3},{3,2},{4,5},{5,4},{6,7},{7,6},{8,9},{9,8},{10,11... | collective-permute-start | bytes 7077896 | tf_op jit(solution)/shard_map/ppermute | solution.py:635
  136.7 35.0 %collective-permute-start.24 = (bf16[384,3072]{1,0:T(8,128)(2,1)}, bf16[384,3072]{1,0:T(8,128)(2,1)}, u32[]{:S(2)}, u32[]{:S(2)}) collective-permute-start(bf16[384,3072]{1,0:T(8,128)(2,1)} %constant_dynamic-update-slice_fusion.18.p0), channel_id=1, source_target_pairs={{0,4},{1,3},{2,6},{3,1},{4,0},{5,7},{6,2},{7,5},{8,12},{9,11},{10,... | collective-permute-start | bytes 7077896 | tf_op jit(solution)/shard_map/ppermute | solution.py:631
  138.4 33.3 %collective-permute-start.26 = (bf16[384,1536]{1,0:T(8,128)(2,1)}, bf16[384,1536]{1,0:T(8,128)(2,1)S(1)}, u32[]{:S(2)}, u32[]{:S(2)}) collective-permute-start(bf16[384,1536]{1,0:T(8,128)(2,1)} %get-tuple-element.344), channel_id=1, source_target_pairs={{0,8},{1,9},{2,10},{3,11},{4,12},{5,13},{6,14},{7,15},{8,0},{9,1},... | collective-permute-start | bytes 3538952 | tf_op jit(solution)/shard_map/ppermute | solution.py:631
  173.5 29.2 %collective-permute-start.31 = (bf16[768,1536]{1,0:T(8,128)(2,1)}, bf16[768,1536]{1,0:T(8,128)(2,1)}, u32[]{:S(2)}, u32[]{:S(2)}) collective-permute-start(bf16[768,1536]{1,0:T(8,128)(2,1)} %constant_dynamic-update-slice_fusion.25.p0), channel_id=1, source_target_pairs={{0,4},{1,3},{2,6},{3,1},{4,0},{5,7},{6,2},{7,5},{8,12},{9,11},{10,... | collective-permute-start | bytes 7077896 | tf_op jit(solution)/shard_map/ppermute | solution.py:631
  175.1 44.0 %collective-permute-start.32 = (bf16[768,1536]{1,0:T(8,128)(2,1)}, bf16[768,1536]{1,0:T(8,128)(2,1)}, u32[]{:S(2)}, u32[]{:S(2)}) collective-permute-start(bf16[768,1536]{1,0:T(8,128)(2,1)} %constant_dynamic-update-slice_fusion.25.p0), channel_id=1, source_target_pairs={{0,1},{1,0},{2,3},{3,2},{4,5},{5,4},{6,7},{7,6},{8,9},{9,8},{10,11... | collective-permute-start | bytes 7077896 | tf_op jit(solution)/shard_map/ppermute | solution.py:635
  219.2 21.2 %collective-permute-start.34 = (bf16[1536,1536]{1,0:T(8,128)(2,1)}, bf16[1536,1536]{1,0:T(8,128)(2,1)}, u32[]{:S(2)}, u32[]{:S(2)}) collective-permute-start(bf16[1536,1536]{1,0:T(8,128)(2,1)} %get-tuple-element.242), channel_id=1, source_target_pairs={{0,1},{1,0},{2,3},{3,2},{4,5},{5,4},{6,7},{7,6},{8,9},{9,8},{10,11... | collective-permute-start | bytes 14155784 | tf_op jit(solution)/shard_map/ppermute | solution.py:635
  243.5 29.0 %collective-permute-start.35 = (bf16[768,1536]{1,0:T(8,128)(2,1)S(1)}, bf16[768,1536]{1,0:T(8,128)(2,1)}, u32[]{:S(2)}, u32[]{:S(2)}) collective-permute-start(bf16[768,1536]{1,0:T(8,128)(2,1)S(1)} %add_convert_fusion.1), channel_id=1, source_target_pairs={{0,4},{1,3},{2,6},{3,1},{4,0},{5,7},{6,2},{7,5},{8,12},{9,11},{10,... | collective-permute-start | bytes 7077896 | tf_op jit(solution)/shard_map/ppermute | solution.py:631
  288.3 20.3 %collective-permute-start.36 = (bf16[768,3072]{1,0:T(8,128)(2,1)}, bf16[768,3072]{1,0:T(8,128)(2,1)S(1)}, u32[]{:S(2)}, u32[]{:S(2)}) collective-permute-start(bf16[768,3072]{1,0:T(8,128)(2,1)} %get-tuple-element.253), channel_id=1, source_target_pairs={{0,1},{1,0},{2,3},{3,2},{4,5},{5,4},{6,7},{7,6},{8,9},{9,8},{10,11... | collective-permute-start | bytes 14155784 | tf_op jit(solution)/shard_map/ppermute | solution.py:635
  307.5 53.8 %collective-permute-start.37 = (bf16[384,1536]{1,0:T(8,128)(2,1)}, bf16[384,1536]{1,0:T(8,128)(2,1)S(1)}, u32[]{:S(2)}, u32[]{:S(2)}) collective-permute-start(bf16[384,1536]{1,0:T(8,128)(2,1)} %add_convert_fusion.4), channel_id=1, source_target_pairs={{0,8},{1,9},{2,10},{3,11},{4,12},{5,13},{6,14},{7,15},{8,0},{9,1},... | collective-permute-start | bytes 3538952 | tf_op jit(solution)/shard_map/ppermute | solution.py:631
  310.9 50.5 %collective-permute-start.38 = (bf16[384,3072]{1,0:T(8,128)(2,1)S(1)}, bf16[384,3072]{1,0:T(8,128)(2,1)}, u32[]{:S(2)}, u32[]{:S(2)}) collective-permute-start(bf16[384,3072]{1,0:T(8,128)(2,1)S(1)} %add_convert_fusion), channel_id=1, source_target_pairs={{0,4},{1,3},{2,6},{3,1},{4,0},{5,7},{6,2},{7,5},{8,12},{9,11},{10,... | collective-permute-start | bytes 7077896 | tf_op jit(solution)/shard_map/ppermute | solution.py:631
  396.1 48.4 %collective-permute-start.43 = (bf16[384,1536]{1,0:T(8,128)(2,1)}, bf16[384,1536]{1,0:T(8,128)(2,1)}, u32[]{:S(2)}, u32[]{:S(2)}) collective-permute-start(bf16[384,1536]{1,0:T(8,128)(2,1)} %add_convert_fusion.2), channel_id=1, source_target_pairs={{0,4},{1,3},{2,6},{3,1},{4,0},{5,7},{6,2},{7,5},{8,12},{9,11},{10,... | collective-permute-start | bytes 3538952 | tf_op jit(solution)/shard_map/ppermute | solution.py:631
  396.7 47.8 %collective-permute-start.41 = (bf16[192,3072]{1,0:T(8,128)(2,1)}, bf16[192,3072]{1,0:T(8,128)(2,1)}, u32[]{:S(2)}, u32[]{:S(2)}) collective-permute-start(bf16[192,3072]{1,0:T(8,128)(2,1)} %add_convert_fusion.3), channel_id=1, source_target_pairs={{0,8},{1,9},{2,10},{3,11},{4,12},{5,13},{6,14},{7,15},{8,0},{9,1},... | collective-permute-start | bytes 3538952 | tf_op jit(solution)/shard_map/ppermute | solution.py:631
  406.8 34.9 %collective-permute-start.68 = (f32[96,1536]{1,0:T(8,128)S(1)}, f32[96,1536]{1,0:T(8,128)S(1)}, u32[]{:S(2)}, u32[]{:S(2)}) collective-permute-start(f32[96,1536]{1,0:T(8,128)S(1)} %convert_add_fusion.1), channel_id=1, source_target_pairs={{0,1},{1,0},{2,3},{3,2},{4,5},{5,4},{6,7},{7,6},{8,9},{9,8},{10,11... | collective-permute-start | bytes 1769480 | tf_op jit(solution)/shard_map/ppermute | solution.py:635
  456.0 29.0 %collective-permute-start.45 = (bf16[768,1024]{1,0:T(8,128)(2,1)}, bf16[768,1024]{1,0:T(8,128)(2,1)}, u32[]{:S(2)}, u32[]{:S(2)}) collective-permute-start(bf16[768,1024]{1,0:T(8,128)(2,1)} %get-tuple-element.284), channel_id=1, source_target_pairs={{0,1},{1,0},{2,3},{3,2},{4,5},{5,4},{6,7},{7,6},{8,9},{9,8},{10,11... | collective-permute-start | bytes 4718600 | tf_op jit(solution)/shard_map/ppermute | solution.py:635
  458.7 26.2 %collective-permute-start.47 = (bf16[192,1536]{1,0:T(8,128)(2,1)}, bf16[192,1536]{1,0:T(8,128)(2,1)S(1)}, u32[]{:S(2)}, u32[]{:S(2)}) collective-permute-start(bf16[192,1536]{1,0:T(8,128)(2,1)} %add_convert_fusion.7), channel_id=1, source_target_pairs={{0,8},{1,9},{2,10},{3,11},{4,12},{5,13},{6,14},{7,15},{8,0},{9,1},... | collective-permute-start | bytes 1769480 | tf_op jit(solution)/shard_map/ppermute | solution.py:631
  461.0 23.9 %collective-permute-start.46 = (bf16[48,3072]{1,0:T(8,128)(2,1)}, bf16[48,3072]{1,0:T(8,128)(2,1)}, u32[]{:S(2)}, u32[]{:S(2)}) collective-permute-start(bf16[48,3072]{1,0:T(8,128)(2,1)} %add_convert_fusion.13), channel_id=1, source_target_pairs={{0,16},{1,17},{2,18},{3,19},{4,20},{5,21},{6,22},{7,23},{8,24},{9,... | collective-permute-start | bytes 884744 | tf_op jit(solution)/shard_map/ppermute | solution.py:631
  521.5 26.1 %collective-permute-start.61 = (bf16[48,1536]{1,0:T(8,128)(2,1)S(1)}, bf16[48,1536]{1,0:T(8,128)(2,1)S(1)}, u32[]{:S(2)}, u32[]{:S(2)}) collective-permute-start(bf16[48,1536]{1,0:T(8,128)(2,1)S(1)} %add_convert_fusion.17), channel_id=1, source_target_pairs={{0,16},{1,17},{2,18},{3,19},{4,20},{5,21},{6,22},{7,23},{8,24},{9,... | collective-permute-start | bytes 442376 | tf_op jit(solution)/shard_map/ppermute | solution.py:631
  (95 other events, 919.8 us)

commit v8 on v7

--- a/solution.py
+++ b/solution.py
@@ -1087,7 +1087,9 @@
         next(small_flow)
         got = []
         for starts in ((near,), (near, middle), (near, middle, far), (near, middle, far)):
-            pairs = [each.step(*got) for each in starts] + [small_flow.send(got)]
+            pairs = [near.step(*got)]
+            ahead = [*got, pairs[0][0]]
+            pairs += [each.step(*ahead) for each in starts[1:]] + [small_flow.send(ahead)]
             got = [pair[1] for pair in pairs]
             if len(starts) == 1:
                 later = (far.held, gate_gather.held, out_gather.held), (tokens, seg_ids, dt_bias, a_log, d_skip, core)
@@ -1095,9 +1097,9 @@
                 far.held, gate_gather.held, out_gather.held = helds
         small_all = small_flow.send(got)
         order, place = block_order(core)
-        sent, got = zip(
-            middle.step(*got), far.step(*got), near.swap(*got), near.swap(*got), gate_gather.step(*got)
-        )
+        swaps = [near.swap(near.seen[3]), near.swap()]
+        got = [*got[1:], swaps[1][0]]
+        sent, got = zip(middle.step(*got), far.step(*got), *swaps, gate_gather.step(*got))
         normed_tie = sent
         conv_tie = sent
         last_pair = got[0], got[1], got[4]

time: 566 us -> 564 us (level)
  transfers between devices with their start and end apart: 69 -> 69, of which waited for: 15 -> 12; matrix products, arithmetic and copies ran while one was open for 23% -> 23% of each run, Pallas kernels for 49% -> 49%
where the time goes in v8:
time: 564 us; the launch traced here: 557 us
  Pallas kernels  300 us (53%)
  other arithmetic  70.5 us (12%)
  starting transfers between devices  61.8 us (11%)
  local copies, waits for them, and re-layouts  47.2 us (8%)
  matrix products  41.7 us (7%)
  waiting for transfers between devices  34.3 us (6%)
    pallas_call x3, Pallas kernels, run_backward(): pl.pallas_call(functools.partial(backward_kernel, before is None, last, s...  104 us
    ppermute x48, starting transfers between devices, exchange(): return lax.ppermute(values, ('shard', 'rep'), pairs)  57.5 us
    pallas_call x5, Pallas kernels, weight_grad(): pl.pallas_call(functools.partial(weight_grad_kernel, block), grid_spec=pl...  57.1 us
    pallas_call x3, Pallas kernels, run_forward(): pl.pallas_call(functools.partial(forward_kernel, first_call, start * GROU...  46.9 us
    dot_general x6, matrix products, dot_f32(): lax.dot_general(a, b, ((contract[0], contract[1]), ((), ())), preferred_e...  41.7 us
    convert_element_type x20, other arithmetic, step(): send = self.rows(cut, 2 * cut).astype(BF16)  37.2 us
    ppermute x48, waiting for transfers between devices, exchange(): return lax.ppermute(values, ('shard', 'rep'), pairs)  32.3 us
    pallas_call x3, Pallas kernels, project(): pl.pallas_call(functools.partial(project_kernel, block, width), grid_spec...  29.9 us
  transfers between devices with their start and end apart: 69, of which 12 were waited for; matrix products, arithmetic and copies ran while one was open for 23% of the time, Pallas kernels for 49%

profile of v8, /device:TPU:0, one launch (start us, length us, event | category | flops | bytes accessed | tf_op | source)
XLA Modules:
  0.0 557.2 jit_solution(788646603047419771)
XLA Ops:
  53.7 5.7 %collective-permute-done.9 = bf16[8,1328]{1,0:T(8,128)(2,1)S(1)} collective-permute-done((bf16[8,1328]{1,0:T(8,128)(2,1)S(1)}, bf16[8,1328]{1,0:T(8,128)(2,1)S(1)}, u32[]{:S(2)}, u32[]{:S(2)}) %collective-permute-start.9) | collective-permute-done | bytes 21280 | tf_op jit(solution)/shard_map/ppermute | solution.py:631
  75.9 9.2 %project.3 = (f32[1024,1024]{1,0:T(8,128)}, bf16[1536,1024]{1,0:T(8,128)(2,1)}) custom-call(s32[32]{0:T(128)} %pad_add_fusion.order_ref, bf16[1024,1536]{1,0:T(8,128)(2,1)} %fusion.3.x_ref.lhs_ref, bf16[384,1024]{1,0:T(8,128)(2,1)} %pad_maximum_fusion.2.p0, bf16[384,1024]{1,0:T(8,128)(2,1)} %collective-permute-done.12.p1, ...), custom_call_target="tpu_custom_call" | custom-call | flops 3221225472 | bytes 13631488 | tf_op jit(solution)/shard_map/project/pallas_call | solution.py:773
  90.3 11.5 %scan_forward.3 = (bf16[1024,3072]{1,0:T(8,128)(2,1)}, bf16[1024,3072]{1,0:T(8,128)(2,1)}, bf16[512,3072]{1,0:T(8,128)(2,1)}, bf16[1024,3072]{1,0:T(8,128)(2,1)}...) custom-call(f32[1024,1024]{1,0:T(8,128)} %get-tuple-element.198.pc_r, ...), custom_call_target="tpu_custom_call" | custom-call | flops 5000000000 | bytes 7340032 | tf_op jit(solution)/shard_map/scan_forward/pallas_call | solution.py:229
  107.3 9.0 %project.4 = (f32[1024,1024]{1,0:T(8,128)}, bf16[1536,1024]{1,0:T(8,128)(2,1)}) custom-call(s32[32]{0:T(128)} %pad_add_fusion.order_ref, bf16[1024,1536]{1,0:T(8,128)(2,1)} %fusion.3.x_ref.lhs_ref, bf16[384,1024]{1,0:T(8,128)(2,1)} %constant_dynamic-update-slice_fusion.p0, bf16[384,1024]{1,0:T(8,128)(2,1)} %copy-done.45, ...), custom_call_target="tpu_custom_call" | custom-call | flops 3221225472 | bytes 13631488 | tf_op jit(solution)/shard_map/project/pallas_call | solution.py:773
  116.4 14.7 %scan_forward.4 = (bf16[1024,3072]{1,0:T(8,128)(2,1)}, bf16[1024,3072]{1,0:T(8,128)(2,1)}, bf16[512,3072]{1,0:T(8,128)(2,1)}, bf16[1024,3072]{1,0:T(8,128)(2,1)}, f32[8,128]{1,0:T(8,128)}) custom-call(f32[1024,1024]{1,0:T(8,128)} %get-tuple-element.211.pc_ref.halo_ref, ...), custom_call_target="tpu_custom_call", output_to_operand_aliasing={{0}: (11, {}), {1}: (12, {}), {2}: (13, {}), {3}: (14, {})} | custom-call | flops 10000000000 | bytes 14680064 | tf_op jit(solution)/shard_map/scan_forward/pallas_call | solution.py:229
  137.4 11.7 %project.5 = (f32[1024,1536]{1,0:T(8,128)}, bf16[1536,1536]{1,0:T(8,128)(2,1)}) custom-call(s32[32]{0:T(128)} %pad_add_fusion.order_ref, bf16[1024,1536]{1,0:T(8,128)(2,1)} %fusion.3.x_ref.lhs_ref, bf16[384,1536]{1,0:T(8,128)(2,1)} %constant_dynamic-update-slice_fusion.14.p0, bf16[384,1536]{1,0:T(8,128)(2,1)} %collective-permute-done.27.p1, ...), custom_call_target="tpu_custom_call" | custom-call | flops 4831838208 | bytes 18874368 | tf_op jit(solution)/shard_map/project/pallas_call | solution.py:773
  149.1 20.7 %scan_forward.5 = (bf16[1024,3072]{1,0:T(8,128)(2,1)}, bf16[1024,3072]{1,0:T(8,128)(2,1)}, bf16[512,3072]{1,0:T(8,128)(2,1)}, bf16[1024,3072]{1,0:T(8,128)(2,1)}, f32[8,128]{1,0:T(8,128)}) custom-call(f32[1024,1536]{1,0:T(8,128)} %get-tuple-element.226.pc_ref.halo_ref, ...), custom_call_target="tpu_custom_call", output_to_operand_aliasing={{0}: (11, {}), {1}: (12, {}), {2}: (13, {}), {3}: (14, {})} | custom-call | flops 15000000512 | bytes 22020096 | tf_op jit(solution)/shard_map/scan_forward/pallas_call | solution.py:229
  174.8 20.9 %project_gate.1 = (bf16[1024,3072]{1,0:T(8,128)(2,1)}, bf16[1536,3072]{1,0:T(8,128)(2,1)}, bf16[1024,3072]{1,0:T(8,128)(2,1)}, f32[1024,128]{1,0:T(8,128)}) custom-call(s32[32]{0:T(128)} %pad_add_fusion.order_ref, bf16[1024,1536]{1,0:T(8,128)(2,1)} %fusion.3.x_ref.lhs_ref, bf16[384,3072]{1,0:T(8,128)(2,1)} %constant_dynamic-update-slice_fusion.18.p0, ...), custom_call_target="tpu_custom_call" | custom-call | flops 9663676416 | bytes 53477376 | tf_op jit(solution)/shard_map/project_gate/pallas_call | solution.py:827
  201.5 15.2 %weight_grad.5 = (bf16[1536,1536]{1,0:T(8,128)(2,1)}, bf16[1536,1536]{1,0:T(8,128)(2,1)}) custom-call(s32[32]{0:T(128)} %fusion.34.place_ref, bf16[1024,3072]{1,0:T(8,128)(2,1)} %get-tuple-element.243.lhs_ref.zg_ref, bf16[1024,1536]{1,0:T(8,128)(2,1)} %fusion.8.rhs_ref), custom_call_target="tpu_custom_call" | custom-call | flops 9663676416 | bytes 18874368 | tf_op jit(solution)/shard_map/weight_grad/pallas_call | solution.py:1022
  218.3 19.6 %project_out.1 = (bf16[3072,1536]{1,0:T(8,128)(2,1)}, bf16[1024,1536]{1,0:T(8,128)(2,1)}, f32[1024,1]{1,0:T(8,128)}) custom-call(s32[32]{0:T(128)} %pad_add_fusion.order_ref, bf16[1024,3072]{1,0:T(8,128)(2,1)} %get-tuple-element.243.lhs_ref.zg_ref, f32[1024,1]{1,0:T(8,128)} %copy.63.inverse_ref, bf16[1024,1536]{1,0:T(8,128)(2,1)} %tokens_ref, ...), custom_call_target="tpu_custom_call" | custom-call | flops 9663676416 | bytes 34603008 | tf_op jit(solution)/shard_map/project_out/pallas_call | solution.py:912
  242.7 21.2 %gate_back.1 = (bf16[1024,3072]{1,0:T(8,128)(2,1)}, bf16[1024,3072]{1,0:T(8,128)(2,1)}) custom-call(bf16[1024,1536]{1,0:T(8,128)(2,1)} %cot_ref.2, bf16[3072,1536]{1,0:T(8,128)(2,1)} %get-tuple-element.249.w_ref, bf16[1024,3072]{1,0:T(8,128)(2,1)} %get-tuple-element.250.gate_ref, bf16[1024,3072]{1,0:T(8,128)(2,1)} %get-tuple-element.236.y_ref, ...), custom_call_target="tpu_custom_call" | custom-call | flops 9663676416 | bytes 34603008 | tf_op jit(solution)/shard_map/gate_back/pallas_call | solution.py:959
  263.9 6.2 %collective-permute-done.35 = bf16[768,1536]{1,0:T(8,128)(2,1)} collective-permute-done((bf16[768,1536]{1,0:T(8,128)(2,1)S(1)}, bf16[768,1536]{1,0:T(8,128)(2,1)}, u32[]{:S(2)}, u32[]{:S(2)}) %collective-permute-start.35) | collective-permute-done | bytes 2359328 | tf_op jit(solution)/shard_map/ppermute | solution.py:631
  270.1 15.8 %weight_grad.6 = (bf16[768,3072]{1,0:T(8,128)(2,1)}, bf16[768,3072]{1,0:T(8,128)(2,1)}) custom-call(s32[32]{0:T(128)} %fusion.34.place_ref, bf16[1024,1536]{1,0:T(8,128)(2,1)} %fusion.3.x_ref.lhs_ref, bf16[1024,3072]{1,0:T(8,128)(2,1)} %get-tuple-element.254.rhs_ref), custom_call_target="tpu_custom_call" | custom-call | flops 9663676416 | bytes 18874368 | tf_op jit(solution)/shard_map/weight_grad/pallas_call | solution.py:1022
  286.0 15.5 %fusion.47 = f32[1024,1536]{1,0:T(8,128)} fusion(bf16[1024,3072]{1,0:T(8,128)(2,1)} %get-tuple-element.254.rhs_ref, bf16[1536,3072]{1,0:T(8,128)(2,1)} %get-tuple-element.255), kind=kOutput, calls=%fused_computation.197 | convolution fusion | flops 9663676416 | bytes 22020096 | tf_op jit(solution)/shard_map/dot_general | solution.py:27
  309.2 49.7 %scan_backward.3 = (bf16[1024,1536]{1,0:T(8,128)(2,1)}, f32[5,8,1536]{2,1,0:T(8,128)}, f32[8,1536]{1,0:T(8,128)}, f32[1024,256]{1,0:T(8,128)}, f32[1024,256]{1,0...) custom-call(bf16[1024,3072]{1,0:T(8,128)(2,1)} %get-tuple-element.287.dy_ref, ...), custom_call_target="tpu_custom_call" | custom-call | flops 35999997952 | bytes 18874368 | tf_op jit(solution)/shard_map/scan_backward/pallas_call | solution.py:562
  361.9 9.7 %weight_grad.7 = (bf16[768,1536]{1,0:T(8,128)(2,1)}, bf16[768,1536]{1,0:T(8,128)(2,1)}) custom-call(s32[32]{0:T(128)} %fusion.34.place_ref, bf16[1024,1536]{1,0:T(8,128)(2,1)} %fusion.3.x_ref.lhs_ref, bf16[1024,1536]{1,0:T(8,128)(2,1)} %get-tuple-element.270.rhs_ref), custom_call_target="tpu_custom_call" | custom-call | flops 4831838208 | bytes 11010048 | tf_op jit(solution)/shard_map/weight_grad/pallas_call | solution.py:1022
  373.0 10.7 %convolution_add_fusion = f32[1024,1536]{1,0:T(8,128)} fusion(f32[1024,1536]{1,0:T(8,128)} %fusion.47, bf16[1024,1536]{1,0:T(8,128)(2,1)} %get-tuple-element.270.rhs_ref, bf16[1536,1536]{1,0:T(8,128)(2,1)} %get-tuple-element.271), kind=kOutput, calls=%fused_computation.18 | convolution fusion | flops 4833411072 | bytes 20447232 | tf_op jit(solution)/shard_map/dot_general | solution.py:27
  394.6 8.3 %collective-permute-done.42 = bf16[96,1536]{1,0:T(8,128)(2,1)S(1)} collective-permute-done((bf16[96,1536]{1,0:T(8,128)(2,1)S(1)}, bf16[96,1536]{1,0:T(8,128)(2,1)S(1)}, u32[]{:S(2)}, u32[]{:S(2)}) %collective-permute-start.42) | collective-permute-done | bytes 294944 | tf_op jit(solution)/shard_map/ppermute | solution.py:631
  404.5 34.8 %scan_backward.4 = (bf16[1024,1024]{1,0:T(8,128)(2,1)}, f32[5,8,1024]{2,1,0:T(8,128)}, f32[8,1024]{1,0:T(8,128)}, f32[1024,256]{1,0:T(8,128)}, f32[1024,256]{1,0...) custom-call(bf16[1024,3072]{1,0:T(8,128)(2,1)} %get-tuple-element.287.dy_ref, ...), custom_call_target="tpu_custom_call" | custom-call | flops 24000000000 | bytes 12582912 | tf_op jit(solution)/shard_map/scan_backward/pallas_call | solution.py:562
  445.5 8.0 %weight_grad.8 = (bf16[768,1024]{1,0:T(8,128)(2,1)}, bf16[768,1024]{1,0:T(8,128)(2,1)}) custom-call(s32[32]{0:T(128)} %fusion.34.place_ref, bf16[1024,1536]{1,0:T(8,128)(2,1)} %fusion.3.x_ref.lhs_ref, bf16[1024,1024]{1,0:T(8,128)(2,1)} %get-tuple-element.307.rhs_ref), custom_call_target="tpu_custom_call" | custom-call | flops 3221225472 | bytes 8388608 | tf_op jit(solution)/shard_map/weight_grad/pallas_call | solution.py:1022
  460.9 19.6 %scan_backward.5 = (bf16[1024,1024]{1,0:T(8,128)(2,1)}, f32[5,8,512]{2,1,0:T(8,128)}, f32[8,512]{1,0:T(8,128)}, f32[5,8,256]{2,1,0:T(8,128)}, f32[2,8,128]{2,1,0:T(8,128)}) custom-call(bf16[1024,3072]{1,0:T(8,128)(2,1)} %get-tuple-element.287.dy_ref, bf16[1024,3072]{1,0:T(8,128)(2,1)} %get-tuple-element.261.x_ref, ...), custom_call_target="tpu_custom_call" | custom-call | flops 12000000000 | bytes 6291456 | tf_op jit(solution)/shard_map/scan_backward/pallas_call | solution.py:562
  486.3 8.3 %weight_grad.9 = (bf16[768,1024]{1,0:T(8,128)(2,1)}, bf16[768,1024]{1,0:T(8,128)(2,1)}) custom-call(s32[32]{0:T(128)} %fusion.34.place_ref, bf16[1024,1536]{1,0:T(8,128)(2,1)} %fusion.3.x_ref.lhs_ref, bf16[1024,1024]{1,0:T(8,128)(2,1)} %get-tuple-element.302.rhs_ref), custom_call_target="tpu_custom_call" | custom-call | flops 3221225472 | bytes 8388608 | tf_op jit(solution)/shard_map/weight_grad/pallas_call | solution.py:1022
  506.4 8.3 %convolution_add_fusion.1 = f32[1024,1536]{1,0:T(8,128)} fusion(f32[1024,1536]{1,0:T(8,128)} %convolution_add_fusion, bf16[1024,1024]{1,0:T(8,128)(2,1)S(1)} %copy-done.48, bf16[1536,1024]{1,0:T(8,128)(2,1)} %get-tuple-element.303), kind=kOutput, calls=%fused_computation.19 | convolution fusion | flops 3222798336 | bytes 17825792 | tf_op jit(solution)/shard_map/dot_general | solution.py:27
  524.0 6.9 %fusion.4 = (f32[1024]{0:T(1024)S(1)}, f32[1024,1536]{1,0:T(8,128)S(1)}) fusion(bf16[1024,1536]{1,0:T(8,128)(2,1)S(1)} %copy-done.2, f32[1024]{0:T(1024)S(1)} %copy-done.33, f32[1536]{0:T(1024)S(1)} %copy-done.35, f32[1024,1536]{1,0:T(8,128)} %convolution_add_fusion.1, bf16[1024,1024]{1,0:T(8,128)(2,1)} %get-tuple-element.307.rhs_ref, ...), kind=kOutput, calls=%fused_computation.9 | convolution fusion | flops 3230661632 | bytes 20985856 | tf_op jit(solution)/shard_map/dot_general | solution.py:27
  (388 shorter events, 194.0 us)
Async XLA Ops:
  62.2 23.0 %collective-permute-start.13 = (bf16[48,3072]{1,0:T(8,128)(2,1)S(1)}, bf16[48,3072]{1,0:T(8,128)(2,1)S(1)}, u32[]{:S(2)}, u32[]{:S(2)}) collective-permute-start(bf16[48,3072]{1,0:T(8,128)(2,1)S(1)} %copy-done.16), channel_id=1, source_target_pairs={{0,16},{1,17},{2,18},{3,19},{4,20},{5,21},{6,22},{7,23},{8,24},{9,... | collective-permute-start | bytes 884744 | tf_op jit(solution)/shard_map/ppermute | solution.py:631
  65.9 19.2 %collective-permute-start.14 = (bf16[384,1024]{1,0:T(8,128)(2,1)}, bf16[384,1024]{1,0:T(8,128)(2,1)S(1)}, u32[]{:S(2)}, u32[]{:S(2)}) collective-permute-start(bf16[384,1024]{1,0:T(8,128)(2,1)} %constant_dynamic-update-slice_fusion.p0), channel_id=1, source_target_pairs={{0,4},{1,3},{2,6},{3,1},{4,0},{5,7},{6,2},{7,5},{8,12},{9,11},{10,... | collective-permute-start | bytes 2359304 | tf_op jit(solution)/shard_map/ppermute | solution.py:631
  71.6 31.0 %collective-permute-start.18 = (bf16[192,1536]{1,0:T(8,128)(2,1)}, bf16[192,1536]{1,0:T(8,128)(2,1)S(1)}, u32[]{:S(2)}, u32[]{:S(2)}) collective-permute-start(bf16[192,1536]{1,0:T(8,128)(2,1)} %copy-done.31), channel_id=1, source_target_pairs={{0,8},{1,9},{2,10},{3,11},{4,12},{5,13},{6,14},{7,15},{8,0},{9,1},... | collective-permute-start | bytes 1769480 | tf_op jit(solution)/shard_map/ppermute | solution.py:631
  103.5 28.1 %collective-permute-start.21 = (bf16[192,1536]{1,0:T(8,128)(2,1)S(1)}, bf16[192,1536]{1,0:T(8,128)(2,1)S(1)}, u32[]{:S(2)}, u32[]{:S(2)}) collective-permute-start(bf16[192,1536]{1,0:T(8,128)(2,1)S(1)} %get-tuple-element.359), channel_id=1, source_target_pairs={{0,2},{1,5},{2,0},{3,7},{4,6},{5,1},{6,4},{7,3},{8,10},{9,13},{10,... | collective-permute-start | bytes 1769480 | tf_op jit(solution)/shard_map/ppermute | solution.py:631
  105.2 27.9 %collective-permute-start.20 = (bf16[192,3072]{1,0:T(8,128)(2,1)}, bf16[192,3072]{1,0:T(8,128)(2,1)S(1)}, u32[]{:S(2)}, u32[]{:S(2)}) collective-permute-start(bf16[192,3072]{1,0:T(8,128)(2,1)} %get-tuple-element.345), channel_id=1, source_target_pairs={{0,8},{1,9},{2,10},{3,11},{4,12},{5,13},{6,14},{7,15},{8,0},{9,1},... | collective-permute-start | bytes 3538952 | tf_op jit(solution)/shard_map/ppermute | solution.py:631
  106.8 24.3 %collective-permute-start.27 = (bf16[384,1536]{1,0:T(8,128)(2,1)}, bf16[384,1536]{1,0:T(8,128)(2,1)}, u32[]{:S(2)}, u32[]{:S(2)}) collective-permute-start(bf16[384,1536]{1,0:T(8,128)(2,1)} %constant_dynamic-update-slice_fusion.14.p0), channel_id=1, source_target_pairs={{0,4},{1,3},{2,6},{3,1},{4,0},{5,7},{6,2},{7,5},{8,12},{9,11},{10,... | collective-permute-start | bytes 3538952 | tf_op jit(solution)/shard_map/ppermute | solution.py:631
  116.3 21.1 %collective-permute-start.28 = (bf16[384,1536]{1,0:T(8,128)(2,1)}, bf16[384,1536]{1,0:T(8,128)(2,1)}, u32[]{:S(2)}, u32[]{:S(2)}) collective-permute-start(bf16[384,1536]{1,0:T(8,128)(2,1)} %constant_dynamic-update-slice_fusion.14.p0), channel_id=1, source_target_pairs={{0,1},{1,0},{2,3},{3,2},{4,5},{5,4},{6,7},{7,6},{8,9},{9,8},{10,11... | collective-permute-start | bytes 3538952 | tf_op jit(solution)/shard_map/ppermute | solution.py:635
  134.2 35.6 %collective-permute-start.25 = (bf16[384,3072]{1,0:T(8,128)(2,1)}, bf16[384,3072]{1,0:T(8,128)(2,1)}, u32[]{:S(2)}, u32[]{:S(2)}) collective-permute-start(bf16[384,3072]{1,0:T(8,128)(2,1)} %constant_dynamic-update-slice_fusion.18.p0), channel_id=1, source_target_pairs={{0,1},{1,0},{2,3},{3,2},{4,5},{5,4},{6,7},{7,6},{8,9},{9,8},{10,11... | collective-permute-start | bytes 7077896 | tf_op jit(solution)/shard_map/ppermute | solution.py:635
  134.2 35.6 %collective-permute-start.24 = (bf16[384,3072]{1,0:T(8,128)(2,1)}, bf16[384,3072]{1,0:T(8,128)(2,1)}, u32[]{:S(2)}, u32[]{:S(2)}) collective-permute-start(bf16[384,3072]{1,0:T(8,128)(2,1)} %constant_dynamic-update-slice_fusion.18.p0), channel_id=1, source_target_pairs={{0,4},{1,3},{2,6},{3,1},{4,0},{5,7},{6,2},{7,5},{8,12},{9,11},{10,... | collective-permute-start | bytes 7077896 | tf_op jit(solution)/shard_map/ppermute | solution.py:631
  136.7 33.2 %collective-permute-start.26 = (bf16[384,1536]{1,0:T(8,128)(2,1)}, bf16[384,1536]{1,0:T(8,128)(2,1)S(1)}, u32[]{:S(2)}, u32[]{:S(2)}) collective-permute-start(bf16[384,1536]{1,0:T(8,128)(2,1)} %get-tuple-element.344), channel_id=1, source_target_pairs={{0,8},{1,9},{2,10},{3,11},{4,12},{5,13},{6,14},{7,15},{8,0},{9,1},... | collective-permute-start | bytes 3538952 | tf_op jit(solution)/shard_map/ppermute | solution.py:631
  171.1 29.2 %collective-permute-start.31 = (bf16[768,1536]{1,0:T(8,128)(2,1)}, bf16[768,1536]{1,0:T(8,128)(2,1)}, u32[]{:S(2)}, u32[]{:S(2)}) collective-permute-start(bf16[768,1536]{1,0:T(8,128)(2,1)} %constant_dynamic-update-slice_fusion.25.p0), channel_id=1, source_target_pairs={{0,4},{1,3},{2,6},{3,1},{4,0},{5,7},{6,2},{7,5},{8,12},{9,11},{10,... | collective-permute-start | bytes 7077896 | tf_op jit(solution)/shard_map/ppermute | solution.py:631
  172.5 44.2 %collective-permute-start.32 = (bf16[768,1536]{1,0:T(8,128)(2,1)}, bf16[768,1536]{1,0:T(8,128)(2,1)}, u32[]{:S(2)}, u32[]{:S(2)}) collective-permute-start(bf16[768,1536]{1,0:T(8,128)(2,1)} %constant_dynamic-update-slice_fusion.25.p0), channel_id=1, source_target_pairs={{0,1},{1,0},{2,3},{3,2},{4,5},{5,4},{6,7},{7,6},{8,9},{9,8},{10,11... | collective-permute-start | bytes 7077896 | tf_op jit(solution)/shard_map/ppermute | solution.py:635
  216.7 21.2 %collective-permute-start.34 = (bf16[1536,1536]{1,0:T(8,128)(2,1)}, bf16[1536,1536]{1,0:T(8,128)(2,1)}, u32[]{:S(2)}, u32[]{:S(2)}) collective-permute-start(bf16[1536,1536]{1,0:T(8,128)(2,1)} %get-tuple-element.242), channel_id=1, source_target_pairs={{0,1},{1,0},{2,3},{3,2},{4,5},{5,4},{6,7},{7,6},{8,9},{9,8},{10,11... | collective-permute-start | bytes 14155784 | tf_op jit(solution)/shard_map/ppermute | solution.py:635
  241.0 29.0 %collective-permute-start.35 = (bf16[768,1536]{1,0:T(8,128)(2,1)S(1)}, bf16[768,1536]{1,0:T(8,128)(2,1)}, u32[]{:S(2)}, u32[]{:S(2)}) collective-permute-start(bf16[768,1536]{1,0:T(8,128)(2,1)S(1)} %add_convert_fusion.1), channel_id=1, source_target_pairs={{0,4},{1,3},{2,6},{3,1},{4,0},{5,7},{6,2},{7,5},{8,12},{9,11},{10,... | collective-permute-start | bytes 7077896 | tf_op jit(solution)/shard_map/ppermute | solution.py:631
  285.9 20.4 %collective-permute-start.36 = (bf16[768,3072]{1,0:T(8,128)(2,1)}, bf16[768,3072]{1,0:T(8,128)(2,1)S(1)}, u32[]{:S(2)}, u32[]{:S(2)}) collective-permute-start(bf16[768,3072]{1,0:T(8,128)(2,1)} %get-tuple-element.253), channel_id=1, source_target_pairs={{0,1},{1,0},{2,3},{3,2},{4,5},{5,4},{6,7},{7,6},{8,9},{9,8},{10,11... | collective-permute-start | bytes 14155784 | tf_op jit(solution)/shard_map/ppermute | solution.py:635
  305.0 53.8 %collective-permute-start.37 = (bf16[384,1536]{1,0:T(8,128)(2,1)}, bf16[384,1536]{1,0:T(8,128)(2,1)S(1)}, u32[]{:S(2)}, u32[]{:S(2)}) collective-permute-start(bf16[384,1536]{1,0:T(8,128)(2,1)} %add_convert_fusion.4), channel_id=1, source_target_pairs={{0,8},{1,9},{2,10},{3,11},{4,12},{5,13},{6,14},{7,15},{8,0},{9,1},... | collective-permute-start | bytes 3538952 | tf_op jit(solution)/shard_map/ppermute | solution.py:631
  308.4 50.4 %collective-permute-start.38 = (bf16[384,3072]{1,0:T(8,128)(2,1)S(1)}, bf16[384,3072]{1,0:T(8,128)(2,1)}, u32[]{:S(2)}, u32[]{:S(2)}) collective-permute-start(bf16[384,3072]{1,0:T(8,128)(2,1)S(1)} %add_convert_fusion), channel_id=1, source_target_pairs={{0,4},{1,3},{2,6},{3,1},{4,0},{5,7},{6,2},{7,5},{8,12},{9,11},{10,... | collective-permute-start | bytes 7077896 | tf_op jit(solution)/shard_map/ppermute | solution.py:631
  393.1 49.0 %collective-permute-start.43 = (bf16[384,1536]{1,0:T(8,128)(2,1)}, bf16[384,1536]{1,0:T(8,128)(2,1)}, u32[]{:S(2)}, u32[]{:S(2)}) collective-permute-start(bf16[384,1536]{1,0:T(8,128)(2,1)} %add_convert_fusion.2), channel_id=1, source_target_pairs={{0,4},{1,3},{2,6},{3,1},{4,0},{5,7},{6,2},{7,5},{8,12},{9,11},{10,... | collective-permute-start | bytes 3538952 | tf_op jit(solution)/shard_map/ppermute | solution.py:631
  393.7 48.5 %collective-permute-start.41 = (bf16[192,3072]{1,0:T(8,128)(2,1)}, bf16[192,3072]{1,0:T(8,128)(2,1)}, u32[]{:S(2)}, u32[]{:S(2)}) collective-permute-start(bf16[192,3072]{1,0:T(8,128)(2,1)} %add_convert_fusion.3), channel_id=1, source_target_pairs={{0,8},{1,9},{2,10},{3,11},{4,12},{5,13},{6,14},{7,15},{8,0},{9,1},... | collective-permute-start | bytes 3538952 | tf_op jit(solution)/shard_map/ppermute | solution.py:631
  404.4 34.9 %collective-permute-start.68 = (f32[96,1536]{1,0:T(8,128)S(1)}, f32[96,1536]{1,0:T(8,128)S(1)}, u32[]{:S(2)}, u32[]{:S(2)}) collective-permute-start(f32[96,1536]{1,0:T(8,128)S(1)} %convert_add_fusion.1), channel_id=1, source_target_pairs={{0,1},{1,0},{2,3},{3,2},{4,5},{5,4},{6,7},{7,6},{8,9},{9,8},{10,11... | collective-permute-start | bytes 1769480 | tf_op jit(solution)/shard_map/ppermute | solution.py:635
  453.6 28.0 %collective-permute-start.45 = (bf16[768,1024]{1,0:T(8,128)(2,1)}, bf16[768,1024]{1,0:T(8,128)(2,1)}, u32[]{:S(2)}, u32[]{:S(2)}) collective-permute-start(bf16[768,1024]{1,0:T(8,128)(2,1)} %get-tuple-element.284), channel_id=1, source_target_pairs={{0,1},{1,0},{2,3},{3,2},{4,5},{5,4},{6,7},{7,6},{8,9},{9,8},{10,11... | collective-permute-start | bytes 4718600 | tf_op jit(solution)/shard_map/ppermute | solution.py:635
  456.3 25.3 %collective-permute-start.47 = (bf16[192,1536]{1,0:T(8,128)(2,1)}, bf16[192,1536]{1,0:T(8,128)(2,1)S(1)}, u32[]{:S(2)}, u32[]{:S(2)}) collective-permute-start(bf16[192,1536]{1,0:T(8,128)(2,1)} %add_convert_fusion.7), channel_id=1, source_target_pairs={{0,8},{1,9},{2,10},{3,11},{4,12},{5,13},{6,14},{7,15},{8,0},{9,1},... | collective-permute-start | bytes 1769480 | tf_op jit(solution)/shard_map/ppermute | solution.py:631
  458.6 22.9 %collective-permute-start.46 = (bf16[48,3072]{1,0:T(8,128)(2,1)}, bf16[48,3072]{1,0:T(8,128)(2,1)}, u32[]{:S(2)}, u32[]{:S(2)}) collective-permute-start(bf16[48,3072]{1,0:T(8,128)(2,1)} %add_convert_fusion.13), channel_id=1, source_target_pairs={{0,16},{1,17},{2,18},{3,19},{4,20},{5,21},{6,22},{7,23},{8,24},{9,... | collective-permute-start | bytes 884744 | tf_op jit(solution)/shard_map/ppermute | solution.py:631
  518.1 26.1 %collective-permute-start.61 = (bf16[48,1536]{1,0:T(8,128)(2,1)S(1)}, bf16[48,1536]{1,0:T(8,128)(2,1)S(1)}, u32[]{:S(2)}, u32[]{:S(2)}) collective-permute-start(bf16[48,1536]{1,0:T(8,128)(2,1)S(1)} %add_convert_fusion.17), channel_id=1, source_target_pairs={{0,16},{1,17},{2,18},{3,19},{4,20},{5,21},{6,22},{7,23},{8,24},{9,... | collective-permute-start | bytes 442376 | tf_op jit(solution)/shard_map/ppermute | solution.py:631
  (95 other events, 960.8 us)

commit v9 on v8

--- a/solution.py
+++ b/solution.py
@@ -1299,7 +1299,7 @@
         gain_sum = 0.0
         for part, a, b in zip(whole, edges, edges[1:]):
             gain_sum = gain_sum + jnp.sum(part * w_in[:, a:b].astype(F32), axis=1)
-        sum_w_out = both_cores(out_sum.finish())
+        sum_w_out = both_cores(out_sum.finish(grad_sums[1].terms[0]))
     else:
         grad_w_out = dot_f32(zg, cot_scaled, ((0,), (0,)))
         rest = [parts[index][0] for index in range(len(calls))]

time: 564 us -> 555 us (0.984)
  waiting for transfers between devices: 34.3 us -> 26 us
    ppermute x48, waiting for transfers between devices: 32.3 us -> 23.9 us  [exchange(): return lax.ppermute(values, ('shard', 'rep'), pairs)]
    unnamed x115 -> x121, local copies, waits for them, and re-layouts: 19 us -> 17.3 us
  transfers between devices with their start and end apart: 69 -> 69, of which waited for: 12 -> 10; matrix products, arithmetic and copies ran while one was open for 23% -> 24% of each run, Pallas kernels for 49% -> 50%
where the time goes in v9:
time: 555 us; the launch traced here: 548 us
  Pallas kernels  300 us (54%)
  other arithmetic  70.9 us (13%)
  starting transfers between devices  62.2 us (11%)
  local copies, waits for them, and re-layouts  45.6 us (8%)
  matrix products  41.7 us (8%)
  waiting for transfers between devices  26 us (5%)
    pallas_call x3, Pallas kernels, run_backward(): pl.pallas_call(functools.partial(backward_kernel, before is None, last, s...  104 us
    ppermute x48, starting transfers between devices, exchange(): return lax.ppermute(values, ('shard', 'rep'), pairs)  58.2 us
    pallas_call x5, Pallas kernels, weight_grad(): pl.pallas_call(functools.partial(weight_grad_kernel, block), grid_spec=pl...  57.1 us
    pallas_call x3, Pallas kernels, run_forward(): pl.pallas_call(functools.partial(forward_kernel, first_call, start * GROU...  46.9 us
    dot_general x6, matrix products, dot_f32(): lax.dot_general(a, b, ((contract[0], contract[1]), ((), ())), preferred_e...  41.7 us
    convert_element_type x20, other arithmetic, step(): send = self.rows(cut, 2 * cut).astype(BF16)  37.2 us
    pallas_call x3, Pallas kernels, project(): pl.pallas_call(functools.partial(project_kernel, block, width), grid_spec...  29.8 us
    ppermute x48, waiting for transfers between devices, exchange(): return lax.ppermute(values, ('shard', 'rep'), pairs)  23.9 us
  transfers between devices with their start and end apart: 69, of which 10 were waited for; matrix products, arithmetic and copies ran while one was open for 24% of the time, Pallas kernels for 50%

profile of v9, /device:TPU:0, one launch (start us, length us, event | category | flops | bytes accessed | tf_op | source)
XLA Modules:
  0.0 548.2 jit_solution(8572517881371781771)
XLA Ops:
  37.2 5.6 %collective-permute-done.5 = bf16[4,1328]{1,0:T(4,128)(2,1)S(1)} collective-permute-done((bf16[4,1328]{1,0:T(4,128)(2,1)S(1)}, bf16[4,1328]{1,0:T(4,128)(2,1)S(1)}, u32[]{:S(2)}, u32[]{:S(2)}) %collective-permute-start.5) | collective-permute-done | bytes 10656 | tf_op jit(solution)/shard_map/ppermute | solution.py:631
  53.7 5.7 %collective-permute-done.9 = bf16[8,1328]{1,0:T(8,128)(2,1)S(1)} collective-permute-done((bf16[8,1328]{1,0:T(8,128)(2,1)S(1)}, bf16[8,1328]{1,0:T(8,128)(2,1)S(1)}, u32[]{:S(2)}, u32[]{:S(2)}) %collective-permute-start.9) | collective-permute-done | bytes 21280 | tf_op jit(solution)/shard_map/ppermute | solution.py:631
  76.0 9.1 %project.3 = (f32[1024,1024]{1,0:T(8,128)}, bf16[1536,1024]{1,0:T(8,128)(2,1)}) custom-call(s32[32]{0:T(128)} %pad_add_fusion.order_ref, bf16[1024,1536]{1,0:T(8,128)(2,1)} %fusion.3.x_ref.lhs_ref, bf16[384,1024]{1,0:T(8,128)(2,1)} %pad_maximum_fusion.2.p0, bf16[384,1024]{1,0:T(8,128)(2,1)} %collective-permute-done.12.p1, ...), custom_call_target="tpu_custom_call" | custom-call | flops 3221225472 | bytes 13631488 | tf_op jit(solution)/shard_map/project/pallas_call | solution.py:773
  90.3 11.4 %scan_forward.3 = (bf16[1024,3072]{1,0:T(8,128)(2,1)}, bf16[1024,3072]{1,0:T(8,128)(2,1)}, bf16[512,3072]{1,0:T(8,128)(2,1)}, bf16[1024,3072]{1,0:T(8,128)(2,1)}...) custom-call(f32[1024,1024]{1,0:T(8,128)} %get-tuple-element.199.pc_r, ...), custom_call_target="tpu_custom_call" | custom-call | flops 5000000000 | bytes 7340032 | tf_op jit(solution)/shard_map/scan_forward/pallas_call | solution.py:229
  107.3 9.0 %project.4 = (f32[1024,1024]{1,0:T(8,128)}, bf16[1536,1024]{1,0:T(8,128)(2,1)}) custom-call(s32[32]{0:T(128)} %pad_add_fusion.order_ref, bf16[1024,1536]{1,0:T(8,128)(2,1)} %fusion.3.x_ref.lhs_ref, bf16[384,1024]{1,0:T(8,128)(2,1)} %constant_dynamic-update-slice_fusion.p0, bf16[384,1024]{1,0:T(8,128)(2,1)} %copy-done.48, ...), custom_call_target="tpu_custom_call" | custom-call | flops 3221225472 | bytes 13631488 | tf_op jit(solution)/shard_map/project/pallas_call | solution.py:773
  116.4 14.7 %scan_forward.4 = (bf16[1024,3072]{1,0:T(8,128)(2,1)}, bf16[1024,3072]{1,0:T(8,128)(2,1)}, bf16[512,3072]{1,0:T(8,128)(2,1)}, bf16[1024,3072]{1,0:T(8,128)(2,1)}, f32[8,128]{1,0:T(8,128)}) custom-call(f32[1024,1024]{1,0:T(8,128)} %get-tuple-element.212.pc_ref.halo_ref, ...), custom_call_target="tpu_custom_call", output_to_operand_aliasing={{0}: (11, {}), {1}: (12, {}), {2}: (13, {}), {3}: (14, {})} | custom-call | flops 10000000000 | bytes 14680064 | tf_op jit(solution)/shard_map/scan_forward/pallas_call | solution.py:229
  137.4 11.7 %project.5 = (f32[1024,1536]{1,0:T(8,128)}, bf16[1536,1536]{1,0:T(8,128)(2,1)}) custom-call(s32[32]{0:T(128)} %pad_add_fusion.order_ref, bf16[1024,1536]{1,0:T(8,128)(2,1)} %fusion.3.x_ref.lhs_ref, bf16[384,1536]{1,0:T(8,128)(2,1)} %constant_dynamic-update-slice_fusion.14.p0, bf16[384,1536]{1,0:T(8,128)(2,1)} %collective-permute-done.27.p1, ...), custom_call_target="tpu_custom_call" | custom-call | flops 4831838208 | bytes 18874368 | tf_op jit(solution)/shard_map/project/pallas_call | solution.py:773
  149.2 20.7 %scan_forward.5 = (bf16[1024,3072]{1,0:T(8,128)(2,1)}, bf16[1024,3072]{1,0:T(8,128)(2,1)}, bf16[512,3072]{1,0:T(8,128)(2,1)}, bf16[1024,3072]{1,0:T(8,128)(2,1)}, f32[8,128]{1,0:T(8,128)}) custom-call(f32[1024,1536]{1,0:T(8,128)} %get-tuple-element.227.pc_ref.halo_ref, ...), custom_call_target="tpu_custom_call", output_to_operand_aliasing={{0}: (11, {}), {1}: (12, {}), {2}: (13, {}), {3}: (14, {})} | custom-call | flops 15000000512 | bytes 22020096 | tf_op jit(solution)/shard_map/scan_forward/pallas_call | solution.py:229
  174.9 20.9 %project_gate.1 = (bf16[1024,3072]{1,0:T(8,128)(2,1)}, bf16[1536,3072]{1,0:T(8,128)(2,1)}, bf16[1024,3072]{1,0:T(8,128)(2,1)}, f32[1024,128]{1,0:T(8,128)}) custom-call(s32[32]{0:T(128)} %pad_add_fusion.order_ref, bf16[1024,1536]{1,0:T(8,128)(2,1)} %fusion.3.x_ref.lhs_ref, bf16[384,3072]{1,0:T(8,128)(2,1)} %constant_dynamic-update-slice_fusion.18.p0, ...), custom_call_target="tpu_custom_call" | custom-call | flops 9663676416 | bytes 53477376 | tf_op jit(solution)/shard_map/project_gate/pallas_call | solution.py:827
  201.6 15.2 %weight_grad.5 = (bf16[1536,1536]{1,0:T(8,128)(2,1)}, bf16[1536,1536]{1,0:T(8,128)(2,1)}) custom-call(s32[32]{0:T(128)} %fusion.34.place_ref, bf16[1024,3072]{1,0:T(8,128)(2,1)} %get-tuple-element.244.lhs_ref.zg_ref, bf16[1024,1536]{1,0:T(8,128)(2,1)} %fusion.8.rhs_ref), custom_call_target="tpu_custom_call" | custom-call | flops 9663676416 | bytes 18874368 | tf_op jit(solution)/shard_map/weight_grad/pallas_call | solution.py:1022
  218.4 19.6 %project_out.1 = (bf16[3072,1536]{1,0:T(8,128)(2,1)}, bf16[1024,1536]{1,0:T(8,128)(2,1)}, f32[1024,1]{1,0:T(8,128)}) custom-call(s32[32]{0:T(128)} %pad_add_fusion.order_ref, bf16[1024,3072]{1,0:T(8,128)(2,1)} %get-tuple-element.244.lhs_ref.zg_ref, f32[1024,1]{1,0:T(8,128)} %copy.63.inverse_ref, bf16[1024,1536]{1,0:T(8,128)(2,1)} %tokens_ref, ...), custom_call_target="tpu_custom_call" | custom-call | flops 9663676416 | bytes 34603008 | tf_op jit(solution)/shard_map/project_out/pallas_call | solution.py:912
  242.7 21.2 %gate_back.1 = (bf16[1024,3072]{1,0:T(8,128)(2,1)}, bf16[1024,3072]{1,0:T(8,128)(2,1)}) custom-call(bf16[1024,1536]{1,0:T(8,128)(2,1)} %cot_ref.2, bf16[3072,1536]{1,0:T(8,128)(2,1)} %get-tuple-element.250.w_ref, bf16[1024,3072]{1,0:T(8,128)(2,1)} %get-tuple-element.251.gate_ref, bf16[1024,3072]{1,0:T(8,128)(2,1)} %get-tuple-element.237.y_ref, ...), custom_call_target="tpu_custom_call" | custom-call | flops 9663676416 | bytes 34603008 | tf_op jit(solution)/shard_map/gate_back/pallas_call | solution.py:959
  264.0 6.1 %collective-permute-done.35 = bf16[768,1536]{1,0:T(8,128)(2,1)} collective-permute-done((bf16[768,1536]{1,0:T(8,128)(2,1)S(1)}, bf16[768,1536]{1,0:T(8,128)(2,1)}, u32[]{:S(2)}, u32[]{:S(2)}) %collective-permute-start.35) | collective-permute-done | bytes 2359328 | tf_op jit(solution)/shard_map/ppermute | solution.py:631
  270.1 15.9 %weight_grad.6 = (bf16[768,3072]{1,0:T(8,128)(2,1)}, bf16[768,3072]{1,0:T(8,128)(2,1)}) custom-call(s32[32]{0:T(128)} %fusion.34.place_ref, bf16[1024,1536]{1,0:T(8,128)(2,1)} %fusion.3.x_ref.lhs_ref, bf16[1024,3072]{1,0:T(8,128)(2,1)} %get-tuple-element.255.rhs_ref), custom_call_target="tpu_custom_call" | custom-call | flops 9663676416 | bytes 18874368 | tf_op jit(solution)/shard_map/weight_grad/pallas_call | solution.py:1022
  286.0 15.5 %fusion.47 = f32[1024,1536]{1,0:T(8,128)} fusion(bf16[1024,3072]{1,0:T(8,128)(2,1)} %get-tuple-element.255.rhs_ref, bf16[1536,3072]{1,0:T(8,128)(2,1)} %get-tuple-element.256), kind=kOutput, calls=%fused_computation.197 | convolution fusion | flops 9663676416 | bytes 22020096 | tf_op jit(solution)/shard_map/dot_general | solution.py:27
  309.3 49.7 %scan_backward.3 = (bf16[1024,1536]{1,0:T(8,128)(2,1)}, f32[5,8,1536]{2,1,0:T(8,128)}, f32[8,1536]{1,0:T(8,128)}, f32[1024,256]{1,0:T(8,128)}, f32[1024,256]{1,0...) custom-call(bf16[1024,3072]{1,0:T(8,128)(2,1)} %get-tuple-element.288.dy_ref, ...), custom_call_target="tpu_custom_call" | custom-call | flops 35999997952 | bytes 18874368 | tf_op jit(solution)/shard_map/scan_backward/pallas_call | solution.py:562
  361.9 9.7 %weight_grad.7 = (bf16[768,1536]{1,0:T(8,128)(2,1)}, bf16[768,1536]{1,0:T(8,128)(2,1)}) custom-call(s32[32]{0:T(128)} %fusion.34.place_ref, bf16[1024,1536]{1,0:T(8,128)(2,1)} %fusion.3.x_ref.lhs_ref, bf16[1024,1536]{1,0:T(8,128)(2,1)} %get-tuple-element.271.rhs_ref), custom_call_target="tpu_custom_call" | custom-call | flops 4831838208 | bytes 11010048 | tf_op jit(solution)/shard_map/weight_grad/pallas_call | solution.py:1022
  373.1 10.7 %convolution_add_fusion = f32[1024,1536]{1,0:T(8,128)} fusion(f32[1024,1536]{1,0:T(8,128)} %fusion.47, bf16[1024,1536]{1,0:T(8,128)(2,1)} %get-tuple-element.271.rhs_ref, bf16[1536,1536]{1,0:T(8,128)(2,1)} %get-tuple-element.272), kind=kOutput, calls=%fused_computation.18 | convolution fusion | flops 4833411072 | bytes 20447232 | tf_op jit(solution)/shard_map/dot_general | solution.py:27
  394.5 34.8 %scan_backward.4 = (bf16[1024,1024]{1,0:T(8,128)(2,1)}, f32[5,8,1024]{2,1,0:T(8,128)}, f32[8,1024]{1,0:T(8,128)}, f32[1024,256]{1,0:T(8,128)}, f32[1024,256]{1,0...) custom-call(bf16[1024,3072]{1,0:T(8,128)(2,1)} %get-tuple-element.288.dy_ref, ...), custom_call_target="tpu_custom_call" | custom-call | flops 24000000000 | bytes 12582912 | tf_op jit(solution)/shard_map/scan_backward/pallas_call | solution.py:562
  433.4 8.0 %weight_grad.8 = (bf16[768,1024]{1,0:T(8,128)(2,1)}, bf16[768,1024]{1,0:T(8,128)(2,1)}) custom-call(s32[32]{0:T(128)} %fusion.34.place_ref, bf16[1024,1536]{1,0:T(8,128)(2,1)} %fusion.3.x_ref.lhs_ref, bf16[1024,1024]{1,0:T(8,128)(2,1)} %get-tuple-element.308.rhs_ref), custom_call_target="tpu_custom_call" | custom-call | flops 3221225472 | bytes 8388608 | tf_op jit(solution)/shard_map/weight_grad/pallas_call | solution.py:1022
  450.8 19.6 %scan_backward.5 = (bf16[1024,1024]{1,0:T(8,128)(2,1)}, f32[5,8,512]{2,1,0:T(8,128)}, f32[8,512]{1,0:T(8,128)}, f32[5,8,256]{2,1,0:T(8,128)}, f32[2,8,128]{2,1,0:T(8,128)}) custom-call(bf16[1024,3072]{1,0:T(8,128)(2,1)} %get-tuple-element.288.dy_ref, bf16[1024,3072]{1,0:T(8,128)(2,1)} %get-tuple-element.262.x_ref, ...), custom_call_target="tpu_custom_call" | custom-call | flops 12000000000 | bytes 6291456 | tf_op jit(solution)/shard_map/scan_backward/pallas_call | solution.py:562
  476.9 8.3 %weight_grad.9 = (bf16[768,1024]{1,0:T(8,128)(2,1)}, bf16[768,1024]{1,0:T(8,128)(2,1)}) custom-call(s32[32]{0:T(128)} %fusion.34.place_ref, bf16[1024,1536]{1,0:T(8,128)(2,1)} %fusion.3.x_ref.lhs_ref, bf16[1024,1024]{1,0:T(8,128)(2,1)} %get-tuple-element.303.rhs_ref), custom_call_target="tpu_custom_call" | custom-call | flops 3221225472 | bytes 8388608 | tf_op jit(solution)/shard_map/weight_grad/pallas_call | solution.py:1022
  497.7 8.3 %convolution_add_fusion.1 = f32[1024,1536]{1,0:T(8,128)} fusion(f32[1024,1536]{1,0:T(8,128)} %convolution_add_fusion, bf16[1024,1024]{1,0:T(8,128)(2,1)S(1)} %copy-done.51, bf16[1536,1024]{1,0:T(8,128)(2,1)} %get-tuple-element.304), kind=kOutput, calls=%fused_computation.19 | convolution fusion | flops 3222798336 | bytes 17825792 | tf_op jit(solution)/shard_map/dot_general | solution.py:27
  515.5 6.9 %fusion.4 = (f32[1024]{0:T(1024)S(1)}, f32[1024,1536]{1,0:T(8,128)S(1)}) fusion(bf16[1024,1536]{1,0:T(8,128)(2,1)S(1)} %copy-done.2, f32[1024]{0:T(1024)S(1)} %copy-done.34, f32[1536]{0:T(1024)S(1)} %copy-done.36, f32[1024,1536]{1,0:T(8,128)} %convolution_add_fusion.1, bf16[1024,1024]{1,0:T(8,128)(2,1)} %get-tuple-element.308.rhs_ref, ...), kind=kOutput, calls=%fused_computation.9 | convolution fusion | flops 3230661632 | bytes 20985856 | tf_op jit(solution)/shard_map/dot_general | solution.py:27
  (394 shorter events, 187.6 us)
Async XLA Ops:
  62.2 22.9 %collective-permute-start.13 = (bf16[48,3072]{1,0:T(8,128)(2,1)S(1)}, bf16[48,3072]{1,0:T(8,128)(2,1)S(1)}, u32[]{:S(2)}, u32[]{:S(2)}) collective-permute-start(bf16[48,3072]{1,0:T(8,128)(2,1)S(1)} %copy-done.16), channel_id=1, source_target_pairs={{0,16},{1,17},{2,18},{3,19},{4,20},{5,21},{6,22},{7,23},{8,24},{9,... | collective-permute-start | bytes 884744 | tf_op jit(solution)/shard_map/ppermute | solution.py:631
  71.7 31.0 %collective-permute-start.18 = (bf16[192,1536]{1,0:T(8,128)(2,1)}, bf16[192,1536]{1,0:T(8,128)(2,1)S(1)}, u32[]{:S(2)}, u32[]{:S(2)}) collective-permute-start(bf16[192,1536]{1,0:T(8,128)(2,1)} %copy-done.32), channel_id=1, source_target_pairs={{0,8},{1,9},{2,10},{3,11},{4,12},{5,13},{6,14},{7,15},{8,0},{9,1},... | collective-permute-start | bytes 1769480 | tf_op jit(solution)/shard_map/ppermute | solution.py:631
  103.6 28.1 %collective-permute-start.21 = (bf16[192,1536]{1,0:T(8,128)(2,1)S(1)}, bf16[192,1536]{1,0:T(8,128)(2,1)S(1)}, u32[]{:S(2)}, u32[]{:S(2)}) collective-permute-start(bf16[192,1536]{1,0:T(8,128)(2,1)S(1)} %get-tuple-element.361), channel_id=1, source_target_pairs={{0,2},{1,5},{2,0},{3,7},{4,6},{5,1},{6,4},{7,3},{8,10},{9,13},{10,... | collective-permute-start | bytes 1769480 | tf_op jit(solution)/shard_map/ppermute | solution.py:631
  105.2 27.9 %collective-permute-start.20 = (bf16[192,3072]{1,0:T(8,128)(2,1)}, bf16[192,3072]{1,0:T(8,128)(2,1)S(1)}, u32[]{:S(2)}, u32[]{:S(2)}) collective-permute-start(bf16[192,3072]{1,0:T(8,128)(2,1)} %get-tuple-element.347), channel_id=1, source_target_pairs={{0,8},{1,9},{2,10},{3,11},{4,12},{5,13},{6,14},{7,15},{8,0},{9,1},... | collective-permute-start | bytes 3538952 | tf_op jit(solution)/shard_map/ppermute | solution.py:631
  106.8 24.3 %collective-permute-start.27 = (bf16[384,1536]{1,0:T(8,128)(2,1)}, bf16[384,1536]{1,0:T(8,128)(2,1)}, u32[]{:S(2)}, u32[]{:S(2)}) collective-permute-start(bf16[384,1536]{1,0:T(8,128)(2,1)} %constant_dynamic-update-slice_fusion.14.p0), channel_id=1, source_target_pairs={{0,4},{1,3},{2,6},{3,1},{4,0},{5,7},{6,2},{7,5},{8,12},{9,11},{10,... | collective-permute-start | bytes 3538952 | tf_op jit(solution)/shard_map/ppermute | solution.py:631
  116.3 21.1 %collective-permute-start.28 = (bf16[384,1536]{1,0:T(8,128)(2,1)}, bf16[384,1536]{1,0:T(8,128)(2,1)}, u32[]{:S(2)}, u32[]{:S(2)}) collective-permute-start(bf16[384,1536]{1,0:T(8,128)(2,1)} %constant_dynamic-update-slice_fusion.14.p0), channel_id=1, source_target_pairs={{0,1},{1,0},{2,3},{3,2},{4,5},{5,4},{6,7},{7,6},{8,9},{9,8},{10,11... | collective-permute-start | bytes 3538952 | tf_op jit(solution)/shard_map/ppermute | solution.py:635
  134.3 35.7 %collective-permute-start.25 = (bf16[384,3072]{1,0:T(8,128)(2,1)}, bf16[384,3072]{1,0:T(8,128)(2,1)}, u32[]{:S(2)}, u32[]{:S(2)}) collective-permute-start(bf16[384,3072]{1,0:T(8,128)(2,1)} %constant_dynamic-update-slice_fusion.18.p0), channel_id=1, source_target_pairs={{0,1},{1,0},{2,3},{3,2},{4,5},{5,4},{6,7},{7,6},{8,9},{9,8},{10,11... | collective-permute-start | bytes 7077896 | tf_op jit(solution)/shard_map/ppermute | solution.py:635
  134.3 35.7 %collective-permute-start.24 = (bf16[384,3072]{1,0:T(8,128)(2,1)}, bf16[384,3072]{1,0:T(8,128)(2,1)}, u32[]{:S(2)}, u32[]{:S(2)}) collective-permute-start(bf16[384,3072]{1,0:T(8,128)(2,1)} %constant_dynamic-update-slice_fusion.18.p0), channel_id=1, source_target_pairs={{0,4},{1,3},{2,6},{3,1},{4,0},{5,7},{6,2},{7,5},{8,12},{9,11},{10,... | collective-permute-start | bytes 7077896 | tf_op jit(solution)/shard_map/ppermute | solution.py:631
  136.7 33.2 %collective-permute-start.26 = (bf16[384,1536]{1,0:T(8,128)(2,1)}, bf16[384,1536]{1,0:T(8,128)(2,1)S(1)}, u32[]{:S(2)}, u32[]{:S(2)}) collective-permute-start(bf16[384,1536]{1,0:T(8,128)(2,1)} %get-tuple-element.346), channel_id=1, source_target_pairs={{0,8},{1,9},{2,10},{3,11},{4,12},{5,13},{6,14},{7,15},{8,0},{9,1},... | collective-permute-start | bytes 3538952 | tf_op jit(solution)/shard_map/ppermute | solution.py:631
  171.1 29.2 %collective-permute-start.31 = (bf16[768,1536]{1,0:T(8,128)(2,1)}, bf16[768,1536]{1,0:T(8,128)(2,1)}, u32[]{:S(2)}, u32[]{:S(2)}) collective-permute-start(bf16[768,1536]{1,0:T(8,128)(2,1)} %constant_dynamic-update-slice_fusion.25.p0), channel_id=1, source_target_pairs={{0,4},{1,3},{2,6},{3,1},{4,0},{5,7},{6,2},{7,5},{8,12},{9,11},{10,... | collective-permute-start | bytes 7077896 | tf_op jit(solution)/shard_map/ppermute | solution.py:631
  172.6 44.2 %collective-permute-start.32 = (bf16[768,1536]{1,0:T(8,128)(2,1)}, bf16[768,1536]{1,0:T(8,128)(2,1)}, u32[]{:S(2)}, u32[]{:S(2)}) collective-permute-start(bf16[768,1536]{1,0:T(8,128)(2,1)} %constant_dynamic-update-slice_fusion.25.p0), channel_id=1, source_target_pairs={{0,1},{1,0},{2,3},{3,2},{4,5},{5,4},{6,7},{7,6},{8,9},{9,8},{10,11... | collective-permute-start | bytes 7077896 | tf_op jit(solution)/shard_map/ppermute | solution.py:635
  216.8 21.2 %collective-permute-start.34 = (bf16[1536,1536]{1,0:T(8,128)(2,1)}, bf16[1536,1536]{1,0:T(8,128)(2,1)}, u32[]{:S(2)}, u32[]{:S(2)}) collective-permute-start(bf16[1536,1536]{1,0:T(8,128)(2,1)} %get-tuple-element.243), channel_id=1, source_target_pairs={{0,1},{1,0},{2,3},{3,2},{4,5},{5,4},{6,7},{7,6},{8,9},{9,8},{10,11... | collective-permute-start | bytes 14155784 | tf_op jit(solution)/shard_map/ppermute | solution.py:635
  241.1 29.0 %collective-permute-start.35 = (bf16[768,1536]{1,0:T(8,128)(2,1)S(1)}, bf16[768,1536]{1,0:T(8,128)(2,1)}, u32[]{:S(2)}, u32[]{:S(2)}) collective-permute-start(bf16[768,1536]{1,0:T(8,128)(2,1)S(1)} %add_convert_fusion.1), channel_id=1, source_target_pairs={{0,4},{1,3},{2,6},{3,1},{4,0},{5,7},{6,2},{7,5},{8,12},{9,11},{10,... | collective-permute-start | bytes 7077896 | tf_op jit(solution)/shard_map/ppermute | solution.py:631
  286.0 20.4 %collective-permute-start.36 = (bf16[768,3072]{1,0:T(8,128)(2,1)}, bf16[768,3072]{1,0:T(8,128)(2,1)S(1)}, u32[]{:S(2)}, u32[]{:S(2)}) collective-permute-start(bf16[768,3072]{1,0:T(8,128)(2,1)} %get-tuple-element.254), channel_id=1, source_target_pairs={{0,1},{1,0},{2,3},{3,2},{4,5},{5,4},{6,7},{7,6},{8,9},{9,8},{10,11... | collective-permute-start | bytes 14155784 | tf_op jit(solution)/shard_map/ppermute | solution.py:635
  305.1 53.8 %collective-permute-start.37 = (bf16[384,1536]{1,0:T(8,128)(2,1)}, bf16[384,1536]{1,0:T(8,128)(2,1)S(1)}, u32[]{:S(2)}, u32[]{:S(2)}) collective-permute-start(bf16[384,1536]{1,0:T(8,128)(2,1)} %add_convert_fusion.4), channel_id=1, source_target_pairs={{0,8},{1,9},{2,10},{3,11},{4,12},{5,13},{6,14},{7,15},{8,0},{9,1},... | collective-permute-start | bytes 3538952 | tf_op jit(solution)/shard_map/ppermute | solution.py:631
  308.5 50.5 %collective-permute-start.38 = (bf16[384,3072]{1,0:T(8,128)(2,1)S(1)}, bf16[384,3072]{1,0:T(8,128)(2,1)}, u32[]{:S(2)}, u32[]{:S(2)}) collective-permute-start(bf16[384,3072]{1,0:T(8,128)(2,1)S(1)} %add_convert_fusion), channel_id=1, source_target_pairs={{0,4},{1,3},{2,6},{3,1},{4,0},{5,7},{6,2},{7,5},{8,12},{9,11},{10,... | collective-permute-start | bytes 7077896 | tf_op jit(solution)/shard_map/ppermute | solution.py:631
  387.5 41.9 %collective-permute-start.42 = (bf16[96,1536]{1,0:T(8,128)(2,1)}, bf16[96,1536]{1,0:T(8,128)(2,1)}, u32[]{:S(2)}, u32[]{:S(2)}) collective-permute-start(bf16[96,1536]{1,0:T(8,128)(2,1)} %add_convert_fusion.14), channel_id=1, source_target_pairs={{0,16},{1,17},{2,18},{3,19},{4,20},{5,21},{6,22},{7,23},{8,24},{9,... | collective-permute-start | bytes 884744 | tf_op jit(solution)/shard_map/ppermute | solution.py:631
  393.0 36.4 %collective-permute-start.43 = (bf16[384,1536]{1,0:T(8,128)(2,1)S(1)}, bf16[384,1536]{1,0:T(8,128)(2,1)}, u32[]{:S(2)}, u32[]{:S(2)}) collective-permute-start(bf16[384,1536]{1,0:T(8,128)(2,1)S(1)} %add_convert_fusion.2), channel_id=1, source_target_pairs={{0,4},{1,3},{2,6},{3,1},{4,0},{5,7},{6,2},{7,5},{8,12},{9,11},{10,... | collective-permute-start | bytes 3538952 | tf_op jit(solution)/shard_map/ppermute | solution.py:631
  393.7 35.7 %collective-permute-start.41 = (bf16[192,3072]{1,0:T(8,128)(2,1)}, bf16[192,3072]{1,0:T(8,128)(2,1)}, u32[]{:S(2)}, u32[]{:S(2)}) collective-permute-start(bf16[192,3072]{1,0:T(8,128)(2,1)} %add_convert_fusion.3), channel_id=1, source_target_pairs={{0,8},{1,9},{2,10},{3,11},{4,12},{5,13},{6,14},{7,15},{8,0},{9,1},... | collective-permute-start | bytes 3538952 | tf_op jit(solution)/shard_map/ppermute | solution.py:631
  441.4 32.2 %collective-permute-start.45 = (bf16[768,1024]{1,0:T(8,128)(2,1)}, bf16[768,1024]{1,0:T(8,128)(2,1)}, u32[]{:S(2)}, u32[]{:S(2)}) collective-permute-start(bf16[768,1024]{1,0:T(8,128)(2,1)} %get-tuple-element.285), channel_id=1, source_target_pairs={{0,1},{1,0},{2,3},{3,2},{4,5},{5,4},{6,7},{7,6},{8,9},{9,8},{10,11... | collective-permute-start | bytes 4718600 | tf_op jit(solution)/shard_map/ppermute | solution.py:635
  443.8 29.8 %collective-permute-start.47 = (bf16[192,1536]{1,0:T(8,128)(2,1)}, bf16[192,1536]{1,0:T(8,128)(2,1)}, u32[]{:S(2)}, u32[]{:S(2)}) collective-permute-start(bf16[192,1536]{1,0:T(8,128)(2,1)} %add_convert_fusion.7), channel_id=1, source_target_pairs={{0,8},{1,9},{2,10},{3,11},{4,12},{5,13},{6,14},{7,15},{8,0},{9,1},... | collective-permute-start | bytes 1769480 | tf_op jit(solution)/shard_map/ppermute | solution.py:631
  446.8 23.7 %collective-permute-start.68 = (f32[96,1536]{1,0:T(8,128)S(1)}, f32[96,1536]{1,0:T(8,128)}, u32[]{:S(2)}, u32[]{:S(2)}) collective-permute-start(f32[96,1536]{1,0:T(8,128)S(1)} %convert_add_fusion.1), channel_id=1, source_target_pairs={{0,1},{1,0},{2,3},{3,2},{4,5},{5,4},{6,7},{7,6},{8,9},{9,8},{10,11... | collective-permute-start | bytes 1769480 | tf_op jit(solution)/shard_map/ppermute | solution.py:635
  449.4 24.3 %collective-permute-start.46 = (bf16[48,3072]{1,0:T(8,128)(2,1)}, bf16[48,3072]{1,0:T(8,128)(2,1)}, u32[]{:S(2)}, u32[]{:S(2)}) collective-permute-start(bf16[48,3072]{1,0:T(8,128)(2,1)} %add_convert_fusion.13), channel_id=1, source_target_pairs={{0,16},{1,17},{2,18},{3,19},{4,20},{5,21},{6,22},{7,23},{8,24},{9,... | collective-permute-start | bytes 884744 | tf_op jit(solution)/shard_map/ppermute | solution.py:631
  509.4 25.6 %collective-permute-start.61 = (bf16[48,1536]{1,0:T(8,128)(2,1)S(1)}, bf16[48,1536]{1,0:T(8,128)(2,1)S(1)}, u32[]{:S(2)}, u32[]{:S(2)}) collective-permute-start(bf16[48,1536]{1,0:T(8,128)(2,1)S(1)} %add_convert_fusion.17), channel_id=1, source_target_pairs={{0,16},{1,17},{2,18},{3,19},{4,20},{5,21},{6,22},{7,23},{8,24},{9,... | collective-permute-start | bytes 442376 | tf_op jit(solution)/shard_map/ppermute | solution.py:631
  (98 other events, 976.1 us)

commit v10 on v9

--- a/solution.py
+++ b/solution.py
@@ -950,7 +950,7 @@
         dgate_ref[rows] = (dz * y * (part + opened * (1.0 - part))).astype(BF16)
 
 
-def gate_back(cot, w, gate, y, gain, inverse, less, width=512):
+def gate_back(cot, w, gate, y, gain, inverse, less, width=256):
     count, model = cot.shape
     di = w.shape[0]
     part = pl.BlockSpec((count, width), lambda i: (0, i))

time: 555 us -> 556 us (level)
  no operation moved by 1% of the time
where the time goes in v10:
time: 556 us; the launch traced here: 549 us
  Pallas kernels  302 us (54%)
  other arithmetic  71 us (13%)
  starting transfers between devices  62.2 us (11%)
  local copies, waits for them, and re-layouts  45.7 us (8%)
  matrix products  41.7 us (8%)
  waiting for transfers between devices  24.1 us (4%)
    pallas_call x3, Pallas kernels, run_backward(): pl.pallas_call(functools.partial(backward_kernel, before is None, last, s...  104 us
    ppermute x48, starting transfers between devices, exchange(): return lax.ppermute(values, ('shard', 'rep'), pairs)  58.1 us
    pallas_call x5, Pallas kernels, weight_grad(): pl.pallas_call(functools.partial(weight_grad_kernel, block), grid_spec=pl...  57 us
    pallas_call x3, Pallas kernels, run_forward(): pl.pallas_call(functools.partial(forward_kernel, first_call, start * GROU...  47.2 us
    dot_general x6, matrix products, dot_f32(): lax.dot_general(a, b, ((contract[0], contract[1]), ((), ())), preferred_e...  41.7 us
    convert_element_type x20, other arithmetic, step(): send = self.rows(cut, 2 * cut).astype(BF16)  37.2 us
    pallas_call x3, Pallas kernels, project(): pl.pallas_call(functools.partial(project_kernel, block, width), grid_spec...  29.8 us
    pallas_call x1, Pallas kernels, gate_back(): pl.pallas_call(gate_back_kernel, grid_spec=pltpu.PrefetchScalarGridSpec(n...  23.2 us
  transfers between devices with their start and end apart: 69, of which 10 were waited for; matrix products, arithmetic and copies ran while one was open for 24% of the time, Pallas kernels for 50%

profile of v10, /device:TPU:0, one launch (start us, length us, event | category | flops | bytes accessed | tf_op | source)
XLA Modules:
  0.0 548.7 jit_solution(12239837211806255750)
XLA Ops:
  37.2 5.6 %collective-permute-done.5 = bf16[4,1328]{1,0:T(4,128)(2,1)S(1)} collective-permute-done((bf16[4,1328]{1,0:T(4,128)(2,1)S(1)}, bf16[4,1328]{1,0:T(4,128)(2,1)S(1)}, u32[]{:S(2)}, u32[]{:S(2)}) %collective-permute-start.5) | collective-permute-done | bytes 10656 | tf_op jit(solution)/shard_map/ppermute | solution.py:631
  53.7 5.7 %collective-permute-done.9 = bf16[8,1328]{1,0:T(8,128)(2,1)S(1)} collective-permute-done((bf16[8,1328]{1,0:T(8,128)(2,1)S(1)}, bf16[8,1328]{1,0:T(8,128)(2,1)S(1)}, u32[]{:S(2)}, u32[]{:S(2)}) %collective-permute-start.9) | collective-permute-done | bytes 21280 | tf_op jit(solution)/shard_map/ppermute | solution.py:631
  76.1 9.1 %project.3 = (f32[1024,1024]{1,0:T(8,128)}, bf16[1536,1024]{1,0:T(8,128)(2,1)}) custom-call(s32[32]{0:T(128)} %pad_add_fusion.order_ref, bf16[1024,1536]{1,0:T(8,128)(2,1)} %fusion.3.x_ref.lhs_ref, bf16[384,1024]{1,0:T(8,128)(2,1)} %pad_maximum_fusion.2.p0, bf16[384,1024]{1,0:T(8,128)(2,1)} %collective-permute-done.12.p1, ...), custom_call_target="tpu_custom_call" | custom-call | flops 3221225472 | bytes 13631488 | tf_op jit(solution)/shard_map/project/pallas_call | solution.py:773
  90.5 11.4 %scan_forward.3 = (bf16[1024,3072]{1,0:T(8,128)(2,1)}, bf16[1024,3072]{1,0:T(8,128)(2,1)}, bf16[512,3072]{1,0:T(8,128)(2,1)}, bf16[1024,3072]{1,0:T(8,128)(2,1)}...) custom-call(f32[1024,1024]{1,0:T(8,128)} %get-tuple-element.199.pc_r, ...), custom_call_target="tpu_custom_call" | custom-call | flops 5000000000 | bytes 7340032 | tf_op jit(solution)/shard_map/scan_forward/pallas_call | solution.py:229
  107.4 9.0 %project.4 = (f32[1024,1024]{1,0:T(8,128)}, bf16[1536,1024]{1,0:T(8,128)(2,1)}) custom-call(s32[32]{0:T(128)} %pad_add_fusion.order_ref, bf16[1024,1536]{1,0:T(8,128)(2,1)} %fusion.3.x_ref.lhs_ref, bf16[384,1024]{1,0:T(8,128)(2,1)} %constant_dynamic-update-slice_fusion.p0, bf16[384,1024]{1,0:T(8,128)(2,1)} %copy-done.48, ...), custom_call_target="tpu_custom_call" | custom-call | flops 3221225472 | bytes 13631488 | tf_op jit(solution)/shard_map/project/pallas_call | solution.py:773
  116.5 14.7 %scan_forward.4 = (bf16[1024,3072]{1,0:T(8,128)(2,1)}, bf16[1024,3072]{1,0:T(8,128)(2,1)}, bf16[512,3072]{1,0:T(8,128)(2,1)}, bf16[1024,3072]{1,0:T(8,128)(2,1)}, f32[8,128]{1,0:T(8,128)}) custom-call(f32[1024,1024]{1,0:T(8,128)} %get-tuple-element.212.pc_ref.halo_ref, ...), custom_call_target="tpu_custom_call", output_to_operand_aliasing={{0}: (11, {}), {1}: (12, {}), {2}: (13, {}), {3}: (14, {})} | custom-call | flops 10000000000 | bytes 14680064 | tf_op jit(solution)/shard_map/scan_forward/pallas_call | solution.py:229
  137.6 11.7 %project.5 = (f32[1024,1536]{1,0:T(8,128)}, bf16[1536,1536]{1,0:T(8,128)(2,1)}) custom-call(s32[32]{0:T(128)} %pad_add_fusion.order_ref, bf16[1024,1536]{1,0:T(8,128)(2,1)} %fusion.3.x_ref.lhs_ref, bf16[384,1536]{1,0:T(8,128)(2,1)} %constant_dynamic-update-slice_fusion.14.p0, bf16[384,1536]{1,0:T(8,128)(2,1)} %collective-permute-done.27.p1, ...), custom_call_target="tpu_custom_call" | custom-call | flops 4831838208 | bytes 18874368 | tf_op jit(solution)/shard_map/project/pallas_call | solution.py:773
  149.3 21.1 %scan_forward.5 = (bf16[1024,3072]{1,0:T(8,128)(2,1)}, bf16[1024,3072]{1,0:T(8,128)(2,1)}, bf16[512,3072]{1,0:T(8,128)(2,1)}, bf16[1024,3072]{1,0:T(8,128)(2,1)}, f32[8,128]{1,0:T(8,128)}) custom-call(f32[1024,1536]{1,0:T(8,128)} %get-tuple-element.227.pc_ref.halo_ref, ...), custom_call_target="tpu_custom_call", output_to_operand_aliasing={{0}: (11, {}), {1}: (12, {}), {2}: (13, {}), {3}: (14, {})} | custom-call | flops 15000000512 | bytes 22020096 | tf_op jit(solution)/shard_map/scan_forward/pallas_call | solution.py:229
  175.3 20.9 %project_gate.1 = (bf16[1024,3072]{1,0:T(8,128)(2,1)}, bf16[1536,3072]{1,0:T(8,128)(2,1)}, bf16[1024,3072]{1,0:T(8,128)(2,1)}, f32[1024,128]{1,0:T(8,128)}) custom-call(s32[32]{0:T(128)} %pad_add_fusion.order_ref, bf16[1024,1536]{1,0:T(8,128)(2,1)} %fusion.3.x_ref.lhs_ref, bf16[384,3072]{1,0:T(8,128)(2,1)} %constant_dynamic-update-slice_fusion.18.p0, ...), custom_call_target="tpu_custom_call" | custom-call | flops 9663676416 | bytes 53477376 | tf_op jit(solution)/shard_map/project_gate/pallas_call | solution.py:827
  202.0 15.2 %weight_grad.5 = (bf16[1536,1536]{1,0:T(8,128)(2,1)}, bf16[1536,1536]{1,0:T(8,128)(2,1)}) custom-call(s32[32]{0:T(128)} %fusion.34.place_ref, bf16[1024,3072]{1,0:T(8,128)(2,1)} %get-tuple-element.244.lhs_ref.zg_ref, bf16[1024,1536]{1,0:T(8,128)(2,1)} %fusion.8.rhs_ref), custom_call_target="tpu_custom_call" | custom-call | flops 9663676416 | bytes 18874368 | tf_op jit(solution)/shard_map/weight_grad/pallas_call | solution.py:1022
  218.8 19.6 %project_out.1 = (bf16[3072,1536]{1,0:T(8,128)(2,1)}, bf16[1024,1536]{1,0:T(8,128)(2,1)}, f32[1024,1]{1,0:T(8,128)}) custom-call(s32[32]{0:T(128)} %pad_add_fusion.order_ref, bf16[1024,3072]{1,0:T(8,128)(2,1)} %get-tuple-element.244.lhs_ref.zg_ref, f32[1024,1]{1,0:T(8,128)} %copy.63.inverse_ref, bf16[1024,1536]{1,0:T(8,128)(2,1)} %tokens_ref, ...), custom_call_target="tpu_custom_call" | custom-call | flops 9663676416 | bytes 34603008 | tf_op jit(solution)/shard_map/project_out/pallas_call | solution.py:912
  243.2 23.2 %gate_back.1 = (bf16[1024,3072]{1,0:T(8,128)(2,1)}, bf16[1024,3072]{1,0:T(8,128)(2,1)}) custom-call(bf16[1024,1536]{1,0:T(8,128)(2,1)} %cot_ref.2, bf16[3072,1536]{1,0:T(8,128)(2,1)} %get-tuple-element.250.w_ref, bf16[1024,3072]{1,0:T(8,128)(2,1)} %get-tuple-element.251.gate_ref, bf16[1024,3072]{1,0:T(8,128)(2,1)} %get-tuple-element.237.y_ref, ...), custom_call_target="tpu_custom_call" | custom-call | flops 9663676416 | bytes 34603008 | tf_op jit(solution)/shard_map/gate_back/pallas_call | solution.py:959
  266.3 4.2 collective-permute-done.35
  270.5 15.9 %weight_grad.6 = (bf16[768,3072]{1,0:T(8,128)(2,1)}, bf16[768,3072]{1,0:T(8,128)(2,1)}) custom-call(s32[32]{0:T(128)} %fusion.34.place_ref, bf16[1024,1536]{1,0:T(8,128)(2,1)} %fusion.3.x_ref.lhs_ref, bf16[1024,3072]{1,0:T(8,128)(2,1)} %get-tuple-element.255.rhs_ref), custom_call_target="tpu_custom_call" | custom-call | flops 9663676416 | bytes 18874368 | tf_op jit(solution)/shard_map/weight_grad/pallas_call | solution.py:1022
  286.5 15.5 %fusion.47 = f32[1024,1536]{1,0:T(8,128)} fusion(bf16[1024,3072]{1,0:T(8,128)(2,1)} %get-tuple-element.255.rhs_ref, bf16[1536,3072]{1,0:T(8,128)(2,1)} %get-tuple-element.256), kind=kOutput, calls=%fused_computation.197 | convolution fusion | flops 9663676416 | bytes 22020096 | tf_op jit(solution)/shard_map/dot_general | solution.py:27
  309.7 49.5 %scan_backward.3 = (bf16[1024,1536]{1,0:T(8,128)(2,1)}, f32[5,8,1536]{2,1,0:T(8,128)}, f32[8,1536]{1,0:T(8,128)}, f32[1024,256]{1,0:T(8,128)}, f32[1024,256]{1,0...) custom-call(bf16[1024,3072]{1,0:T(8,128)(2,1)} %get-tuple-element.288.dy_ref, ...), custom_call_target="tpu_custom_call" | custom-call | flops 35999997952 | bytes 18874368 | tf_op jit(solution)/shard_map/scan_backward/pallas_call | solution.py:562
  362.2 9.9 %weight_grad.7 = (bf16[768,1536]{1,0:T(8,128)(2,1)}, bf16[768,1536]{1,0:T(8,128)(2,1)}) custom-call(s32[32]{0:T(128)} %fusion.34.place_ref, bf16[1024,1536]{1,0:T(8,128)(2,1)} %fusion.3.x_ref.lhs_ref, bf16[1024,1536]{1,0:T(8,128)(2,1)} %get-tuple-element.271.rhs_ref), custom_call_target="tpu_custom_call" | custom-call | flops 4831838208 | bytes 11010048 | tf_op jit(solution)/shard_map/weight_grad/pallas_call | solution.py:1022
  373.5 10.7 %convolution_add_fusion = f32[1024,1536]{1,0:T(8,128)} fusion(f32[1024,1536]{1,0:T(8,128)} %fusion.47, bf16[1024,1536]{1,0:T(8,128)(2,1)} %get-tuple-element.271.rhs_ref, bf16[1536,1536]{1,0:T(8,128)(2,1)} %get-tuple-element.272), kind=kOutput, calls=%fused_computation.18 | convolution fusion | flops 4833411072 | bytes 20447232 | tf_op jit(solution)/shard_map/dot_general | solution.py:27
  395.0 34.6 %scan_backward.4 = (bf16[1024,1024]{1,0:T(8,128)(2,1)}, f32[5,8,1024]{2,1,0:T(8,128)}, f32[8,1024]{1,0:T(8,128)}, f32[1024,256]{1,0:T(8,128)}, f32[1024,256]{1,0...) custom-call(bf16[1024,3072]{1,0:T(8,128)(2,1)} %get-tuple-element.288.dy_ref, ...), custom_call_target="tpu_custom_call" | custom-call | flops 24000000000 | bytes 12582912 | tf_op jit(solution)/shard_map/scan_backward/pallas_call | solution.py:562
  433.7 8.0 %weight_grad.8 = (bf16[768,1024]{1,0:T(8,128)(2,1)}, bf16[768,1024]{1,0:T(8,128)(2,1)}) custom-call(s32[32]{0:T(128)} %fusion.34.place_ref, bf16[1024,1536]{1,0:T(8,128)(2,1)} %fusion.3.x_ref.lhs_ref, bf16[1024,1024]{1,0:T(8,128)(2,1)} %get-tuple-element.308.rhs_ref), custom_call_target="tpu_custom_call" | custom-call | flops 3221225472 | bytes 8388608 | tf_op jit(solution)/shard_map/weight_grad/pallas_call | solution.py:1022
  451.0 20.0 %scan_backward.5 = (bf16[1024,1024]{1,0:T(8,128)(2,1)}, f32[5,8,512]{2,1,0:T(8,128)}, f32[8,512]{1,0:T(8,128)}, f32[5,8,256]{2,1,0:T(8,128)}, f32[2,8,128]{2,1,0:T(8,128)}) custom-call(bf16[1024,3072]{1,0:T(8,128)(2,1)} %get-tuple-element.288.dy_ref, bf16[1024,3072]{1,0:T(8,128)(2,1)} %get-tuple-element.262.x_ref, ...), custom_call_target="tpu_custom_call" | custom-call | flops 12000000000 | bytes 6291456 | tf_op jit(solution)/shard_map/scan_backward/pallas_call | solution.py:562
  477.5 8.1 %weight_grad.9 = (bf16[768,1024]{1,0:T(8,128)(2,1)}, bf16[768,1024]{1,0:T(8,128)(2,1)}) custom-call(s32[32]{0:T(128)} %fusion.34.place_ref, bf16[1024,1536]{1,0:T(8,128)(2,1)} %fusion.3.x_ref.lhs_ref, bf16[1024,1024]{1,0:T(8,128)(2,1)} %get-tuple-element.303.rhs_ref), custom_call_target="tpu_custom_call" | custom-call | flops 3221225472 | bytes 8388608 | tf_op jit(solution)/shard_map/weight_grad/pallas_call | solution.py:1022
  498.1 8.3 %convolution_add_fusion.1 = f32[1024,1536]{1,0:T(8,128)} fusion(f32[1024,1536]{1,0:T(8,128)} %convolution_add_fusion, bf16[1024,1024]{1,0:T(8,128)(2,1)S(1)} %copy-done.51, bf16[1536,1024]{1,0:T(8,128)(2,1)} %get-tuple-element.304), kind=kOutput, calls=%fused_computation.19 | convolution fusion | flops 3222798336 | bytes 17825792 | tf_op jit(solution)/shard_map/dot_general | solution.py:27
  515.9 6.9 %fusion.4 = (f32[1024]{0:T(1024)S(1)}, f32[1024,1536]{1,0:T(8,128)S(1)}) fusion(bf16[1024,1536]{1,0:T(8,128)(2,1)S(1)} %copy-done.2, f32[1024]{0:T(1024)S(1)} %copy-done.34, f32[1536]{0:T(1024)S(1)} %copy-done.36, f32[1024,1536]{1,0:T(8,128)} %convolution_add_fusion.1, bf16[1024,1024]{1,0:T(8,128)(2,1)} %get-tuple-element.308.rhs_ref, ...), kind=kOutput, calls=%fused_computation.9 | convolution fusion | flops 3230661632 | bytes 20985856 | tf_op jit(solution)/shard_map/dot_general | solution.py:27
  (394 shorter events, 187.9 us)
Async XLA Ops:
  62.2 23.1 %collective-permute-start.13 = (bf16[48,3072]{1,0:T(8,128)(2,1)S(1)}, bf16[48,3072]{1,0:T(8,128)(2,1)S(1)}, u32[]{:S(2)}, u32[]{:S(2)}) collective-permute-start(bf16[48,3072]{1,0:T(8,128)(2,1)S(1)} %copy-done.16), channel_id=1, source_target_pairs={{0,16},{1,17},{2,18},{3,19},{4,20},{5,21},{6,22},{7,23},{8,24},{9,... | collective-permute-start | bytes 884744 | tf_op jit(solution)/shard_map/ppermute | solution.py:631
  71.7 31.1 %collective-permute-start.18 = (bf16[192,1536]{1,0:T(8,128)(2,1)}, bf16[192,1536]{1,0:T(8,128)(2,1)S(1)}, u32[]{:S(2)}, u32[]{:S(2)}) collective-permute-start(bf16[192,1536]{1,0:T(8,128)(2,1)} %copy-done.32), channel_id=1, source_target_pairs={{0,8},{1,9},{2,10},{3,11},{4,12},{5,13},{6,14},{7,15},{8,0},{9,1},... | collective-permute-start | bytes 1769480 | tf_op jit(solution)/shard_map/ppermute | solution.py:631
  103.7 28.1 %collective-permute-start.21 = (bf16[192,1536]{1,0:T(8,128)(2,1)S(1)}, bf16[192,1536]{1,0:T(8,128)(2,1)S(1)}, u32[]{:S(2)}, u32[]{:S(2)}) collective-permute-start(bf16[192,1536]{1,0:T(8,128)(2,1)S(1)} %get-tuple-element.361), channel_id=1, source_target_pairs={{0,2},{1,5},{2,0},{3,7},{4,6},{5,1},{6,4},{7,3},{8,10},{9,13},{10,... | collective-permute-start | bytes 1769480 | tf_op jit(solution)/shard_map/ppermute | solution.py:631
  105.4 27.9 %collective-permute-start.20 = (bf16[192,3072]{1,0:T(8,128)(2,1)}, bf16[192,3072]{1,0:T(8,128)(2,1)S(1)}, u32[]{:S(2)}, u32[]{:S(2)}) collective-permute-start(bf16[192,3072]{1,0:T(8,128)(2,1)} %get-tuple-element.347), channel_id=1, source_target_pairs={{0,8},{1,9},{2,10},{3,11},{4,12},{5,13},{6,14},{7,15},{8,0},{9,1},... | collective-permute-start | bytes 3538952 | tf_op jit(solution)/shard_map/ppermute | solution.py:631
  106.9 24.3 %collective-permute-start.27 = (bf16[384,1536]{1,0:T(8,128)(2,1)}, bf16[384,1536]{1,0:T(8,128)(2,1)}, u32[]{:S(2)}, u32[]{:S(2)}) collective-permute-start(bf16[384,1536]{1,0:T(8,128)(2,1)} %constant_dynamic-update-slice_fusion.14.p0), channel_id=1, source_target_pairs={{0,4},{1,3},{2,6},{3,1},{4,0},{5,7},{6,2},{7,5},{8,12},{9,11},{10,... | collective-permute-start | bytes 3538952 | tf_op jit(solution)/shard_map/ppermute | solution.py:631
  116.4 21.1 %collective-permute-start.28 = (bf16[384,1536]{1,0:T(8,128)(2,1)}, bf16[384,1536]{1,0:T(8,128)(2,1)}, u32[]{:S(2)}, u32[]{:S(2)}) collective-permute-start(bf16[384,1536]{1,0:T(8,128)(2,1)} %constant_dynamic-update-slice_fusion.14.p0), channel_id=1, source_target_pairs={{0,1},{1,0},{2,3},{3,2},{4,5},{5,4},{6,7},{7,6},{8,9},{9,8},{10,11... | collective-permute-start | bytes 3538952 | tf_op jit(solution)/shard_map/ppermute | solution.py:635
  134.4 36.0 %collective-permute-start.25 = (bf16[384,3072]{1,0:T(8,128)(2,1)}, bf16[384,3072]{1,0:T(8,128)(2,1)}, u32[]{:S(2)}, u32[]{:S(2)}) collective-permute-start(bf16[384,3072]{1,0:T(8,128)(2,1)} %constant_dynamic-update-slice_fusion.18.p0), channel_id=1, source_target_pairs={{0,1},{1,0},{2,3},{3,2},{4,5},{5,4},{6,7},{7,6},{8,9},{9,8},{10,11... | collective-permute-start | bytes 7077896 | tf_op jit(solution)/shard_map/ppermute | solution.py:635
  134.4 36.0 %collective-permute-start.24 = (bf16[384,3072]{1,0:T(8,128)(2,1)}, bf16[384,3072]{1,0:T(8,128)(2,1)}, u32[]{:S(2)}, u32[]{:S(2)}) collective-permute-start(bf16[384,3072]{1,0:T(8,128)(2,1)} %constant_dynamic-update-slice_fusion.18.p0), channel_id=1, source_target_pairs={{0,4},{1,3},{2,6},{3,1},{4,0},{5,7},{6,2},{7,5},{8,12},{9,11},{10,... | collective-permute-start | bytes 7077896 | tf_op jit(solution)/shard_map/ppermute | solution.py:631
  136.9 33.5 %collective-permute-start.26 = (bf16[384,1536]{1,0:T(8,128)(2,1)}, bf16[384,1536]{1,0:T(8,128)(2,1)S(1)}, u32[]{:S(2)}, u32[]{:S(2)}) collective-permute-start(bf16[384,1536]{1,0:T(8,128)(2,1)} %get-tuple-element.346), channel_id=1, source_target_pairs={{0,8},{1,9},{2,10},{3,11},{4,12},{5,13},{6,14},{7,15},{8,0},{9,1},... | collective-permute-start | bytes 3538952 | tf_op jit(solution)/shard_map/ppermute | solution.py:631
  171.6 29.2 %collective-permute-start.31 = (bf16[768,1536]{1,0:T(8,128)(2,1)}, bf16[768,1536]{1,0:T(8,128)(2,1)}, u32[]{:S(2)}, u32[]{:S(2)}) collective-permute-start(bf16[768,1536]{1,0:T(8,128)(2,1)} %constant_dynamic-update-slice_fusion.25.p0), channel_id=1, source_target_pairs={{0,4},{1,3},{2,6},{3,1},{4,0},{5,7},{6,2},{7,5},{8,12},{9,11},{10,... | collective-permute-start | bytes 7077896 | tf_op jit(solution)/shard_map/ppermute | solution.py:631
  173.0 44.2 %collective-permute-start.32 = (bf16[768,1536]{1,0:T(8,128)(2,1)}, bf16[768,1536]{1,0:T(8,128)(2,1)}, u32[]{:S(2)}, u32[]{:S(2)}) collective-permute-start(bf16[768,1536]{1,0:T(8,128)(2,1)} %constant_dynamic-update-slice_fusion.25.p0), channel_id=1, source_target_pairs={{0,1},{1,0},{2,3},{3,2},{4,5},{5,4},{6,7},{7,6},{8,9},{9,8},{10,11... | collective-permute-start | bytes 7077896 | tf_op jit(solution)/shard_map/ppermute | solution.py:635
  217.2 21.2 %collective-permute-start.34 = (bf16[1536,1536]{1,0:T(8,128)(2,1)}, bf16[1536,1536]{1,0:T(8,128)(2,1)}, u32[]{:S(2)}, u32[]{:S(2)}) collective-permute-start(bf16[1536,1536]{1,0:T(8,128)(2,1)} %get-tuple-element.243), channel_id=1, source_target_pairs={{0,1},{1,0},{2,3},{3,2},{4,5},{5,4},{6,7},{7,6},{8,9},{9,8},{10,11... | collective-permute-start | bytes 14155784 | tf_op jit(solution)/shard_map/ppermute | solution.py:635
  241.5 29.0 %collective-permute-start.35 = (bf16[768,1536]{1,0:T(8,128)(2,1)S(1)}, bf16[768,1536]{1,0:T(8,128)(2,1)}, u32[]{:S(2)}, u32[]{:S(2)}) collective-permute-start(bf16[768,1536]{1,0:T(8,128)(2,1)S(1)} %add_convert_fusion.1), channel_id=1, source_target_pairs={{0,4},{1,3},{2,6},{3,1},{4,0},{5,7},{6,2},{7,5},{8,12},{9,11},{10,... | collective-permute-start | bytes 7077896 | tf_op jit(solution)/shard_map/ppermute | solution.py:631
  286.4 20.4 %collective-permute-start.36 = (bf16[768,3072]{1,0:T(8,128)(2,1)}, bf16[768,3072]{1,0:T(8,128)(2,1)S(1)}, u32[]{:S(2)}, u32[]{:S(2)}) collective-permute-start(bf16[768,3072]{1,0:T(8,128)(2,1)} %get-tuple-element.254), channel_id=1, source_target_pairs={{0,1},{1,0},{2,3},{3,2},{4,5},{5,4},{6,7},{7,6},{8,9},{9,8},{10,11... | collective-permute-start | bytes 14155784 | tf_op jit(solution)/shard_map/ppermute | solution.py:635
  305.6 53.7 %collective-permute-start.37 = (bf16[384,1536]{1,0:T(8,128)(2,1)}, bf16[384,1536]{1,0:T(8,128)(2,1)S(1)}, u32[]{:S(2)}, u32[]{:S(2)}) collective-permute-start(bf16[384,1536]{1,0:T(8,128)(2,1)} %add_convert_fusion.4), channel_id=1, source_target_pairs={{0,8},{1,9},{2,10},{3,11},{4,12},{5,13},{6,14},{7,15},{8,0},{9,1},... | collective-permute-start | bytes 3538952 | tf_op jit(solution)/shard_map/ppermute | solution.py:631
  309.0 50.3 %collective-permute-start.38 = (bf16[384,3072]{1,0:T(8,128)(2,1)S(1)}, bf16[384,3072]{1,0:T(8,128)(2,1)}, u32[]{:S(2)}, u32[]{:S(2)}) collective-permute-start(bf16[384,3072]{1,0:T(8,128)(2,1)S(1)} %add_convert_fusion), channel_id=1, source_target_pairs={{0,4},{1,3},{2,6},{3,1},{4,0},{5,7},{6,2},{7,5},{8,12},{9,11},{10,... | collective-permute-start | bytes 7077896 | tf_op jit(solution)/shard_map/ppermute | solution.py:631
  387.9 41.7 %collective-permute-start.42 = (bf16[96,1536]{1,0:T(8,128)(2,1)}, bf16[96,1536]{1,0:T(8,128)(2,1)}, u32[]{:S(2)}, u32[]{:S(2)}) collective-permute-start(bf16[96,1536]{1,0:T(8,128)(2,1)} %add_convert_fusion.14), channel_id=1, source_target_pairs={{0,16},{1,17},{2,18},{3,19},{4,20},{5,21},{6,22},{7,23},{8,24},{9,... | collective-permute-start | bytes 884744 | tf_op jit(solution)/shard_map/ppermute | solution.py:631
  393.4 36.2 %collective-permute-start.43 = (bf16[384,1536]{1,0:T(8,128)(2,1)S(1)}, bf16[384,1536]{1,0:T(8,128)(2,1)}, u32[]{:S(2)}, u32[]{:S(2)}) collective-permute-start(bf16[384,1536]{1,0:T(8,128)(2,1)S(1)} %add_convert_fusion.2), channel_id=1, source_target_pairs={{0,4},{1,3},{2,6},{3,1},{4,0},{5,7},{6,2},{7,5},{8,12},{9,11},{10,... | collective-permute-start | bytes 3538952 | tf_op jit(solution)/shard_map/ppermute | solution.py:631
  394.1 35.5 %collective-permute-start.41 = (bf16[192,3072]{1,0:T(8,128)(2,1)}, bf16[192,3072]{1,0:T(8,128)(2,1)}, u32[]{:S(2)}, u32[]{:S(2)}) collective-permute-start(bf16[192,3072]{1,0:T(8,128)(2,1)} %add_convert_fusion.3), channel_id=1, source_target_pairs={{0,8},{1,9},{2,10},{3,11},{4,12},{5,13},{6,14},{7,15},{8,0},{9,1},... | collective-permute-start | bytes 3538952 | tf_op jit(solution)/shard_map/ppermute | solution.py:631
  441.7 32.6 %collective-permute-start.45 = (bf16[768,1024]{1,0:T(8,128)(2,1)}, bf16[768,1024]{1,0:T(8,128)(2,1)}, u32[]{:S(2)}, u32[]{:S(2)}) collective-permute-start(bf16[768,1024]{1,0:T(8,128)(2,1)} %get-tuple-element.285), channel_id=1, source_target_pairs={{0,1},{1,0},{2,3},{3,2},{4,5},{5,4},{6,7},{7,6},{8,9},{9,8},{10,11... | collective-permute-start | bytes 4718600 | tf_op jit(solution)/shard_map/ppermute | solution.py:635
  444.1 30.2 %collective-permute-start.47 = (bf16[192,1536]{1,0:T(8,128)(2,1)}, bf16[192,1536]{1,0:T(8,128)(2,1)}, u32[]{:S(2)}, u32[]{:S(2)}) collective-permute-start(bf16[192,1536]{1,0:T(8,128)(2,1)} %add_convert_fusion.7), channel_id=1, source_target_pairs={{0,8},{1,9},{2,10},{3,11},{4,12},{5,13},{6,14},{7,15},{8,0},{9,1},... | collective-permute-start | bytes 1769480 | tf_op jit(solution)/shard_map/ppermute | solution.py:631
  447.0 24.1 %collective-permute-start.68 = (f32[96,1536]{1,0:T(8,128)S(1)}, f32[96,1536]{1,0:T(8,128)}, u32[]{:S(2)}, u32[]{:S(2)}) collective-permute-start(f32[96,1536]{1,0:T(8,128)S(1)} %convert_add_fusion.1), channel_id=1, source_target_pairs={{0,1},{1,0},{2,3},{3,2},{4,5},{5,4},{6,7},{7,6},{8,9},{9,8},{10,11... | collective-permute-start | bytes 1769480 | tf_op jit(solution)/shard_map/ppermute | solution.py:635
  449.6 24.7 %collective-permute-start.46 = (bf16[48,3072]{1,0:T(8,128)(2,1)}, bf16[48,3072]{1,0:T(8,128)(2,1)}, u32[]{:S(2)}, u32[]{:S(2)}) collective-permute-start(bf16[48,3072]{1,0:T(8,128)(2,1)} %add_convert_fusion.13), channel_id=1, source_target_pairs={{0,16},{1,17},{2,18},{3,19},{4,20},{5,21},{6,22},{7,23},{8,24},{9,... | collective-permute-start | bytes 884744 | tf_op jit(solution)/shard_map/ppermute | solution.py:631
  509.9 25.8 %collective-permute-start.61 = (bf16[48,1536]{1,0:T(8,128)(2,1)S(1)}, bf16[48,1536]{1,0:T(8,128)(2,1)S(1)}, u32[]{:S(2)}, u32[]{:S(2)}) collective-permute-start(bf16[48,1536]{1,0:T(8,128)(2,1)S(1)} %add_convert_fusion.17), channel_id=1, source_target_pairs={{0,16},{1,17},{2,18},{3,19},{4,20},{5,21},{6,22},{7,23},{8,24},{9,... | collective-permute-start | bytes 442376 | tf_op jit(solution)/shard_map/ppermute | solution.py:631
  (98 other events, 976.2 us)
